TPU v7x, 32 devices: a whole 2x2x4 slice. The times are simulated.
32 devices in a mesh: sky: 8 (over z, y), band: 4 (over x, core).
Axes of the slice: x: 2, y: 2, z: 4, core: 2. Of those that a mesh axis runs over, the one named last changes fastest.
Arguments:
- exposures: bfloat16 [8, 4, 1024, 1024], P('sky', 'band'), may hold values from -6 to 6
- inv_variance: bfloat16 [8, 4, 1024, 1024], P('sky', 'band'), may hold values from 0.25 to 4
- mask_planes: int32 [8, 4, 2, 35], P('sky', 'band'), may hold values from 0 to 1073741823, as said below
- sky_columns: int32 [8, 4, 8], replicated, may hold values from 0 to 7, as said below
- basis_rows: float32 [9, 25], replicated, may hold values from -1 to 1
- basis_cols: float32 [9, 25], replicated, may hold values from -1 to 1
- match_coeffs: float32 [8, 4, 9], P('sky', 'band'), may hold values from -2 to 2
- detect_taps: float32 [4, 31], P('band'), may hold values from 0.05 to 0.3
Outputs:
- difference: bfloat16 [8, 4, 1024, 1024], P('sky', 'band')
- detection: float32 [1024, 1024], P('band', 'sky')
Inputs may be any that keep to these rules, and one draw needn't show every extreme that they name: Each row sky_columns[e, b] holds 8 consecutive sky tile columns in order, counted modulo 8; every sky tile column is covered by some exposure of every band. Bit j of mask_planes[e, b, 0, w] marks pixel column 30 w + j of that exposure as bad and bit j of mask_planes[e, b, 1, w] pixel row 30 w + j; bits past 1024 are ignored. In every draw some word has all 30 bits set.
All inputs are finite; a program needn't handle non-finite values.
Results may differ from a plain program's by a relative error of at most 0.0095.
Values may be sent and summed in bfloat16 or wider, within the bound.
No kernel may reach another device: no remote copies, remote signals or barrier semaphores. Data moves between devices by JAX's collectives and lax.ppermute only.
A program may use at most 128 MiB of HBM per device.

v0:
```python
import functools

import jax
import jax.numpy as jnp
from jax import lax
from jax.experimental import pallas as pl
from jax.experimental.pallas import tpu as pltpu
from jax.sharding import PartitionSpec as P


TILE = 128
NB = 9
TAPS = 25
DTAPS = 31
BITS = 30
EDGE = 16
WINDOW = TILE + 2 * EDGE
SHIFT = TILE // 2
CHUNKS = 2
START, OWN, OTHER, LINE, SKY, BAND = range(6)
F32 = jnp.float32
BF16 = jnp.bfloat16


def toeplitz(base_row, rows):
    wide = jnp.broadcast_to(base_row, (rows, base_row.shape[1]))
    return pltpu.roll(wide, 0, 1, stride=1, stride_axis=0)


def prepare_kernel(base_ref, column_ref, row_ref, across_ref, down_ref):
    for k in range(NB):
        column_ref[:, k * TILE : (k + 1) * TILE] = toeplitz(base_ref[k : k + 1, :], TILE).T.astype(BF16)
        row_ref[:, k * WINDOW : (k + 1) * WINDOW] = toeplitz(base_ref[NB + k : NB + k + 1, :], TILE)[
            :, :WINDOW
        ].astype(BF16)
    across_ref[...] = toeplitz(base_ref[2 * NB : 2 * NB + 1, :], TILE).T.astype(BF16)
    down_ref[...] = toeplitz(base_ref[2 * NB + 1 : 2 * NB + 2, :], TILE)[:, :WINDOW].astype(BF16)


def place_left(taps, offset):
    return jnp.pad(taps, ((0, 0), (offset, 2 * TILE - offset - taps.shape[1])))


def prepare(match_coeffs, basis_cols, basis_rows, detect_taps):
    column_taps = (match_coeffs[:, None] * basis_cols).astype(BF16).astype(F32)
    row_taps = basis_rows.astype(BF16).astype(F32)
    taps = detect_taps.astype(BF16).astype(F32)
    base = jnp.concatenate(
        [
            place_left(column_taps, SHIFT - TAPS // 2),
            place_left(row_taps, EDGE - TAPS // 2),
            place_left(taps, SHIFT - DTAPS // 2),
            place_left(taps, EDGE - DTAPS // 2),
        ],
        0,
    )
    return pl.pallas_call(
        prepare_kernel,
        out_shape=(
            jax.ShapeDtypeStruct((2 * TILE, NB * TILE), BF16),
            jax.ShapeDtypeStruct((TILE, NB * WINDOW), BF16),
            jax.ShapeDtypeStruct((2 * TILE, TILE), BF16),
            jax.ShapeDtypeStruct((TILE, WINDOW), BF16),
        ),
        compiler_params=pltpu.CompilerParams(vmem_limit_bytes=16 << 20),
        name="prepare",
    )(base)


def bad_bits(words_ref, plane, first_word, count, places):
    last = words_ref.shape[1] - 1
    word = jnp.full(places.shape, words_ref[plane, jnp.minimum(first_word, last)])
    begin = jnp.full(places.shape, first_word * BITS)
    for step in range(1, count):
        index = first_word + step
        reached = places >= index * BITS
        word = jnp.where(reached, words_ref[plane, jnp.minimum(index, last)], word)
        begin = jnp.where(reached, index * BITS, begin)
    return jnp.bitwise_and(jnp.right_shift(word, places - begin), 1)


def weight_kernel(sky_count, half_slot, half_blocks, meta_ref, words_ref, variance_ref, weight_ref):
    rows, side = variance_ref.shape
    first_row = (meta_ref[half_slot] * half_blocks + pl.program_id(0)) * rows
    lanes = lax.broadcasted_iota(jnp.int32, (8, side), 1)
    column_bad = bad_bits(words_ref, 0, 0, words_ref.shape[1], lanes)[0:1, :]
    places = first_row + lax.broadcasted_iota(jnp.int32, (rows, TILE), 0)
    row_bad = bad_bits(words_ref, 1, first_row // BITS, rows // BITS + 2, places)
    if sky_count * TILE != side:
        weight_ref[...] = jnp.zeros_like(weight_ref)
    for tile in range(side // TILE):
        window = slice(tile * TILE, (tile + 1) * TILE)
        bad = row_bad + column_bad[:, window]
        kept = jnp.where(bad == 0, variance_ref[:, window].astype(F32), 0.0)
        target = lax.rem(meta_ref[START] + tile, sky_count) * TILE
        weight_ref[:, pl.ds(pl.multiple_of(target, TILE), TILE)] = kept.astype(BF16)


def weigh(inv_variance, words, meta, half_slot, half_rows, sky_count):
    side = inv_variance.shape[0]
    rows = min(256, half_rows)
    blocks = half_rows // rows
    return pl.pallas_call(
        functools.partial(weight_kernel, sky_count, half_slot, blocks),
        out_shape=jax.ShapeDtypeStruct((half_rows, sky_count * TILE), BF16),
        grid_spec=pltpu.PrefetchScalarGridSpec(
            num_scalar_prefetch=2,
            grid=(blocks,),
            in_specs=[pl.BlockSpec((rows, side), lambda i, m, w: (m[half_slot] * blocks + i, 0))],
            out_specs=pl.BlockSpec((rows, sky_count * TILE), lambda i, m, w: (i, 0)),
        ),
        cost_estimate=pl.CostEstimate(flops=half_rows * side * 8, bytes_accessed=half_rows * side * 4, transcendentals=0),
        compiler_params=pltpu.CompilerParams(vmem_limit_bytes=20 << 20),
        name="weigh",
    )(meta, words, inv_variance)


def match_kernel(sky_count, half_slot, half_blocks, offset, meta_ref, picture_ref, column_ref, row_ref, weight_ref, matched_ref, product_ref, windows, stacked):
    side = picture_ref.shape[0]
    block = meta_ref[half_slot] * half_blocks + offset + pl.program_id(0)
    last_block = side // TILE - 1
    first = pl.multiple_of(block * TILE, TILE)
    nothing = jnp.zeros((TILE, SHIFT), BF16)

    def spread(values):
        edge = nothing[: values.shape[0]]
        return jnp.concatenate([edge, values, edge], axis=1)

    above = picture_ref[pl.ds(pl.multiple_of(jnp.maximum(first - EDGE, 0), EDGE), EDGE), :]
    below = picture_ref[pl.ds(pl.multiple_of(jnp.minimum(first + TILE, side - EDGE), EDGE), EDGE), :]
    tiles = side // TILE
    parts = (
        (0, spread(jnp.where(block > 0, above, jnp.zeros_like(above)))),
        (EDGE, spread(picture_ref[pl.ds(first, TILE), :])),
        (EDGE + TILE, spread(jnp.where(block < last_block, below, jnp.zeros_like(below)))),
    )
    for tile in range(tiles):
        for row, part in parts:
            row = tile * WINDOW + row
            windows[row : row + part.shape[0], :] = part[:, tile * TILE : (tile + 2) * TILE]
    for group in range(0, NB, 2):
        bands = range(group, min(group + 2, NB))
        passed = jnp.dot(
            windows[...], column_ref[:, group * TILE : (bands[-1] + 1) * TILE], preferred_element_type=F32
        ).astype(BF16)
        for k in bands:
            for tile in range(tiles):
                stacked[k * WINDOW : (k + 1) * WINDOW, tile * TILE : (tile + 1) * TILE] = passed[
                    tile * WINDOW : (tile + 1) * WINDOW, (k - group) * TILE : (k - group + 1) * TILE
                ]
    if sky_count != tiles:
        product_ref[...] = jnp.zeros_like(product_ref)
    for pair in range(tiles // 2):
        both = slice(pair * 2 * TILE, (pair + 1) * 2 * TILE)
        summed = jnp.dot(row_ref[...], stacked[:, both], preferred_element_type=F32).astype(BF16)
        matched_ref[:, both] = summed
        for part in range(2):
            target = pl.multiple_of(lax.rem(meta_ref[START] + 2 * pair + part, sky_count) * TILE, TILE)
            weight = weight_ref[:, pl.ds(target, TILE)].astype(F32)
            product = weight * summed[:, part * TILE : (part + 1) * TILE].astype(F32)
            product_ref[:, pl.ds(target, TILE)] = product.astype(BF16)


def match(picture, column_band, row_band, weight, meta, half_slot, chunk, half_rows, sky_count):
    side = picture.shape[0]
    chunk_rows = half_rows // CHUNKS
    steps = chunk_rows // TILE
    stripe = sky_count * TILE
    return pl.pallas_call(
        functools.partial(match_kernel, sky_count, half_slot, CHUNKS * steps, chunk * steps),
        out_shape=(
            jax.ShapeDtypeStruct((chunk_rows, side), BF16),
            jax.ShapeDtypeStruct((chunk_rows, stripe), BF16),
        ),
        grid_spec=pltpu.PrefetchScalarGridSpec(
            num_scalar_prefetch=1,
            grid=(steps,),
            in_specs=[
                pl.BlockSpec((side, side), lambda i, m: (0, 0)),
                pl.BlockSpec(column_band.shape, lambda i, m: (0, 0)),
                pl.BlockSpec(row_band.shape, lambda i, m: (0, 0)),
                pl.BlockSpec((TILE, stripe), lambda i, m: (chunk * steps + i, 0)),
            ],
            out_specs=(
                pl.BlockSpec((TILE, side), lambda i, m: (i, 0)),
                pl.BlockSpec((TILE, stripe), lambda i, m: (i, 0)),
            ),
            scratch_shapes=[
                pltpu.VMEM((side // TILE * WINDOW, 2 * TILE), BF16),
                pltpu.VMEM((NB * WINDOW, side), BF16),
            ],
        ),
        cost_estimate=pl.CostEstimate(
            flops=2 * chunk_rows * side * NB * (2 * TILE + WINDOW), bytes_accessed=chunk_rows * side * 8, transcendentals=0
        ),
        compiler_params=pltpu.CompilerParams(vmem_limit_bytes=28 << 20),
        name="match",
    )(meta, picture, column_band, row_band, weight)


def row_of(place, line, chunk_rows):
    row = 0
    for bit in range(line.bit_length() - 1):
        row = row + lax.rem(place >> bit, 2) * (chunk_rows >> (bit + 1))
    return row


def piece_rows(meta_ref, step, line, chunk_rows, part_rows):
    row = row_of(lax.rem(meta_ref[LINE] + line - step, line), line, chunk_rows)
    return pl.ds(pl.multiple_of(row, part_rows), part_rows)


def difference_kernel(sky_count, pair, line, meta_ref, *refs):
    matched = refs[:pair]
    pieces = refs[pair : pair + pair * line]
    out_ref = refs[-1]
    part_rows = pieces[0].shape[0]
    chunk_rows, side = matched[0].shape
    for group in range(pair):
        half = meta_ref[OWN + group]
        for step in range(line):
            rows = piece_rows(meta_ref, step, line, chunk_rows, part_rows)
            piece = pieces[group * line + step]
            for tile in range(side // TILE):
                window = slice(tile * TILE, (tile + 1) * TILE)
                source = pl.multiple_of(lax.rem(meta_ref[START] + tile, sky_count) * TILE, TILE)
                picked = piece[:, pl.ds(source, TILE)].astype(F32)
                out_ref[half, 0, rows, window] = (matched[group][rows, window].astype(F32) - picked).astype(BF16)


def subtract(matched, pieces, meta, chunk, before, sky_count):
    chunk_rows, side = matched[0].shape
    pair = len(matched)
    line = len(pieces) // pair
    operands = [*matched, *pieces]
    specs = [pl.BlockSpec(array.shape, lambda i, m: (0, 0)) for array in operands]
    aliases = {}
    if before is not None:
        operands.append(before)
        specs.append(pl.BlockSpec(memory_space=pl.ANY))
        aliases = {len(operands): 0}
    return pl.pallas_call(
        functools.partial(difference_kernel, sky_count, pair, line),
        out_shape=jax.ShapeDtypeStruct((pair, CHUNKS, chunk_rows, side), BF16),
        grid_spec=pltpu.PrefetchScalarGridSpec(
            num_scalar_prefetch=1,
            grid=(1,),
            in_specs=specs,
            out_specs=pl.BlockSpec((pair, 1, chunk_rows, side), lambda i, m: (0, chunk, 0, 0)),
        ),
        input_output_aliases=aliases,
        cost_estimate=pl.CostEstimate(
            flops=pair * chunk_rows * side, bytes_accessed=pair * chunk_rows * side * 6, transcendentals=0
        ),
        compiler_params=pltpu.CompilerParams(vmem_limit_bytes=24 << 20),
        name="subtract",
    )(meta, *operands)


def smooth_kernel(sky_count, pair, line, meta_ref, across_ref, *refs):
    pieces, out_ref = refs[:-1], refs[-1]
    part_rows = pieces[0].shape[0]
    chunk_rows = out_ref.shape[1]

    def column(piece, away):
        source = lax.rem(meta_ref[SKY] + away, sky_count) * TILE
        return piece[:, pl.ds(pl.multiple_of(source, TILE), TILE)]

    for group in range(pair):
        half = meta_ref[OWN + group]
        for step in range(line):
            rows = piece_rows(meta_ref, step, line, chunk_rows, part_rows)
            piece = pieces[group * line + step]
            window = jnp.concatenate(
                [column(piece, sky_count - 1)[:, SHIFT:], column(piece, 0), column(piece, 1)[:, :SHIFT]], axis=1
            )
            out_ref[half, rows, :] = jnp.dot(window, across_ref[...], preferred_element_type=F32).astype(BF16)


def smooth(pieces, across_band, meta, pair, chunk_rows, sky_count):
    line = len(pieces) // pair
    operands = [across_band, *pieces]
    return pl.pallas_call(
        functools.partial(smooth_kernel, sky_count, pair, line),
        out_shape=jax.ShapeDtypeStruct((pair, chunk_rows, TILE), BF16),
        grid_spec=pltpu.PrefetchScalarGridSpec(
            num_scalar_prefetch=1,
            grid=(1,),
            in_specs=[pl.BlockSpec(array.shape, lambda i, m: (0, 0)) for array in operands],
            out_specs=pl.BlockSpec((pair, chunk_rows, TILE), lambda i, m: (0, 0, 0)),
        ),
        cost_estimate=pl.CostEstimate(
            flops=pair * chunk_rows * TILE * 512, bytes_accessed=pair * chunk_rows * sky_count * TILE * 2, transcendentals=0
        ),
        compiler_params=pltpu.CompilerParams(vmem_limit_bytes=20 << 20),
        name="smooth",
    )(meta, *operands)


def power_kernel(band_count, meta_ref, down_ref, *refs):
    sources, powers, smoothed = refs[:CHUNKS], refs[CHUNKS : CHUNKS + band_count], refs[-1]
    pair, chunk_rows = sources[0].shape[:2]
    side = pair * CHUNKS * chunk_rows
    rows = side // band_count
    smoothed[0:EDGE, :] = jnp.zeros((EDGE, TILE), BF16)
    smoothed[EDGE + side :, :] = jnp.zeros((EDGE, TILE), BF16)
    for half in range(pair):
        for chunk in range(CHUNKS):
            first = EDGE + (half * CHUNKS + chunk) * chunk_rows
            smoothed[first : first + chunk_rows, :] = sources[chunk][half]
    for step in range(band_count):
        first = lax.rem(meta_ref[BAND] + step, band_count) * rows
        for inner in range(rows // TILE):
            source = pl.multiple_of(first + inner * TILE, TILE)
            filtered = jnp.dot(down_ref[...], smoothed[pl.ds(source, WINDOW), :], preferred_element_type=F32)
            powers[step][inner * TILE : (inner + 1) * TILE, :] = filtered * filtered


def power(sources, down_band, meta, band_count):
    side = CHUNKS * sources[0].shape[0] * sources[0].shape[1]
    return pl.pallas_call(
        functools.partial(power_kernel, band_count),
        out_shape=[jax.ShapeDtypeStruct((side // band_count, TILE), F32)] * band_count,
        grid_spec=pltpu.PrefetchScalarGridSpec(
            num_scalar_prefetch=1,
            grid=(1,),
            in_specs=[pl.BlockSpec(down_band.shape, lambda i, m: (0, 0))]
            + [pl.BlockSpec(array.shape, lambda i, m: (0, 0, 0)) for array in sources],
            out_specs=[pl.BlockSpec((side // band_count, TILE), lambda i, m: (0, 0))] * band_count,
            scratch_shapes=[pltpu.VMEM((side + 2 * EDGE, TILE), BF16)],
        ),
        cost_estimate=pl.CostEstimate(flops=side * TILE * 320, bytes_accessed=side * TILE * 6, transcendentals=0),
        compiler_params=pltpu.CompilerParams(vmem_limit_bytes=16 << 20),
        name="power",
    )(meta, down_band, *sources)


def body(exposures, inv_variance, mask_planes, sky_columns, basis_rows, basis_cols, match_coeffs, detect_taps):
    picture = exposures[0, 0]
    side = picture.shape[0]
    sky_count = lax.axis_size("sky")
    band_count = lax.axis_size("band")
    own_sky = lax.axis_index("sky")
    own_band = lax.axis_index("band")
    pair = 2
    line = sky_count // pair
    low = lax.rem(own_sky, pair)
    high = own_sky // pair
    half_rows = side // pair
    chunk_rows = half_rows // CHUNKS
    slots = jnp.arange(8, dtype=jnp.int32)
    meta = jnp.zeros((8,), jnp.int32)
    scalars = {START: sky_columns[own_sky, own_band, 0], OWN: low, OTHER: 1 - low, LINE: high, SKY: own_sky, BAND: own_band}
    for slot, value in scalars.items():
        meta = jnp.where(slots == slot, value, meta)

    def exchange(block, bit):
        return lax.ppermute(block, "sky", [(i, i ^ (1 << bit)) for i in range(sky_count)])

    def reduce_line(terms):
        rows = chunk_rows
        bit = 1
        while 1 << bit < sky_count:
            rows = rows // 2
            mine = lax.rem(own_sky >> bit, 2)
            leaving = sum(lax.dynamic_slice_in_dim(t, (1 - mine) * rows, rows, -2).astype(F32) for t in terms)
            arrived = exchange(leaving.astype(BF16), bit)
            terms = [lax.dynamic_slice_in_dim(t, mine * rows, rows, -2) for t in terms] + [arrived]
            bit += 1
        return sum(t.astype(F32) for t in terms)

    words = mask_planes[0, 0]
    variance = inv_variance[0, 0]
    weight_other = weigh(variance, words, meta, OTHER, half_rows, sky_count)
    weight_in = exchange(weight_other, 0)
    column_band, row_band, across_band, down_band = prepare(
        match_coeffs[0, 0], basis_cols, basis_rows, detect_taps
    )

    def matching(weight, half_slot, chunk):
        return match(picture, column_band, row_band, weight, meta, half_slot, chunk, half_rows, sky_count)

    away, product_in, home, product_own = ([None] * CHUNKS for _ in range(4))
    for c in range(CHUNKS):
        away[c], product = matching(weight_other, OTHER, c)
        product_in[c] = exchange(product, 0)
    weight_own = weigh(variance, words, meta, OWN, half_rows, sky_count)
    for c in range(CHUNKS):
        home[c], product_own[c] = matching(weight_own, OWN, c)

    by_chunk = (CHUNKS, chunk_rows, sky_count * TILE)
    denom = reduce_line([weight_own.reshape(by_chunk), weight_in.reshape(by_chunk)])
    shifts = [[(i, (i // pair + step) % line * pair + i % pair) for i in range(sky_count)] for step in range(line)]
    smoothed = [None] * CHUNKS
    difference = None
    for c in range(CHUNKS):
        numer = reduce_line([product_own[c], product_in[c]])
        if c:
            numer, _ = lax.optimization_barrier((numer, block))
        block = (numer / jnp.maximum(denom[c], 1.0)).astype(BF16)
        near, far = [block], []
        far.append(exchange(block, 0))
        for step in range(1, line):
            near.append(lax.ppermute(block, "sky", shifts[step]))
        for step in range(1, line):
            far.append(exchange(near[step], 0))
        pieces = near + far
        smoothed[c] = smooth(pieces, across_band, meta, pair, chunk_rows, sky_count)
        difference = subtract([home[c], away[c]], pieces, meta, c, difference, sky_count)

    powers = power(smoothed, down_band, meta, band_count)
    detection = powers[0]
    for step in range(1, band_count):
        ring = [(i, (i + step) % band_count) for i in range(band_count)]
        detection = detection + lax.ppermute(powers[step], "band", ring)
    return (difference.reshape(1, 1, side, side), detection)


def solution(mesh):
    in_specs = (
        P("sky", "band", None, None),
        P("sky", "band", None, None),
        P("sky", "band", None, None),
        P(),
        P(),
        P(),
        P("sky", "band", None),
        P("band", None),
    )
    out_specs = (P("sky", "band", None, None), P("band", "sky"))

    return jax.shard_map(body, mesh=mesh, in_specs=in_specs, out_specs=out_specs, check_vma=False)
```

profile of v0, /device:TPU:0, one launch (start us, length us, event | category | flops | bytes accessed | tf_op | source)
XLA Modules:
  0.0 136.7 jit_solution(4661111333085123469)
XLA Ops:
  0.7 0.7 copy-done
  1.4 0.5 constant_dynamic-slice_fusion
  1.9 0.6 compare_select_fusion.5.meta_ref
  2.5 1.6 %copy-done.1 = bf16[1,1,1024,1024]{3,2,1,0:T(8,128)(2,1)S(1)} copy-done((bf16[1,1,1024,1024]{3,2,1,0:T(8,128)(2,1)S(1)}, bf16[1,1,1024,1024]{3,2,1,0:T(8,128)(2,1)}, u32[]{:S(2)}) %copy-start.1) | copy-done | bytes 2097176
  4.1 0.7 copy-done.7
  4.8 2.2 %weigh.3.weight_ref = bf16[512,1024]{1,0:T(8,128)(2,1)} custom-call(s32[8]{0:T(128)S(1)} %compare_select_fusion.5.meta_ref, s32[2,35]{1,0:T(2,128)S(1)} %bitcast.25, bf16[1024,1024]{1,0:T(8,128)(2,1)S(1)} %bitcast.20), custom_call_target="tpu_custom_call" | custom-call | flops 4194304 | bytes 2097152 | tf_op jit(solution)/shard_map/weigh/pallas_call | solution.py:103
  7.0 3.0 %collective-permute-start.6 = (bf16[512,1024]{1,0:T(8,128)(2,1)}, bf16[512,1024]{1,0:T(8,128)(2,1)}, u32[]{:S(2)}, u32[]{:S(2)}) collective-permute-start(bf16[512,1024]{1,0:T(8,128)(2,1)} %weigh.3.weight_ref), channel_id=1, source_target_pairs={{0,4},{4,0},{8,12},{12,8},{16,20},{20,16},{24,28},{28,24},{1,5},{5... | collective-permute-start | bytes 3145736 | tf_op jit(solution)/shard_map/ppermute | solution.py:358
  10.3 1.1 prepare.1
  11.4 5.5 %match.5 = (bf16[256,1024]{1,0:T(8,128)(2,1)S(1)}, bf16[256,1024]{1,0:T(8,128)(2,1)}) custom-call(s32[8]{0:T(128)S(1)} %compare_select_fusion.5.meta_ref, bf16[1024,1024]{1,0:T(8,128)(2,1)S(1)} %bitcast.27, bf16[256,1152]{1,0:T(8,128)(2,1)S(1)} %get-tuple-element.19.column_ref, bf16[128,1440]{1,0:T(8,128)(2,1)S(1)} %get-tuple-element.20.row_ref, ...), custom_call_target="tpu_custom_call" | custom-call | flops 1962934272 | bytes 2097152 | tf_op jit(solution)/shard_map/match/pallas_call | solution.py:169
  16.9 0.8 copy-done.3
  17.7 5.5 %match.7 = (bf16[256,1024]{1,0:T(8,128)(2,1)S(1)}, bf16[256,1024]{1,0:T(8,128)(2,1)}) custom-call(s32[8]{0:T(128)S(1)} %compare_select_fusion.5.meta_ref, bf16[1024,1024]{1,0:T(8,128)(2,1)S(1)} %bitcast.28, bf16[256,1152]{1,0:T(8,128)(2,1)S(1)} %get-tuple-element.19.column_ref, bf16[128,1440]{1,0:T(8,128)(2,1)S(1)} %get-tuple-element.20.row_ref, ...), custom_call_target="tpu_custom_call" | custom-call | flops 1962934272 | bytes 2097152 | tf_op jit(solution)/shard_map/match/pallas_call | solution.py:169
  23.2 0.8 copy-done.5
  24.0 1.9 %collective-permute-start.3 = (bf16[256,1024]{1,0:T(8,128)(2,1)}, bf16[256,1024]{1,0:T(8,128)(2,1)}, u32[]{:S(2)}, u32[]{:S(2)}) collective-permute-start(bf16[256,1024]{1,0:T(8,128)(2,1)} %get-tuple-element.26), channel_id=1, source_target_pairs={{0,4},{4,0},{8,12},{12,8},{16,20},{20,16},{24,28},{28,24},{1,5},{5... | collective-permute-start | bytes 1572872 | tf_op jit(solution)/shard_map/ppermute | solution.py:358
  25.9 1.4 %weigh.2.weight_ref = bf16[512,1024]{1,0:T(8,128)(2,1)S(1)} custom-call(s32[8]{0:T(128)S(1)} %compare_select_fusion.5.meta_ref, s32[2,35]{1,0:T(2,128)S(1)} %bitcast.26, bf16[1024,1024]{1,0:T(8,128)(2,1)S(1)} %bitcast.21), custom_call_target="tpu_custom_call" | custom-call | flops 4194304 | bytes 2097152 | tf_op jit(solution)/shard_map/weigh/pallas_call | solution.py:103
  27.7 3.8 %match.4 = (bf16[256,1024]{1,0:T(8,128)(2,1)S(1)}, bf16[256,1024]{1,0:T(8,128)(2,1)S(1)}) custom-call(s32[8]{0:T(128)S(1)} %compare_select_fusion.5.meta_ref, bf16[1024,1024]{1,0:T(8,128)(2,1)S(1)} %bitcast.29, bf16[256,1152]{1,0:T(8,128)(2,1)S(1)} %copy-done.12, bf16[128,1440]{1,0:T(8,128)(2,1)S(1)} %copy-done.14, bf16[512,1024]{1,0:T(8,128)(2,1)S(1)} %weigh.2.weight_ref), custom_call_target="tpu_custom_call" | custom-call | flops 1962934272 | bytes 2097152 | tf_op jit(solution)/shard_map/match/pallas_call | solution.py:169
  31.5 2.8 %collective-permute-done.6 = bf16[512,1024]{1,0:T(8,128)(2,1)} collective-permute-done((bf16[512,1024]{1,0:T(8,128)(2,1)}, bf16[512,1024]{1,0:T(8,128)(2,1)}, u32[]{:S(2)}, u32[]{:S(2)}) %collective-permute-start.6) | collective-permute-done | bytes 1048608 | tf_op jit(solution)/shard_map/ppermute | solution.py:358
  34.3 2.0 %add_convert_fusion = bf16[2,128,1024]{2,1,0:T(8,128)(2,1)} fusion(bf16[2,256,1024]{2,1,0:T(8,128)(2,1)} %bitcast.6, s32[]{:T(128)S(6)} %select_n.87, bf16[2,256,1024]{2,1,0:T(8,128)(2,1)S(1)} %bitcast.22), kind=kLoop, calls=%fused_computation | loop fusion | flops 1048576 | bytes 1572868 | tf_op jit(solution)/shard_map/convert_element_type | solution.py:367
  36.4 2.1 %collective-permute-start.7 = (bf16[2,128,1024]{2,1,0:T(8,128)(2,1)}, bf16[2,128,1024]{2,1,0:T(8,128)(2,1)}, u32[]{:S(2)}, u32[]{:S(2)}) collective-permute-start(bf16[2,128,1024]{2,1,0:T(8,128)(2,1)} %add_convert_fusion), channel_id=1, source_target_pairs={{0,8},{4,12},{8,0},{12,4},{16,24},{20,28},{24,16},{28,20},{1,9},{5... | collective-permute-start | bytes 1572872 | tf_op jit(solution)/shard_map/ppermute | solution.py:358
  38.5 7.1 %collective-permute-done = bf16[256,1024]{1,0:T(8,128)(2,1)} collective-permute-done((bf16[256,1024]{1,0:T(8,128)(2,1)}, bf16[256,1024]{1,0:T(8,128)(2,1)}, u32[]{:S(2)}, u32[]{:S(2)}) %collective-permute-start) | collective-permute-done | bytes 524320 | tf_op jit(solution)/shard_map/ppermute | solution.py:358
  45.6 1.7 %add_convert_fusion.3 = bf16[128,1024]{1,0:T(8,128)(2,1)} fusion(bf16[256,1024]{1,0:T(8,128)(2,1)} %collective-permute-done, s32[]{:T(128)S(6)} %select_n.87, bf16[256,1024]{1,0:T(8,128)(2,1)S(1)} %get-tuple-element.23), kind=kLoop, calls=%fused_computation.4 | loop fusion | flops 524288 | bytes 786436 | tf_op jit(solution)/shard_map/convert_element_type | solution.py:367
  47.3 2.1 %collective-permute-start.1 = (bf16[128,1024]{1,0:T(8,128)(2,1)}, bf16[128,1024]{1,0:T(8,128)(2,1)}, u32[]{:S(2)}, u32[]{:S(2)}) collective-permute-start(bf16[128,1024]{1,0:T(8,128)(2,1)} %add_convert_fusion.3), channel_id=1, source_target_pairs={{0,8},{4,12},{8,0},{12,4},{16,24},{20,28},{24,16},{28,20},{1,9},{5... | collective-permute-start | bytes 786440 | tf_op jit(solution)/shard_map/ppermute | solution.py:358
  49.4 3.8 %match.6 = (bf16[256,1024]{1,0:T(8,128)(2,1)S(1)}, bf16[256,1024]{1,0:T(8,128)(2,1)S(1)}) custom-call(s32[8]{0:T(128)S(1)} %compare_select_fusion.5.meta_ref, bf16[1024,1024]{1,0:T(8,128)(2,1)S(1)} %bitcast.30, bf16[256,1152]{1,0:T(8,128)(2,1)S(1)} %copy-done.12, bf16[128,1440]{1,0:T(8,128)(2,1)S(1)} %copy-done.14, bf16[512,1024]{1,0:T(8,128)(2,1)S(1)} %weigh.2.weight_ref), custom_call_target="tpu_custom_call" | custom-call | flops 1962934272 | bytes 2097152 | tf_op jit(solution)/shard_map/match/pallas_call | solution.py:169
  53.2 2.8 %collective-permute-done.3 = bf16[256,1024]{1,0:T(8,128)(2,1)} collective-permute-done((bf16[256,1024]{1,0:T(8,128)(2,1)}, bf16[256,1024]{1,0:T(8,128)(2,1)}, u32[]{:S(2)}, u32[]{:S(2)}) %collective-permute-start.3) | collective-permute-done | bytes 524320 | tf_op jit(solution)/shard_map/ppermute | solution.py:358
  55.9 1.7 %add_convert_fusion.2 = bf16[128,1024]{1,0:T(8,128)(2,1)} fusion(bf16[256,1024]{1,0:T(8,128)(2,1)} %collective-permute-done.3, s32[]{:T(128)S(6)} %select_n.87, bf16[256,1024]{1,0:T(8,128)(2,1)S(1)} %get-tuple-element.25), kind=kLoop, calls=%fused_computation.3 | loop fusion | flops 524288 | bytes 786436 | tf_op jit(solution)/shard_map/convert_element_type | solution.py:367
  57.7 1.8 %collective-permute-start.4 = (bf16[128,1024]{1,0:T(8,128)(2,1)}, bf16[128,1024]{1,0:T(8,128)(2,1)}, u32[]{:S(2)}, u32[]{:S(2)}) collective-permute-start(bf16[128,1024]{1,0:T(8,128)(2,1)} %add_convert_fusion.2), channel_id=1, source_target_pairs={{0,8},{4,12},{8,0},{12,4},{16,24},{20,28},{24,16},{28,20},{1,9},{5... | collective-permute-start | bytes 786440 | tf_op jit(solution)/shard_map/ppermute | solution.py:358
  59.5 1.1 add_convert_fusion.5
  60.5 2.7 %collective-permute-start.2 = (bf16[64,1024]{1,0:T(8,128)(2,1)S(1)}, bf16[64,1024]{1,0:T(8,128)(2,1)S(1)}, u32[]{:S(2)}, u32[]{:S(2)}) collective-permute-start(bf16[64,1024]{1,0:T(8,128)(2,1)S(1)} %add_convert_fusion.5), channel_id=1, source_target_pairs={{0,16},{4,20},{8,24},{12,28},{16,0},{20,4},{24,8},{28,12},{1,17},{... | collective-permute-start | bytes 393224 | tf_op jit(solution)/shard_map/ppermute | solution.py:358
  63.2 1.2 add_convert_fusion.1
  64.8 4.0 %collective-permute-done.4 = bf16[128,1024]{1,0:T(8,128)(2,1)} collective-permute-done((bf16[128,1024]{1,0:T(8,128)(2,1)}, bf16[128,1024]{1,0:T(8,128)(2,1)}, u32[]{:S(2)}, u32[]{:S(2)}) %collective-permute-start.4) | collective-permute-done | bytes 262176 | tf_op jit(solution)/shard_map/ppermute | solution.py:358
  68.8 1.1 add_convert_fusion.4
  69.9 1.8 %collective-permute-start.5 = (bf16[64,1024]{1,0:T(8,128)(2,1)S(1)}, bf16[64,1024]{1,0:T(8,128)(2,1)S(1)}, u32[]{:S(2)}, u32[]{:S(2)}) collective-permute-start(bf16[64,1024]{1,0:T(8,128)(2,1)S(1)} %add_convert_fusion.4), channel_id=1, source_target_pairs={{0,16},{4,20},{8,24},{12,28},{16,0},{20,4},{24,8},{28,12},{1,17},{... | collective-permute-start | bytes 393224 | tf_op jit(solution)/shard_map/ppermute | solution.py:358
  71.7 1.1 convert_add_fusion.1
  72.7 11.3 %collective-permute-done.8 = bf16[2,64,1024]{2,1,0:T(8,128)(2,1)S(1)} collective-permute-done((bf16[2,64,1024]{2,1,0:T(8,128)(2,1)S(1)}, bf16[2,64,1024]{2,1,0:T(8,128)(2,1)S(1)}, u32[]{:S(2)}, u32[]{:S(2)}) %collective-permute-start.8) | collective-permute-done | bytes 262176 | tf_op jit(solution)/shard_map/ppermute | solution.py:358
  84.0 1.2 convert_add_fusion
  85.2 0.9 collective-permute-done.5
  86.1 1.1 fusion.5.refs_2_.refs_0_
  87.3 1.6 %collective-permute-start.12 = (bf16[64,1024]{1,0:T(8,128)(2,1)S(1)}, bf16[64,1024]{1,0:T(8,128)(2,1)S(1)}, u32[]{:S(2)}, u32[]{:S(2)}) collective-permute-start(bf16[64,1024]{1,0:T(8,128)(2,1)S(1)} %fusion.2.refs_2_.refs_0_), channel_id=1, source_target_pairs={{0,4},{4,0},{8,12},{12,8},{16,20},{20,16},{24,28},{28,24},{1,5},{5... | collective-permute-start | bytes 393224 | tf_op jit(solution)/shard_map/ppermute | solution.py:358
  88.9 1.7 %collective-permute-start.11 = (bf16[64,1024]{1,0:T(8,128)(2,1)S(1)}, bf16[64,1024]{1,0:T(8,128)(2,1)S(1)}, u32[]{:S(2)}, u32[]{:S(2)}) collective-permute-start(bf16[64,1024]{1,0:T(8,128)(2,1)S(1)} %fusion.2.refs_2_.refs_0_), channel_id=1, source_target_pairs={{0,24},{4,28},{8,0},{12,4},{16,8},{20,12},{24,16},{28,20},{1,25},{... | collective-permute-start | bytes 393224 | tf_op jit(solution)/shard_map/ppermute | solution.py:404
  90.5 0.6 collective-permute-start.9
  91.1 3.3 %collective-permute-start.18 = (bf16[64,1024]{1,0:T(8,128)(2,1)S(1)}, bf16[64,1024]{1,0:T(8,128)(2,1)S(1)}, u32[]{:S(2)}, u32[]{:S(2)}) collective-permute-start(bf16[64,1024]{1,0:T(8,128)(2,1)S(1)} %fusion.5.refs_2_.refs_0_), channel_id=1, source_target_pairs={{0,24},{4,28},{8,0},{12,4},{16,8},{20,12},{24,16},{28,20},{1,25},{... | collective-permute-start | bytes 393224 | tf_op jit(solution)/shard_map/ppermute | solution.py:404
  94.4 1.1 collective-permute-start.17
  95.5 1.9 %collective-permute-done.11.refs_5_.refs_3_ = bf16[64,1024]{1,0:T(8,128)(2,1)S(1)} collective-permute-done((bf16[64,1024]{1,0:T(8,128)(2,1)S(1)}, bf16[64,1024]{1,0:T(8,128)(2,1)S(1)}, u32[]{:S(2)}, u32[]{:S(2)}) %collective-permute-start.11) | collective-permute-done | bytes 131104 | tf_op jit(solution)/shard_map/ppermute | solution.py:404
  97.4 10.2 %collective-permute-done.10.refs_4_.refs_2_ = bf16[64,1024]{1,0:T(8,128)(2,1)S(1)} collective-permute-done((bf16[64,1024]{1,0:T(8,128)(2,1)S(1)}, bf16[64,1024]{1,0:T(8,128)(2,1)S(1)}, u32[]{:S(2)}, u32[]{:S(2)}) %collective-permute-start.10) | collective-permute-done | bytes 131104 | tf_op jit(solution)/shard_map/ppermute | solution.py:404
  108.1 1.5 %collective-permute-start.14 = (bf16[64,1024]{1,0:T(8,128)(2,1)S(1)}, bf16[64,1024]{1,0:T(8,128)(2,1)S(1)}, u32[]{:S(2)}, u32[]{:S(2)}) collective-permute-start(bf16[64,1024]{1,0:T(8,128)(2,1)S(1)} %collective-permute-done.10.refs_4_.refs_2_), channel_id=1, source_target_pairs={{0,4},{4,0},{8,12},{12,8},{16,20},{20,16},{24,28},{28,24},{1,5},{5... | collective-permute-start | bytes 393224 | tf_op jit(solution)/shard_map/ppermute | solution.py:358
  109.7 0.5 collective-permute-start.13
  110.2 1.6 %collective-permute-done.17.refs_4_.refs_2_ = bf16[64,1024]{1,0:T(8,128)(2,1)S(1)} collective-permute-done((bf16[64,1024]{1,0:T(8,128)(2,1)S(1)}, bf16[64,1024]{1,0:T(8,128)(2,1)S(1)}, u32[]{:S(2)}, u32[]{:S(2)}) %collective-permute-start.17) | collective-permute-done | bytes 131104 | tf_op jit(solution)/shard_map/ppermute | solution.py:404
  112.3 1.5 %collective-permute-start.22 = (bf16[64,1024]{1,0:T(8,128)(2,1)S(1)}, bf16[64,1024]{1,0:T(8,128)(2,1)S(1)}, u32[]{:S(2)}, u32[]{:S(2)}) collective-permute-start(bf16[64,1024]{1,0:T(8,128)(2,1)S(1)} %collective-permute-done.18.refs_5_.refs_3_), channel_id=1, source_target_pairs={{0,4},{4,0},{8,12},{12,8},{16,20},{20,16},{24,28},{28,24},{1,5},{5... | collective-permute-start | bytes 393224 | tf_op jit(solution)/shard_map/ppermute | solution.py:358
  113.8 0.5 collective-permute-start.21
  114.3 0.9 collective-permute-done.14.refs_8_.refs_6_
  115.2 0.8 collective-permute-start.20
  116.0 2.1 %collective-permute-done.13.refs_7_.refs_5_ = bf16[64,1024]{1,0:T(8,128)(2,1)S(1)} collective-permute-done((bf16[64,1024]{1,0:T(8,128)(2,1)S(1)}, bf16[64,1024]{1,0:T(8,128)(2,1)S(1)}, u32[]{:S(2)}, u32[]{:S(2)}) %collective-permute-start.13) | collective-permute-done | bytes 131104 | tf_op jit(solution)/shard_map/ppermute | solution.py:358
  118.0 0.8 smooth.3.refs_1_
  118.9 2.0 %collective-permute-done.19.refs_6_.refs_4_ = bf16[64,1024]{1,0:T(8,128)(2,1)S(1)} collective-permute-done((bf16[64,1024]{1,0:T(8,128)(2,1)S(1)}, bf16[64,1024]{1,0:T(8,128)(2,1)S(1)}, u32[]{:S(2)}, u32[]{:S(2)}) %collective-permute-start.19) | collective-permute-done | bytes 131104 | tf_op jit(solution)/shard_map/ppermute | solution.py:358
  120.9 2.8 %collective-permute-done.22.refs_9_.refs_7_ = bf16[64,1024]{1,0:T(8,128)(2,1)S(1)} collective-permute-done((bf16[64,1024]{1,0:T(8,128)(2,1)S(1)}, bf16[64,1024]{1,0:T(8,128)(2,1)S(1)}, u32[]{:S(2)}, u32[]{:S(2)}) %collective-permute-start.22) | collective-permute-done | bytes 131104 | tf_op jit(solution)/shard_map/ppermute | solution.py:358
  123.7 1.6 %collective-permute-done.21.refs_8_.refs_6_ = bf16[64,1024]{1,0:T(8,128)(2,1)S(1)} collective-permute-done((bf16[64,1024]{1,0:T(8,128)(2,1)S(1)}, bf16[64,1024]{1,0:T(8,128)(2,1)S(1)}, u32[]{:S(2)}, u32[]{:S(2)}) %collective-permute-start.21) | collective-permute-done | bytes 131104 | tf_op jit(solution)/shard_map/ppermute | solution.py:358
  125.2 1.4 %collective-permute-done.20.refs_7_.refs_5_ = bf16[64,1024]{1,0:T(8,128)(2,1)S(1)} collective-permute-done((bf16[64,1024]{1,0:T(8,128)(2,1)S(1)}, bf16[64,1024]{1,0:T(8,128)(2,1)S(1)}, u32[]{:S(2)}, u32[]{:S(2)}) %collective-permute-start.20) | collective-permute-done | bytes 131104 | tf_op jit(solution)/shard_map/ppermute | solution.py:358
  126.6 0.8 smooth.2.refs_0_
  127.5 0.8 power.1
  128.4 1.6 %collective-permute-start.24 = (f32[256,128]{1,0:T(8,128)S(1)}, f32[256,128]{1,0:T(8,128)S(1)}, u32[]{:S(2)}, u32[]{:S(2)}) collective-permute-start(f32[256,128]{1,0:T(8,128)S(1)} %get-tuple-element.34), channel_id=1, source_target_pairs={{0,2},{1,3},{2,0},{3,1},{4,6},{5,7},{6,4},{7,5},{8,10},{9,11},{10,... | collective-permute-start | bytes 393224 | tf_op jit(solution)/shard_map/ppermute | solution.py:415
  130.0 1.4 %collective-permute-start.25 = (f32[256,128]{1,0:T(8,128)S(1)}, f32[256,128]{1,0:T(8,128)S(1)}, u32[]{:S(2)}, u32[]{:S(2)}) collective-permute-start(f32[256,128]{1,0:T(8,128)S(1)} %get-tuple-element.35), channel_id=1, source_target_pairs={{0,3},{1,0},{2,1},{3,2},{4,7},{5,4},{6,5},{7,6},{8,11},{9,8},{10,9... | collective-permute-start | bytes 393224 | tf_op jit(solution)/shard_map/ppermute | solution.py:415
  131.4 1.9 %subtract.2.refs_10_ = bf16[2,2,256,1024]{3,2,1,0:T(8,128)(2,1)} custom-call(s32[8]{0:T(128)S(1)} %compare_select_fusion.5.meta_ref, bf16[256,1024]{1,0:T(8,128)(2,1)S(1)} %get-tuple-element.28.refs_0_, bf16[256,1024]{1,0:T(8,128)(2,1)S(1)} %copy-done.6, bf16[64,1024]{1,0:T(8,128)(2,1)S(1)} %fusion.5.refs_2_.refs_0_, ...), custom_call_target="tpu_custom_call" | custom-call | flops 524288 | bytes 3145728 | tf_op jit(solution)/shard_map/subtract/pallas_call | solution.py:242
  133.2 1.9 %subtract.3 = bf16[2,2,256,1024]{3,2,1,0:T(8,128)(2,1)} custom-call(s32[8]{0:T(128)S(1)} %compare_select_fusion.5.meta_ref, bf16[256,1024]{1,0:T(8,128)(2,1)S(1)} %get-tuple-element.21.refs_0_, bf16[256,1024]{1,0:T(8,128)(2,1)S(1)} %copy-done.4, bf16[64,1024]{1,0:T(8,128)(2,1)S(1)} %fusion.2.refs_2_.refs_0_, ...), custom_call_target="tpu_custom_call", output_to_operand_aliasing={{}: (11, {})} | custom-call | flops 524288 | bytes 3145728 | tf_op jit(solution)/shard_map/subtract/pallas_call | solution.py:242
  135.1 0.9 collective-permute-done.25
  136.0 0.7 add_add_fusion
  (56 shorter events, 2.2 us)
Async XLA Ops:
  0.6 0.7 copy-start
  0.6 9.4 %copy-start.17 = (f32[1,1,9]{2,1,0:T(1,128)S(1)}, f32[1,1,9]{2,1,0:T(1,128)}, u32[]{:S(2)}) copy-start(f32[1,1,9]{2,1,0:T(1,128)} %param.14) | copy-start | bytes 112
  0.7 9.4 %copy-start.16 = (f32[9,25]{1,0:T(8,128)S(1)}, f32[9,25]{1,0:T(8,128)}, u32[]{:S(2)}) copy-start(f32[9,25]{1,0:T(8,128)} %param.13) | copy-start | bytes 2704
  0.7 9.4 %copy-start.15 = (f32[9,25]{1,0:T(8,128)S(1)}, f32[9,25]{1,0:T(8,128)}, u32[]{:S(2)}) copy-start(f32[9,25]{1,0:T(8,128)} %param.12) | copy-start | bytes 2704
  0.7 9.5 %copy-start.18 = (f32[1,31]{1,0:T(1,128)S(1)}, f32[1,31]{1,0:T(1,128)}, u32[]{:S(2)}) copy-start(f32[1,31]{1,0:T(1,128)} %param.15) | copy-start | bytes 376
  2.5 1.6 %copy-start.1 = (bf16[1,1,1024,1024]{3,2,1,0:T(8,128)(2,1)S(1)}, bf16[1,1,1024,1024]{3,2,1,0:T(8,128)(2,1)}, u32[]{:S(2)}) copy-start(bf16[1,1,1024,1024]{3,2,1,0:T(8,128)(2,1)} %param.9) | copy-start | bytes 6291460
  4.1 0.7 copy-start.7
  4.8 6.6 %copy-start.9 = (bf16[1,1,1024,1024]{3,2,1,0:T(8,128)(2,1)S(1)}, bf16[1,1,1024,1024]{3,2,1,0:T(8,128)(2,1)}, u32[]{:S(2)}) copy-start(bf16[1,1,1024,1024]{3,2,1,0:T(8,128)(2,1)} %param.8) | copy-start | bytes 6291460
  7.0 27.3 %collective-permute-start.6 = (bf16[512,1024]{1,0:T(8,128)(2,1)}, bf16[512,1024]{1,0:T(8,128)(2,1)}, u32[]{:S(2)}, u32[]{:S(2)}) collective-permute-start(bf16[512,1024]{1,0:T(8,128)(2,1)} %weigh.3.weight_ref), channel_id=1, source_target_pairs={{0,4},{4,0},{8,12},{12,8},{16,20},{20,16},{24,28},{28,24},{1,5},{5... | collective-permute-start | bytes 3145736 | tf_op jit(solution)/shard_map/ppermute | solution.py:358
  11.3 6.3 %copy-start.11 = (bf16[256,1152]{1,0:T(8,128)(2,1)}, bf16[256,1152]{1,0:T(8,128)(2,1)S(1)}, u32[]{:S(2)}) copy-start(bf16[256,1152]{1,0:T(8,128)(2,1)S(1)} %get-tuple-element.19.column_ref) | copy-start | bytes 1769476
  11.3 6.3 %copy-start.13 = (bf16[128,1440]{1,0:T(8,128)(2,1)}, bf16[128,1440]{1,0:T(8,128)(2,1)S(1)}, u32[]{:S(2)}) copy-start(bf16[128,1440]{1,0:T(8,128)(2,1)S(1)} %get-tuple-element.20.row_ref) | copy-start | bytes 1105924
  16.8 0.8 copy-start.3
  17.6 8.3 %copy-start.2 = (bf16[1,1,1024,1024]{3,2,1,0:T(8,128)(2,1)S(1)}, bf16[1,1,1024,1024]{3,2,1,0:T(8,128)(2,1)}, u32[]{:S(2)}) copy-start(bf16[1,1,1024,1024]{3,2,1,0:T(8,128)(2,1)} %param.9) | copy-start | bytes 6291460
  17.6 8.3 %copy-start.8 = (s32[1,1,2,35]{3,2,1,0:T(2,128)S(1)}, s32[1,1,2,35]{3,2,1,0:T(2,128)}, u32[]{:S(2)}) copy-start(s32[1,1,2,35]{3,2,1,0:T(2,128)} %param.10) | copy-start | bytes 844
  17.6 27.9 %collective-permute-start = (bf16[256,1024]{1,0:T(8,128)(2,1)}, bf16[256,1024]{1,0:T(8,128)(2,1)}, u32[]{:S(2)}, u32[]{:S(2)}) collective-permute-start(bf16[256,1024]{1,0:T(8,128)(2,1)} %get-tuple-element.24), channel_id=1, source_target_pairs={{0,4},{4,0},{8,12},{12,8},{16,20},{20,16},{24,28},{28,24},{1,5},{5... | collective-permute-start | bytes 1572872 | tf_op jit(solution)/shard_map/ppermute | solution.py:358
  23.2 0.8 copy-start.5
  24.0 32.0 %collective-permute-start.3 = (bf16[256,1024]{1,0:T(8,128)(2,1)}, bf16[256,1024]{1,0:T(8,128)(2,1)}, u32[]{:S(2)}, u32[]{:S(2)}) collective-permute-start(bf16[256,1024]{1,0:T(8,128)(2,1)} %get-tuple-element.26), channel_id=1, source_target_pairs={{0,4},{4,0},{8,12},{12,8},{16,20},{20,16},{24,28},{28,24},{1,5},{5... | collective-permute-start | bytes 1572872 | tf_op jit(solution)/shard_map/ppermute | solution.py:358
  25.9 1.6 %copy-start.10 = (bf16[1,1,1024,1024]{3,2,1,0:T(8,128)(2,1)S(1)}, bf16[1,1,1024,1024]{3,2,1,0:T(8,128)(2,1)}, u32[]{:S(2)}) copy-start(bf16[1,1,1024,1024]{3,2,1,0:T(8,128)(2,1)} %param.8) | copy-start | bytes 6291460
  25.9 1.7 %copy-start.12 = (bf16[256,1152]{1,0:T(8,128)(2,1)S(1)}, bf16[256,1152]{1,0:T(8,128)(2,1)}, u32[]{:S(2)}) copy-start(bf16[256,1152]{1,0:T(8,128)(2,1)} %copy-done.11) | copy-start | bytes 1769476
  25.9 1.8 %copy-start.14 = (bf16[128,1440]{1,0:T(8,128)(2,1)S(1)}, bf16[128,1440]{1,0:T(8,128)(2,1)}, u32[]{:S(2)}) copy-start(bf16[128,1440]{1,0:T(8,128)(2,1)} %copy-done.13) | copy-start | bytes 1105924
  36.4 26.8 %collective-permute-start.7 = (bf16[2,128,1024]{2,1,0:T(8,128)(2,1)}, bf16[2,128,1024]{2,1,0:T(8,128)(2,1)}, u32[]{:S(2)}, u32[]{:S(2)}) collective-permute-start(bf16[2,128,1024]{2,1,0:T(8,128)(2,1)} %add_convert_fusion), channel_id=1, source_target_pairs={{0,8},{4,12},{8,0},{12,4},{16,24},{20,28},{24,16},{28,20},{1,9},{5... | collective-permute-start | bytes 1572872 | tf_op jit(solution)/shard_map/ppermute | solution.py:358
  47.3 12.2 %collective-permute-start.1 = (bf16[128,1024]{1,0:T(8,128)(2,1)}, bf16[128,1024]{1,0:T(8,128)(2,1)}, u32[]{:S(2)}, u32[]{:S(2)}) collective-permute-start(bf16[128,1024]{1,0:T(8,128)(2,1)} %add_convert_fusion.3), channel_id=1, source_target_pairs={{0,8},{4,12},{8,0},{12,4},{16,24},{20,28},{24,16},{28,20},{1,9},{5... | collective-permute-start | bytes 786440 | tf_op jit(solution)/shard_map/ppermute | solution.py:358
  57.7 11.1 %collective-permute-start.4 = (bf16[128,1024]{1,0:T(8,128)(2,1)}, bf16[128,1024]{1,0:T(8,128)(2,1)}, u32[]{:S(2)}, u32[]{:S(2)}) collective-permute-start(bf16[128,1024]{1,0:T(8,128)(2,1)} %add_convert_fusion.2), channel_id=1, source_target_pairs={{0,8},{4,12},{8,0},{12,4},{16,24},{20,28},{24,16},{28,20},{1,9},{5... | collective-permute-start | bytes 786440 | tf_op jit(solution)/shard_map/ppermute | solution.py:358
  60.5 11.1 %collective-permute-start.2 = (bf16[64,1024]{1,0:T(8,128)(2,1)S(1)}, bf16[64,1024]{1,0:T(8,128)(2,1)S(1)}, u32[]{:S(2)}, u32[]{:S(2)}) collective-permute-start(bf16[64,1024]{1,0:T(8,128)(2,1)S(1)} %add_convert_fusion.5), channel_id=1, source_target_pairs={{0,16},{4,20},{8,24},{12,28},{16,0},{20,4},{24,8},{28,12},{1,17},{... | collective-permute-start | bytes 393224 | tf_op jit(solution)/shard_map/ppermute | solution.py:358
  64.4 19.6 %collective-permute-start.8 = (bf16[2,64,1024]{2,1,0:T(8,128)(2,1)S(1)}, bf16[2,64,1024]{2,1,0:T(8,128)(2,1)S(1)}, u32[]{:S(2)}, u32[]{:S(2)}) collective-permute-start(bf16[2,64,1024]{2,1,0:T(8,128)(2,1)S(1)} %add_convert_fusion.1), channel_id=1, source_target_pairs={{0,16},{4,20},{8,24},{12,28},{16,0},{20,4},{24,8},{28,12},{1,17},{... | collective-permute-start | bytes 786440 | tf_op jit(solution)/shard_map/ppermute | solution.py:358
  69.9 16.3 %collective-permute-start.5 = (bf16[64,1024]{1,0:T(8,128)(2,1)S(1)}, bf16[64,1024]{1,0:T(8,128)(2,1)S(1)}, u32[]{:S(2)}, u32[]{:S(2)}) collective-permute-start(bf16[64,1024]{1,0:T(8,128)(2,1)S(1)} %add_convert_fusion.4), channel_id=1, source_target_pairs={{0,16},{4,20},{8,24},{12,28},{16,0},{20,4},{24,8},{28,12},{1,17},{... | collective-permute-start | bytes 393224 | tf_op jit(solution)/shard_map/ppermute | solution.py:358
  85.2 46.1 %copy-start.6 = (bf16[256,1024]{1,0:T(8,128)(2,1)S(1)}, bf16[256,1024]{1,0:T(8,128)(2,1)}, u32[]{:S(2)}) copy-start(bf16[256,1024]{1,0:T(8,128)(2,1)} %copy-done.5) | copy-start | bytes 1572868
  87.3 7.1 %collective-permute-start.12 = (bf16[64,1024]{1,0:T(8,128)(2,1)S(1)}, bf16[64,1024]{1,0:T(8,128)(2,1)S(1)}, u32[]{:S(2)}, u32[]{:S(2)}) collective-permute-start(bf16[64,1024]{1,0:T(8,128)(2,1)S(1)} %fusion.2.refs_2_.refs_0_), channel_id=1, source_target_pairs={{0,4},{4,0},{8,12},{12,8},{16,20},{20,16},{24,28},{28,24},{1,5},{5... | collective-permute-start | bytes 393224 | tf_op jit(solution)/shard_map/ppermute | solution.py:358
  88.9 8.5 %collective-permute-start.11 = (bf16[64,1024]{1,0:T(8,128)(2,1)S(1)}, bf16[64,1024]{1,0:T(8,128)(2,1)S(1)}, u32[]{:S(2)}, u32[]{:S(2)}) collective-permute-start(bf16[64,1024]{1,0:T(8,128)(2,1)S(1)} %fusion.2.refs_2_.refs_0_), channel_id=1, source_target_pairs={{0,24},{4,28},{8,0},{12,4},{16,8},{20,12},{24,16},{28,20},{1,25},{... | collective-permute-start | bytes 393224 | tf_op jit(solution)/shard_map/ppermute | solution.py:404
  90.5 17.1 %collective-permute-start.10 = (bf16[64,1024]{1,0:T(8,128)(2,1)S(1)}, bf16[64,1024]{1,0:T(8,128)(2,1)S(1)}, u32[]{:S(2)}, u32[]{:S(2)}) collective-permute-start(bf16[64,1024]{1,0:T(8,128)(2,1)S(1)} %fusion.2.refs_2_.refs_0_), channel_id=1, source_target_pairs={{0,16},{4,20},{8,24},{12,28},{16,0},{20,4},{24,8},{28,12},{1,17},{... | collective-permute-start | bytes 393224 | tf_op jit(solution)/shard_map/ppermute | solution.py:404
  90.5 17.6 %collective-permute-start.9 = (bf16[64,1024]{1,0:T(8,128)(2,1)S(1)}, bf16[64,1024]{1,0:T(8,128)(2,1)S(1)}, u32[]{:S(2)}, u32[]{:S(2)}) collective-permute-start(bf16[64,1024]{1,0:T(8,128)(2,1)S(1)} %fusion.2.refs_2_.refs_0_), channel_id=1, source_target_pairs={{0,8},{4,12},{8,16},{12,20},{16,24},{20,28},{24,0},{28,4},{1,9},{5... | collective-permute-start | bytes 393224 | tf_op jit(solution)/shard_map/ppermute | solution.py:404
  91.1 18.6 %collective-permute-start.18 = (bf16[64,1024]{1,0:T(8,128)(2,1)S(1)}, bf16[64,1024]{1,0:T(8,128)(2,1)S(1)}, u32[]{:S(2)}, u32[]{:S(2)}) collective-permute-start(bf16[64,1024]{1,0:T(8,128)(2,1)S(1)} %fusion.5.refs_2_.refs_0_), channel_id=1, source_target_pairs={{0,24},{4,28},{8,0},{12,4},{16,8},{20,12},{24,16},{28,20},{1,25},{... | collective-permute-start | bytes 393224 | tf_op jit(solution)/shard_map/ppermute | solution.py:404
  94.4 17.4 %collective-permute-start.17 = (bf16[64,1024]{1,0:T(8,128)(2,1)S(1)}, bf16[64,1024]{1,0:T(8,128)(2,1)S(1)}, u32[]{:S(2)}, u32[]{:S(2)}) collective-permute-start(bf16[64,1024]{1,0:T(8,128)(2,1)S(1)} %fusion.5.refs_2_.refs_0_), channel_id=1, source_target_pairs={{0,16},{4,20},{8,24},{12,28},{16,0},{20,4},{24,8},{28,12},{1,17},{... | collective-permute-start | bytes 393224 | tf_op jit(solution)/shard_map/ppermute | solution.py:404
  97.4 14.9 %collective-permute-start.16 = (bf16[64,1024]{1,0:T(8,128)(2,1)S(1)}, bf16[64,1024]{1,0:T(8,128)(2,1)S(1)}, u32[]{:S(2)}, u32[]{:S(2)}) collective-permute-start(bf16[64,1024]{1,0:T(8,128)(2,1)S(1)} %fusion.5.refs_2_.refs_0_), channel_id=1, source_target_pairs={{0,8},{4,12},{8,16},{12,20},{16,24},{20,28},{24,0},{28,4},{1,9},{5... | collective-permute-start | bytes 393224 | tf_op jit(solution)/shard_map/ppermute | solution.py:404
  107.6 6.2 %collective-permute-start.15 = (bf16[64,1024]{1,0:T(8,128)(2,1)S(1)}, bf16[64,1024]{1,0:T(8,128)(2,1)S(1)}, u32[]{:S(2)}, u32[]{:S(2)}) collective-permute-start(bf16[64,1024]{1,0:T(8,128)(2,1)S(1)} %collective-permute-done.11.refs_5_.refs_3_), channel_id=1, source_target_pairs={{0,4},{4,0},{8,12},{12,8},{16,20},{20,16},{24,28},{28,24},{1,5},{5... | collective-permute-start | bytes 393224 | tf_op jit(solution)/shard_map/ppermute | solution.py:358
  108.1 7.1 %collective-permute-start.14 = (bf16[64,1024]{1,0:T(8,128)(2,1)S(1)}, bf16[64,1024]{1,0:T(8,128)(2,1)S(1)}, u32[]{:S(2)}, u32[]{:S(2)}) collective-permute-start(bf16[64,1024]{1,0:T(8,128)(2,1)S(1)} %collective-permute-done.10.refs_4_.refs_2_), channel_id=1, source_target_pairs={{0,4},{4,0},{8,12},{12,8},{16,20},{20,16},{24,28},{28,24},{1,5},{5... | collective-permute-start | bytes 393224 | tf_op jit(solution)/shard_map/ppermute | solution.py:358
  109.7 8.4 %collective-permute-start.13 = (bf16[64,1024]{1,0:T(8,128)(2,1)S(1)}, bf16[64,1024]{1,0:T(8,128)(2,1)S(1)}, u32[]{:S(2)}, u32[]{:S(2)}) collective-permute-start(bf16[64,1024]{1,0:T(8,128)(2,1)S(1)} %collective-permute-done.9.refs_3_.refs_1_), channel_id=1, source_target_pairs={{0,4},{4,0},{8,12},{12,8},{16,20},{20,16},{24,28},{28,24},{1,5},{5... | collective-permute-start | bytes 393224 | tf_op jit(solution)/shard_map/ppermute | solution.py:358
  111.8 9.1 %collective-permute-start.19 = (bf16[64,1024]{1,0:T(8,128)(2,1)S(1)}, bf16[64,1024]{1,0:T(8,128)(2,1)S(1)}, u32[]{:S(2)}, u32[]{:S(2)}) collective-permute-start(bf16[64,1024]{1,0:T(8,128)(2,1)S(1)} %fusion.5.refs_2_.refs_0_), channel_id=1, source_target_pairs={{0,4},{4,0},{8,12},{12,8},{16,20},{20,16},{24,28},{28,24},{1,5},{5... | collective-permute-start | bytes 393224 | tf_op jit(solution)/shard_map/ppermute | solution.py:358
  112.3 11.4 %collective-permute-start.22 = (bf16[64,1024]{1,0:T(8,128)(2,1)S(1)}, bf16[64,1024]{1,0:T(8,128)(2,1)S(1)}, u32[]{:S(2)}, u32[]{:S(2)}) collective-permute-start(bf16[64,1024]{1,0:T(8,128)(2,1)S(1)} %collective-permute-done.18.refs_5_.refs_3_), channel_id=1, source_target_pairs={{0,4},{4,0},{8,12},{12,8},{16,20},{20,16},{24,28},{28,24},{1,5},{5... | collective-permute-start | bytes 393224 | tf_op jit(solution)/shard_map/ppermute | solution.py:358
  113.8 11.4 %collective-permute-start.21 = (bf16[64,1024]{1,0:T(8,128)(2,1)S(1)}, bf16[64,1024]{1,0:T(8,128)(2,1)S(1)}, u32[]{:S(2)}, u32[]{:S(2)}) collective-permute-start(bf16[64,1024]{1,0:T(8,128)(2,1)S(1)} %collective-permute-done.17.refs_4_.refs_2_), channel_id=1, source_target_pairs={{0,4},{4,0},{8,12},{12,8},{16,20},{20,16},{24,28},{28,24},{1,5},{5... | collective-permute-start | bytes 393224 | tf_op jit(solution)/shard_map/ppermute | solution.py:358
  115.2 11.4 %collective-permute-start.20 = (bf16[64,1024]{1,0:T(8,128)(2,1)S(1)}, bf16[64,1024]{1,0:T(8,128)(2,1)S(1)}, u32[]{:S(2)}, u32[]{:S(2)}) collective-permute-start(bf16[64,1024]{1,0:T(8,128)(2,1)S(1)} %collective-permute-done.16.refs_3_.refs_1_), channel_id=1, source_target_pairs={{0,4},{4,0},{8,12},{12,8},{16,20},{20,16},{24,28},{28,24},{1,5},{5... | collective-permute-start | bytes 393224 | tf_op jit(solution)/shard_map/ppermute | solution.py:358
  128.3 6.8 %collective-permute-start.23 = (f32[256,128]{1,0:T(8,128)S(1)}, f32[256,128]{1,0:T(8,128)S(1)}, u32[]{:S(2)}, u32[]{:S(2)}) collective-permute-start(f32[256,128]{1,0:T(8,128)S(1)} %get-tuple-element.33), channel_id=1, source_target_pairs={{0,1},{1,2},{2,3},{3,0},{4,5},{5,6},{6,7},{7,4},{8,9},{9,10},{10,1... | collective-permute-start | bytes 393224 | tf_op jit(solution)/shard_map/ppermute | solution.py:415
  128.4 6.7 %collective-permute-start.24 = (f32[256,128]{1,0:T(8,128)S(1)}, f32[256,128]{1,0:T(8,128)S(1)}, u32[]{:S(2)}, u32[]{:S(2)}) collective-permute-start(f32[256,128]{1,0:T(8,128)S(1)} %get-tuple-element.34), channel_id=1, source_target_pairs={{0,2},{1,3},{2,0},{3,1},{4,6},{5,7},{6,4},{7,5},{8,10},{9,11},{10,... | collective-permute-start | bytes 393224 | tf_op jit(solution)/shard_map/ppermute | solution.py:415
  130.0 6.0 %collective-permute-start.25 = (f32[256,128]{1,0:T(8,128)S(1)}, f32[256,128]{1,0:T(8,128)S(1)}, u32[]{:S(2)}, u32[]{:S(2)}) collective-permute-start(f32[256,128]{1,0:T(8,128)S(1)} %get-tuple-element.35), channel_id=1, source_target_pairs={{0,3},{1,0},{2,1},{3,2},{4,7},{5,4},{6,5},{7,6},{8,11},{9,8},{10,9... | collective-permute-start | bytes 393224 | tf_op jit(solution)/shard_map/ppermute | solution.py:415
  131.4 1.9 %copy-start.4 = (bf16[256,1024]{1,0:T(8,128)(2,1)S(1)}, bf16[256,1024]{1,0:T(8,128)(2,1)}, u32[]{:S(2)}) copy-start(bf16[256,1024]{1,0:T(8,128)(2,1)} %copy-done.3) | copy-start | bytes 1572868
where the time goes:
time: 138 us; the launch traced here: 137 us
  waiting for transfers between devices  54.2 us (39%)
  starting transfers between devices  32.8 us (24%)
  Pallas kernels  29.6 us (21%)
  other arithmetic  13.8 us (10%)
  local copies, waits for them, and re-layouts  5.43 us (4%)
    ppermute x17, waiting for transfers between devices, exchange(): lax.ppermute(block, 'sky', [(i, i ^ 1 << bit) for i in range(sky_count)])  39.5 us
    ppermute x17, starting transfers between devices, exchange(): lax.ppermute(block, 'sky', [(i, i ^ 1 << bit) for i in range(sky_count)])  23.2 us
    pallas_call x4, Pallas kernels, match(): pl.pallas_call(functools.partial(match_kernel, sky_count, half_slot, CHUN...  18.6 us
    ppermute x6, waiting for transfers between devices, body(): near.append(lax.ppermute(block, 'sky', shifts[step]))  13.8 us
    convert_element_type x6, other arithmetic, reduce_line(): arrived = exchange(leaving.astype(BF16), bit)  8.8 us
    ppermute x6, starting transfers between devices, body(): near.append(lax.ppermute(block, 'sky', shifts[step]))  6.61 us
    unnamed x38, local copies, waits for them, and re-layouts  4.91 us
    pallas_call x2, Pallas kernels, subtract(): pl.pallas_call(functools.partial(difference_kernel, sky_count, pair, line...  3.75 us
  transfers between devices with their start and end apart: 26, of which 16 were waited for; matrix products, arithmetic and copies ran while one was open for 8% of the time, Pallas kernels for 19%

commit v1 on v0

--- a/solution.py
+++ b/solution.py
@@ -79,9 +79,12 @@
     return jnp.bitwise_and(jnp.right_shift(word, places - begin), 1)
 
 
-def weight_kernel(sky_count, half_slot, half_blocks, meta_ref, words_ref, variance_ref, weight_ref):
+def weight_kernel(sky_count, halves, chunk, meta_ref, words_ref, variance_ref, weight_ref):
     rows, side = variance_ref.shape
-    first_row = (meta_ref[half_slot] * half_blocks + pl.program_id(0)) * rows
+    half = meta_ref[halves[0]]
+    for index in range(1, len(halves)):
+        half = jnp.where(pl.program_id(0) == index, meta_ref[halves[index]], half)
+    first_row = (half * CHUNKS + chunk) * rows
     lanes = lax.broadcasted_iota(jnp.int32, (8, side), 1)
     column_bad = bad_bits(words_ref, 0, 0, words_ref.shape[1], lanes)[0:1, :]
     places = first_row + lax.broadcasted_iota(jnp.int32, (rows, TILE), 0)
@@ -93,23 +96,31 @@
         bad = row_bad + column_bad[:, window]
         kept = jnp.where(bad == 0, variance_ref[:, window].astype(F32), 0.0)
         target = lax.rem(meta_ref[START] + tile, sky_count) * TILE
-        weight_ref[:, pl.ds(pl.multiple_of(target, TILE), TILE)] = kept.astype(BF16)
-
-
-def weigh(inv_variance, words, meta, half_slot, half_rows, sky_count):
+        weight_ref[0, :, pl.ds(pl.multiple_of(target, TILE), TILE)] = kept.astype(BF16)
+
+
+def weigh(inv_variance, words, meta, halves, chunk, rows, sky_count):
     side = inv_variance.shape[0]
-    rows = min(256, half_rows)
-    blocks = half_rows // rows
-    return pl.pallas_call(
-        functools.partial(weight_kernel, sky_count, half_slot, blocks),
-        out_shape=jax.ShapeDtypeStruct((half_rows, sky_count * TILE), BF16),
+    stripe = sky_count * TILE
+
+    def source(i, m, w):
+        half = m[halves[0]]
+        for index in range(1, len(halves)):
+            half = jnp.where(i == index, m[halves[index]], half)
+        return (half * CHUNKS + chunk, 0)
+
+    return pl.pallas_call(
+        functools.partial(weight_kernel, sky_count, halves, chunk),
+        out_shape=jax.ShapeDtypeStruct((len(halves), rows, stripe), BF16),
         grid_spec=pltpu.PrefetchScalarGridSpec(
             num_scalar_prefetch=2,
-            grid=(blocks,),
-            in_specs=[pl.BlockSpec((rows, side), lambda i, m, w: (m[half_slot] * blocks + i, 0))],
-            out_specs=pl.BlockSpec((rows, sky_count * TILE), lambda i, m, w: (i, 0)),
-        ),
-        cost_estimate=pl.CostEstimate(flops=half_rows * side * 8, bytes_accessed=half_rows * side * 4, transcendentals=0),
+            grid=(len(halves),),
+            in_specs=[pl.BlockSpec((rows, side), source)],
+            out_specs=pl.BlockSpec((1, rows, stripe), lambda i, m, w: (i, 0, 0)),
+        ),
+        cost_estimate=pl.CostEstimate(
+            flops=len(halves) * rows * side * 8, bytes_accessed=len(halves) * rows * side * 4, transcendentals=0
+        ),
         compiler_params=pltpu.CompilerParams(vmem_limit_bytes=20 << 20),
         name="weigh",
     )(meta, words, inv_variance)
@@ -161,7 +172,7 @@
             product_ref[:, pl.ds(target, TILE)] = product.astype(BF16)
 
 
-def match(picture, column_band, row_band, weight, meta, half_slot, chunk, half_rows, sky_count):
+def match(picture, column_band, row_band, weight, which, meta, half_slot, chunk, half_rows, sky_count):
     side = picture.shape[0]
     chunk_rows = half_rows // CHUNKS
     steps = chunk_rows // TILE
@@ -179,7 +190,7 @@
                 pl.BlockSpec((side, side), lambda i, m: (0, 0)),
                 pl.BlockSpec(column_band.shape, lambda i, m: (0, 0)),
                 pl.BlockSpec(row_band.shape, lambda i, m: (0, 0)),
-                pl.BlockSpec((TILE, stripe), lambda i, m: (chunk * steps + i, 0)),
+                pl.BlockSpec((None, TILE, stripe), lambda i, m: (which, i, 0)),
             ],
             out_specs=(
                 pl.BlockSpec((TILE, side), lambda i, m: (i, 0)),
@@ -367,37 +378,51 @@
             arrived = exchange(leaving.astype(BF16), bit)
             terms = [lax.dynamic_slice_in_dim(t, mine * rows, rows, -2) for t in terms] + [arrived]
             bit += 1
+        return terms
+
+    def total(terms):
         return sum(t.astype(F32) for t in terms)
 
     words = mask_planes[0, 0]
     variance = inv_variance[0, 0]
-    weight_other = weigh(variance, words, meta, OTHER, half_rows, sky_count)
-    weight_in = exchange(weight_other, 0)
+
+    def weighing(halves, chunk):
+        return weigh(variance, words, meta, halves, chunk, chunk_rows, sky_count)
+
+    def matching(weight, which, half_slot, chunk):
+        return match(
+            picture, column_band, row_band, weight, which, meta, half_slot, chunk, half_rows, sky_count
+        )
+
+    weight_other = weighing((OTHER,), 0)
+    weight_in = exchange(weight_other[0], 0)
+    weight_both = weighing((OTHER, OWN), 1)
+    both_terms = reduce_line([weight_both])
     column_band, row_band, across_band, down_band = prepare(
         match_coeffs[0, 0], basis_cols, basis_rows, detect_taps
     )
-
-    def matching(weight, half_slot, chunk):
-        return match(picture, column_band, row_band, weight, meta, half_slot, chunk, half_rows, sky_count)
+    weight_own = weighing((OWN,), 0)
 
     away, product_in, home, product_own = ([None] * CHUNKS for _ in range(4))
     for c in range(CHUNKS):
-        away[c], product = matching(weight_other, OTHER, c)
+        away[c], product = matching(weight_both if c else weight_other, 0, OTHER, c)
         product_in[c] = exchange(product, 0)
-    weight_own = weigh(variance, words, meta, OWN, half_rows, sky_count)
     for c in range(CHUNKS):
-        home[c], product_own[c] = matching(weight_own, OWN, c)
-
-    by_chunk = (CHUNKS, chunk_rows, sky_count * TILE)
-    denom = reduce_line([weight_own.reshape(by_chunk), weight_in.reshape(by_chunk)])
+        home[c], product_own[c] = matching(weight_both if c else weight_own, c, OWN, c)
+    both_in = exchange(total([t[0] for t in both_terms]).astype(BF16), 0)
+    denoms = [
+        total(reduce_line([weight_own[0], weight_in])),
+        total([t[1] for t in both_terms] + [both_in]),
+    ]
+
     shifts = [[(i, (i // pair + step) % line * pair + i % pair) for i in range(sky_count)] for step in range(line)]
     smoothed = [None] * CHUNKS
     difference = None
     for c in range(CHUNKS):
-        numer = reduce_line([product_own[c], product_in[c]])
+        numer = total(reduce_line([product_own[c], product_in[c]]))
         if c:
             numer, _ = lax.optimization_barrier((numer, block))
-        block = (numer / jnp.maximum(denom[c], 1.0)).astype(BF16)
+        block = (numer / jnp.maximum(denoms[c], 1.0)).astype(BF16)
         near, far = [block], []
         far.append(exchange(block, 0))
         for step in range(1, line):

time: 138 us -> 141 us (1.022)
  starting transfers between devices: 32.8 us -> 42.6 us
  waiting for transfers between devices: 54.2 us -> 45 us
  local copies, waits for them, and re-layouts: 5.43 us -> 7.08 us
    ppermute x6, waiting for transfers between devices: 13.8 us -> 7.12 us  [body(): near.append(lax.ppermute(block, 'sky', shifts[step]))]
    ppermute x17 -> x20, starting transfers between devices: 23.2 us -> 28.6 us  [exchange(): lax.ppermute(block, 'sky', [(i, i ^ 1 << bit) for i in range(sky_count)])]
    ppermute x6, starting transfers between devices: 6.61 us -> 10.9 us  [body(): near.append(lax.ppermute(block, 'sky', shifts[step]))]
    ppermute x17 -> x20, waiting for transfers between devices: 39.5 us -> 37 us  [exchange(): lax.ppermute(block, 'sky', [(i, i ^ 1 << bit) for i in range(sky_count)])]
    convert_element_type x2 -> x3, other arithmetic: 1.16 us -> 3.29 us  [the longest x2 2.32 us: body(): block = (numer / jnp.maximum(denoms[c], 1.0)).astype(BF16)]
    convert_element_type x6 -> x7, other arithmetic: 8.8 us -> 7.1 us  [reduce_line(): arrived = exchange(leaving.astype(BF16), bit)]
    unnamed x38 -> x34, local copies, waits for them, and re-layouts: 4.91 us -> 5.64 us
    pallas_call x2 -> x3, Pallas kernels: 3.61 us -> 4.12 us  [weigh(): pl.pallas_call(functools.partial(weight_kernel, sky_count, halves, chunk)...]
  transfers between devices with their start and end apart: 26 -> 29, of which waited for: 16 -> 14; matrix products, arithmetic and copies ran while one was open for 8% -> 8% of each run, Pallas kernels for 19% -> 14%
where the time goes in v1:
time: 141 us; the launch traced here: 140 us
  waiting for transfers between devices  45 us (32%)
  starting transfers between devices  42.6 us (30%)
  Pallas kernels  29.2 us (21%)
  other arithmetic  15 us (11%)
  local copies, waits for them, and re-layouts  7.08 us (5%)
    ppermute x20, waiting for transfers between devices, exchange(): lax.ppermute(block, 'sky', [(i, i ^ 1 << bit) for i in range(sky_count)])  37 us
    ppermute x20, starting transfers between devices, exchange(): lax.ppermute(block, 'sky', [(i, i ^ 1 << bit) for i in range(sky_count)])  28.6 us
    pallas_call x4, Pallas kernels, match(): pl.pallas_call(functools.partial(match_kernel, sky_count, half_slot, CHUN...  17.7 us
    ppermute x6, starting transfers between devices, body(): near.append(lax.ppermute(block, 'sky', shifts[step]))  10.9 us
    ppermute x6, waiting for transfers between devices, body(): near.append(lax.ppermute(block, 'sky', shifts[step]))  7.12 us
    convert_element_type x7, other arithmetic, reduce_line(): arrived = exchange(leaving.astype(BF16), bit)  7.1 us
    unnamed x34, local copies, waits for them, and re-layouts  5.64 us
    pallas_call x3, Pallas kernels, weigh(): pl.pallas_call(functools.partial(weight_kernel, sky_count, halves, chunk)...  4.12 us
  transfers between devices with their start and end apart: 29, of which 14 were waited for; matrix products, arithmetic and copies ran while one was open for 8% of the time, Pallas kernels for 14%

profile of v1, /device:TPU:0, one launch (start us, length us, event | category | flops | bytes accessed | tf_op | source)
XLA Modules:
  0.0 139.8 jit_solution(9296702315815708062)
XLA Ops:
  2.0 0.8 multiply_convert_fusion
  2.9 1.1 prepare.1
  5.3 1.6 %copy-done.1 = bf16[1,1,1024,1024]{3,2,1,0:T(8,128)(2,1)S(1)} copy-done((bf16[1,1,1024,1024]{3,2,1,0:T(8,128)(2,1)S(1)}, bf16[1,1,1024,1024]{3,2,1,0:T(8,128)(2,1)}, u32[]{:S(2)}) %copy-start.1) | copy-done | bytes 2097176
  7.6 1.8 %weigh.5.weight_ref = bf16[1,256,1024]{2,1,0:T(8,128)(2,1)} custom-call(s32[8]{0:T(128)S(1)} %compare_select_fusion.5.meta_ref, s32[2,35]{1,0:T(2,128)S(1)} %bitcast.29, bf16[1024,1024]{1,0:T(8,128)(2,1)S(1)} %bitcast.26), custom_call_target="tpu_custom_call" | custom-call | flops 2097152 | bytes 1048576 | tf_op jit(solution)/shard_map/weigh/pallas_call | solution.py:112
  9.3 5.5 %match.7 = (bf16[256,1024]{1,0:T(8,128)(2,1)S(1)}, bf16[256,1024]{1,0:T(8,128)(2,1)}) custom-call(s32[8]{0:T(128)S(1)} %compare_select_fusion.5.meta_ref, bf16[1024,1024]{1,0:T(8,128)(2,1)S(1)} %bitcast.32, bf16[256,1152]{1,0:T(8,128)(2,1)S(1)} %get-tuple-element.19.column_ref, bf16[128,1440]{1,0:T(8,128)(2,1)S(1)} %get-tuple-element.20.row_ref, ...), custom_call_target="tpu_custom_call" | custom-call | flops 1962934272 | bytes 2097152 | tf_op jit(solution)/shard_map/match/pallas_call | solution.py:180
  14.9 0.8 copy-done.5
  15.7 3.0 %collective-permute-start.3 = (bf16[256,1024]{1,0:T(8,128)(2,1)}, bf16[256,1024]{1,0:T(8,128)(2,1)}, u32[]{:S(2)}, u32[]{:S(2)}) collective-permute-start(bf16[256,1024]{1,0:T(8,128)(2,1)} %get-tuple-element.26), channel_id=1, source_target_pairs={{0,4},{4,0},{8,12},{12,8},{16,20},{20,16},{24,28},{28,24},{1,5},{5... | collective-permute-start | bytes 1572872 | tf_op jit(solution)/shard_map/ppermute | solution.py:369
  18.7 1.4 %weigh.3.weight_ref = bf16[2,256,1024]{2,1,0:T(8,128)(2,1)S(1)} custom-call(s32[8]{0:T(128)S(1)} %compare_select_fusion.5.meta_ref, s32[2,35]{1,0:T(2,128)S(1)} %bitcast.30, bf16[1024,1024]{1,0:T(8,128)(2,1)S(1)} %bitcast.27), custom_call_target="tpu_custom_call" | custom-call | flops 4194304 | bytes 2097152 | tf_op jit(solution)/shard_map/weigh/pallas_call | solution.py:112
  20.2 4.5 %match.5 = (bf16[256,1024]{1,0:T(8,128)(2,1)S(1)}, bf16[256,1024]{1,0:T(8,128)(2,1)}) custom-call(s32[8]{0:T(128)S(1)} %compare_select_fusion.5.meta_ref, bf16[1024,1024]{1,0:T(8,128)(2,1)S(1)} %bitcast.33, bf16[256,1152]{1,0:T(8,128)(2,1)S(1)} %copy-done.12, bf16[128,1440]{1,0:T(8,128)(2,1)S(1)} %copy-done.15, bf16[2,256,1024]{2,1,0:T(8,128)(2,1)S(1)} %weigh.3.weight_ref), custom_call_target="tpu_custom_call" | custom-call | flops 1962934272 | bytes 2097152 | tf_op jit(solution)/shard_map/match/pallas_call | solution.py:180
  24.7 0.8 copy-done.3
  25.5 2.0 %collective-permute-start = (bf16[256,1024]{1,0:T(8,128)(2,1)}, bf16[256,1024]{1,0:T(8,128)(2,1)}, u32[]{:S(2)}, u32[]{:S(2)}) collective-permute-start(bf16[256,1024]{1,0:T(8,128)(2,1)} %get-tuple-element.24), channel_id=1, source_target_pairs={{0,4},{4,0},{8,12},{12,8},{16,20},{20,16},{24,28},{28,24},{1,5},{5... | collective-permute-start | bytes 1572872 | tf_op jit(solution)/shard_map/ppermute | solution.py:369
  27.5 0.8 constant_dynamic-slice_fusion
  28.4 1.6 %collective-permute-start.9 = (bf16[2,128,1024]{2,1,0:T(8,128)(2,1)}, bf16[2,128,1024]{2,1,0:T(8,128)(2,1)}, u32[]{:S(2)}, u32[]{:S(2)}) collective-permute-start(bf16[2,128,1024]{2,1,0:T(8,128)(2,1)} %constant_dynamic-slice_fusion), channel_id=1, source_target_pairs={{0,8},{4,12},{8,0},{12,4},{16,24},{20,28},{24,16},{28,20},{1,9},{5... | collective-permute-start | bytes 1572872 | tf_op jit(solution)/shard_map/ppermute | solution.py:369
  30.0 1.0 weigh.4.weight_ref
  31.6 1.1 copy-done.13
  32.7 3.8 %match.4 = (bf16[256,1024]{1,0:T(8,128)(2,1)S(1)}, bf16[256,1024]{1,0:T(8,128)(2,1)S(1)}) custom-call(s32[8]{0:T(128)S(1)} %compare_select_fusion.5.meta_ref, bf16[1024,1024]{1,0:T(8,128)(2,1)S(1)} %bitcast.34, bf16[256,1152]{1,0:T(8,128)(2,1)S(1)} %copy-done.13, bf16[128,1440]{1,0:T(8,128)(2,1)S(1)} %copy-done.16, bf16[2,256,1024]{2,1,0:T(8,128)(2,1)S(1)} %weigh.3.weight_ref), custom_call_target="tpu_custom_call" | custom-call | flops 1962934272 | bytes 2097152 | tf_op jit(solution)/shard_map/match/pallas_call | solution.py:180
  36.5 3.8 %match.6 = (bf16[256,1024]{1,0:T(8,128)(2,1)S(1)}, bf16[256,1024]{1,0:T(8,128)(2,1)S(1)}) custom-call(s32[8]{0:T(128)S(1)} %compare_select_fusion.5.meta_ref, bf16[1024,1024]{1,0:T(8,128)(2,1)S(1)} %bitcast.35, bf16[256,1152]{1,0:T(8,128)(2,1)S(1)} %copy-done.13, bf16[128,1440]{1,0:T(8,128)(2,1)S(1)} %copy-done.16, bf16[1,256,1024]{2,1,0:T(8,128)(2,1)S(1)} %weigh.4.weight_ref), custom_call_target="tpu_custom_call" | custom-call | flops 1962934272 | bytes 2097152 | tf_op jit(solution)/shard_map/match/pallas_call | solution.py:180
  40.3 1.0 add_convert_fusion.1
  41.8 1.2 collective-permute-done.6
  43.0 1.0 fusion
  44.0 2.1 %collective-permute-start.7 = (bf16[128,1024]{1,0:T(8,128)(2,1)S(1)}, bf16[128,1024]{1,0:T(8,128)(2,1)S(1)}, u32[]{:S(2)}, u32[]{:S(2)}) collective-permute-start(bf16[128,1024]{1,0:T(8,128)(2,1)S(1)} %fusion), channel_id=1, source_target_pairs={{0,8},{4,12},{8,0},{12,4},{16,24},{20,28},{24,16},{28,20},{1,9},{5... | collective-permute-start | bytes 786440 | tf_op jit(solution)/shard_map/ppermute | solution.py:369
  46.2 7.2 %collective-permute-done = bf16[256,1024]{1,0:T(8,128)(2,1)} collective-permute-done((bf16[256,1024]{1,0:T(8,128)(2,1)}, bf16[256,1024]{1,0:T(8,128)(2,1)}, u32[]{:S(2)}, u32[]{:S(2)}) %collective-permute-start) | collective-permute-done | bytes 524320 | tf_op jit(solution)/shard_map/ppermute | solution.py:369
  53.4 1.0 add_convert_fusion.2
  54.4 1.8 %collective-permute-start.1 = (bf16[128,1024]{1,0:T(8,128)(2,1)S(1)}, bf16[128,1024]{1,0:T(8,128)(2,1)S(1)}, u32[]{:S(2)}, u32[]{:S(2)}) collective-permute-start(bf16[128,1024]{1,0:T(8,128)(2,1)S(1)} %add_convert_fusion.2), channel_id=1, source_target_pairs={{0,8},{4,12},{8,0},{12,4},{16,24},{20,28},{24,16},{28,20},{1,9},{5... | collective-permute-start | bytes 786440 | tf_op jit(solution)/shard_map/ppermute | solution.py:369
  56.3 1.1 add_convert_fusion
  57.3 2.7 %collective-permute-start.10 = (bf16[2,64,1024]{2,1,0:T(8,128)(2,1)S(1)}, bf16[2,64,1024]{2,1,0:T(8,128)(2,1)S(1)}, u32[]{:S(2)}, u32[]{:S(2)}) collective-permute-start(bf16[2,64,1024]{2,1,0:T(8,128)(2,1)S(1)} %add_convert_fusion), channel_id=1, source_target_pairs={{0,16},{4,20},{8,24},{12,28},{16,0},{20,4},{24,8},{28,12},{1,17},{... | collective-permute-start | bytes 786440 | tf_op jit(solution)/shard_map/ppermute | solution.py:369
  60.0 1.0 add_convert_fusion.4
  61.4 1.0 fusion.2
  62.4 2.7 %collective-permute-start.8 = (bf16[64,1024]{1,0:T(8,128)(2,1)S(1)}, bf16[64,1024]{1,0:T(8,128)(2,1)S(1)}, u32[]{:S(2)}, u32[]{:S(2)}) collective-permute-start(bf16[64,1024]{1,0:T(8,128)(2,1)S(1)} %fusion.2), channel_id=1, source_target_pairs={{0,16},{4,20},{8,24},{12,28},{16,0},{20,4},{24,8},{28,12},{1,17},{... | collective-permute-start | bytes 393224 | tf_op jit(solution)/shard_map/ppermute | solution.py:369
  65.1 1.4 collective-permute-done.1
  66.4 1.0 add_convert_fusion.5
  67.8 13.7 %collective-permute-done.10 = bf16[2,64,1024]{2,1,0:T(8,128)(2,1)S(1)} collective-permute-done((bf16[2,64,1024]{2,1,0:T(8,128)(2,1)S(1)}, bf16[2,64,1024]{2,1,0:T(8,128)(2,1)S(1)}, u32[]{:S(2)}, u32[]{:S(2)}) %collective-permute-start.10) | collective-permute-done | bytes 262176 | tf_op jit(solution)/shard_map/ppermute | solution.py:369
  81.5 1.0 fusion.11
  82.5 1.6 %collective-permute-start.11 = (bf16[64,1024]{1,0:T(8,128)(2,1)S(1)}, bf16[64,1024]{1,0:T(8,128)(2,1)S(1)}, u32[]{:S(2)}, u32[]{:S(2)}) collective-permute-start(bf16[64,1024]{1,0:T(8,128)(2,1)S(1)} %fusion.11), channel_id=1, source_target_pairs={{0,4},{4,0},{8,12},{12,8},{16,20},{20,16},{24,28},{28,24},{1,5},{5... | collective-permute-start | bytes 393224 | tf_op jit(solution)/shard_map/ppermute | solution.py:369
  84.1 3.6 %collective-permute-done.2 = bf16[64,1024]{1,0:T(8,128)(2,1)S(1)} collective-permute-done((bf16[64,1024]{1,0:T(8,128)(2,1)S(1)}, bf16[64,1024]{1,0:T(8,128)(2,1)S(1)}, u32[]{:S(2)}, u32[]{:S(2)}) %collective-permute-start.2) | collective-permute-done | bytes 131104 | tf_op jit(solution)/shard_map/ppermute | solution.py:369
  87.7 1.0 convert_add_fusion.3
  88.8 1.2 fusion.10.refs_2_.refs_0_
  90.0 1.1 fusion.9.refs_2_.refs_0_
  91.2 3.1 %collective-permute-start.13 = (bf16[64,1024]{1,0:T(8,128)(2,1)S(1)}, bf16[64,1024]{1,0:T(8,128)(2,1)S(1)}, u32[]{:S(2)}, u32[]{:S(2)}) collective-permute-start(bf16[64,1024]{1,0:T(8,128)(2,1)S(1)} %fusion.9.refs_2_.refs_0_), channel_id=1, source_target_pairs={{0,16},{4,20},{8,24},{12,28},{16,0},{20,4},{24,8},{28,12},{1,17},{... | collective-permute-start | bytes 393224 | tf_op jit(solution)/shard_map/ppermute | solution.py:429
  94.2 0.7 collective-permute-start.14
  95.0 1.5 %collective-permute-start.15 = (bf16[64,1024]{1,0:T(8,128)(2,1)S(1)}, bf16[64,1024]{1,0:T(8,128)(2,1)S(1)}, u32[]{:S(2)}, u32[]{:S(2)}) collective-permute-start(bf16[64,1024]{1,0:T(8,128)(2,1)S(1)} %fusion.9.refs_2_.refs_0_), channel_id=1, source_target_pairs={{0,4},{4,0},{8,12},{12,8},{16,20},{20,16},{24,28},{28,24},{1,5},{5... | collective-permute-start | bytes 393224 | tf_op jit(solution)/shard_map/ppermute | solution.py:369
  96.5 1.3 collective-permute-start.19
  97.8 1.7 %collective-permute-done.12.refs_3_.refs_1_ = bf16[64,1024]{1,0:T(8,128)(2,1)S(1)} collective-permute-done((bf16[64,1024]{1,0:T(8,128)(2,1)S(1)}, bf16[64,1024]{1,0:T(8,128)(2,1)S(1)}, u32[]{:S(2)}, u32[]{:S(2)}) %collective-permute-start.12) | collective-permute-done | bytes 131104 | tf_op jit(solution)/shard_map/ppermute | solution.py:429
  100.0 5.4 %collective-permute-done.13.refs_4_.refs_2_ = bf16[64,1024]{1,0:T(8,128)(2,1)S(1)} collective-permute-done((bf16[64,1024]{1,0:T(8,128)(2,1)S(1)}, bf16[64,1024]{1,0:T(8,128)(2,1)S(1)}, u32[]{:S(2)}, u32[]{:S(2)}) %collective-permute-start.13) | collective-permute-done | bytes 131104 | tf_op jit(solution)/shard_map/ppermute | solution.py:429
  105.4 5.3 %collective-permute-start.21 = (bf16[64,1024]{1,0:T(8,128)(2,1)S(1)}, bf16[64,1024]{1,0:T(8,128)(2,1)S(1)}, u32[]{:S(2)}, u32[]{:S(2)}) collective-permute-start(bf16[64,1024]{1,0:T(8,128)(2,1)S(1)} %fusion.10.refs_2_.refs_0_), channel_id=1, source_target_pairs={{0,24},{4,28},{8,0},{12,4},{16,8},{20,12},{24,16},{28,20},{1,25},{... | collective-permute-start | bytes 393224 | tf_op jit(solution)/shard_map/ppermute | solution.py:429
  110.7 1.5 %collective-permute-start.16 = (bf16[64,1024]{1,0:T(8,128)(2,1)S(1)}, bf16[64,1024]{1,0:T(8,128)(2,1)S(1)}, u32[]{:S(2)}, u32[]{:S(2)}) collective-permute-start(bf16[64,1024]{1,0:T(8,128)(2,1)S(1)} %collective-permute-done.12.refs_3_.refs_1_), channel_id=1, source_target_pairs={{0,4},{4,0},{8,12},{12,8},{16,20},{20,16},{24,28},{28,24},{1,5},{5... | collective-permute-start | bytes 393224 | tf_op jit(solution)/shard_map/ppermute | solution.py:369
  112.7 1.5 %collective-permute-start.18 = (bf16[64,1024]{1,0:T(8,128)(2,1)S(1)}, bf16[64,1024]{1,0:T(8,128)(2,1)S(1)}, u32[]{:S(2)}, u32[]{:S(2)}) collective-permute-start(bf16[64,1024]{1,0:T(8,128)(2,1)S(1)} %collective-permute-done.14.refs_5_.refs_3_), channel_id=1, source_target_pairs={{0,4},{4,0},{8,12},{12,8},{16,20},{20,16},{24,28},{28,24},{1,5},{5... | collective-permute-start | bytes 393224 | tf_op jit(solution)/shard_map/ppermute | solution.py:369
  114.7 1.5 %collective-permute-start.23 = (bf16[64,1024]{1,0:T(8,128)(2,1)S(1)}, bf16[64,1024]{1,0:T(8,128)(2,1)S(1)}, u32[]{:S(2)}, u32[]{:S(2)}) collective-permute-start(bf16[64,1024]{1,0:T(8,128)(2,1)S(1)} %collective-permute-done.19.refs_3_.refs_1_), channel_id=1, source_target_pairs={{0,4},{4,0},{8,12},{12,8},{16,20},{20,16},{24,28},{28,24},{1,5},{5... | collective-permute-start | bytes 393224 | tf_op jit(solution)/shard_map/ppermute | solution.py:369
  116.2 1.1 collective-permute-start.24
  117.4 1.2 collective-permute-done.17.refs_8_.refs_6_
  118.6 1.6 %collective-permute-start.25 = (bf16[64,1024]{1,0:T(8,128)(2,1)S(1)}, bf16[64,1024]{1,0:T(8,128)(2,1)S(1)}, u32[]{:S(2)}, u32[]{:S(2)}) collective-permute-start(bf16[64,1024]{1,0:T(8,128)(2,1)S(1)} %collective-permute-done.21.refs_5_.refs_3_), channel_id=1, source_target_pairs={{0,4},{4,0},{8,12},{12,8},{16,20},{20,16},{24,28},{28,24},{1,5},{5... | collective-permute-start | bytes 393224 | tf_op jit(solution)/shard_map/ppermute | solution.py:369
  120.2 1.2 collective-permute-done.18.refs_9_.refs_7_
  121.4 0.8 smooth.3.refs_1_
  122.3 2.0 %collective-permute-done.22.refs_6_.refs_4_ = bf16[64,1024]{1,0:T(8,128)(2,1)S(1)} collective-permute-done((bf16[64,1024]{1,0:T(8,128)(2,1)S(1)}, bf16[64,1024]{1,0:T(8,128)(2,1)S(1)}, u32[]{:S(2)}, u32[]{:S(2)}) %collective-permute-start.22) | collective-permute-done | bytes 131104 | tf_op jit(solution)/shard_map/ppermute | solution.py:369
  124.2 2.6 %collective-permute-done.23.refs_7_.refs_5_ = bf16[64,1024]{1,0:T(8,128)(2,1)S(1)} collective-permute-done((bf16[64,1024]{1,0:T(8,128)(2,1)S(1)}, bf16[64,1024]{1,0:T(8,128)(2,1)S(1)}, u32[]{:S(2)}, u32[]{:S(2)}) %collective-permute-start.23) | collective-permute-done | bytes 131104 | tf_op jit(solution)/shard_map/ppermute | solution.py:369
  126.9 1.4 %collective-permute-done.24.refs_8_.refs_6_ = bf16[64,1024]{1,0:T(8,128)(2,1)S(1)} collective-permute-done((bf16[64,1024]{1,0:T(8,128)(2,1)S(1)}, bf16[64,1024]{1,0:T(8,128)(2,1)S(1)}, u32[]{:S(2)}, u32[]{:S(2)}) %collective-permute-start.24) | collective-permute-done | bytes 131104 | tf_op jit(solution)/shard_map/ppermute | solution.py:369
  128.3 1.4 %collective-permute-done.25.refs_9_.refs_7_ = bf16[64,1024]{1,0:T(8,128)(2,1)S(1)} collective-permute-done((bf16[64,1024]{1,0:T(8,128)(2,1)S(1)}, bf16[64,1024]{1,0:T(8,128)(2,1)S(1)}, u32[]{:S(2)}, u32[]{:S(2)}) %collective-permute-start.25) | collective-permute-done | bytes 131104 | tf_op jit(solution)/shard_map/ppermute | solution.py:369
  129.7 0.8 smooth.2.refs_0_
  130.5 0.8 power.1
  131.4 1.6 %collective-permute-start.27 = (f32[256,128]{1,0:T(8,128)S(1)}, f32[256,128]{1,0:T(8,128)S(1)}, u32[]{:S(2)}, u32[]{:S(2)}) collective-permute-start(f32[256,128]{1,0:T(8,128)S(1)} %get-tuple-element.34), channel_id=1, source_target_pairs={{0,2},{1,3},{2,0},{3,1},{4,6},{5,7},{6,4},{7,5},{8,10},{9,11},{10,... | collective-permute-start | bytes 393224 | tf_op jit(solution)/shard_map/ppermute | solution.py:440
  133.1 1.4 collective-permute-start.28
  134.4 1.9 %subtract.2.refs_10_ = bf16[2,2,256,1024]{3,2,1,0:T(8,128)(2,1)} custom-call(s32[8]{0:T(128)S(1)} %compare_select_fusion.5.meta_ref, bf16[256,1024]{1,0:T(8,128)(2,1)S(1)} %get-tuple-element.28.refs_0_, bf16[256,1024]{1,0:T(8,128)(2,1)S(1)} %copy-done.6, bf16[64,1024]{1,0:T(8,128)(2,1)S(1)} %fusion.10.refs_2_.refs_0_, ...), custom_call_target="tpu_custom_call" | custom-call | flops 524288 | bytes 3145728 | tf_op jit(solution)/shard_map/subtract/pallas_call | solution.py:253
  136.3 1.9 %subtract.3 = bf16[2,2,256,1024]{3,2,1,0:T(8,128)(2,1)} custom-call(s32[8]{0:T(128)S(1)} %compare_select_fusion.5.meta_ref, bf16[256,1024]{1,0:T(8,128)(2,1)S(1)} %get-tuple-element.21.refs_0_, bf16[256,1024]{1,0:T(8,128)(2,1)S(1)} %copy-done.4, bf16[64,1024]{1,0:T(8,128)(2,1)S(1)} %fusion.9.refs_2_.refs_0_, ...), custom_call_target="tpu_custom_call", output_to_operand_aliasing={{}: (11, {})} | custom-call | flops 524288 | bytes 3145728 | tf_op jit(solution)/shard_map/subtract/pallas_call | solution.py:253
  138.2 0.9 collective-permute-done.28
  (61 shorter events, 7.9 us)
Async XLA Ops:
  0.6 3.4 %copy-start = (s32[8,4,8]{2,1,0:T(4,128)S(1)}, s32[8,4,8]{2,1,0:T(4,128)}, u32[]{:S(2)}) copy-start(s32[8,4,8]{2,1,0:T(4,128)} %param.11) | copy-start | bytes 3076
  4.0 10.9 %copy-start.11 = (bf16[256,1152]{1,0:T(8,128)(2,1)}, bf16[256,1152]{1,0:T(8,128)(2,1)S(1)}, u32[]{:S(2)}) copy-start(bf16[256,1152]{1,0:T(8,128)(2,1)S(1)} %get-tuple-element.19.column_ref) | copy-start | bytes 1769476
  4.0 10.9 %copy-start.14 = (bf16[128,1440]{1,0:T(8,128)(2,1)}, bf16[128,1440]{1,0:T(8,128)(2,1)S(1)}, u32[]{:S(2)}) copy-start(bf16[128,1440]{1,0:T(8,128)(2,1)S(1)} %get-tuple-element.20.row_ref) | copy-start | bytes 1105924
  5.3 1.6 %copy-start.1 = (bf16[1,1,1024,1024]{3,2,1,0:T(8,128)(2,1)S(1)}, bf16[1,1,1024,1024]{3,2,1,0:T(8,128)(2,1)}, u32[]{:S(2)}) copy-start(bf16[1,1,1024,1024]{3,2,1,0:T(8,128)(2,1)} %param.9) | copy-start | bytes 6291460
  6.9 0.7 copy-start.7
  7.6 1.8 %copy-start.9 = (bf16[1,1,1024,1024]{3,2,1,0:T(8,128)(2,1)S(1)}, bf16[1,1,1024,1024]{3,2,1,0:T(8,128)(2,1)}, u32[]{:S(2)}) copy-start(bf16[1,1,1024,1024]{3,2,1,0:T(8,128)(2,1)} %param.8) | copy-start | bytes 6291460
  9.3 9.4 %copy-start.2 = (bf16[1,1,1024,1024]{3,2,1,0:T(8,128)(2,1)S(1)}, bf16[1,1,1024,1024]{3,2,1,0:T(8,128)(2,1)}, u32[]{:S(2)}) copy-start(bf16[1,1,1024,1024]{3,2,1,0:T(8,128)(2,1)} %param.9) | copy-start | bytes 6291460
  9.3 9.4 %copy-start.8 = (s32[1,1,2,35]{3,2,1,0:T(2,128)S(1)}, s32[1,1,2,35]{3,2,1,0:T(2,128)}, u32[]{:S(2)}) copy-start(s32[1,1,2,35]{3,2,1,0:T(2,128)} %param.10) | copy-start | bytes 844
  14.9 0.8 copy-start.5
  15.7 4.5 %copy-start.12 = (bf16[256,1152]{1,0:T(8,128)(2,1)S(1)}, bf16[256,1152]{1,0:T(8,128)(2,1)}, u32[]{:S(2)}) copy-start(bf16[256,1152]{1,0:T(8,128)(2,1)} %copy-done.11) | copy-start | bytes 1769476
  15.7 4.5 %copy-start.15 = (bf16[128,1440]{1,0:T(8,128)(2,1)S(1)}, bf16[128,1440]{1,0:T(8,128)(2,1)}, u32[]{:S(2)}) copy-start(bf16[128,1440]{1,0:T(8,128)(2,1)} %copy-done.14) | copy-start | bytes 1105924
  15.7 24.6 %collective-permute-start.3 = (bf16[256,1024]{1,0:T(8,128)(2,1)}, bf16[256,1024]{1,0:T(8,128)(2,1)}, u32[]{:S(2)}, u32[]{:S(2)}) collective-permute-start(bf16[256,1024]{1,0:T(8,128)(2,1)} %get-tuple-element.26), channel_id=1, source_target_pairs={{0,4},{4,0},{8,12},{12,8},{16,20},{20,16},{24,28},{28,24},{1,5},{5... | collective-permute-start | bytes 1572872 | tf_op jit(solution)/shard_map/ppermute | solution.py:369
  18.7 24.3 %collective-permute-start.6 = (bf16[256,1024]{1,0:T(8,128)(2,1)}, bf16[256,1024]{1,0:T(8,128)(2,1)}, u32[]{:S(2)}, u32[]{:S(2)}) collective-permute-start(bf16[256,1024]{1,0:T(8,128)(2,1)} %bitcast.6), channel_id=1, source_target_pairs={{0,4},{4,0},{8,12},{12,8},{16,20},{20,16},{24,28},{28,24},{1,5},{5... | collective-permute-start | bytes 1572872 | tf_op jit(solution)/shard_map/ppermute | solution.py:369
  24.7 0.8 copy-start.3
  25.5 27.9 %collective-permute-start = (bf16[256,1024]{1,0:T(8,128)(2,1)}, bf16[256,1024]{1,0:T(8,128)(2,1)}, u32[]{:S(2)}, u32[]{:S(2)}) collective-permute-start(bf16[256,1024]{1,0:T(8,128)(2,1)} %get-tuple-element.24), channel_id=1, source_target_pairs={{0,4},{4,0},{8,12},{12,8},{16,20},{20,16},{24,28},{28,24},{1,5},{5... | collective-permute-start | bytes 1572872 | tf_op jit(solution)/shard_map/ppermute | solution.py:369
  28.4 27.9 %collective-permute-start.9 = (bf16[2,128,1024]{2,1,0:T(8,128)(2,1)}, bf16[2,128,1024]{2,1,0:T(8,128)(2,1)}, u32[]{:S(2)}, u32[]{:S(2)}) collective-permute-start(bf16[2,128,1024]{2,1,0:T(8,128)(2,1)} %constant_dynamic-slice_fusion), channel_id=1, source_target_pairs={{0,8},{4,12},{8,0},{12,4},{16,24},{20,28},{24,16},{28,20},{1,9},{5... | collective-permute-start | bytes 1572872 | tf_op jit(solution)/shard_map/ppermute | solution.py:369
  30.0 1.6 %copy-start.10 = (bf16[1,1,1024,1024]{3,2,1,0:T(8,128)(2,1)S(1)}, bf16[1,1,1024,1024]{3,2,1,0:T(8,128)(2,1)}, u32[]{:S(2)}) copy-start(bf16[1,1,1024,1024]{3,2,1,0:T(8,128)(2,1)} %param.8) | copy-start | bytes 6291460
  30.0 1.6 %copy-start.16 = (bf16[128,1440]{1,0:T(8,128)(2,1)S(1)}, bf16[128,1440]{1,0:T(8,128)(2,1)}, u32[]{:S(2)}) copy-start(bf16[128,1440]{1,0:T(8,128)(2,1)} %copy-done.14) | copy-start | bytes 1105924
  31.6 1.1 copy-start.13
  41.3 18.7 %collective-permute-start.4 = (bf16[128,1024]{1,0:T(8,128)(2,1)S(1)}, bf16[128,1024]{1,0:T(8,128)(2,1)S(1)}, u32[]{:S(2)}, u32[]{:S(2)}) collective-permute-start(bf16[128,1024]{1,0:T(8,128)(2,1)S(1)} %add_convert_fusion.1), channel_id=1, source_target_pairs={{0,8},{4,12},{8,0},{12,4},{16,24},{20,28},{24,16},{28,20},{1,9},{5... | collective-permute-start | bytes 786440 | tf_op jit(solution)/shard_map/ppermute | solution.py:369
  44.0 17.4 %collective-permute-start.7 = (bf16[128,1024]{1,0:T(8,128)(2,1)S(1)}, bf16[128,1024]{1,0:T(8,128)(2,1)S(1)}, u32[]{:S(2)}, u32[]{:S(2)}) collective-permute-start(bf16[128,1024]{1,0:T(8,128)(2,1)S(1)} %fusion), channel_id=1, source_target_pairs={{0,8},{4,12},{8,0},{12,4},{16,24},{20,28},{24,16},{28,20},{1,9},{5... | collective-permute-start | bytes 786440 | tf_op jit(solution)/shard_map/ppermute | solution.py:369
  54.4 12.0 %collective-permute-start.1 = (bf16[128,1024]{1,0:T(8,128)(2,1)S(1)}, bf16[128,1024]{1,0:T(8,128)(2,1)S(1)}, u32[]{:S(2)}, u32[]{:S(2)}) collective-permute-start(bf16[128,1024]{1,0:T(8,128)(2,1)S(1)} %add_convert_fusion.2), channel_id=1, source_target_pairs={{0,8},{4,12},{8,0},{12,4},{16,24},{20,28},{24,16},{28,20},{1,9},{5... | collective-permute-start | bytes 786440 | tf_op jit(solution)/shard_map/ppermute | solution.py:369
  57.3 24.2 %collective-permute-start.10 = (bf16[2,64,1024]{2,1,0:T(8,128)(2,1)S(1)}, bf16[2,64,1024]{2,1,0:T(8,128)(2,1)S(1)}, u32[]{:S(2)}, u32[]{:S(2)}) collective-permute-start(bf16[2,64,1024]{2,1,0:T(8,128)(2,1)S(1)} %add_convert_fusion), channel_id=1, source_target_pairs={{0,16},{4,20},{8,24},{12,28},{16,0},{20,4},{24,8},{28,12},{1,17},{... | collective-permute-start | bytes 786440 | tf_op jit(solution)/shard_map/ppermute | solution.py:369
  61.0 27.7 %collective-permute-start.5 = (bf16[64,1024]{1,0:T(8,128)(2,1)S(1)}, bf16[64,1024]{1,0:T(8,128)(2,1)S(1)}, u32[]{:S(2)}, u32[]{:S(2)}) collective-permute-start(bf16[64,1024]{1,0:T(8,128)(2,1)S(1)} %add_convert_fusion.4), channel_id=1, source_target_pairs={{0,16},{4,20},{8,24},{12,28},{16,0},{20,4},{24,8},{28,12},{1,17},{... | collective-permute-start | bytes 393224 | tf_op jit(solution)/shard_map/ppermute | solution.py:369
  62.4 26.3 %collective-permute-start.8 = (bf16[64,1024]{1,0:T(8,128)(2,1)S(1)}, bf16[64,1024]{1,0:T(8,128)(2,1)S(1)}, u32[]{:S(2)}, u32[]{:S(2)}) collective-permute-start(bf16[64,1024]{1,0:T(8,128)(2,1)S(1)} %fusion.2), channel_id=1, source_target_pairs={{0,16},{4,20},{8,24},{12,28},{16,0},{20,4},{24,8},{28,12},{1,17},{... | collective-permute-start | bytes 393224 | tf_op jit(solution)/shard_map/ppermute | solution.py:369
  67.4 20.3 %collective-permute-start.2 = (bf16[64,1024]{1,0:T(8,128)(2,1)S(1)}, bf16[64,1024]{1,0:T(8,128)(2,1)S(1)}, u32[]{:S(2)}, u32[]{:S(2)}) collective-permute-start(bf16[64,1024]{1,0:T(8,128)(2,1)S(1)} %add_convert_fusion.5), channel_id=1, source_target_pairs={{0,16},{4,20},{8,24},{12,28},{16,0},{20,4},{24,8},{28,12},{1,17},{... | collective-permute-start | bytes 393224 | tf_op jit(solution)/shard_map/ppermute | solution.py:369
  82.5 7.5 %collective-permute-start.11 = (bf16[64,1024]{1,0:T(8,128)(2,1)S(1)}, bf16[64,1024]{1,0:T(8,128)(2,1)S(1)}, u32[]{:S(2)}, u32[]{:S(2)}) collective-permute-start(bf16[64,1024]{1,0:T(8,128)(2,1)S(1)} %fusion.11), channel_id=1, source_target_pairs={{0,4},{4,0},{8,12},{12,8},{16,20},{20,16},{24,28},{28,24},{1,5},{5... | collective-permute-start | bytes 393224 | tf_op jit(solution)/shard_map/ppermute | solution.py:369
  90.0 44.5 %copy-start.6 = (bf16[256,1024]{1,0:T(8,128)(2,1)S(1)}, bf16[256,1024]{1,0:T(8,128)(2,1)}, u32[]{:S(2)}) copy-start(bf16[256,1024]{1,0:T(8,128)(2,1)} %copy-done.5) | copy-start | bytes 1572868
  91.1 8.3 %collective-permute-start.12 = (bf16[64,1024]{1,0:T(8,128)(2,1)S(1)}, bf16[64,1024]{1,0:T(8,128)(2,1)S(1)}, u32[]{:S(2)}, u32[]{:S(2)}) collective-permute-start(bf16[64,1024]{1,0:T(8,128)(2,1)S(1)} %fusion.9.refs_2_.refs_0_), channel_id=1, source_target_pairs={{0,8},{4,12},{8,16},{12,20},{16,24},{20,28},{24,0},{28,4},{1,9},{5... | collective-permute-start | bytes 393224 | tf_op jit(solution)/shard_map/ppermute | solution.py:429
  91.2 14.2 %collective-permute-start.13 = (bf16[64,1024]{1,0:T(8,128)(2,1)S(1)}, bf16[64,1024]{1,0:T(8,128)(2,1)S(1)}, u32[]{:S(2)}, u32[]{:S(2)}) collective-permute-start(bf16[64,1024]{1,0:T(8,128)(2,1)S(1)} %fusion.9.refs_2_.refs_0_), channel_id=1, source_target_pairs={{0,16},{4,20},{8,24},{12,28},{16,0},{20,4},{24,8},{28,12},{1,17},{... | collective-permute-start | bytes 393224 | tf_op jit(solution)/shard_map/ppermute | solution.py:429
  94.2 16.4 %collective-permute-start.14 = (bf16[64,1024]{1,0:T(8,128)(2,1)S(1)}, bf16[64,1024]{1,0:T(8,128)(2,1)S(1)}, u32[]{:S(2)}, u32[]{:S(2)}) collective-permute-start(bf16[64,1024]{1,0:T(8,128)(2,1)S(1)} %fusion.9.refs_2_.refs_0_), channel_id=1, source_target_pairs={{0,24},{4,28},{8,0},{12,4},{16,8},{20,12},{24,16},{28,20},{1,25},{... | collective-permute-start | bytes 393224 | tf_op jit(solution)/shard_map/ppermute | solution.py:429
  95.0 17.2 %collective-permute-start.15 = (bf16[64,1024]{1,0:T(8,128)(2,1)S(1)}, bf16[64,1024]{1,0:T(8,128)(2,1)S(1)}, u32[]{:S(2)}, u32[]{:S(2)}) collective-permute-start(bf16[64,1024]{1,0:T(8,128)(2,1)S(1)} %fusion.9.refs_2_.refs_0_), channel_id=1, source_target_pairs={{0,4},{4,0},{8,12},{12,8},{16,20},{20,16},{24,28},{28,24},{1,5},{5... | collective-permute-start | bytes 393224 | tf_op jit(solution)/shard_map/ppermute | solution.py:369
  96.5 16.2 %collective-permute-start.19 = (bf16[64,1024]{1,0:T(8,128)(2,1)S(1)}, bf16[64,1024]{1,0:T(8,128)(2,1)S(1)}, u32[]{:S(2)}, u32[]{:S(2)}) collective-permute-start(bf16[64,1024]{1,0:T(8,128)(2,1)S(1)} %fusion.10.refs_2_.refs_0_), channel_id=1, source_target_pairs={{0,8},{4,12},{8,16},{12,20},{16,24},{20,28},{24,0},{28,4},{1,9},{5... | collective-permute-start | bytes 393224 | tf_op jit(solution)/shard_map/ppermute | solution.py:429
  99.4 14.8 %collective-permute-start.20 = (bf16[64,1024]{1,0:T(8,128)(2,1)S(1)}, bf16[64,1024]{1,0:T(8,128)(2,1)S(1)}, u32[]{:S(2)}, u32[]{:S(2)}) collective-permute-start(bf16[64,1024]{1,0:T(8,128)(2,1)S(1)} %fusion.10.refs_2_.refs_0_), channel_id=1, source_target_pairs={{0,16},{4,20},{8,24},{12,28},{16,0},{20,4},{24,8},{28,12},{1,17},{... | collective-permute-start | bytes 393224 | tf_op jit(solution)/shard_map/ppermute | solution.py:429
  105.4 9.3 %collective-permute-start.21 = (bf16[64,1024]{1,0:T(8,128)(2,1)S(1)}, bf16[64,1024]{1,0:T(8,128)(2,1)S(1)}, u32[]{:S(2)}, u32[]{:S(2)}) collective-permute-start(bf16[64,1024]{1,0:T(8,128)(2,1)S(1)} %fusion.10.refs_2_.refs_0_), channel_id=1, source_target_pairs={{0,24},{4,28},{8,0},{12,4},{16,8},{20,12},{24,16},{28,20},{1,25},{... | collective-permute-start | bytes 393224 | tf_op jit(solution)/shard_map/ppermute | solution.py:429
  110.7 5.6 %collective-permute-start.16 = (bf16[64,1024]{1,0:T(8,128)(2,1)S(1)}, bf16[64,1024]{1,0:T(8,128)(2,1)S(1)}, u32[]{:S(2)}, u32[]{:S(2)}) collective-permute-start(bf16[64,1024]{1,0:T(8,128)(2,1)S(1)} %collective-permute-done.12.refs_3_.refs_1_), channel_id=1, source_target_pairs={{0,4},{4,0},{8,12},{12,8},{16,20},{20,16},{24,28},{28,24},{1,5},{5... | collective-permute-start | bytes 393224 | tf_op jit(solution)/shard_map/ppermute | solution.py:369
  112.2 6.4 %collective-permute-start.17 = (bf16[64,1024]{1,0:T(8,128)(2,1)S(1)}, bf16[64,1024]{1,0:T(8,128)(2,1)S(1)}, u32[]{:S(2)}, u32[]{:S(2)}) collective-permute-start(bf16[64,1024]{1,0:T(8,128)(2,1)S(1)} %collective-permute-done.13.refs_4_.refs_2_), channel_id=1, source_target_pairs={{0,4},{4,0},{8,12},{12,8},{16,20},{20,16},{24,28},{28,24},{1,5},{5... | collective-permute-start | bytes 393224 | tf_op jit(solution)/shard_map/ppermute | solution.py:369
  112.7 8.7 %collective-permute-start.18 = (bf16[64,1024]{1,0:T(8,128)(2,1)S(1)}, bf16[64,1024]{1,0:T(8,128)(2,1)S(1)}, u32[]{:S(2)}, u32[]{:S(2)}) collective-permute-start(bf16[64,1024]{1,0:T(8,128)(2,1)S(1)} %collective-permute-done.14.refs_5_.refs_3_), channel_id=1, source_target_pairs={{0,4},{4,0},{8,12},{12,8},{16,20},{20,16},{24,28},{28,24},{1,5},{5... | collective-permute-start | bytes 393224 | tf_op jit(solution)/shard_map/ppermute | solution.py:369
  114.2 10.0 %collective-permute-start.22 = (bf16[64,1024]{1,0:T(8,128)(2,1)S(1)}, bf16[64,1024]{1,0:T(8,128)(2,1)S(1)}, u32[]{:S(2)}, u32[]{:S(2)}) collective-permute-start(bf16[64,1024]{1,0:T(8,128)(2,1)S(1)} %fusion.10.refs_2_.refs_0_), channel_id=1, source_target_pairs={{0,4},{4,0},{8,12},{12,8},{16,20},{20,16},{24,28},{28,24},{1,5},{5... | collective-permute-start | bytes 393224 | tf_op jit(solution)/shard_map/ppermute | solution.py:369
  114.7 12.1 %collective-permute-start.23 = (bf16[64,1024]{1,0:T(8,128)(2,1)S(1)}, bf16[64,1024]{1,0:T(8,128)(2,1)S(1)}, u32[]{:S(2)}, u32[]{:S(2)}) collective-permute-start(bf16[64,1024]{1,0:T(8,128)(2,1)S(1)} %collective-permute-done.19.refs_3_.refs_1_), channel_id=1, source_target_pairs={{0,4},{4,0},{8,12},{12,8},{16,20},{20,16},{24,28},{28,24},{1,5},{5... | collective-permute-start | bytes 393224 | tf_op jit(solution)/shard_map/ppermute | solution.py:369
  116.2 12.0 %collective-permute-start.24 = (bf16[64,1024]{1,0:T(8,128)(2,1)S(1)}, bf16[64,1024]{1,0:T(8,128)(2,1)S(1)}, u32[]{:S(2)}, u32[]{:S(2)}) collective-permute-start(bf16[64,1024]{1,0:T(8,128)(2,1)S(1)} %collective-permute-done.20.refs_4_.refs_2_), channel_id=1, source_target_pairs={{0,4},{4,0},{8,12},{12,8},{16,20},{20,16},{24,28},{28,24},{1,5},{5... | collective-permute-start | bytes 393224 | tf_op jit(solution)/shard_map/ppermute | solution.py:369
  118.6 11.1 %collective-permute-start.25 = (bf16[64,1024]{1,0:T(8,128)(2,1)S(1)}, bf16[64,1024]{1,0:T(8,128)(2,1)S(1)}, u32[]{:S(2)}, u32[]{:S(2)}) collective-permute-start(bf16[64,1024]{1,0:T(8,128)(2,1)S(1)} %collective-permute-done.21.refs_5_.refs_3_), channel_id=1, source_target_pairs={{0,4},{4,0},{8,12},{12,8},{16,20},{20,16},{24,28},{28,24},{1,5},{5... | collective-permute-start | bytes 393224 | tf_op jit(solution)/shard_map/ppermute | solution.py:369
  131.4 6.8 %collective-permute-start.26 = (f32[256,128]{1,0:T(8,128)S(1)}, f32[256,128]{1,0:T(8,128)S(1)}, u32[]{:S(2)}, u32[]{:S(2)}) collective-permute-start(f32[256,128]{1,0:T(8,128)S(1)} %get-tuple-element.33), channel_id=1, source_target_pairs={{0,1},{1,2},{2,3},{3,0},{4,5},{5,6},{6,7},{7,4},{8,9},{9,10},{10,1... | collective-permute-start | bytes 393224 | tf_op jit(solution)/shard_map/ppermute | solution.py:440
  131.4 6.8 %collective-permute-start.27 = (f32[256,128]{1,0:T(8,128)S(1)}, f32[256,128]{1,0:T(8,128)S(1)}, u32[]{:S(2)}, u32[]{:S(2)}) collective-permute-start(f32[256,128]{1,0:T(8,128)S(1)} %get-tuple-element.34), channel_id=1, source_target_pairs={{0,2},{1,3},{2,0},{3,1},{4,6},{5,7},{6,4},{7,5},{8,10},{9,11},{10,... | collective-permute-start | bytes 393224 | tf_op jit(solution)/shard_map/ppermute | solution.py:440
  133.1 6.0 %collective-permute-start.28 = (f32[256,128]{1,0:T(8,128)S(1)}, f32[256,128]{1,0:T(8,128)S(1)}, u32[]{:S(2)}, u32[]{:S(2)}) collective-permute-start(f32[256,128]{1,0:T(8,128)S(1)} %get-tuple-element.35), channel_id=1, source_target_pairs={{0,3},{1,0},{2,1},{3,2},{4,7},{5,4},{6,5},{7,6},{8,11},{9,8},{10,9... | collective-permute-start | bytes 393224 | tf_op jit(solution)/shard_map/ppermute | solution.py:440
  134.4 1.9 %copy-start.4 = (bf16[256,1024]{1,0:T(8,128)(2,1)S(1)}, bf16[256,1024]{1,0:T(8,128)(2,1)}, u32[]{:S(2)}) copy-start(bf16[256,1024]{1,0:T(8,128)(2,1)} %copy-done.3) | copy-start | bytes 1572868

commit v2 on v1

--- a/solution.py
+++ b/solution.py
@@ -17,9 +17,19 @@
 WINDOW = TILE + 2 * EDGE
 SHIFT = TILE // 2
 CHUNKS = 2
-START, OWN, OTHER, LINE, SKY, BAND = range(6)
+OWN, OTHER = 0, 1
+EARLY_GRANT = 60 << 20
 F32 = jnp.float32
 BF16 = jnp.bfloat16
+
+
+def start_column(sky_ref):
+    return sky_ref[lax.axis_index("sky"), lax.axis_index("band"), 0]
+
+
+def half_of(which):
+    low = lax.rem(lax.axis_index("sky"), 2)
+    return low if which == OWN else 1 - low
 
 
 def toeplitz(base_row, rows):
@@ -79,12 +89,17 @@
     return jnp.bitwise_and(jnp.right_shift(word, places - begin), 1)
 
 
-def weight_kernel(sky_count, halves, chunk, meta_ref, words_ref, variance_ref, weight_ref):
+def pick_half(index, halves):
+    half = half_of(halves[0])
+    for place in range(1, len(halves)):
+        half = jnp.where(index == place, half_of(halves[place]), half)
+    return half
+
+
+def weight_kernel(sky_count, halves, chunk, sky_ref, words_ref, variance_ref, weight_ref):
     rows, side = variance_ref.shape
-    half = meta_ref[halves[0]]
-    for index in range(1, len(halves)):
-        half = jnp.where(pl.program_id(0) == index, meta_ref[halves[index]], half)
-    first_row = (half * CHUNKS + chunk) * rows
+    start = start_column(sky_ref)
+    first_row = (pick_half(pl.program_id(0), halves) * CHUNKS + chunk) * rows
     lanes = lax.broadcasted_iota(jnp.int32, (8, side), 1)
     column_bad = bad_bits(words_ref, 0, 0, words_ref.shape[1], lanes)[0:1, :]
     places = first_row + lax.broadcasted_iota(jnp.int32, (rows, TILE), 0)
@@ -95,54 +110,62 @@
         window = slice(tile * TILE, (tile + 1) * TILE)
         bad = row_bad + column_bad[:, window]
         kept = jnp.where(bad == 0, variance_ref[:, window].astype(F32), 0.0)
-        target = lax.rem(meta_ref[START] + tile, sky_count) * TILE
+        target = lax.rem(start + tile, sky_count) * TILE
         weight_ref[0, :, pl.ds(pl.multiple_of(target, TILE), TILE)] = kept.astype(BF16)
 
 
-def weigh(inv_variance, words, meta, halves, chunk, rows, sky_count):
+def weigh(inv_variance, words, sky_columns, halves, chunk, rows, sky_count):
     side = inv_variance.shape[0]
     stripe = sky_count * TILE
-
-    def source(i, m, w):
-        half = m[halves[0]]
-        for index in range(1, len(halves)):
-            half = jnp.where(i == index, m[halves[index]], half)
-        return (half * CHUNKS + chunk, 0)
-
     return pl.pallas_call(
         functools.partial(weight_kernel, sky_count, halves, chunk),
         out_shape=jax.ShapeDtypeStruct((len(halves), rows, stripe), BF16),
         grid_spec=pltpu.PrefetchScalarGridSpec(
             num_scalar_prefetch=2,
             grid=(len(halves),),
-            in_specs=[pl.BlockSpec((rows, side), source)],
+            in_specs=[pl.BlockSpec((rows, side), lambda i, m, w: (pick_half(i, halves) * CHUNKS + chunk, 0))],
             out_specs=pl.BlockSpec((1, rows, stripe), lambda i, m, w: (i, 0, 0)),
         ),
         cost_estimate=pl.CostEstimate(
             flops=len(halves) * rows * side * 8, bytes_accessed=len(halves) * rows * side * 4, transcendentals=0
         ),
-        compiler_params=pltpu.CompilerParams(vmem_limit_bytes=20 << 20),
+        compiler_params=pltpu.CompilerParams(vmem_limit_bytes=EARLY_GRANT),
         name="weigh",
-    )(meta, words, inv_variance)
-
-
-def match_kernel(sky_count, half_slot, half_blocks, offset, meta_ref, picture_ref, column_ref, row_ref, weight_ref, matched_ref, product_ref, windows, stacked):
-    side = picture_ref.shape[0]
-    block = meta_ref[half_slot] * half_blocks + offset + pl.program_id(0)
+    )(sky_columns, words, inv_variance)
+
+
+def match_kernel(
+    sky_count,
+    which,
+    offset,
+    half_blocks,
+    sky_ref,
+    above_ref,
+    main_ref,
+    below_ref,
+    column_ref,
+    row_ref,
+    weight_ref,
+    matched_ref,
+    product_ref,
+    windows,
+    stacked,
+):
+    side = main_ref.shape[1]
+    start = start_column(sky_ref)
+    block = half_of(which) * half_blocks + offset + pl.program_id(0)
     last_block = side // TILE - 1
-    first = pl.multiple_of(block * TILE, TILE)
     nothing = jnp.zeros((TILE, SHIFT), BF16)
 
     def spread(values):
         edge = nothing[: values.shape[0]]
         return jnp.concatenate([edge, values, edge], axis=1)
 
-    above = picture_ref[pl.ds(pl.multiple_of(jnp.maximum(first - EDGE, 0), EDGE), EDGE), :]
-    below = picture_ref[pl.ds(pl.multiple_of(jnp.minimum(first + TILE, side - EDGE), EDGE), EDGE), :]
+    above, below = above_ref[...], below_ref[...]
     tiles = side // TILE
     parts = (
         (0, spread(jnp.where(block > 0, above, jnp.zeros_like(above)))),
-        (EDGE, spread(picture_ref[pl.ds(first, TILE), :])),
+        (EDGE, spread(main_ref[...])),
         (EDGE + TILE, spread(jnp.where(block < last_block, below, jnp.zeros_like(below)))),
     )
     for tile in range(tiles):
@@ -166,19 +189,24 @@
         summed = jnp.dot(row_ref[...], stacked[:, both], preferred_element_type=F32).astype(BF16)
         matched_ref[:, both] = summed
         for part in range(2):
-            target = pl.multiple_of(lax.rem(meta_ref[START] + 2 * pair + part, sky_count) * TILE, TILE)
+            target = pl.multiple_of(lax.rem(start + 2 * pair + part, sky_count) * TILE, TILE)
             weight = weight_ref[:, pl.ds(target, TILE)].astype(F32)
             product = weight * summed[:, part * TILE : (part + 1) * TILE].astype(F32)
             product_ref[:, pl.ds(target, TILE)] = product.astype(BF16)
 
 
-def match(picture, column_band, row_band, weight, which, meta, half_slot, chunk, half_rows, sky_count):
+def match(picture, column_band, row_band, weight, which_weight, sky_columns, which, chunk, half_rows, sky_count):
     side = picture.shape[0]
     chunk_rows = half_rows // CHUNKS
     steps = chunk_rows // TILE
     stripe = sky_count * TILE
-    return pl.pallas_call(
-        functools.partial(match_kernel, sky_count, half_slot, CHUNKS * steps, chunk * steps),
+    edges = TILE // EDGE
+
+    def block(i):
+        return (half_of(which) * CHUNKS + chunk) * steps + i
+
+    return pl.pallas_call(
+        functools.partial(match_kernel, sky_count, which, chunk * steps, CHUNKS * steps),
         out_shape=(
             jax.ShapeDtypeStruct((chunk_rows, side), BF16),
             jax.ShapeDtypeStruct((chunk_rows, stripe), BF16),
@@ -187,10 +215,12 @@
             num_scalar_prefetch=1,
             grid=(steps,),
             in_specs=[
-                pl.BlockSpec((side, side), lambda i, m: (0, 0)),
-                pl.BlockSpec(column_band.shape, lambda i, m: (0, 0)),
-                pl.BlockSpec(row_band.shape, lambda i, m: (0, 0)),
-                pl.BlockSpec((None, TILE, stripe), lambda i, m: (which, i, 0)),
+                pl.BlockSpec((EDGE, side), lambda i, m: (jnp.maximum(block(i) * edges - 1, 0), 0)),
+                pl.BlockSpec((TILE, side), lambda i, m: (block(i), 0)),
+                pl.BlockSpec((EDGE, side), lambda i, m: (jnp.minimum((block(i) + 1) * edges, side // EDGE - 1), 0)),
+                pl.BlockSpec(column_band.shape, lambda i, m: (0, 0), pipeline_mode=pl.Buffered(1)),
+                pl.BlockSpec(row_band.shape, lambda i, m: (0, 0), pipeline_mode=pl.Buffered(1)),
+                pl.BlockSpec((None, TILE, stripe), lambda i, m: (which_weight, i, 0)),
             ],
             out_specs=(
                 pl.BlockSpec((TILE, side), lambda i, m: (i, 0)),
@@ -204,9 +234,9 @@
         cost_estimate=pl.CostEstimate(
             flops=2 * chunk_rows * side * NB * (2 * TILE + WINDOW), bytes_accessed=chunk_rows * side * 8, transcendentals=0
         ),
-        compiler_params=pltpu.CompilerParams(vmem_limit_bytes=28 << 20),
+        compiler_params=pltpu.CompilerParams(vmem_limit_bytes=EARLY_GRANT),
         name="match",
-    )(meta, picture, column_band, row_band, weight)
+    )(sky_columns, picture, picture, picture, column_band, row_band, weight)
 
 
 def row_of(place, line, chunk_rows):
@@ -216,30 +246,31 @@
     return row
 
 
-def piece_rows(meta_ref, step, line, chunk_rows, part_rows):
-    row = row_of(lax.rem(meta_ref[LINE] + line - step, line), line, chunk_rows)
+def piece_rows(step, line, chunk_rows, part_rows):
+    row = row_of(lax.axis_index("sky") // 2 ^ step, line, chunk_rows)
     return pl.ds(pl.multiple_of(row, part_rows), part_rows)
 
 
-def difference_kernel(sky_count, pair, line, meta_ref, *refs):
+def difference_kernel(sky_count, pair, line, sky_ref, *refs):
     matched = refs[:pair]
     pieces = refs[pair : pair + pair * line]
     out_ref = refs[-1]
+    start = start_column(sky_ref)
     part_rows = pieces[0].shape[0]
     chunk_rows, side = matched[0].shape
     for group in range(pair):
-        half = meta_ref[OWN + group]
+        half = half_of((OWN, OTHER)[group])
         for step in range(line):
-            rows = piece_rows(meta_ref, step, line, chunk_rows, part_rows)
+            rows = piece_rows(step, line, chunk_rows, part_rows)
             piece = pieces[group * line + step]
             for tile in range(side // TILE):
                 window = slice(tile * TILE, (tile + 1) * TILE)
-                source = pl.multiple_of(lax.rem(meta_ref[START] + tile, sky_count) * TILE, TILE)
+                source = pl.multiple_of(lax.rem(start + tile, sky_count) * TILE, TILE)
                 picked = piece[:, pl.ds(source, TILE)].astype(F32)
                 out_ref[half, 0, rows, window] = (matched[group][rows, window].astype(F32) - picked).astype(BF16)
 
 
-def subtract(matched, pieces, meta, chunk, before, sky_count):
+def subtract(matched, pieces, sky_columns, chunk, before, sky_count):
     chunk_rows, side = matched[0].shape
     pair = len(matched)
     line = len(pieces) // pair
@@ -265,22 +296,22 @@
         ),
         compiler_params=pltpu.CompilerParams(vmem_limit_bytes=24 << 20),
         name="subtract",
-    )(meta, *operands)
-
-
-def smooth_kernel(sky_count, pair, line, meta_ref, across_ref, *refs):
+    )(sky_columns, *operands)
+
+
+def smooth_kernel(sky_count, pair, line, sky_ref, across_ref, *refs):
     pieces, out_ref = refs[:-1], refs[-1]
     part_rows = pieces[0].shape[0]
     chunk_rows = out_ref.shape[1]
 
     def column(piece, away):
-        source = lax.rem(meta_ref[SKY] + away, sky_count) * TILE
+        source = lax.rem(lax.axis_index("sky") + away, sky_count) * TILE
         return piece[:, pl.ds(pl.multiple_of(source, TILE), TILE)]
 
     for group in range(pair):
-        half = meta_ref[OWN + group]
+        half = half_of((OWN, OTHER)[group])
         for step in range(line):
-            rows = piece_rows(meta_ref, step, line, chunk_rows, part_rows)
+            rows = piece_rows(step, line, chunk_rows, part_rows)
             piece = pieces[group * line + step]
             window = jnp.concatenate(
                 [column(piece, sky_count - 1)[:, SHIFT:], column(piece, 0), column(piece, 1)[:, :SHIFT]], axis=1
@@ -288,7 +319,7 @@
             out_ref[half, rows, :] = jnp.dot(window, across_ref[...], preferred_element_type=F32).astype(BF16)
 
 
-def smooth(pieces, across_band, meta, pair, chunk_rows, sky_count):
+def smooth(pieces, across_band, sky_columns, pair, chunk_rows, sky_count):
     line = len(pieces) // pair
     operands = [across_band, *pieces]
     return pl.pallas_call(
@@ -305,10 +336,10 @@
         ),
         compiler_params=pltpu.CompilerParams(vmem_limit_bytes=20 << 20),
         name="smooth",
-    )(meta, *operands)
-
-
-def power_kernel(band_count, meta_ref, down_ref, *refs):
+    )(sky_columns, *operands)
+
+
+def power_kernel(band_count, sky_ref, down_ref, *refs):
     sources, powers, smoothed = refs[:CHUNKS], refs[CHUNKS : CHUNKS + band_count], refs[-1]
     pair, chunk_rows = sources[0].shape[:2]
     side = pair * CHUNKS * chunk_rows
@@ -320,18 +351,20 @@
             first = EDGE + (half * CHUNKS + chunk) * chunk_rows
             smoothed[first : first + chunk_rows, :] = sources[chunk][half]
     for step in range(band_count):
-        first = lax.rem(meta_ref[BAND] + step, band_count) * rows
+        first = lax.rem(lax.axis_index("band") + step, band_count) * rows
         for inner in range(rows // TILE):
             source = pl.multiple_of(first + inner * TILE, TILE)
             filtered = jnp.dot(down_ref[...], smoothed[pl.ds(source, WINDOW), :], preferred_element_type=F32)
-            powers[step][inner * TILE : (inner + 1) * TILE, :] = filtered * filtered
-
-
-def power(sources, down_band, meta, band_count):
+            powers[step][inner * TILE : (inner + 1) * TILE, :] = (filtered * filtered).astype(powers[step].dtype)
+
+
+def power(sources, down_band, sky_columns, band_count):
     side = CHUNKS * sources[0].shape[0] * sources[0].shape[1]
     return pl.pallas_call(
         functools.partial(power_kernel, band_count),
-        out_shape=[jax.ShapeDtypeStruct((side // band_count, TILE), F32)] * band_count,
+        out_shape=[
+            jax.ShapeDtypeStruct((side // band_count, TILE), BF16 if step else F32) for step in range(band_count)
+        ],
         grid_spec=pltpu.PrefetchScalarGridSpec(
             num_scalar_prefetch=1,
             grid=(1,),
@@ -343,7 +376,7 @@
         cost_estimate=pl.CostEstimate(flops=side * TILE * 320, bytes_accessed=side * TILE * 6, transcendentals=0),
         compiler_params=pltpu.CompilerParams(vmem_limit_bytes=16 << 20),
         name="power",
-    )(meta, down_band, *sources)
+    )(sky_columns, down_band, *sources)
 
 
 def body(exposures, inv_variance, mask_planes, sky_columns, basis_rows, basis_cols, match_coeffs, detect_taps):
@@ -352,18 +385,10 @@
     sky_count = lax.axis_size("sky")
     band_count = lax.axis_size("band")
     own_sky = lax.axis_index("sky")
-    own_band = lax.axis_index("band")
     pair = 2
     line = sky_count // pair
-    low = lax.rem(own_sky, pair)
-    high = own_sky // pair
     half_rows = side // pair
     chunk_rows = half_rows // CHUNKS
-    slots = jnp.arange(8, dtype=jnp.int32)
-    meta = jnp.zeros((8,), jnp.int32)
-    scalars = {START: sky_columns[own_sky, own_band, 0], OWN: low, OTHER: 1 - low, LINE: high, SKY: own_sky, BAND: own_band}
-    for slot, value in scalars.items():
-        meta = jnp.where(slots == slot, value, meta)
 
     def exchange(block, bit):
         return lax.ppermute(block, "sky", [(i, i ^ (1 << bit)) for i in range(sky_count)])
@@ -387,11 +412,11 @@
     variance = inv_variance[0, 0]
 
     def weighing(halves, chunk):
-        return weigh(variance, words, meta, halves, chunk, chunk_rows, sky_count)
+        return weigh(variance, words, sky_columns, halves, chunk, chunk_rows, sky_count)
 
     def matching(weight, which, half_slot, chunk):
         return match(
-            picture, column_band, row_band, weight, which, meta, half_slot, chunk, half_rows, sky_count
+            picture, column_band, row_band, weight, which, sky_columns, half_slot, chunk, half_rows, sky_count
         )
 
     weight_other = weighing((OTHER,), 0)
@@ -415,7 +440,6 @@
         total([t[1] for t in both_terms] + [both_in]),
     ]
 
-    shifts = [[(i, (i // pair + step) % line * pair + i % pair) for i in range(sky_count)] for step in range(line)]
     smoothed = [None] * CHUNKS
     difference = None
     for c in range(CHUNKS):
@@ -423,21 +447,23 @@
         if c:
             numer, _ = lax.optimization_barrier((numer, block))
         block = (numer / jnp.maximum(denoms[c], 1.0)).astype(BF16)
-        near, far = [block], []
-        far.append(exchange(block, 0))
+        near, far = {0: block}, {}
+        far[0] = exchange(block, 0)
+        for bit in reversed(range(line.bit_length() - 1)):
+            for held in list(near):
+                step = held | 1 << bit
+                near[step] = exchange(near[held], bit + 1)
         for step in range(1, line):
-            near.append(lax.ppermute(block, "sky", shifts[step]))
-        for step in range(1, line):
-            far.append(exchange(near[step], 0))
-        pieces = near + far
-        smoothed[c] = smooth(pieces, across_band, meta, pair, chunk_rows, sky_count)
-        difference = subtract([home[c], away[c]], pieces, meta, c, difference, sky_count)
-
-    powers = power(smoothed, down_band, meta, band_count)
+            far[step] = exchange(near[step], 0)
+        pieces = [near[step] for step in range(line)] + [far[step] for step in range(line)]
+        smoothed[c] = smooth(pieces, across_band, sky_columns, pair, chunk_rows, sky_count)
+        difference = subtract([home[c], away[c]], pieces, sky_columns, c, difference, sky_count)
+
+    powers = power(smoothed, down_band, sky_columns, band_count)
     detection = powers[0]
     for step in range(1, band_count):
         ring = [(i, (i + step) % band_count) for i in range(band_count)]
-        detection = detection + lax.ppermute(powers[step], "band", ring)
+        detection = detection + lax.ppermute(powers[step], "band", ring).astype(F32)
     return (difference.reshape(1, 1, side, side), detection)
 
 

time: 141 us -> 136 us (0.965)
  Pallas kernels: 29.2 us -> 45.4 us
  starting transfers between devices: 42.6 us -> 29.7 us
  other arithmetic: 15 us -> 7.95 us
  local copies, waits for them, and re-layouts: 7.08 us -> 1.65 us
  waiting for transfers between devices: 45 us -> 49.5 us
    ppermute x20 -> x26, waiting for transfers between devices: 37 us -> 49.5 us  [exchange(): lax.ppermute(block, 'sky', [(i, i ^ 1 << bit) for i in range(sky_count)])]
    ppermute x9 -> x3, starting transfers between devices: 14 us -> 2.91 us  [body(): detection = detection + lax.ppermute(powers[step], 'band', ring).astype(F32)]
    pallas_call x4, Pallas kernels: 17.7 us -> 26.4 us  [match(): pl.pallas_call(functools.partial(match_kernel, sky_count, which, chunk *...]
    ppermute x9 -> x3, waiting for transfers between devices: 8.01 us -> 0.01 us  [body(): detection = detection + lax.ppermute(powers[step], 'band', ring).astype(F32)]
    pallas_call x3, Pallas kernels: 4.12 us -> 10.2 us  [weigh(): pl.pallas_call(functools.partial(weight_kernel, sky_count, halves, chunk)...]
    unnamed x34 -> x26, local copies, waits for them, and re-layouts: 5.64 us -> 1.61 us
    convert_element_type x7, other arithmetic: 7.1 us -> 3.51 us  [reduce_line(): arrived = exchange(leaving.astype(BF16), bit)]
    ppermute x20 -> x26, starting transfers between devices: 28.6 us -> 26.7 us  [exchange(): lax.ppermute(block, 'sky', [(i, i ^ 1 << bit) for i in range(sky_count)])]
  transfers between devices with their start and end apart: 29 -> 29, of which waited for: 14 -> 10; matrix products, arithmetic and copies ran while one was open for 8% -> 4% of each run, Pallas kernels for 14% -> 24%
where the time goes in v2:
time: 136 us; the launch traced here: 135 us
  waiting for transfers between devices  49.5 us (36%)
  Pallas kernels  45.4 us (33%)
  starting transfers between devices  29.7 us (22%)
  other arithmetic  7.95 us (6%)
  local copies, waits for them, and re-layouts  1.65 us (1%)
    ppermute x26, waiting for transfers between devices, exchange(): lax.ppermute(block, 'sky', [(i, i ^ 1 << bit) for i in range(sky_count)])  49.5 us
    ppermute x26, starting transfers between devices, exchange(): lax.ppermute(block, 'sky', [(i, i ^ 1 << bit) for i in range(sky_count)])  26.7 us
    pallas_call x4, Pallas kernels, match(): pl.pallas_call(functools.partial(match_kernel, sky_count, which, chunk *...  26.4 us
    pallas_call x3, Pallas kernels, weigh(): pl.pallas_call(functools.partial(weight_kernel, sky_count, halves, chunk)...  10.2 us
    pallas_call x2, Pallas kernels, subtract(): pl.pallas_call(functools.partial(difference_kernel, sky_count, pair, line...  4.47 us
    convert_element_type x7, other arithmetic, reduce_line(): arrived = exchange(leaving.astype(BF16), bit)  3.51 us
    ppermute x3, starting transfers between devices, body(): detection = detection + lax.ppermute(powers[step], 'band', ring).astype(F32)  2.91 us
  transfers between devices with their start and end apart: 29, of which 10 were waited for; matrix products, arithmetic and copies ran while one was open for 4% of the time, Pallas kernels for 24%

profile of v2, /device:TPU:0, one launch (start us, length us, event | category | flops | bytes accessed | tf_op | source)
XLA Modules:
  0.0 135.0 jit_solution(6686598328098980105)
XLA Ops:
  0.6 0.7 convert_element_type.190
  1.3 0.7 convert_convert_fusion
  2.0 0.8 multiply_convert_fusion
  2.8 0.1 pad_convert_fusion
  2.8 0.1 select_maximum_fusion.base_ref
  2.9 1.1 prepare.1
  4.0 0.8 copy-done
  4.8 0.8 copy-done.1
  5.6 3.2 %weigh.5.weight_ref = bf16[1,256,1024]{2,1,0:T(8,128)(2,1)} custom-call(s32[8,4,8]{2,1,0:T(4,128)} %sky_ref.23, s32[2,35]{1,0:T(2,128)} %bitcast.42, bf16[1024,1024]{1,0:T(8,128)(2,1)} %bitcast.37), custom_call_target="tpu_custom_call" | custom-call | flops 2097152 | bytes 1048576 | tf_op jit(solution)/shard_map/weigh/pallas_call | solution.py:120
  8.8 6.7 %match.7 = (bf16[256,1024]{1,0:T(8,128)(2,1)}, bf16[256,1024]{1,0:T(8,128)(2,1)}) custom-call(s32[8,4,8]{2,1,0:T(4,128)} %sky_ref.23, bf16[1024,1024]{1,0:T(8,128)(2,1)} %bitcast.25, bf16[1024,1024]{1,0:T(8,128)(2,1)} %bitcast.26, bf16[1024,1024]{1,0:T(8,128)(2,1)} %bitcast.27, bf16[256,1152]{1,0:T(8,128)(2,1)} %copy-done, bf16[128,1440]{1,0:T(8,128)(2,1)} %copy-done.1, ...), custom_call_target="tpu_custom_call" | custom-call | flops 1962934272 | bytes 2097152 | tf_op jit(solution)/shard_map/match/pallas_call | solution.py:208
  15.4 3.0 %collective-permute-start.3 = (bf16[256,1024]{1,0:T(8,128)(2,1)}, bf16[256,1024]{1,0:T(8,128)(2,1)S(1)}, u32[]{:S(2)}, u32[]{:S(2)}) collective-permute-start(bf16[256,1024]{1,0:T(8,128)(2,1)} %get-tuple-element.26), channel_id=1, source_target_pairs={{0,4},{4,0},{8,12},{12,8},{16,20},{20,16},{24,28},{28,24},{1,5},{5... | collective-permute-start | bytes 1572872 | tf_op jit(solution)/shard_map/ppermute | solution.py:394
  18.4 0.1 collective-permute-start.6
  18.5 3.7 %weigh.3.weight_ref = bf16[2,256,1024]{2,1,0:T(8,128)(2,1)} custom-call(s32[8,4,8]{2,1,0:T(4,128)} %sky_ref.23, s32[2,35]{1,0:T(2,128)} %bitcast.43, bf16[1024,1024]{1,0:T(8,128)(2,1)} %bitcast.38), custom_call_target="tpu_custom_call" | custom-call | flops 4194304 | bytes 2097152 | tf_op jit(solution)/shard_map/weigh/pallas_call | solution.py:120
  22.2 6.6 %match.5 = (bf16[256,1024]{1,0:T(8,128)(2,1)}, bf16[256,1024]{1,0:T(8,128)(2,1)}) custom-call(s32[8,4,8]{2,1,0:T(4,128)} %sky_ref.23, bf16[1024,1024]{1,0:T(8,128)(2,1)} %bitcast.28, bf16[1024,1024]{1,0:T(8,128)(2,1)} %bitcast.29, bf16[1024,1024]{1,0:T(8,128)(2,1)} %bitcast.30, bf16[256,1152]{1,0:T(8,128)(2,1)} %copy-done, bf16[128,1440]{1,0:T(8,128)(2,1)} %copy-done.1, ...), custom_call_target="tpu_custom_call" | custom-call | flops 1962934272 | bytes 2097152 | tf_op jit(solution)/shard_map/match/pallas_call | solution.py:208
  28.8 2.0 %collective-permute-start = (bf16[256,1024]{1,0:T(8,128)(2,1)}, bf16[256,1024]{1,0:T(8,128)(2,1)S(1)}, u32[]{:S(2)}, u32[]{:S(2)}) collective-permute-start(bf16[256,1024]{1,0:T(8,128)(2,1)} %get-tuple-element.24), channel_id=1, source_target_pairs={{0,4},{4,0},{8,12},{12,8},{16,20},{20,16},{24,28},{28,24},{1,5},{5... | collective-permute-start | bytes 1572872 | tf_op jit(solution)/shard_map/ppermute | solution.py:394
  30.8 1.7 %collective-permute-start.9 = (bf16[2,128,1024]{2,1,0:T(8,128)(2,1)S(1)}, bf16[2,128,1024]{2,1,0:T(8,128)(2,1)S(1)}, u32[]{:S(2)}, u32[]{:S(2)}) collective-permute-start(bf16[2,128,1024]{2,1,0:T(8,128)(2,1)S(1)} %constant_dynamic-slice_fusion), channel_id=1, source_target_pairs={{0,8},{4,12},{8,0},{12,4},{16,24},{20,28},{24,16},{28,20},{1,9},{5... | collective-permute-start | bytes 1572872 | tf_op jit(solution)/shard_map/ppermute | solution.py:394
  32.5 3.2 %weigh.4.weight_ref = bf16[1,256,1024]{2,1,0:T(8,128)(2,1)} custom-call(s32[8,4,8]{2,1,0:T(4,128)} %sky_ref.23, s32[2,35]{1,0:T(2,128)} %bitcast.44, bf16[1024,1024]{1,0:T(8,128)(2,1)} %bitcast.39), custom_call_target="tpu_custom_call" | custom-call | flops 2097152 | bytes 1048576 | tf_op jit(solution)/shard_map/weigh/pallas_call | solution.py:120
  35.7 6.5 %match.4 = (bf16[256,1024]{1,0:T(8,128)(2,1)}, bf16[256,1024]{1,0:T(8,128)(2,1)}) custom-call(s32[8,4,8]{2,1,0:T(4,128)} %sky_ref.23, bf16[1024,1024]{1,0:T(8,128)(2,1)} %bitcast.31, bf16[1024,1024]{1,0:T(8,128)(2,1)} %bitcast.32, bf16[1024,1024]{1,0:T(8,128)(2,1)} %bitcast.33, bf16[256,1152]{1,0:T(8,128)(2,1)} %copy-done, bf16[128,1440]{1,0:T(8,128)(2,1)} %copy-done.1, ...), custom_call_target="tpu_custom_call" | custom-call | flops 1962934272 | bytes 2097152 | tf_op jit(solution)/shard_map/match/pallas_call | solution.py:208
  42.2 6.7 %match.6 = (bf16[256,1024]{1,0:T(8,128)(2,1)}, bf16[256,1024]{1,0:T(8,128)(2,1)}) custom-call(s32[8,4,8]{2,1,0:T(4,128)} %sky_ref.23, bf16[1024,1024]{1,0:T(8,128)(2,1)} %bitcast.34, bf16[1024,1024]{1,0:T(8,128)(2,1)} %bitcast.35, bf16[1024,1024]{1,0:T(8,128)(2,1)} %bitcast.36, bf16[256,1152]{1,0:T(8,128)(2,1)} %copy-done, bf16[128,1440]{1,0:T(8,128)(2,1)} %copy-done.1, ...), custom_call_target="tpu_custom_call" | custom-call | flops 1962934272 | bytes 2097152 | tf_op jit(solution)/shard_map/match/pallas_call | solution.py:208
  48.9 1.1 add_convert_fusion.1
  50.0 0.5 collective-permute-start.4
  50.6 1.0 fusion
  51.6 1.7 %collective-permute-start.7 = (bf16[128,1024]{1,0:T(8,128)(2,1)S(1)}, bf16[128,1024]{1,0:T(8,128)(2,1)S(1)}, u32[]{:S(2)}, u32[]{:S(2)}) collective-permute-start(bf16[128,1024]{1,0:T(8,128)(2,1)S(1)} %fusion), channel_id=1, source_target_pairs={{0,8},{4,12},{8,0},{12,4},{16,24},{20,28},{24,16},{28,20},{1,9},{5... | collective-permute-start | bytes 786440 | tf_op jit(solution)/shard_map/ppermute | solution.py:394
  53.3 1.7 %collective-permute-start.1 = (bf16[128,1024]{1,0:T(8,128)(2,1)S(1)}, bf16[128,1024]{1,0:T(8,128)(2,1)S(1)}, u32[]{:S(2)}, u32[]{:S(2)}) collective-permute-start(bf16[128,1024]{1,0:T(8,128)(2,1)S(1)} %add_convert_fusion.2), channel_id=1, source_target_pairs={{0,8},{4,12},{8,0},{12,4},{16,24},{20,28},{24,16},{28,20},{1,9},{5... | collective-permute-start | bytes 786440 | tf_op jit(solution)/shard_map/ppermute | solution.py:394
  55.0 0.1 add_convert_fusion
  55.1 2.7 %collective-permute-start.10 = (bf16[2,64,1024]{2,1,0:T(8,128)(2,1)S(1)}, bf16[2,64,1024]{2,1,0:T(8,128)(2,1)S(1)}, u32[]{:S(2)}, u32[]{:S(2)}) collective-permute-start(bf16[2,64,1024]{2,1,0:T(8,128)(2,1)S(1)} %add_convert_fusion), channel_id=1, source_target_pairs={{0,16},{4,20},{8,24},{12,28},{16,0},{20,4},{24,8},{28,12},{1,17},{... | collective-permute-start | bytes 786440 | tf_op jit(solution)/shard_map/ppermute | solution.py:394
  57.7 8.6 %collective-permute-done.4 = bf16[128,1024]{1,0:T(8,128)(2,1)S(1)} collective-permute-done((bf16[128,1024]{1,0:T(8,128)(2,1)S(1)}, bf16[128,1024]{1,0:T(8,128)(2,1)S(1)}, u32[]{:S(2)}, u32[]{:S(2)}) %collective-permute-start.4) | collective-permute-done | bytes 262176 | tf_op jit(solution)/shard_map/ppermute | solution.py:394
  66.3 0.1 add_convert_fusion.4
  66.4 0.6 collective-permute-start.5
  67.0 5.8 %collective-permute-done.7 = bf16[128,1024]{1,0:T(8,128)(2,1)S(1)} collective-permute-done((bf16[128,1024]{1,0:T(8,128)(2,1)S(1)}, bf16[128,1024]{1,0:T(8,128)(2,1)S(1)}, u32[]{:S(2)}, u32[]{:S(2)}) %collective-permute-start.7) | collective-permute-done | bytes 262176 | tf_op jit(solution)/shard_map/ppermute | solution.py:394
  72.8 1.0 fusion.2
  73.8 0.1 collective-permute-start.8
  73.9 2.3 %collective-permute-done.1 = bf16[128,1024]{1,0:T(8,128)(2,1)S(1)} collective-permute-done((bf16[128,1024]{1,0:T(8,128)(2,1)S(1)}, bf16[128,1024]{1,0:T(8,128)(2,1)S(1)}, u32[]{:S(2)}, u32[]{:S(2)}) %collective-permute-start.1) | collective-permute-done | bytes 262176 | tf_op jit(solution)/shard_map/ppermute | solution.py:394
  76.2 0.1 add_convert_fusion.5
  76.3 0.7 collective-permute-start.2
  77.0 0.1 fusion.11
  77.1 0.6 collective-permute-start.11
  77.6 12.9 %collective-permute-done.2 = bf16[64,1024]{1,0:T(8,128)(2,1)S(1)} collective-permute-done((bf16[64,1024]{1,0:T(8,128)(2,1)S(1)}, bf16[64,1024]{1,0:T(8,128)(2,1)S(1)}, u32[]{:S(2)}, u32[]{:S(2)}) %collective-permute-start.2) | collective-permute-done | bytes 131104 | tf_op jit(solution)/shard_map/ppermute | solution.py:394
  90.6 0.1 convert_add_fusion.3
  90.7 1.2 fusion.10.refs_2_.refs_0_
  91.9 0.1 fusion.9.refs_2_.refs_0_
  92.0 0.1 collective-permute-start.13
  92.1 1.6 %collective-permute-start.12 = (bf16[64,1024]{1,0:T(8,128)(2,1)S(1)}, bf16[64,1024]{1,0:T(8,128)(2,1)S(1)}, u32[]{:S(2)}, u32[]{:S(2)}) collective-permute-start(bf16[64,1024]{1,0:T(8,128)(2,1)S(1)} %fusion.9.refs_2_.refs_0_), channel_id=1, source_target_pairs={{0,8},{4,12},{8,0},{12,4},{16,24},{20,28},{24,16},{28,20},{1,9},{5... | collective-permute-start | bytes 393224 | tf_op jit(solution)/shard_map/ppermute | solution.py:394
  93.7 0.4 collective-permute-start.15
  94.0 1.5 %collective-permute-start.20 = (bf16[64,1024]{1,0:T(8,128)(2,1)S(1)}, bf16[64,1024]{1,0:T(8,128)(2,1)S(1)}, u32[]{:S(2)}, u32[]{:S(2)}) collective-permute-start(bf16[64,1024]{1,0:T(8,128)(2,1)S(1)} %fusion.10.refs_2_.refs_0_), channel_id=1, source_target_pairs={{0,16},{4,20},{8,24},{12,28},{16,0},{20,4},{24,8},{28,12},{1,17},{... | collective-permute-start | bytes 393224 | tf_op jit(solution)/shard_map/ppermute | solution.py:394
  95.5 6.7 %collective-permute-done.13.refs_4_.refs_2_ = bf16[64,1024]{1,0:T(8,128)(2,1)S(1)} collective-permute-done((bf16[64,1024]{1,0:T(8,128)(2,1)S(1)}, bf16[64,1024]{1,0:T(8,128)(2,1)S(1)}, u32[]{:S(2)}, u32[]{:S(2)}) %collective-permute-start.13) | collective-permute-done | bytes 131104 | tf_op jit(solution)/shard_map/ppermute | solution.py:394
  102.2 2.0 %collective-permute-start.19 = (bf16[64,1024]{1,0:T(8,128)(2,1)S(1)}, bf16[64,1024]{1,0:T(8,128)(2,1)S(1)}, u32[]{:S(2)}, u32[]{:S(2)}) collective-permute-start(bf16[64,1024]{1,0:T(8,128)(2,1)S(1)} %fusion.10.refs_2_.refs_0_), channel_id=1, source_target_pairs={{0,8},{4,12},{8,0},{12,4},{16,24},{20,28},{24,16},{28,20},{1,9},{5... | collective-permute-start | bytes 393224 | tf_op jit(solution)/shard_map/ppermute | solution.py:394
  104.3 2.0 %collective-permute-start.17 = (bf16[64,1024]{1,0:T(8,128)(2,1)S(1)}, bf16[64,1024]{1,0:T(8,128)(2,1)S(1)}, u32[]{:S(2)}, u32[]{:S(2)}) collective-permute-start(bf16[64,1024]{1,0:T(8,128)(2,1)S(1)} %collective-permute-done.13.refs_4_.refs_2_), channel_id=1, source_target_pairs={{0,4},{4,0},{8,12},{12,8},{16,20},{20,16},{24,28},{28,24},{1,5},{5... | collective-permute-start | bytes 393224 | tf_op jit(solution)/shard_map/ppermute | solution.py:394
  106.3 2.3 %collective-permute-done.14.refs_5_.refs_3_ = bf16[64,1024]{1,0:T(8,128)(2,1)S(1)} collective-permute-done((bf16[64,1024]{1,0:T(8,128)(2,1)S(1)}, bf16[64,1024]{1,0:T(8,128)(2,1)S(1)}, u32[]{:S(2)}, u32[]{:S(2)}) %collective-permute-start.14) | collective-permute-done | bytes 131104 | tf_op jit(solution)/shard_map/ppermute | solution.py:394
  108.6 2.8 %collective-permute-done.19.refs_3_.refs_1_ = bf16[64,1024]{1,0:T(8,128)(2,1)S(1)} collective-permute-done((bf16[64,1024]{1,0:T(8,128)(2,1)S(1)}, bf16[64,1024]{1,0:T(8,128)(2,1)S(1)}, u32[]{:S(2)}, u32[]{:S(2)}) %collective-permute-start.19) | collective-permute-done | bytes 131104 | tf_op jit(solution)/shard_map/ppermute | solution.py:394
  111.5 2.0 %collective-permute-start.24 = (bf16[64,1024]{1,0:T(8,128)(2,1)S(1)}, bf16[64,1024]{1,0:T(8,128)(2,1)S(1)}, u32[]{:S(2)}, u32[]{:S(2)}) collective-permute-start(bf16[64,1024]{1,0:T(8,128)(2,1)S(1)} %collective-permute-done.20.refs_4_.refs_2_), channel_id=1, source_target_pairs={{0,4},{4,0},{8,12},{12,8},{16,20},{20,16},{24,28},{28,24},{1,5},{5... | collective-permute-start | bytes 393224 | tf_op jit(solution)/shard_map/ppermute | solution.py:394
  113.4 0.1 collective-permute-start.23
  113.5 2.0 %collective-permute-start.25 = (bf16[64,1024]{1,0:T(8,128)(2,1)S(1)}, bf16[64,1024]{1,0:T(8,128)(2,1)S(1)}, u32[]{:S(2)}, u32[]{:S(2)}) collective-permute-start(bf16[64,1024]{1,0:T(8,128)(2,1)S(1)} %collective-permute-done.21.refs_5_.refs_3_), channel_id=1, source_target_pairs={{0,4},{4,0},{8,12},{12,8},{16,20},{20,16},{24,28},{28,24},{1,5},{5... | collective-permute-start | bytes 393224 | tf_op jit(solution)/shard_map/ppermute | solution.py:394
  115.5 1.1 smooth.3.refs_1_
  116.6 1.5 %collective-permute-done.22.refs_6_.refs_4_ = bf16[64,1024]{1,0:T(8,128)(2,1)S(1)} collective-permute-done((bf16[64,1024]{1,0:T(8,128)(2,1)S(1)}, bf16[64,1024]{1,0:T(8,128)(2,1)S(1)}, u32[]{:S(2)}, u32[]{:S(2)}) %collective-permute-start.22) | collective-permute-done | bytes 131104 | tf_op jit(solution)/shard_map/ppermute | solution.py:394
  118.1 5.2 %collective-permute-done.23.refs_7_.refs_5_ = bf16[64,1024]{1,0:T(8,128)(2,1)S(1)} collective-permute-done((bf16[64,1024]{1,0:T(8,128)(2,1)S(1)}, bf16[64,1024]{1,0:T(8,128)(2,1)S(1)}, u32[]{:S(2)}, u32[]{:S(2)}) %collective-permute-start.23) | collective-permute-done | bytes 131104 | tf_op jit(solution)/shard_map/ppermute | solution.py:394
  123.3 1.4 %collective-permute-done.25.refs_9_.refs_7_ = bf16[64,1024]{1,0:T(8,128)(2,1)S(1)} collective-permute-done((bf16[64,1024]{1,0:T(8,128)(2,1)S(1)}, bf16[64,1024]{1,0:T(8,128)(2,1)S(1)}, u32[]{:S(2)}, u32[]{:S(2)}) %collective-permute-start.25) | collective-permute-done | bytes 131104 | tf_op jit(solution)/shard_map/ppermute | solution.py:394
  124.7 1.1 smooth.2.refs_0_
  125.8 1.1 power.1
  127.0 1.5 %collective-permute-start.27 = (bf16[256,128]{1,0:T(8,128)(2,1)S(1)}, bf16[256,128]{1,0:T(8,128)(2,1)S(1)}, u32[]{:S(2)}, u32[]{:S(2)}) collective-permute-start(bf16[256,128]{1,0:T(8,128)(2,1)S(1)} %get-tuple-element.34), channel_id=1, source_target_pairs={{0,2},{1,3},{2,0},{3,1},{4,6},{5,7},{6,4},{7,5},{8,10},{9,11},{10,... | collective-permute-start | bytes 196616 | tf_op jit(solution)/shard_map/ppermute | solution.py:466
  128.4 1.4 %collective-permute-start.28 = (bf16[256,128]{1,0:T(8,128)(2,1)S(1)}, bf16[256,128]{1,0:T(8,128)(2,1)S(1)}, u32[]{:S(2)}, u32[]{:S(2)}) collective-permute-start(bf16[256,128]{1,0:T(8,128)(2,1)S(1)} %get-tuple-element.35), channel_id=1, source_target_pairs={{0,3},{1,0},{2,1},{3,2},{4,7},{5,4},{6,5},{7,6},{8,11},{9,8},{10,9... | collective-permute-start | bytes 196616 | tf_op jit(solution)/shard_map/ppermute | solution.py:466
  129.8 2.2 %subtract.2.refs_10_ = bf16[2,2,256,1024]{3,2,1,0:T(8,128)(2,1)} custom-call(s32[8,4,8]{2,1,0:T(4,128)S(1)} %copy-done.2, bf16[256,1024]{1,0:T(8,128)(2,1)S(1)} %copy-done.6, bf16[256,1024]{1,0:T(8,128)(2,1)S(1)} %copy-done.5, bf16[64,1024]{1,0:T(8,128)(2,1)S(1)} %fusion.10.refs_2_.refs_0_, bf16[64,1024]{1,0:T(8,128)(2,1)S(1)} %collective-permute-done.19.refs_3_.refs_1_, ...), custom_call_target="tpu_custom_call" | custom-call | flops 524288 | bytes 3145728 | tf_op jit(solution)/shard_map/subtract/pallas_call | solution.py:284
  132.1 2.2 %subtract.3 = bf16[2,2,256,1024]{3,2,1,0:T(8,128)(2,1)} custom-call(s32[8,4,8]{2,1,0:T(4,128)S(1)} %copy-done.2, bf16[256,1024]{1,0:T(8,128)(2,1)S(1)} %copy-done.4, bf16[256,1024]{1,0:T(8,128)(2,1)S(1)} %copy-done.3, bf16[64,1024]{1,0:T(8,128)(2,1)S(1)} %fusion.9.refs_2_.refs_0_, ...), custom_call_target="tpu_custom_call", output_to_operand_aliasing={{}: (11, {})} | custom-call | flops 524288 | bytes 3145728 | tf_op jit(solution)/shard_map/subtract/pallas_call | solution.py:284
  134.3 0.7 convert_add_fusion.4
  (51 shorter events, 0.5 us)
Async XLA Ops:
  4.0 0.8 copy-start
  4.8 0.8 copy-start.1
  8.8 9.7 %copy-start.10 = (bf16[1,256,1024]{2,1,0:T(8,128)(2,1)S(1)}, bf16[1,256,1024]{2,1,0:T(8,128)(2,1)}, u32[]{:S(2)}) copy-start(bf16[1,256,1024]{2,1,0:T(8,128)(2,1)} %weigh.5.weight_ref) | copy-start | bytes 1572868
  15.4 33.5 %collective-permute-start.3 = (bf16[256,1024]{1,0:T(8,128)(2,1)}, bf16[256,1024]{1,0:T(8,128)(2,1)S(1)}, u32[]{:S(2)}, u32[]{:S(2)}) collective-permute-start(bf16[256,1024]{1,0:T(8,128)(2,1)} %get-tuple-element.26), channel_id=1, source_target_pairs={{0,4},{4,0},{8,12},{12,8},{16,20},{20,16},{24,28},{28,24},{1,5},{5... | collective-permute-start | bytes 1572872 | tf_op jit(solution)/shard_map/ppermute | solution.py:394
  18.4 32.1 %collective-permute-start.6 = (bf16[256,1024]{1,0:T(8,128)(2,1)S(1)}, bf16[256,1024]{1,0:T(8,128)(2,1)}, u32[]{:S(2)}, u32[]{:S(2)}) collective-permute-start(bf16[256,1024]{1,0:T(8,128)(2,1)S(1)} %bitcast.41), channel_id=1, source_target_pairs={{0,4},{4,0},{8,12},{12,8},{16,20},{20,16},{24,28},{28,24},{1,5},{5... | collective-permute-start | bytes 1572872 | tf_op jit(solution)/shard_map/ppermute | solution.py:394
  22.2 8.6 %copy-start.7 = (bf16[2,256,1024]{2,1,0:T(8,128)(2,1)S(1)}, bf16[2,256,1024]{2,1,0:T(8,128)(2,1)}, u32[]{:S(2)}) copy-start(bf16[2,256,1024]{2,1,0:T(8,128)(2,1)} %weigh.3.weight_ref) | copy-start | bytes 3145732
  28.8 24.4 %collective-permute-start = (bf16[256,1024]{1,0:T(8,128)(2,1)}, bf16[256,1024]{1,0:T(8,128)(2,1)S(1)}, u32[]{:S(2)}, u32[]{:S(2)}) collective-permute-start(bf16[256,1024]{1,0:T(8,128)(2,1)} %get-tuple-element.24), channel_id=1, source_target_pairs={{0,4},{4,0},{8,12},{12,8},{16,20},{20,16},{24,28},{28,24},{1,5},{5... | collective-permute-start | bytes 1572872 | tf_op jit(solution)/shard_map/ppermute | solution.py:394
  30.8 24.2 %collective-permute-start.9 = (bf16[2,128,1024]{2,1,0:T(8,128)(2,1)S(1)}, bf16[2,128,1024]{2,1,0:T(8,128)(2,1)S(1)}, u32[]{:S(2)}, u32[]{:S(2)}) collective-permute-start(bf16[2,128,1024]{2,1,0:T(8,128)(2,1)S(1)} %constant_dynamic-slice_fusion), channel_id=1, source_target_pairs={{0,8},{4,12},{8,0},{12,4},{16,24},{20,28},{24,16},{28,20},{1,9},{5... | collective-permute-start | bytes 1572872 | tf_op jit(solution)/shard_map/ppermute | solution.py:394
  42.2 8.3 %copy-start.9 = (bf16[1,256,1024]{2,1,0:T(8,128)(2,1)S(1)}, bf16[1,256,1024]{2,1,0:T(8,128)(2,1)}, u32[]{:S(2)}) copy-start(bf16[1,256,1024]{2,1,0:T(8,128)(2,1)} %weigh.4.weight_ref) | copy-start | bytes 1572868
  42.2 11.0 %copy-start.11 = (bf16[256,1024]{1,0:T(8,128)(2,1)S(1)}, bf16[256,1024]{1,0:T(8,128)(2,1)}, u32[]{:S(2)}) copy-start(bf16[256,1024]{1,0:T(8,128)(2,1)} %get-tuple-element.23) | copy-start | bytes 1572868
  48.9 6.1 %copy-start.8 = (bf16[2,256,1024]{2,1,0:T(8,128)(2,1)S(1)}, bf16[2,256,1024]{2,1,0:T(8,128)(2,1)}, u32[]{:S(2)}) copy-start(bf16[2,256,1024]{2,1,0:T(8,128)(2,1)} %weigh.3.weight_ref) | copy-start | bytes 3145732
  48.9 17.4 %copy-start.12 = (bf16[256,1024]{1,0:T(8,128)(2,1)S(1)}, bf16[256,1024]{1,0:T(8,128)(2,1)}, u32[]{:S(2)}) copy-start(bf16[256,1024]{1,0:T(8,128)(2,1)} %get-tuple-element.25) | copy-start | bytes 1572868
  50.0 16.3 %collective-permute-start.4 = (bf16[128,1024]{1,0:T(8,128)(2,1)S(1)}, bf16[128,1024]{1,0:T(8,128)(2,1)S(1)}, u32[]{:S(2)}, u32[]{:S(2)}) collective-permute-start(bf16[128,1024]{1,0:T(8,128)(2,1)S(1)} %add_convert_fusion.1), channel_id=1, source_target_pairs={{0,8},{4,12},{8,0},{12,4},{16,24},{20,28},{24,16},{28,20},{1,9},{5... | collective-permute-start | bytes 786440 | tf_op jit(solution)/shard_map/ppermute | solution.py:394
  51.6 21.2 %collective-permute-start.7 = (bf16[128,1024]{1,0:T(8,128)(2,1)S(1)}, bf16[128,1024]{1,0:T(8,128)(2,1)S(1)}, u32[]{:S(2)}, u32[]{:S(2)}) collective-permute-start(bf16[128,1024]{1,0:T(8,128)(2,1)S(1)} %fusion), channel_id=1, source_target_pairs={{0,8},{4,12},{8,0},{12,4},{16,24},{20,28},{24,16},{28,20},{1,9},{5... | collective-permute-start | bytes 786440 | tf_op jit(solution)/shard_map/ppermute | solution.py:394
  53.3 22.9 %collective-permute-start.1 = (bf16[128,1024]{1,0:T(8,128)(2,1)S(1)}, bf16[128,1024]{1,0:T(8,128)(2,1)S(1)}, u32[]{:S(2)}, u32[]{:S(2)}) collective-permute-start(bf16[128,1024]{1,0:T(8,128)(2,1)S(1)} %add_convert_fusion.2), channel_id=1, source_target_pairs={{0,8},{4,12},{8,0},{12,4},{16,24},{20,28},{24,16},{28,20},{1,9},{5... | collective-permute-start | bytes 786440 | tf_op jit(solution)/shard_map/ppermute | solution.py:394
  55.1 21.9 %collective-permute-start.10 = (bf16[2,64,1024]{2,1,0:T(8,128)(2,1)S(1)}, bf16[2,64,1024]{2,1,0:T(8,128)(2,1)S(1)}, u32[]{:S(2)}, u32[]{:S(2)}) collective-permute-start(bf16[2,64,1024]{2,1,0:T(8,128)(2,1)S(1)} %add_convert_fusion), channel_id=1, source_target_pairs={{0,16},{4,20},{8,24},{12,28},{16,0},{20,4},{24,8},{28,12},{1,17},{... | collective-permute-start | bytes 786440 | tf_op jit(solution)/shard_map/ppermute | solution.py:394
  66.4 24.3 %collective-permute-start.5 = (bf16[64,1024]{1,0:T(8,128)(2,1)S(1)}, bf16[64,1024]{1,0:T(8,128)(2,1)S(1)}, u32[]{:S(2)}, u32[]{:S(2)}) collective-permute-start(bf16[64,1024]{1,0:T(8,128)(2,1)S(1)} %add_convert_fusion.4), channel_id=1, source_target_pairs={{0,16},{4,20},{8,24},{12,28},{16,0},{20,4},{24,8},{28,12},{1,17},{... | collective-permute-start | bytes 393224 | tf_op jit(solution)/shard_map/ppermute | solution.py:394
  73.8 41.6 %copy-start.2 = (s32[8,4,8]{2,1,0:T(4,128)S(1)}, s32[8,4,8]{2,1,0:T(4,128)}, u32[]{:S(2)}) copy-start(s32[8,4,8]{2,1,0:T(4,128)} %sky_ref.23) | copy-start | bytes 3076
  73.8 16.9 %collective-permute-start.8 = (bf16[64,1024]{1,0:T(8,128)(2,1)S(1)}, bf16[64,1024]{1,0:T(8,128)(2,1)S(1)}, u32[]{:S(2)}, u32[]{:S(2)}) collective-permute-start(bf16[64,1024]{1,0:T(8,128)(2,1)S(1)} %fusion.2), channel_id=1, source_target_pairs={{0,16},{4,20},{8,24},{12,28},{16,0},{20,4},{24,8},{28,12},{1,17},{... | collective-permute-start | bytes 393224 | tf_op jit(solution)/shard_map/ppermute | solution.py:394
  76.3 14.3 %collective-permute-start.2 = (bf16[64,1024]{1,0:T(8,128)(2,1)S(1)}, bf16[64,1024]{1,0:T(8,128)(2,1)S(1)}, u32[]{:S(2)}, u32[]{:S(2)}) collective-permute-start(bf16[64,1024]{1,0:T(8,128)(2,1)S(1)} %add_convert_fusion.5), channel_id=1, source_target_pairs={{0,16},{4,20},{8,24},{12,28},{16,0},{20,4},{24,8},{28,12},{1,17},{... | collective-permute-start | bytes 393224 | tf_op jit(solution)/shard_map/ppermute | solution.py:394
  77.1 14.8 %collective-permute-start.11 = (bf16[64,1024]{1,0:T(8,128)(2,1)S(1)}, bf16[64,1024]{1,0:T(8,128)(2,1)S(1)}, u32[]{:S(2)}, u32[]{:S(2)}) collective-permute-start(bf16[64,1024]{1,0:T(8,128)(2,1)S(1)} %fusion.11), channel_id=1, source_target_pairs={{0,4},{4,0},{8,12},{12,8},{16,20},{20,16},{24,28},{28,24},{1,5},{5... | collective-permute-start | bytes 393224 | tf_op jit(solution)/shard_map/ppermute | solution.py:394
  91.9 38.0 %copy-start.5 = (bf16[256,1024]{1,0:T(8,128)(2,1)S(1)}, bf16[256,1024]{1,0:T(8,128)(2,1)}, u32[]{:S(2)}) copy-start(bf16[256,1024]{1,0:T(8,128)(2,1)} %get-tuple-element.29.refs_1_) | copy-start | bytes 1572868
  91.9 38.0 %copy-start.6 = (bf16[256,1024]{1,0:T(8,128)(2,1)S(1)}, bf16[256,1024]{1,0:T(8,128)(2,1)}, u32[]{:S(2)}) copy-start(bf16[256,1024]{1,0:T(8,128)(2,1)} %get-tuple-element.28.refs_0_) | copy-start | bytes 1572868
  92.0 10.2 %collective-permute-start.13 = (bf16[64,1024]{1,0:T(8,128)(2,1)S(1)}, bf16[64,1024]{1,0:T(8,128)(2,1)S(1)}, u32[]{:S(2)}, u32[]{:S(2)}) collective-permute-start(bf16[64,1024]{1,0:T(8,128)(2,1)S(1)} %fusion.9.refs_2_.refs_0_), channel_id=1, source_target_pairs={{0,16},{4,20},{8,24},{12,28},{16,0},{20,4},{24,8},{28,12},{1,17},{... | collective-permute-start | bytes 393224 | tf_op jit(solution)/shard_map/ppermute | solution.py:394
  92.1 12.1 %collective-permute-start.12 = (bf16[64,1024]{1,0:T(8,128)(2,1)S(1)}, bf16[64,1024]{1,0:T(8,128)(2,1)S(1)}, u32[]{:S(2)}, u32[]{:S(2)}) collective-permute-start(bf16[64,1024]{1,0:T(8,128)(2,1)S(1)} %fusion.9.refs_2_.refs_0_), channel_id=1, source_target_pairs={{0,8},{4,12},{8,0},{12,4},{16,24},{20,28},{24,16},{28,20},{1,9},{5... | collective-permute-start | bytes 393224 | tf_op jit(solution)/shard_map/ppermute | solution.py:394
  93.7 10.6 %collective-permute-start.15 = (bf16[64,1024]{1,0:T(8,128)(2,1)S(1)}, bf16[64,1024]{1,0:T(8,128)(2,1)S(1)}, u32[]{:S(2)}, u32[]{:S(2)}) collective-permute-start(bf16[64,1024]{1,0:T(8,128)(2,1)S(1)} %fusion.9.refs_2_.refs_0_), channel_id=1, source_target_pairs={{0,4},{4,0},{8,12},{12,8},{16,20},{20,16},{24,28},{28,24},{1,5},{5... | collective-permute-start | bytes 393224 | tf_op jit(solution)/shard_map/ppermute | solution.py:394
  94.0 12.2 %collective-permute-start.20 = (bf16[64,1024]{1,0:T(8,128)(2,1)S(1)}, bf16[64,1024]{1,0:T(8,128)(2,1)S(1)}, u32[]{:S(2)}, u32[]{:S(2)}) collective-permute-start(bf16[64,1024]{1,0:T(8,128)(2,1)S(1)} %fusion.10.refs_2_.refs_0_), channel_id=1, source_target_pairs={{0,16},{4,20},{8,24},{12,28},{16,0},{20,4},{24,8},{28,12},{1,17},{... | collective-permute-start | bytes 393224 | tf_op jit(solution)/shard_map/ppermute | solution.py:394
  102.2 6.4 %collective-permute-start.14 = (bf16[64,1024]{1,0:T(8,128)(2,1)S(1)}, bf16[64,1024]{1,0:T(8,128)(2,1)S(1)}, u32[]{:S(2)}, u32[]{:S(2)}) collective-permute-start(bf16[64,1024]{1,0:T(8,128)(2,1)S(1)} %collective-permute-done.13.refs_4_.refs_2_), channel_id=1, source_target_pairs={{0,8},{4,12},{8,0},{12,4},{16,24},{20,28},{24,16},{28,20},{1,9},{5... | collective-permute-start | bytes 393224 | tf_op jit(solution)/shard_map/ppermute | solution.py:394
  102.2 9.2 %collective-permute-start.19 = (bf16[64,1024]{1,0:T(8,128)(2,1)S(1)}, bf16[64,1024]{1,0:T(8,128)(2,1)S(1)}, u32[]{:S(2)}, u32[]{:S(2)}) collective-permute-start(bf16[64,1024]{1,0:T(8,128)(2,1)S(1)} %fusion.10.refs_2_.refs_0_), channel_id=1, source_target_pairs={{0,8},{4,12},{8,0},{12,4},{16,24},{20,28},{24,16},{28,20},{1,9},{5... | collective-permute-start | bytes 393224 | tf_op jit(solution)/shard_map/ppermute | solution.py:394
  104.2 7.2 %collective-permute-start.16 = (bf16[64,1024]{1,0:T(8,128)(2,1)S(1)}, bf16[64,1024]{1,0:T(8,128)(2,1)S(1)}, u32[]{:S(2)}, u32[]{:S(2)}) collective-permute-start(bf16[64,1024]{1,0:T(8,128)(2,1)S(1)} %collective-permute-done.12.refs_3_.refs_1_), channel_id=1, source_target_pairs={{0,4},{4,0},{8,12},{12,8},{16,20},{20,16},{24,28},{28,24},{1,5},{5... | collective-permute-start | bytes 393224 | tf_op jit(solution)/shard_map/ppermute | solution.py:394
  104.3 9.1 %collective-permute-start.17 = (bf16[64,1024]{1,0:T(8,128)(2,1)S(1)}, bf16[64,1024]{1,0:T(8,128)(2,1)S(1)}, u32[]{:S(2)}, u32[]{:S(2)}) collective-permute-start(bf16[64,1024]{1,0:T(8,128)(2,1)S(1)} %collective-permute-done.13.refs_4_.refs_2_), channel_id=1, source_target_pairs={{0,4},{4,0},{8,12},{12,8},{16,20},{20,16},{24,28},{28,24},{1,5},{5... | collective-permute-start | bytes 393224 | tf_op jit(solution)/shard_map/ppermute | solution.py:394
  106.3 7.2 %collective-permute-start.21 = (bf16[64,1024]{1,0:T(8,128)(2,1)S(1)}, bf16[64,1024]{1,0:T(8,128)(2,1)S(1)}, u32[]{:S(2)}, u32[]{:S(2)}) collective-permute-start(bf16[64,1024]{1,0:T(8,128)(2,1)S(1)} %collective-permute-done.20.refs_4_.refs_2_), channel_id=1, source_target_pairs={{0,8},{4,12},{8,0},{12,4},{16,24},{20,28},{24,16},{28,20},{1,9},{5... | collective-permute-start | bytes 393224 | tf_op jit(solution)/shard_map/ppermute | solution.py:394
  108.6 6.9 %collective-permute-start.18 = (bf16[64,1024]{1,0:T(8,128)(2,1)S(1)}, bf16[64,1024]{1,0:T(8,128)(2,1)S(1)}, u32[]{:S(2)}, u32[]{:S(2)}) collective-permute-start(bf16[64,1024]{1,0:T(8,128)(2,1)S(1)} %collective-permute-done.14.refs_5_.refs_3_), channel_id=1, source_target_pairs={{0,4},{4,0},{8,12},{12,8},{16,20},{20,16},{24,28},{28,24},{1,5},{5... | collective-permute-start | bytes 393224 | tf_op jit(solution)/shard_map/ppermute | solution.py:394
  111.4 6.7 %collective-permute-start.22 = (bf16[64,1024]{1,0:T(8,128)(2,1)S(1)}, bf16[64,1024]{1,0:T(8,128)(2,1)S(1)}, u32[]{:S(2)}, u32[]{:S(2)}) collective-permute-start(bf16[64,1024]{1,0:T(8,128)(2,1)S(1)} %fusion.10.refs_2_.refs_0_), channel_id=1, source_target_pairs={{0,4},{4,0},{8,12},{12,8},{16,20},{20,16},{24,28},{28,24},{1,5},{5... | collective-permute-start | bytes 393224 | tf_op jit(solution)/shard_map/ppermute | solution.py:394
  111.5 11.8 %collective-permute-start.24 = (bf16[64,1024]{1,0:T(8,128)(2,1)S(1)}, bf16[64,1024]{1,0:T(8,128)(2,1)S(1)}, u32[]{:S(2)}, u32[]{:S(2)}) collective-permute-start(bf16[64,1024]{1,0:T(8,128)(2,1)S(1)} %collective-permute-done.20.refs_4_.refs_2_), channel_id=1, source_target_pairs={{0,4},{4,0},{8,12},{12,8},{16,20},{20,16},{24,28},{28,24},{1,5},{5... | collective-permute-start | bytes 393224 | tf_op jit(solution)/shard_map/ppermute | solution.py:394
  113.4 9.8 %collective-permute-start.23 = (bf16[64,1024]{1,0:T(8,128)(2,1)S(1)}, bf16[64,1024]{1,0:T(8,128)(2,1)S(1)}, u32[]{:S(2)}, u32[]{:S(2)}) collective-permute-start(bf16[64,1024]{1,0:T(8,128)(2,1)S(1)} %collective-permute-done.19.refs_3_.refs_1_), channel_id=1, source_target_pairs={{0,4},{4,0},{8,12},{12,8},{16,20},{20,16},{24,28},{28,24},{1,5},{5... | collective-permute-start | bytes 393224 | tf_op jit(solution)/shard_map/ppermute | solution.py:394
  113.5 11.2 %collective-permute-start.25 = (bf16[64,1024]{1,0:T(8,128)(2,1)S(1)}, bf16[64,1024]{1,0:T(8,128)(2,1)S(1)}, u32[]{:S(2)}, u32[]{:S(2)}) collective-permute-start(bf16[64,1024]{1,0:T(8,128)(2,1)S(1)} %collective-permute-done.21.refs_5_.refs_3_), channel_id=1, source_target_pairs={{0,4},{4,0},{8,12},{12,8},{16,20},{20,16},{24,28},{28,24},{1,5},{5... | collective-permute-start | bytes 393224 | tf_op jit(solution)/shard_map/ppermute | solution.py:394
  126.9 7.4 %collective-permute-start.26 = (bf16[256,128]{1,0:T(8,128)(2,1)S(1)}, bf16[256,128]{1,0:T(8,128)(2,1)S(1)}, u32[]{:S(2)}, u32[]{:S(2)}) collective-permute-start(bf16[256,128]{1,0:T(8,128)(2,1)S(1)} %get-tuple-element.33), channel_id=1, source_target_pairs={{0,1},{1,2},{2,3},{3,0},{4,5},{5,6},{6,7},{7,4},{8,9},{9,10},{10,1... | collective-permute-start | bytes 196616 | tf_op jit(solution)/shard_map/ppermute | solution.py:466
  127.0 7.3 %collective-permute-start.27 = (bf16[256,128]{1,0:T(8,128)(2,1)S(1)}, bf16[256,128]{1,0:T(8,128)(2,1)S(1)}, u32[]{:S(2)}, u32[]{:S(2)}) collective-permute-start(bf16[256,128]{1,0:T(8,128)(2,1)S(1)} %get-tuple-element.34), channel_id=1, source_target_pairs={{0,2},{1,3},{2,0},{3,1},{4,6},{5,7},{6,4},{7,5},{8,10},{9,11},{10,... | collective-permute-start | bytes 196616 | tf_op jit(solution)/shard_map/ppermute | solution.py:466
  128.4 5.9 %collective-permute-start.28 = (bf16[256,128]{1,0:T(8,128)(2,1)S(1)}, bf16[256,128]{1,0:T(8,128)(2,1)S(1)}, u32[]{:S(2)}, u32[]{:S(2)}) collective-permute-start(bf16[256,128]{1,0:T(8,128)(2,1)S(1)} %get-tuple-element.35), channel_id=1, source_target_pairs={{0,3},{1,0},{2,1},{3,2},{4,7},{5,4},{6,5},{7,6},{8,11},{9,8},{10,9... | collective-permute-start | bytes 196616 | tf_op jit(solution)/shard_map/ppermute | solution.py:466
  129.8 2.2 %copy-start.3 = (bf16[256,1024]{1,0:T(8,128)(2,1)S(1)}, bf16[256,1024]{1,0:T(8,128)(2,1)}, u32[]{:S(2)}) copy-start(bf16[256,1024]{1,0:T(8,128)(2,1)} %get-tuple-element.22.refs_1_) | copy-start | bytes 1572868
  129.8 2.2 %copy-start.4 = (bf16[256,1024]{1,0:T(8,128)(2,1)S(1)}, bf16[256,1024]{1,0:T(8,128)(2,1)}, u32[]{:S(2)}) copy-start(bf16[256,1024]{1,0:T(8,128)(2,1)} %get-tuple-element.21.refs_0_) | copy-start | bytes 1572868

commit v3 on v2

--- a/solution.py
+++ b/solution.py
@@ -18,9 +18,14 @@
 SHIFT = TILE // 2
 CHUNKS = 2
 OWN, OTHER = 0, 1
-EARLY_GRANT = 60 << 20
+EARLY_GRANT = 20 << 20
+LATE_GRANT = 24 << 20
 F32 = jnp.float32
 BF16 = jnp.bfloat16
+
+
+def in_hbm(array):
+    return pltpu.with_memory_space_constraint(array, pltpu.HBM)
 
 
 def start_column(sky_ref):
@@ -89,17 +94,17 @@
     return jnp.bitwise_and(jnp.right_shift(word, places - begin), 1)
 
 
-def pick_half(index, halves):
+def pick_block(index, halves, chunk, blocks):
     half = half_of(halves[0])
     for place in range(1, len(halves)):
-        half = jnp.where(index == place, half_of(halves[place]), half)
-    return half
-
-
-def weight_kernel(sky_count, halves, chunk, sky_ref, words_ref, variance_ref, weight_ref):
+        half = jnp.where(index >= place * blocks, half_of(halves[place]), half)
+    return (half * CHUNKS + chunk) * blocks + lax.rem(index, blocks)
+
+
+def weight_kernel(sky_count, halves, chunk, blocks, sky_ref, words_ref, variance_ref, weight_ref):
     rows, side = variance_ref.shape
     start = start_column(sky_ref)
-    first_row = (pick_half(pl.program_id(0), halves) * CHUNKS + chunk) * rows
+    first_row = pick_block(pl.program_id(0), halves, chunk, blocks) * rows
     lanes = lax.broadcasted_iota(jnp.int32, (8, side), 1)
     column_bad = bad_bits(words_ref, 0, 0, words_ref.shape[1], lanes)[0:1, :]
     places = first_row + lax.broadcasted_iota(jnp.int32, (rows, TILE), 0)
@@ -114,24 +119,28 @@
         weight_ref[0, :, pl.ds(pl.multiple_of(target, TILE), TILE)] = kept.astype(BF16)
 
 
-def weigh(inv_variance, words, sky_columns, halves, chunk, rows, sky_count):
+def weigh(inv_variance, words, sky_columns, halves, chunk, chunk_rows, sky_count):
     side = inv_variance.shape[0]
     stripe = sky_count * TILE
+    rows = min(TILE, chunk_rows)
+    blocks = chunk_rows // rows
     return pl.pallas_call(
-        functools.partial(weight_kernel, sky_count, halves, chunk),
-        out_shape=jax.ShapeDtypeStruct((len(halves), rows, stripe), BF16),
+        functools.partial(weight_kernel, sky_count, halves, chunk, blocks),
+        out_shape=jax.ShapeDtypeStruct((len(halves), chunk_rows, stripe), BF16),
         grid_spec=pltpu.PrefetchScalarGridSpec(
             num_scalar_prefetch=2,
-            grid=(len(halves),),
-            in_specs=[pl.BlockSpec((rows, side), lambda i, m, w: (pick_half(i, halves) * CHUNKS + chunk, 0))],
-            out_specs=pl.BlockSpec((1, rows, stripe), lambda i, m, w: (i, 0, 0)),
+            grid=(len(halves) * blocks,),
+            in_specs=[pl.BlockSpec((rows, side), lambda i, m, w: (pick_block(i, halves, chunk, blocks), 0))],
+            out_specs=pl.BlockSpec((1, rows, stripe), lambda i, m, w: (i // blocks, lax.rem(i, blocks), 0)),
         ),
         cost_estimate=pl.CostEstimate(
-            flops=len(halves) * rows * side * 8, bytes_accessed=len(halves) * rows * side * 4, transcendentals=0
+            flops=len(halves) * chunk_rows * side * 8,
+            bytes_accessed=len(halves) * chunk_rows * side * 4,
+            transcendentals=0,
         ),
         compiler_params=pltpu.CompilerParams(vmem_limit_bytes=EARLY_GRANT),
         name="weigh",
-    )(sky_columns, words, inv_variance)
+    )(in_hbm(sky_columns), in_hbm(words), in_hbm(inv_variance))
 
 
 def match_kernel(
@@ -208,8 +217,10 @@
     return pl.pallas_call(
         functools.partial(match_kernel, sky_count, which, chunk * steps, CHUNKS * steps),
         out_shape=(
-            jax.ShapeDtypeStruct((chunk_rows, side), BF16),
-            jax.ShapeDtypeStruct((chunk_rows, stripe), BF16),
+            pltpu.HBM((chunk_rows, side), BF16),
+            pltpu.HBM((chunk_rows, stripe), BF16)
+            if which == OTHER
+            else jax.ShapeDtypeStruct((chunk_rows, stripe), BF16),
         ),
         grid_spec=pltpu.PrefetchScalarGridSpec(
             num_scalar_prefetch=1,
@@ -236,7 +247,7 @@
         ),
         compiler_params=pltpu.CompilerParams(vmem_limit_bytes=EARLY_GRANT),
         name="match",
-    )(sky_columns, picture, picture, picture, column_band, row_band, weight)
+    )(in_hbm(sky_columns), *[in_hbm(picture)] * 3, column_band, row_band, weight)
 
 
 def row_of(place, line, chunk_rows):
@@ -296,34 +307,39 @@
         ),
         compiler_params=pltpu.CompilerParams(vmem_limit_bytes=24 << 20),
         name="subtract",
-    )(sky_columns, *operands)
-
-
-def smooth_kernel(sky_count, pair, line, sky_ref, across_ref, *refs):
-    pieces, out_ref = refs[:-1], refs[-1]
-    part_rows = pieces[0].shape[0]
-    chunk_rows = out_ref.shape[1]
-
+    )(in_hbm(sky_columns), *operands)
+
+
+def smooth_pieces(sky_count, line, across, pieces, chunk_rows, store):
     def column(piece, away):
         source = lax.rem(lax.axis_index("sky") + away, sky_count) * TILE
         return piece[:, pl.ds(pl.multiple_of(source, TILE), TILE)]
 
-    for group in range(pair):
-        half = half_of((OWN, OTHER)[group])
+    for group in range(len(pieces) // line):
         for step in range(line):
-            rows = piece_rows(step, line, chunk_rows, part_rows)
             piece = pieces[group * line + step]
             window = jnp.concatenate(
                 [column(piece, sky_count - 1)[:, SHIFT:], column(piece, 0), column(piece, 1)[:, :SHIFT]], axis=1
             )
-            out_ref[half, rows, :] = jnp.dot(window, across_ref[...], preferred_element_type=F32).astype(BF16)
+            row = row_of(lax.axis_index("sky") // 2 ^ step, line, chunk_rows)
+            store(half_of((OWN, OTHER)[group]), row, jnp.dot(window, across, preferred_element_type=F32).astype(BF16))
+
+
+def smooth_kernel(sky_count, line, sky_ref, across_ref, *refs):
+    pieces, out_ref = refs[:-1], refs[-1]
+    part_rows, chunk_rows = pieces[0].shape[0], out_ref.shape[1]
+
+    def store(half, row, values):
+        out_ref[half, pl.ds(pl.multiple_of(row, part_rows), part_rows), :] = values
+
+    smooth_pieces(sky_count, line, across_ref[...], pieces, chunk_rows, store)
 
 
 def smooth(pieces, across_band, sky_columns, pair, chunk_rows, sky_count):
     line = len(pieces) // pair
     operands = [across_band, *pieces]
     return pl.pallas_call(
-        functools.partial(smooth_kernel, sky_count, pair, line),
+        functools.partial(smooth_kernel, sky_count, line),
         out_shape=jax.ShapeDtypeStruct((pair, chunk_rows, TILE), BF16),
         grid_spec=pltpu.PrefetchScalarGridSpec(
             num_scalar_prefetch=1,
@@ -334,22 +350,32 @@
         cost_estimate=pl.CostEstimate(
             flops=pair * chunk_rows * TILE * 512, bytes_accessed=pair * chunk_rows * sky_count * TILE * 2, transcendentals=0
         ),
-        compiler_params=pltpu.CompilerParams(vmem_limit_bytes=20 << 20),
+        compiler_params=pltpu.CompilerParams(vmem_limit_bytes=LATE_GRANT),
         name="smooth",
-    )(sky_columns, *operands)
-
-
-def power_kernel(band_count, sky_ref, down_ref, *refs):
-    sources, powers, smoothed = refs[:CHUNKS], refs[CHUNKS : CHUNKS + band_count], refs[-1]
-    pair, chunk_rows = sources[0].shape[:2]
+    )(in_hbm(sky_columns), *operands)
+
+
+def power_kernel(sky_count, line, band_count, sky_ref, across_ref, down_ref, *refs):
+    sources = refs[: CHUNKS - 1]
+    pieces = refs[CHUNKS - 1 : -band_count - 1]
+    powers, smoothed = refs[-band_count - 1 : -1], refs[-1]
+    part_rows = pieces[0].shape[0]
+    pair = len(pieces) // line
+    chunk_rows = part_rows * line
     side = pair * CHUNKS * chunk_rows
     rows = side // band_count
     smoothed[0:EDGE, :] = jnp.zeros((EDGE, TILE), BF16)
     smoothed[EDGE + side :, :] = jnp.zeros((EDGE, TILE), BF16)
     for half in range(pair):
-        for chunk in range(CHUNKS):
+        for chunk in range(CHUNKS - 1):
             first = EDGE + (half * CHUNKS + chunk) * chunk_rows
             smoothed[first : first + chunk_rows, :] = sources[chunk][half]
+
+    def store(half, row, values):
+        first = EDGE + (half * CHUNKS + CHUNKS - 1) * chunk_rows + row
+        smoothed[pl.ds(pl.multiple_of(first, EDGE), part_rows), :] = values
+
+    smooth_pieces(sky_count, line, across_ref[...], pieces, chunk_rows, store)
     for step in range(band_count):
         first = lax.rem(lax.axis_index("band") + step, band_count) * rows
         for inner in range(rows // TILE):
@@ -358,25 +384,26 @@
             powers[step][inner * TILE : (inner + 1) * TILE, :] = (filtered * filtered).astype(powers[step].dtype)
 
 
-def power(sources, down_band, sky_columns, band_count):
-    side = CHUNKS * sources[0].shape[0] * sources[0].shape[1]
+def power(sources, pieces, across_band, down_band, sky_columns, pair, sky_count, band_count):
+    line = len(pieces) // pair
+    side = CHUNKS * pair * line * pieces[0].shape[0]
+    operands = [across_band, down_band, *sources, *pieces]
     return pl.pallas_call(
-        functools.partial(power_kernel, band_count),
+        functools.partial(power_kernel, sky_count, line, band_count),
         out_shape=[
             jax.ShapeDtypeStruct((side // band_count, TILE), BF16 if step else F32) for step in range(band_count)
         ],
         grid_spec=pltpu.PrefetchScalarGridSpec(
             num_scalar_prefetch=1,
             grid=(1,),
-            in_specs=[pl.BlockSpec(down_band.shape, lambda i, m: (0, 0))]
-            + [pl.BlockSpec(array.shape, lambda i, m: (0, 0, 0)) for array in sources],
+            in_specs=[pl.BlockSpec(array.shape, lambda i, m, n=array.ndim: (0,) * n) for array in operands],
             out_specs=[pl.BlockSpec((side // band_count, TILE), lambda i, m: (0, 0))] * band_count,
             scratch_shapes=[pltpu.VMEM((side + 2 * EDGE, TILE), BF16)],
         ),
-        cost_estimate=pl.CostEstimate(flops=side * TILE * 320, bytes_accessed=side * TILE * 6, transcendentals=0),
-        compiler_params=pltpu.CompilerParams(vmem_limit_bytes=16 << 20),
+        cost_estimate=pl.CostEstimate(flops=side * TILE * 600, bytes_accessed=side * TILE * 12, transcendentals=0),
+        compiler_params=pltpu.CompilerParams(vmem_limit_bytes=LATE_GRANT),
         name="power",
-    )(sky_columns, down_band, *sources)
+    )(in_hbm(sky_columns), *operands)
 
 
 def body(exposures, inv_variance, mask_planes, sky_columns, basis_rows, basis_cols, match_coeffs, detect_taps):
@@ -456,10 +483,14 @@
         for step in range(1, line):
             far[step] = exchange(near[step], 0)
         pieces = [near[step] for step in range(line)] + [far[step] for step in range(line)]
-        smoothed[c] = smooth(pieces, across_band, sky_columns, pair, chunk_rows, sky_count)
+        if c < CHUNKS - 1:
+            smoothed[c] = smooth(pieces, across_band, sky_columns, pair, chunk_rows, sky_count)
+        else:
+            powers = power(
+                smoothed[:-1], pieces, across_band, down_band, sky_columns, pair, sky_count, band_count
+            )
         difference = subtract([home[c], away[c]], pieces, sky_columns, c, difference, sky_count)
 
-    powers = power(smoothed, down_band, sky_columns, band_count)
     detection = powers[0]
     for step in range(1, band_count):
         ring = [(i, (i + step) % band_count) for i in range(band_count)]

time: 136 us -> 127 us (0.934)
  waiting for transfers between devices: 49.5 us -> 40 us
  Pallas kernels: 45.4 us -> 41.1 us
  other arithmetic: 7.95 us -> 11.6 us
  starting transfers between devices: 29.7 us -> 31.1 us
    ppermute x26, waiting for transfers between devices: 49.5 us -> 40 us  [exchange(): lax.ppermute(block, 'sky', [(i, i ^ 1 << bit) for i in range(sky_count)])]
    convert_element_type x7, other arithmetic: 3.51 us -> 6.15 us  [reduce_line(): arrived = exchange(leaving.astype(BF16), bit)]
    pallas_call x4, Pallas kernels: 26.4 us -> 24 us  [match(): pl.pallas_call(functools.partial(match_kernel, sky_count, which, chunk *...]
    pallas_call x6 -> x5, Pallas kernels: 13.5 us -> 11.2 us  [the longest x3 8.37 us: weigh(): pl.pallas_call(functools.partial(weight_kernel, sky_count, halves, chunk,...]
    unnamed x26 -> x8, local copies, waits for them, and re-layouts: 1.61 us -> 0.02 us
    ppermute x26, starting transfers between devices: 26.7 us -> 28.2 us  [exchange(): lax.ppermute(block, 'sky', [(i, i ^ 1 << bit) for i in range(sky_count)])]
  transfers between devices with their start and end apart: 29 -> 29, of which waited for: 10 -> 14; matrix products, arithmetic and copies ran while one was open for 4% -> 8% of each run, Pallas kernels for 24% -> 24%
where the time goes in v3:
time: 127 us; the launch traced here: 125 us
  Pallas kernels  41.1 us (32%)
  waiting for transfers between devices  40 us (31%)
  starting transfers between devices  31.1 us (24%)
  other arithmetic  11.6 us (9%)
    ppermute x26, waiting for transfers between devices, exchange(): lax.ppermute(block, 'sky', [(i, i ^ 1 << bit) for i in range(sky_count)])  40 us
    ppermute x26, starting transfers between devices, exchange(): lax.ppermute(block, 'sky', [(i, i ^ 1 << bit) for i in range(sky_count)])  28.2 us
    pallas_call x4, Pallas kernels, match(): pl.pallas_call(functools.partial(match_kernel, sky_count, which, chunk *...  24 us
    pallas_call x3, Pallas kernels, weigh(): pl.pallas_call(functools.partial(weight_kernel, sky_count, halves, chunk,...  8.37 us
    convert_element_type x7, other arithmetic, reduce_line(): arrived = exchange(leaving.astype(BF16), bit)  6.15 us
    pallas_call x2, Pallas kernels, subtract(): pl.pallas_call(functools.partial(difference_kernel, sky_count, pair, line...  4.84 us
    ppermute x3, starting transfers between devices, body(): detection = detection + lax.ppermute(powers[step], 'band', ring).astype(F32)  2.98 us
  transfers between devices with their start and end apart: 29, of which 14 were waited for; matrix products, arithmetic and copies ran while one was open for 8% of the time, Pallas kernels for 24%

profile of v3, /device:TPU:0, one launch (start us, length us, event | category | flops | bytes accessed | tf_op | source)
XLA Modules:
  0.0 125.5 jit_solution(3817869509140503751)
XLA Ops:
  0.6 0.7 convert_element_type.190
  1.3 0.7 convert_convert_fusion
  2.0 0.8 multiply_convert_fusion
  2.8 0.1 pad_convert_fusion
  2.8 0.1 select_maximum_fusion.base_ref
  2.9 1.1 prepare.1
  4.0 2.4 %weigh.5.weight_ref = bf16[1,256,1024]{2,1,0:T(8,128)(2,1)S(1)} custom-call(s32[8,4,8]{2,1,0:T(4,128)} %sky_ref.21, s32[2,35]{1,0:T(2,128)} %bitcast.42, bf16[1024,1024]{1,0:T(8,128)(2,1)} %bitcast.38), custom_call_target="tpu_custom_call" | custom-call | flops 2097152 | bytes 1048576 | tf_op jit(solution)/shard_map/weigh/pallas_call | solution.py:127
  6.4 6.1 %match.7 = (bf16[256,1024]{1,0:T(8,128)(2,1)}, bf16[256,1024]{1,0:T(8,128)(2,1)}) custom-call(s32[8,4,8]{2,1,0:T(4,128)} %sky_ref.21, bf16[1024,1024]{1,0:T(8,128)(2,1)} %bitcast.26, bf16[1024,1024]{1,0:T(8,128)(2,1)} %bitcast.27, bf16[1024,1024]{1,0:T(8,128)(2,1)} %bitcast.28, bf16[256,1152]{1,0:T(8,128)(2,1)S(1)} %get-tuple-element.19.column_ref, ...), custom_call_target="tpu_custom_call" | custom-call | flops 1962934272 | bytes 2097152 | tf_op jit(solution)/shard_map/match/pallas_call | solution.py:217
  12.5 3.0 %collective-permute-start.3 = (bf16[256,1024]{1,0:T(8,128)(2,1)}, bf16[256,1024]{1,0:T(8,128)(2,1)}, u32[]{:S(2)}, u32[]{:S(2)}) collective-permute-start(bf16[256,1024]{1,0:T(8,128)(2,1)} %get-tuple-element.26), channel_id=1, source_target_pairs={{0,4},{4,0},{8,12},{12,8},{16,20},{20,16},{24,28},{28,24},{1,5},{5... | collective-permute-start | bytes 1572872 | tf_op jit(solution)/shard_map/ppermute | solution.py:421
  15.5 3.6 %weigh.3.weight_ref = bf16[2,256,1024]{2,1,0:T(8,128)(2,1)S(1)} custom-call(s32[8,4,8]{2,1,0:T(4,128)} %sky_ref.21, s32[2,35]{1,0:T(2,128)} %bitcast.43, bf16[1024,1024]{1,0:T(8,128)(2,1)} %bitcast.39), custom_call_target="tpu_custom_call" | custom-call | flops 4194304 | bytes 2097152 | tf_op jit(solution)/shard_map/weigh/pallas_call | solution.py:127
  19.1 6.0 %match.5 = (bf16[256,1024]{1,0:T(8,128)(2,1)}, bf16[256,1024]{1,0:T(8,128)(2,1)}) custom-call(s32[8,4,8]{2,1,0:T(4,128)} %sky_ref.21, bf16[1024,1024]{1,0:T(8,128)(2,1)} %bitcast.29, bf16[1024,1024]{1,0:T(8,128)(2,1)} %bitcast.30, bf16[1024,1024]{1,0:T(8,128)(2,1)} %bitcast.31, bf16[256,1152]{1,0:T(8,128)(2,1)S(1)} %get-tuple-element.19.column_ref, ...), custom_call_target="tpu_custom_call" | custom-call | flops 1962934272 | bytes 2097152 | tf_op jit(solution)/shard_map/match/pallas_call | solution.py:217
  25.1 2.0 %collective-permute-start = (bf16[256,1024]{1,0:T(8,128)(2,1)}, bf16[256,1024]{1,0:T(8,128)(2,1)}, u32[]{:S(2)}, u32[]{:S(2)}) collective-permute-start(bf16[256,1024]{1,0:T(8,128)(2,1)} %get-tuple-element.24), channel_id=1, source_target_pairs={{0,4},{4,0},{8,12},{12,8},{16,20},{20,16},{24,28},{28,24},{1,5},{5... | collective-permute-start | bytes 1572872 | tf_op jit(solution)/shard_map/ppermute | solution.py:421
  27.1 0.8 constant_dynamic-slice_fusion
  28.0 1.6 %collective-permute-start.9 = (bf16[2,128,1024]{2,1,0:T(8,128)(2,1)}, bf16[2,128,1024]{2,1,0:T(8,128)(2,1)S(1)}, u32[]{:S(2)}, u32[]{:S(2)}) collective-permute-start(bf16[2,128,1024]{2,1,0:T(8,128)(2,1)} %constant_dynamic-slice_fusion), channel_id=1, source_target_pairs={{0,8},{4,12},{8,0},{12,4},{16,24},{20,28},{24,16},{28,20},{1,9},{5... | collective-permute-start | bytes 1572872 | tf_op jit(solution)/shard_map/ppermute | solution.py:421
  29.6 2.4 %weigh.4.weight_ref = bf16[1,256,1024]{2,1,0:T(8,128)(2,1)S(1)} custom-call(s32[8,4,8]{2,1,0:T(4,128)} %sky_ref.21, s32[2,35]{1,0:T(2,128)} %bitcast.44, bf16[1024,1024]{1,0:T(8,128)(2,1)} %bitcast.40), custom_call_target="tpu_custom_call" | custom-call | flops 2097152 | bytes 1048576 | tf_op jit(solution)/shard_map/weigh/pallas_call | solution.py:127
  32.0 6.0 %match.4 = (bf16[256,1024]{1,0:T(8,128)(2,1)}, bf16[256,1024]{1,0:T(8,128)(2,1)S(1)}) custom-call(s32[8,4,8]{2,1,0:T(4,128)} %sky_ref.21, bf16[1024,1024]{1,0:T(8,128)(2,1)} %bitcast.32, bf16[1024,1024]{1,0:T(8,128)(2,1)} %bitcast.33, bf16[1024,1024]{1,0:T(8,128)(2,1)} %bitcast.34, bf16[256,1152]{1,0:T(8,128)(2,1)S(1)} %get-tuple-element.19.column_ref, ...), custom_call_target="tpu_custom_call" | custom-call | flops 1962934272 | bytes 2097152 | tf_op jit(solution)/shard_map/match/pallas_call | solution.py:217
  37.9 5.9 %match.6 = (bf16[256,1024]{1,0:T(8,128)(2,1)}, bf16[256,1024]{1,0:T(8,128)(2,1)S(1)}) custom-call(s32[8,4,8]{2,1,0:T(4,128)} %sky_ref.21, bf16[1024,1024]{1,0:T(8,128)(2,1)} %bitcast.35, bf16[1024,1024]{1,0:T(8,128)(2,1)} %bitcast.36, bf16[1024,1024]{1,0:T(8,128)(2,1)} %bitcast.37, bf16[256,1152]{1,0:T(8,128)(2,1)S(1)} %get-tuple-element.19.column_ref, ...), custom_call_target="tpu_custom_call" | custom-call | flops 1962934272 | bytes 2097152 | tf_op jit(solution)/shard_map/match/pallas_call | solution.py:217
  43.9 1.0 add_convert_fusion.1
  44.9 0.5 collective-permute-start.4
  45.4 1.0 fusion
  46.4 1.6 %collective-permute-start.7 = (bf16[128,1024]{1,0:T(8,128)(2,1)S(1)}, bf16[128,1024]{1,0:T(8,128)(2,1)S(1)}, u32[]{:S(2)}, u32[]{:S(2)}) collective-permute-start(bf16[128,1024]{1,0:T(8,128)(2,1)S(1)} %fusion), channel_id=1, source_target_pairs={{0,8},{4,12},{8,0},{12,4},{16,24},{20,28},{24,16},{28,20},{1,9},{5... | collective-permute-start | bytes 786440 | tf_op jit(solution)/shard_map/ppermute | solution.py:421
  48.1 2.1 %collective-permute-done = bf16[256,1024]{1,0:T(8,128)(2,1)} collective-permute-done((bf16[256,1024]{1,0:T(8,128)(2,1)}, bf16[256,1024]{1,0:T(8,128)(2,1)}, u32[]{:S(2)}, u32[]{:S(2)}) %collective-permute-start) | collective-permute-done | bytes 524320 | tf_op jit(solution)/shard_map/ppermute | solution.py:421
  50.2 1.0 add_convert_fusion.2
  51.2 1.8 %collective-permute-start.1 = (bf16[128,1024]{1,0:T(8,128)(2,1)S(1)}, bf16[128,1024]{1,0:T(8,128)(2,1)S(1)}, u32[]{:S(2)}, u32[]{:S(2)}) collective-permute-start(bf16[128,1024]{1,0:T(8,128)(2,1)S(1)} %add_convert_fusion.2), channel_id=1, source_target_pairs={{0,8},{4,12},{8,0},{12,4},{16,24},{20,28},{24,16},{28,20},{1,9},{5... | collective-permute-start | bytes 786440 | tf_op jit(solution)/shard_map/ppermute | solution.py:421
  53.0 0.1 add_convert_fusion
  53.2 2.7 %collective-permute-start.10 = (bf16[2,64,1024]{2,1,0:T(8,128)(2,1)S(1)}, bf16[2,64,1024]{2,1,0:T(8,128)(2,1)S(1)}, u32[]{:S(2)}, u32[]{:S(2)}) collective-permute-start(bf16[2,64,1024]{2,1,0:T(8,128)(2,1)S(1)} %add_convert_fusion), channel_id=1, source_target_pairs={{0,16},{4,20},{8,24},{12,28},{16,0},{20,4},{24,8},{28,12},{1,17},{... | collective-permute-start | bytes 786440 | tf_op jit(solution)/shard_map/ppermute | solution.py:421
  55.8 1.0 add_convert_fusion.4
  56.8 0.9 collective-permute-start.5
  57.7 11.8 %collective-permute-done.7 = bf16[128,1024]{1,0:T(8,128)(2,1)S(1)} collective-permute-done((bf16[128,1024]{1,0:T(8,128)(2,1)S(1)}, bf16[128,1024]{1,0:T(8,128)(2,1)S(1)}, u32[]{:S(2)}, u32[]{:S(2)}) %collective-permute-start.7) | collective-permute-done | bytes 262176 | tf_op jit(solution)/shard_map/ppermute | solution.py:421
  69.6 1.0 fusion.2
  70.6 0.1 collective-permute-start.8
  70.6 2.3 %collective-permute-done.1 = bf16[128,1024]{1,0:T(8,128)(2,1)S(1)} collective-permute-done((bf16[128,1024]{1,0:T(8,128)(2,1)S(1)}, bf16[128,1024]{1,0:T(8,128)(2,1)S(1)}, u32[]{:S(2)}, u32[]{:S(2)}) %collective-permute-start.1) | collective-permute-done | bytes 262176 | tf_op jit(solution)/shard_map/ppermute | solution.py:421
  72.9 1.0 add_convert_fusion.5
  73.9 0.7 collective-permute-start.2
  74.6 0.1 fusion.11
  74.8 4.6 %collective-permute-done.5 = bf16[64,1024]{1,0:T(8,128)(2,1)S(1)} collective-permute-done((bf16[64,1024]{1,0:T(8,128)(2,1)S(1)}, bf16[64,1024]{1,0:T(8,128)(2,1)S(1)}, u32[]{:S(2)}, u32[]{:S(2)}) %collective-permute-start.5) | collective-permute-done | bytes 131104 | tf_op jit(solution)/shard_map/ppermute | solution.py:421
  79.4 4.3 %collective-permute-done.8 = bf16[64,1024]{1,0:T(8,128)(2,1)S(1)} collective-permute-done((bf16[64,1024]{1,0:T(8,128)(2,1)S(1)}, bf16[64,1024]{1,0:T(8,128)(2,1)S(1)}, u32[]{:S(2)}, u32[]{:S(2)}) %collective-permute-start.8) | collective-permute-done | bytes 131104 | tf_op jit(solution)/shard_map/ppermute | solution.py:421
  83.7 1.2 fusion.10.refs_2_.refs_0_
  85.0 3.8 %collective-permute-start.19 = (bf16[64,1024]{1,0:T(8,128)(2,1)S(1)}, bf16[64,1024]{1,0:T(8,128)(2,1)S(1)}, u32[]{:S(2)}, u32[]{:S(2)}) collective-permute-start(bf16[64,1024]{1,0:T(8,128)(2,1)S(1)} %fusion.10.refs_2_.refs_0_), channel_id=1, source_target_pairs={{0,8},{4,12},{8,0},{12,4},{16,24},{20,28},{24,16},{28,20},{1,9},{5... | collective-permute-start | bytes 393224 | tf_op jit(solution)/shard_map/ppermute | solution.py:421
  88.8 1.0 convert_add_fusion.3
  89.8 0.1 fusion.9.refs_2_.refs_1_
  90.0 0.1 collective-permute-start.13
  90.1 3.6 %collective-permute-done.20.refs_4_.refs_2_ = bf16[64,1024]{1,0:T(8,128)(2,1)S(1)} collective-permute-done((bf16[64,1024]{1,0:T(8,128)(2,1)S(1)}, bf16[64,1024]{1,0:T(8,128)(2,1)S(1)}, u32[]{:S(2)}, u32[]{:S(2)}) %collective-permute-start.20) | collective-permute-done | bytes 131104 | tf_op jit(solution)/shard_map/ppermute | solution.py:421
  93.7 2.0 %collective-permute-start.12 = (bf16[64,1024]{1,0:T(8,128)(2,1)S(1)}, bf16[64,1024]{1,0:T(8,128)(2,1)S(1)}, u32[]{:S(2)}, u32[]{:S(2)}) collective-permute-start(bf16[64,1024]{1,0:T(8,128)(2,1)S(1)} %fusion.9.refs_2_.refs_1_), channel_id=1, source_target_pairs={{0,8},{4,12},{8,0},{12,4},{16,24},{20,28},{24,16},{28,20},{1,9},{5... | collective-permute-start | bytes 393224 | tf_op jit(solution)/shard_map/ppermute | solution.py:421
  95.7 0.6 collective-permute-done.19.refs_3_.refs_1_
  96.4 2.0 %collective-permute-start.24 = (bf16[64,1024]{1,0:T(8,128)(2,1)S(1)}, bf16[64,1024]{1,0:T(8,128)(2,1)S(1)}, u32[]{:S(2)}, u32[]{:S(2)}) collective-permute-start(bf16[64,1024]{1,0:T(8,128)(2,1)S(1)} %collective-permute-done.20.refs_4_.refs_2_), channel_id=1, source_target_pairs={{0,4},{4,0},{8,12},{12,8},{16,20},{20,16},{24,28},{28,24},{1,5},{5... | collective-permute-start | bytes 393224 | tf_op jit(solution)/shard_map/ppermute | solution.py:421
  98.4 1.7 %collective-permute-done.21.refs_5_.refs_3_ = bf16[64,1024]{1,0:T(8,128)(2,1)S(1)} collective-permute-done((bf16[64,1024]{1,0:T(8,128)(2,1)S(1)}, bf16[64,1024]{1,0:T(8,128)(2,1)S(1)}, u32[]{:S(2)}, u32[]{:S(2)}) %collective-permute-start.21) | collective-permute-done | bytes 131104 | tf_op jit(solution)/shard_map/ppermute | solution.py:421
  100.1 0.9 collective-permute-start.25
  101.0 0.6 collective-permute-done.12.refs_3_.refs_2_
  101.6 0.8 collective-permute-start.15
  102.4 1.2 collective-permute-start.17
  103.7 1.5 %collective-permute-done.24.refs_8_.refs_6_ = bf16[64,1024]{1,0:T(8,128)(2,1)S(1)} collective-permute-done((bf16[64,1024]{1,0:T(8,128)(2,1)S(1)}, bf16[64,1024]{1,0:T(8,128)(2,1)S(1)}, u32[]{:S(2)}, u32[]{:S(2)}) %collective-permute-start.24) | collective-permute-done | bytes 131104 | tf_op jit(solution)/shard_map/ppermute | solution.py:421
  105.2 2.0 %collective-permute-start.18 = (bf16[64,1024]{1,0:T(8,128)(2,1)S(1)}, bf16[64,1024]{1,0:T(8,128)(2,1)S(1)}, u32[]{:S(2)}, u32[]{:S(2)}) collective-permute-start(bf16[64,1024]{1,0:T(8,128)(2,1)S(1)} %collective-permute-done.14.refs_5_.refs_4_), channel_id=1, source_target_pairs={{0,4},{4,0},{8,12},{12,8},{16,20},{20,16},{24,28},{28,24},{1,5},{5... | collective-permute-start | bytes 393224 | tf_op jit(solution)/shard_map/ppermute | solution.py:421
  107.2 0.8 collective-permute-done.25.refs_9_.refs_7_
  108.0 1.2 smooth.1.refs_0_
  109.2 1.6 %collective-permute-done.15.refs_6_.refs_5_ = bf16[64,1024]{1,0:T(8,128)(2,1)S(1)} collective-permute-done((bf16[64,1024]{1,0:T(8,128)(2,1)S(1)}, bf16[64,1024]{1,0:T(8,128)(2,1)S(1)}, u32[]{:S(2)}, u32[]{:S(2)}) %collective-permute-start.15) | collective-permute-done | bytes 131104 | tf_op jit(solution)/shard_map/ppermute | solution.py:421
  110.8 3.2 %collective-permute-done.16.refs_7_.refs_6_ = bf16[64,1024]{1,0:T(8,128)(2,1)S(1)} collective-permute-done((bf16[64,1024]{1,0:T(8,128)(2,1)S(1)}, bf16[64,1024]{1,0:T(8,128)(2,1)S(1)}, u32[]{:S(2)}, u32[]{:S(2)}) %collective-permute-start.16) | collective-permute-done | bytes 131104 | tf_op jit(solution)/shard_map/ppermute | solution.py:421
  114.0 1.4 %collective-permute-done.18.refs_9_.refs_8_ = bf16[64,1024]{1,0:T(8,128)(2,1)S(1)} collective-permute-done((bf16[64,1024]{1,0:T(8,128)(2,1)S(1)}, bf16[64,1024]{1,0:T(8,128)(2,1)S(1)}, u32[]{:S(2)}, u32[]{:S(2)}) %collective-permute-start.18) | collective-permute-done | bytes 131104 | tf_op jit(solution)/shard_map/ppermute | solution.py:421
  115.4 1.5 %power.1 = (f32[256,128]{1,0:T(8,128)S(1)}, bf16[256,128]{1,0:T(8,128)(2,1)S(1)}, bf16[256,128]{1,0:T(8,128)(2,1)S(1)}, bf16[256,128]{1,0:T(8,128)(2,1)S(1)}) custom-call(s32[8,4,8]{2,1,0:T(4,128)} %sky_ref.21, bf16[256,128]{1,0:T(8,128)(2,1)S(1)} %get-tuple-element.30.across_ref, bf16[128,160]{1,0:T(8,128)(2,1)S(1)} %get-tuple-element.31.down_ref, ...), custom_call_target="tpu_custom_call" | custom-call | flops 78643200 | bytes 1572864 | tf_op jit(solution)/shard_map/power/pallas_call | solution.py:391
  117.0 1.5 %collective-permute-start.27 = (bf16[256,128]{1,0:T(8,128)(2,1)S(1)}, bf16[256,128]{1,0:T(8,128)(2,1)S(1)}, u32[]{:S(2)}, u32[]{:S(2)}) collective-permute-start(bf16[256,128]{1,0:T(8,128)(2,1)S(1)} %get-tuple-element.34), channel_id=1, source_target_pairs={{0,2},{1,3},{2,0},{3,1},{4,6},{5,7},{6,4},{7,5},{8,10},{9,11},{10,... | collective-permute-start | bytes 196616 | tf_op jit(solution)/shard_map/ppermute | solution.py:497
  118.5 1.4 %collective-permute-start.28 = (bf16[256,128]{1,0:T(8,128)(2,1)S(1)}, bf16[256,128]{1,0:T(8,128)(2,1)S(1)}, u32[]{:S(2)}, u32[]{:S(2)}) collective-permute-start(bf16[256,128]{1,0:T(8,128)(2,1)S(1)} %get-tuple-element.35), channel_id=1, source_target_pairs={{0,3},{1,0},{2,1},{3,2},{4,7},{5,4},{6,5},{7,6},{8,11},{9,8},{10,9... | collective-permute-start | bytes 196616 | tf_op jit(solution)/shard_map/ppermute | solution.py:497
  119.9 2.5 %subtract.2.refs_10_ = bf16[2,2,256,1024]{3,2,1,0:T(8,128)(2,1)} custom-call(s32[8,4,8]{2,1,0:T(4,128)} %sky_ref.21, bf16[256,1024]{1,0:T(8,128)(2,1)S(1)} %copy-done.3, bf16[256,1024]{1,0:T(8,128)(2,1)S(1)} %copy-done.2, bf16[64,1024]{1,0:T(8,128)(2,1)S(1)} %fusion.10.refs_2_.refs_0_, bf16[64,1024]{1,0:T(8,128)(2,1)S(1)} %collective-permute-done.19.refs_3_.refs_1_, ...), custom_call_target="tpu_custom_call" | custom-call | flops 524288 | bytes 3145728 | tf_op jit(solution)/shard_map/subtract/pallas_call | solution.py:295
  122.4 2.4 %subtract.3 = bf16[2,2,256,1024]{3,2,1,0:T(8,128)(2,1)} custom-call(s32[8,4,8]{2,1,0:T(4,128)} %sky_ref.21, bf16[256,1024]{1,0:T(8,128)(2,1)S(1)} %copy-done.1, bf16[256,1024]{1,0:T(8,128)(2,1)S(1)} %copy-done, bf16[64,1024]{1,0:T(8,128)(2,1)S(1)} %fusion.9.refs_2_.refs_1_, ...), custom_call_target="tpu_custom_call", output_to_operand_aliasing={{}: (11, {})} | custom-call | flops 524288 | bytes 3145728 | tf_op jit(solution)/shard_map/subtract/pallas_call | solution.py:295
  124.8 0.7 convert_add_fusion.4
  (32 shorter events, 0.3 us)
Async XLA Ops:
  12.5 31.4 %collective-permute-start.3 = (bf16[256,1024]{1,0:T(8,128)(2,1)}, bf16[256,1024]{1,0:T(8,128)(2,1)}, u32[]{:S(2)}, u32[]{:S(2)}) collective-permute-start(bf16[256,1024]{1,0:T(8,128)(2,1)} %get-tuple-element.26), channel_id=1, source_target_pairs={{0,4},{4,0},{8,12},{12,8},{16,20},{20,16},{24,28},{28,24},{1,5},{5... | collective-permute-start | bytes 1572872 | tf_op jit(solution)/shard_map/ppermute | solution.py:421
  15.5 29.9 %collective-permute-start.6 = (bf16[256,1024]{1,0:T(8,128)(2,1)S(1)}, bf16[256,1024]{1,0:T(8,128)(2,1)}, u32[]{:S(2)}, u32[]{:S(2)}) collective-permute-start(bf16[256,1024]{1,0:T(8,128)(2,1)S(1)} %bitcast.25), channel_id=1, source_target_pairs={{0,4},{4,0},{8,12},{12,8},{16,20},{20,16},{24,28},{28,24},{1,5},{5... | collective-permute-start | bytes 1572872 | tf_op jit(solution)/shard_map/ppermute | solution.py:421
  25.1 25.0 %collective-permute-start = (bf16[256,1024]{1,0:T(8,128)(2,1)}, bf16[256,1024]{1,0:T(8,128)(2,1)}, u32[]{:S(2)}, u32[]{:S(2)}) collective-permute-start(bf16[256,1024]{1,0:T(8,128)(2,1)} %get-tuple-element.24), channel_id=1, source_target_pairs={{0,4},{4,0},{8,12},{12,8},{16,20},{20,16},{24,28},{28,24},{1,5},{5... | collective-permute-start | bytes 1572872 | tf_op jit(solution)/shard_map/ppermute | solution.py:421
  28.0 25.1 %collective-permute-start.9 = (bf16[2,128,1024]{2,1,0:T(8,128)(2,1)}, bf16[2,128,1024]{2,1,0:T(8,128)(2,1)S(1)}, u32[]{:S(2)}, u32[]{:S(2)}) collective-permute-start(bf16[2,128,1024]{2,1,0:T(8,128)(2,1)} %constant_dynamic-slice_fusion), channel_id=1, source_target_pairs={{0,8},{4,12},{8,0},{12,4},{16,24},{20,28},{24,16},{28,20},{1,9},{5... | collective-permute-start | bytes 1572872 | tf_op jit(solution)/shard_map/ppermute | solution.py:421
  44.9 10.9 %collective-permute-start.4 = (bf16[128,1024]{1,0:T(8,128)(2,1)S(1)}, bf16[128,1024]{1,0:T(8,128)(2,1)S(1)}, u32[]{:S(2)}, u32[]{:S(2)}) collective-permute-start(bf16[128,1024]{1,0:T(8,128)(2,1)S(1)} %add_convert_fusion.1), channel_id=1, source_target_pairs={{0,8},{4,12},{8,0},{12,4},{16,24},{20,28},{24,16},{28,20},{1,9},{5... | collective-permute-start | bytes 786440 | tf_op jit(solution)/shard_map/ppermute | solution.py:421
  46.4 23.1 %collective-permute-start.7 = (bf16[128,1024]{1,0:T(8,128)(2,1)S(1)}, bf16[128,1024]{1,0:T(8,128)(2,1)S(1)}, u32[]{:S(2)}, u32[]{:S(2)}) collective-permute-start(bf16[128,1024]{1,0:T(8,128)(2,1)S(1)} %fusion), channel_id=1, source_target_pairs={{0,8},{4,12},{8,0},{12,4},{16,24},{20,28},{24,16},{28,20},{1,9},{5... | collective-permute-start | bytes 786440 | tf_op jit(solution)/shard_map/ppermute | solution.py:421
  51.2 21.7 %collective-permute-start.1 = (bf16[128,1024]{1,0:T(8,128)(2,1)S(1)}, bf16[128,1024]{1,0:T(8,128)(2,1)S(1)}, u32[]{:S(2)}, u32[]{:S(2)}) collective-permute-start(bf16[128,1024]{1,0:T(8,128)(2,1)S(1)} %add_convert_fusion.2), channel_id=1, source_target_pairs={{0,8},{4,12},{8,0},{12,4},{16,24},{20,28},{24,16},{28,20},{1,9},{5... | collective-permute-start | bytes 786440 | tf_op jit(solution)/shard_map/ppermute | solution.py:421
  53.2 21.5 %collective-permute-start.10 = (bf16[2,64,1024]{2,1,0:T(8,128)(2,1)S(1)}, bf16[2,64,1024]{2,1,0:T(8,128)(2,1)S(1)}, u32[]{:S(2)}, u32[]{:S(2)}) collective-permute-start(bf16[2,64,1024]{2,1,0:T(8,128)(2,1)S(1)} %add_convert_fusion), channel_id=1, source_target_pairs={{0,16},{4,20},{8,24},{12,28},{16,0},{20,4},{24,8},{28,12},{1,17},{... | collective-permute-start | bytes 786440 | tf_op jit(solution)/shard_map/ppermute | solution.py:421
  56.8 22.5 %collective-permute-start.5 = (bf16[64,1024]{1,0:T(8,128)(2,1)S(1)}, bf16[64,1024]{1,0:T(8,128)(2,1)S(1)}, u32[]{:S(2)}, u32[]{:S(2)}) collective-permute-start(bf16[64,1024]{1,0:T(8,128)(2,1)S(1)} %add_convert_fusion.4), channel_id=1, source_target_pairs={{0,16},{4,20},{8,24},{12,28},{16,0},{20,4},{24,8},{28,12},{1,17},{... | collective-permute-start | bytes 393224 | tf_op jit(solution)/shard_map/ppermute | solution.py:421
  70.6 13.1 %collective-permute-start.8 = (bf16[64,1024]{1,0:T(8,128)(2,1)S(1)}, bf16[64,1024]{1,0:T(8,128)(2,1)S(1)}, u32[]{:S(2)}, u32[]{:S(2)}) collective-permute-start(bf16[64,1024]{1,0:T(8,128)(2,1)S(1)} %fusion.2), channel_id=1, source_target_pairs={{0,16},{4,20},{8,24},{12,28},{16,0},{20,4},{24,8},{28,12},{1,17},{... | collective-permute-start | bytes 393224 | tf_op jit(solution)/shard_map/ppermute | solution.py:421
  73.9 14.9 %collective-permute-start.2 = (bf16[64,1024]{1,0:T(8,128)(2,1)S(1)}, bf16[64,1024]{1,0:T(8,128)(2,1)S(1)}, u32[]{:S(2)}, u32[]{:S(2)}) collective-permute-start(bf16[64,1024]{1,0:T(8,128)(2,1)S(1)} %add_convert_fusion.5), channel_id=1, source_target_pairs={{0,16},{4,20},{8,24},{12,28},{16,0},{20,4},{24,8},{28,12},{1,17},{... | collective-permute-start | bytes 393224 | tf_op jit(solution)/shard_map/ppermute | solution.py:421
  74.7 15.1 %collective-permute-start.11 = (bf16[64,1024]{1,0:T(8,128)(2,1)S(1)}, bf16[64,1024]{1,0:T(8,128)(2,1)S(1)}, u32[]{:S(2)}, u32[]{:S(2)}) collective-permute-start(bf16[64,1024]{1,0:T(8,128)(2,1)S(1)} %fusion.11), channel_id=1, source_target_pairs={{0,4},{4,0},{8,12},{12,8},{16,20},{20,16},{24,28},{28,24},{1,5},{5... | collective-permute-start | bytes 393224 | tf_op jit(solution)/shard_map/ppermute | solution.py:421
  84.9 35.0 %copy-start.2 = (bf16[256,1024]{1,0:T(8,128)(2,1)S(1)}, bf16[256,1024]{1,0:T(8,128)(2,1)}, u32[]{:S(2)}) copy-start(bf16[256,1024]{1,0:T(8,128)(2,1)} %get-tuple-element.29.refs_1_) | copy-start | bytes 1572868
  84.9 35.0 %copy-start.3 = (bf16[256,1024]{1,0:T(8,128)(2,1)S(1)}, bf16[256,1024]{1,0:T(8,128)(2,1)}, u32[]{:S(2)}) copy-start(bf16[256,1024]{1,0:T(8,128)(2,1)} %get-tuple-element.28.refs_0_) | copy-start | bytes 1572868
  84.9 8.8 %collective-permute-start.20 = (bf16[64,1024]{1,0:T(8,128)(2,1)S(1)}, bf16[64,1024]{1,0:T(8,128)(2,1)S(1)}, u32[]{:S(2)}, u32[]{:S(2)}) collective-permute-start(bf16[64,1024]{1,0:T(8,128)(2,1)S(1)} %fusion.10.refs_2_.refs_0_), channel_id=1, source_target_pairs={{0,16},{4,20},{8,24},{12,28},{16,0},{20,4},{24,8},{28,12},{1,17},{... | collective-permute-start | bytes 393224 | tf_op jit(solution)/shard_map/ppermute | solution.py:421
  85.0 11.4 %collective-permute-start.19 = (bf16[64,1024]{1,0:T(8,128)(2,1)S(1)}, bf16[64,1024]{1,0:T(8,128)(2,1)S(1)}, u32[]{:S(2)}, u32[]{:S(2)}) collective-permute-start(bf16[64,1024]{1,0:T(8,128)(2,1)S(1)} %fusion.10.refs_2_.refs_0_), channel_id=1, source_target_pairs={{0,8},{4,12},{8,0},{12,4},{16,24},{20,28},{24,16},{28,20},{1,9},{5... | collective-permute-start | bytes 393224 | tf_op jit(solution)/shard_map/ppermute | solution.py:421
  88.8 7.5 %collective-permute-start.22 = (bf16[64,1024]{1,0:T(8,128)(2,1)S(1)}, bf16[64,1024]{1,0:T(8,128)(2,1)S(1)}, u32[]{:S(2)}, u32[]{:S(2)}) collective-permute-start(bf16[64,1024]{1,0:T(8,128)(2,1)S(1)} %fusion.10.refs_2_.refs_0_), channel_id=1, source_target_pairs={{0,4},{4,0},{8,12},{12,8},{16,20},{20,16},{24,28},{28,24},{1,5},{5... | collective-permute-start | bytes 393224 | tf_op jit(solution)/shard_map/ppermute | solution.py:421
  90.0 8.4 %collective-permute-start.13 = (bf16[64,1024]{1,0:T(8,128)(2,1)S(1)}, bf16[64,1024]{1,0:T(8,128)(2,1)S(1)}, u32[]{:S(2)}, u32[]{:S(2)}) collective-permute-start(bf16[64,1024]{1,0:T(8,128)(2,1)S(1)} %fusion.9.refs_2_.refs_1_), channel_id=1, source_target_pairs={{0,16},{4,20},{8,24},{12,28},{16,0},{20,4},{24,8},{28,12},{1,17},{... | collective-permute-start | bytes 393224 | tf_op jit(solution)/shard_map/ppermute | solution.py:421
  93.7 6.4 %collective-permute-start.21 = (bf16[64,1024]{1,0:T(8,128)(2,1)S(1)}, bf16[64,1024]{1,0:T(8,128)(2,1)S(1)}, u32[]{:S(2)}, u32[]{:S(2)}) collective-permute-start(bf16[64,1024]{1,0:T(8,128)(2,1)S(1)} %collective-permute-done.20.refs_4_.refs_2_), channel_id=1, source_target_pairs={{0,8},{4,12},{8,0},{12,4},{16,24},{20,28},{24,16},{28,20},{1,9},{5... | collective-permute-start | bytes 393224 | tf_op jit(solution)/shard_map/ppermute | solution.py:421
  93.7 7.9 %collective-permute-start.12 = (bf16[64,1024]{1,0:T(8,128)(2,1)S(1)}, bf16[64,1024]{1,0:T(8,128)(2,1)S(1)}, u32[]{:S(2)}, u32[]{:S(2)}) collective-permute-start(bf16[64,1024]{1,0:T(8,128)(2,1)S(1)} %fusion.9.refs_2_.refs_1_), channel_id=1, source_target_pairs={{0,8},{4,12},{8,0},{12,4},{16,24},{20,28},{24,16},{28,20},{1,9},{5... | collective-permute-start | bytes 393224 | tf_op jit(solution)/shard_map/ppermute | solution.py:421
  96.3 6.1 %collective-permute-start.23 = (bf16[64,1024]{1,0:T(8,128)(2,1)S(1)}, bf16[64,1024]{1,0:T(8,128)(2,1)S(1)}, u32[]{:S(2)}, u32[]{:S(2)}) collective-permute-start(bf16[64,1024]{1,0:T(8,128)(2,1)S(1)} %collective-permute-done.19.refs_3_.refs_1_), channel_id=1, source_target_pairs={{0,4},{4,0},{8,12},{12,8},{16,20},{20,16},{24,28},{28,24},{1,5},{5... | collective-permute-start | bytes 393224 | tf_op jit(solution)/shard_map/ppermute | solution.py:421
  96.4 8.8 %collective-permute-start.24 = (bf16[64,1024]{1,0:T(8,128)(2,1)S(1)}, bf16[64,1024]{1,0:T(8,128)(2,1)S(1)}, u32[]{:S(2)}, u32[]{:S(2)}) collective-permute-start(bf16[64,1024]{1,0:T(8,128)(2,1)S(1)} %collective-permute-done.20.refs_4_.refs_2_), channel_id=1, source_target_pairs={{0,4},{4,0},{8,12},{12,8},{16,20},{20,16},{24,28},{28,24},{1,5},{5... | collective-permute-start | bytes 393224 | tf_op jit(solution)/shard_map/ppermute | solution.py:421
  98.4 6.8 %collective-permute-start.14 = (bf16[64,1024]{1,0:T(8,128)(2,1)S(1)}, bf16[64,1024]{1,0:T(8,128)(2,1)S(1)}, u32[]{:S(2)}, u32[]{:S(2)}) collective-permute-start(bf16[64,1024]{1,0:T(8,128)(2,1)S(1)} %collective-permute-done.13.refs_4_.refs_3_), channel_id=1, source_target_pairs={{0,8},{4,12},{8,0},{12,4},{16,24},{20,28},{24,16},{28,20},{1,9},{5... | collective-permute-start | bytes 393224 | tf_op jit(solution)/shard_map/ppermute | solution.py:421
  100.1 7.9 %collective-permute-start.25 = (bf16[64,1024]{1,0:T(8,128)(2,1)S(1)}, bf16[64,1024]{1,0:T(8,128)(2,1)S(1)}, u32[]{:S(2)}, u32[]{:S(2)}) collective-permute-start(bf16[64,1024]{1,0:T(8,128)(2,1)S(1)} %collective-permute-done.21.refs_5_.refs_3_), channel_id=1, source_target_pairs={{0,4},{4,0},{8,12},{12,8},{16,20},{20,16},{24,28},{28,24},{1,5},{5... | collective-permute-start | bytes 393224 | tf_op jit(solution)/shard_map/ppermute | solution.py:421
  101.6 9.1 %collective-permute-start.15 = (bf16[64,1024]{1,0:T(8,128)(2,1)S(1)}, bf16[64,1024]{1,0:T(8,128)(2,1)S(1)}, u32[]{:S(2)}, u32[]{:S(2)}) collective-permute-start(bf16[64,1024]{1,0:T(8,128)(2,1)S(1)} %fusion.9.refs_2_.refs_1_), channel_id=1, source_target_pairs={{0,4},{4,0},{8,12},{12,8},{16,20},{20,16},{24,28},{28,24},{1,5},{5... | collective-permute-start | bytes 393224 | tf_op jit(solution)/shard_map/ppermute | solution.py:421
  102.4 11.5 %collective-permute-start.17 = (bf16[64,1024]{1,0:T(8,128)(2,1)S(1)}, bf16[64,1024]{1,0:T(8,128)(2,1)S(1)}, u32[]{:S(2)}, u32[]{:S(2)}) collective-permute-start(bf16[64,1024]{1,0:T(8,128)(2,1)S(1)} %collective-permute-done.13.refs_4_.refs_3_), channel_id=1, source_target_pairs={{0,4},{4,0},{8,12},{12,8},{16,20},{20,16},{24,28},{28,24},{1,5},{5... | collective-permute-start | bytes 393224 | tf_op jit(solution)/shard_map/ppermute | solution.py:421
  105.2 8.8 %collective-permute-start.16 = (bf16[64,1024]{1,0:T(8,128)(2,1)S(1)}, bf16[64,1024]{1,0:T(8,128)(2,1)S(1)}, u32[]{:S(2)}, u32[]{:S(2)}) collective-permute-start(bf16[64,1024]{1,0:T(8,128)(2,1)S(1)} %collective-permute-done.12.refs_3_.refs_2_), channel_id=1, source_target_pairs={{0,4},{4,0},{8,12},{12,8},{16,20},{20,16},{24,28},{28,24},{1,5},{5... | collective-permute-start | bytes 393224 | tf_op jit(solution)/shard_map/ppermute | solution.py:421
  105.2 10.2 %collective-permute-start.18 = (bf16[64,1024]{1,0:T(8,128)(2,1)S(1)}, bf16[64,1024]{1,0:T(8,128)(2,1)S(1)}, u32[]{:S(2)}, u32[]{:S(2)}) collective-permute-start(bf16[64,1024]{1,0:T(8,128)(2,1)S(1)} %collective-permute-done.14.refs_5_.refs_4_), channel_id=1, source_target_pairs={{0,4},{4,0},{8,12},{12,8},{16,20},{20,16},{24,28},{28,24},{1,5},{5... | collective-permute-start | bytes 393224 | tf_op jit(solution)/shard_map/ppermute | solution.py:421
  116.9 7.8 %collective-permute-start.26 = (bf16[256,128]{1,0:T(8,128)(2,1)S(1)}, bf16[256,128]{1,0:T(8,128)(2,1)S(1)}, u32[]{:S(2)}, u32[]{:S(2)}) collective-permute-start(bf16[256,128]{1,0:T(8,128)(2,1)S(1)} %get-tuple-element.33), channel_id=1, source_target_pairs={{0,1},{1,2},{2,3},{3,0},{4,5},{5,6},{6,7},{7,4},{8,9},{9,10},{10,1... | collective-permute-start | bytes 196616 | tf_op jit(solution)/shard_map/ppermute | solution.py:497
  117.0 7.8 %collective-permute-start.27 = (bf16[256,128]{1,0:T(8,128)(2,1)S(1)}, bf16[256,128]{1,0:T(8,128)(2,1)S(1)}, u32[]{:S(2)}, u32[]{:S(2)}) collective-permute-start(bf16[256,128]{1,0:T(8,128)(2,1)S(1)} %get-tuple-element.34), channel_id=1, source_target_pairs={{0,2},{1,3},{2,0},{3,1},{4,6},{5,7},{6,4},{7,5},{8,10},{9,11},{10,... | collective-permute-start | bytes 196616 | tf_op jit(solution)/shard_map/ppermute | solution.py:497
  118.5 6.3 %collective-permute-start.28 = (bf16[256,128]{1,0:T(8,128)(2,1)S(1)}, bf16[256,128]{1,0:T(8,128)(2,1)S(1)}, u32[]{:S(2)}, u32[]{:S(2)}) collective-permute-start(bf16[256,128]{1,0:T(8,128)(2,1)S(1)} %get-tuple-element.35), channel_id=1, source_target_pairs={{0,3},{1,0},{2,1},{3,2},{4,7},{5,4},{6,5},{7,6},{8,11},{9,8},{10,9... | collective-permute-start | bytes 196616 | tf_op jit(solution)/shard_map/ppermute | solution.py:497
  119.9 2.5 %copy-start = (bf16[256,1024]{1,0:T(8,128)(2,1)S(1)}, bf16[256,1024]{1,0:T(8,128)(2,1)}, u32[]{:S(2)}) copy-start(bf16[256,1024]{1,0:T(8,128)(2,1)} %get-tuple-element.22.refs_1_) | copy-start | bytes 1572868
  119.9 2.5 %copy-start.1 = (bf16[256,1024]{1,0:T(8,128)(2,1)S(1)}, bf16[256,1024]{1,0:T(8,128)(2,1)}, u32[]{:S(2)}) copy-start(bf16[256,1024]{1,0:T(8,128)(2,1)} %get-tuple-element.21.refs_0_) | copy-start | bytes 1572868

commit v4 on v3

--- a/solution.py
+++ b/solution.py
@@ -20,6 +20,7 @@
 OWN, OTHER = 0, 1
 EARLY_GRANT = 20 << 20
 LATE_GRANT = 24 << 20
+SCALARS = pl.BlockSpec(memory_space=pltpu.SMEM)
 F32 = jnp.float32
 BF16 = jnp.bfloat16
 
@@ -128,10 +129,10 @@
         functools.partial(weight_kernel, sky_count, halves, chunk, blocks),
         out_shape=jax.ShapeDtypeStruct((len(halves), chunk_rows, stripe), BF16),
         grid_spec=pltpu.PrefetchScalarGridSpec(
-            num_scalar_prefetch=2,
+            num_scalar_prefetch=0,
             grid=(len(halves) * blocks,),
-            in_specs=[pl.BlockSpec((rows, side), lambda i, m, w: (pick_block(i, halves, chunk, blocks), 0))],
-            out_specs=pl.BlockSpec((1, rows, stripe), lambda i, m, w: (i // blocks, lax.rem(i, blocks), 0)),
+            in_specs=[SCALARS, SCALARS, pl.BlockSpec((rows, side), lambda i: (pick_block(i, halves, chunk, blocks), 0))],
+            out_specs=pl.BlockSpec((1, rows, stripe), lambda i: (i // blocks, lax.rem(i, blocks), 0)),
         ),
         cost_estimate=pl.CostEstimate(
             flops=len(halves) * chunk_rows * side * 8,
@@ -223,19 +224,20 @@
             else jax.ShapeDtypeStruct((chunk_rows, stripe), BF16),
         ),
         grid_spec=pltpu.PrefetchScalarGridSpec(
-            num_scalar_prefetch=1,
+            num_scalar_prefetch=0,
             grid=(steps,),
             in_specs=[
-                pl.BlockSpec((EDGE, side), lambda i, m: (jnp.maximum(block(i) * edges - 1, 0), 0)),
-                pl.BlockSpec((TILE, side), lambda i, m: (block(i), 0)),
-                pl.BlockSpec((EDGE, side), lambda i, m: (jnp.minimum((block(i) + 1) * edges, side // EDGE - 1), 0)),
-                pl.BlockSpec(column_band.shape, lambda i, m: (0, 0), pipeline_mode=pl.Buffered(1)),
-                pl.BlockSpec(row_band.shape, lambda i, m: (0, 0), pipeline_mode=pl.Buffered(1)),
-                pl.BlockSpec((None, TILE, stripe), lambda i, m: (which_weight, i, 0)),
+                SCALARS,
+                pl.BlockSpec((EDGE, side), lambda i: (jnp.maximum(block(i) * edges - 1, 0), 0)),
+                pl.BlockSpec((TILE, side), lambda i: (block(i), 0)),
+                pl.BlockSpec((EDGE, side), lambda i: (jnp.minimum((block(i) + 1) * edges, side // EDGE - 1), 0)),
+                pl.BlockSpec(column_band.shape, lambda i: (0, 0), pipeline_mode=pl.Buffered(1)),
+                pl.BlockSpec(row_band.shape, lambda i: (0, 0), pipeline_mode=pl.Buffered(1)),
+                pl.BlockSpec((None, TILE, stripe), lambda i: (which_weight, i, 0)),
             ],
             out_specs=(
-                pl.BlockSpec((TILE, side), lambda i, m: (i, 0)),
-                pl.BlockSpec((TILE, stripe), lambda i, m: (i, 0)),
+                pl.BlockSpec((TILE, side), lambda i: (i, 0)),
+                pl.BlockSpec((TILE, stripe), lambda i: (i, 0)),
             ),
             scratch_shapes=[
                 pltpu.VMEM((side // TILE * WINDOW, 2 * TILE), BF16),
@@ -285,8 +287,8 @@
     chunk_rows, side = matched[0].shape
     pair = len(matched)
     line = len(pieces) // pair
-    operands = [*matched, *pieces]
-    specs = [pl.BlockSpec(array.shape, lambda i, m: (0, 0)) for array in operands]
+    operands = [*map(in_hbm, matched), *pieces]
+    specs = [SCALARS] + [pl.BlockSpec(array.shape, lambda i: (0, 0)) for array in operands]
     aliases = {}
     if before is not None:
         operands.append(before)
@@ -296,10 +298,10 @@
         functools.partial(difference_kernel, sky_count, pair, line),
         out_shape=jax.ShapeDtypeStruct((pair, CHUNKS, chunk_rows, side), BF16),
         grid_spec=pltpu.PrefetchScalarGridSpec(
-            num_scalar_prefetch=1,
+            num_scalar_prefetch=0,
             grid=(1,),
             in_specs=specs,
-            out_specs=pl.BlockSpec((pair, 1, chunk_rows, side), lambda i, m: (0, chunk, 0, 0)),
+            out_specs=pl.BlockSpec((pair, 1, chunk_rows, side), lambda i: (0, chunk, 0, 0)),
         ),
         input_output_aliases=aliases,
         cost_estimate=pl.CostEstimate(
@@ -342,10 +344,10 @@
         functools.partial(smooth_kernel, sky_count, line),
         out_shape=jax.ShapeDtypeStruct((pair, chunk_rows, TILE), BF16),
         grid_spec=pltpu.PrefetchScalarGridSpec(
-            num_scalar_prefetch=1,
+            num_scalar_prefetch=0,
             grid=(1,),
-            in_specs=[pl.BlockSpec(array.shape, lambda i, m: (0, 0)) for array in operands],
-            out_specs=pl.BlockSpec((pair, chunk_rows, TILE), lambda i, m: (0, 0, 0)),
+            in_specs=[SCALARS] + [pl.BlockSpec(array.shape, lambda i: (0, 0)) for array in operands],
+            out_specs=pl.BlockSpec((pair, chunk_rows, TILE), lambda i: (0, 0, 0)),
         ),
         cost_estimate=pl.CostEstimate(
             flops=pair * chunk_rows * TILE * 512, bytes_accessed=pair * chunk_rows * sky_count * TILE * 2, transcendentals=0
@@ -394,10 +396,11 @@
             jax.ShapeDtypeStruct((side // band_count, TILE), BF16 if step else F32) for step in range(band_count)
         ],
         grid_spec=pltpu.PrefetchScalarGridSpec(
-            num_scalar_prefetch=1,
+            num_scalar_prefetch=0,
             grid=(1,),
-            in_specs=[pl.BlockSpec(array.shape, lambda i, m, n=array.ndim: (0,) * n) for array in operands],
-            out_specs=[pl.BlockSpec((side // band_count, TILE), lambda i, m: (0, 0))] * band_count,
+            in_specs=[SCALARS]
+            + [pl.BlockSpec(array.shape, lambda i, n=array.ndim: (0,) * n) for array in operands],
+            out_specs=[pl.BlockSpec((side // band_count, TILE), lambda i: (0, 0))] * band_count,
             scratch_shapes=[pltpu.VMEM((side + 2 * EDGE, TILE), BF16)],
         ),
         cost_estimate=pl.CostEstimate(flops=side * TILE * 600, bytes_accessed=side * TILE * 12, transcendentals=0),

time: 127 us -> 124 us (0.976)
  Pallas kernels: 41.1 us -> 36.2 us
  starting transfers between devices: 31.1 us -> 35.4 us
  waiting for transfers between devices: 40 us -> 38.5 us
    ppermute x26, starting transfers between devices: 28.2 us -> 32.4 us  [exchange(): lax.ppermute(block, 'sky', [(i, i ^ 1 << bit) for i in range(sky_count)])]
    pallas_call x4, Pallas kernels: 24 us -> 21.1 us  [match(): pl.pallas_call(functools.partial(match_kernel, sky_count, which, chunk *...]
    pallas_call x3, Pallas kernels: 8.37 us -> 5.97 us  [weigh(): pl.pallas_call(functools.partial(weight_kernel, sky_count, halves, chunk,...]
    ppermute x26, waiting for transfers between devices: 40 us -> 38.4 us  [exchange(): lax.ppermute(block, 'sky', [(i, i ^ 1 << bit) for i in range(sky_count)])]
  transfers between devices with their start and end apart: 29 -> 29, of which waited for: 14 -> 12; matrix products, arithmetic and copies ran while one was open for 8% -> 8% of each run, Pallas kernels for 24% -> 22%
where the time goes in v4:
time: 124 us; the launch traced here: 123 us
  waiting for transfers between devices  38.5 us (31%)
  Pallas kernels  36.2 us (29%)
  starting transfers between devices  35.4 us (29%)
  other arithmetic  11.6 us (9%)
    ppermute x26, waiting for transfers between devices, exchange(): lax.ppermute(block, 'sky', [(i, i ^ 1 << bit) for i in range(sky_count)])  38.4 us
    ppermute x26, starting transfers between devices, exchange(): lax.ppermute(block, 'sky', [(i, i ^ 1 << bit) for i in range(sky_count)])  32.4 us
    pallas_call x4, Pallas kernels, match(): pl.pallas_call(functools.partial(match_kernel, sky_count, which, chunk *...  21.1 us
    convert_element_type x7, other arithmetic, reduce_line(): arrived = exchange(leaving.astype(BF16), bit)  6.15 us
    pallas_call x3, Pallas kernels, weigh(): pl.pallas_call(functools.partial(weight_kernel, sky_count, halves, chunk,...  5.97 us
    pallas_call x2, Pallas kernels, subtract(): pl.pallas_call(functools.partial(difference_kernel, sky_count, pair, line...  5.27 us
    ppermute x3, starting transfers between devices, body(): detection = detection + lax.ppermute(powers[step], 'band', ring).astype(F32)  2.98 us
  transfers between devices with their start and end apart: 29, of which 12 were waited for; matrix products, arithmetic and copies ran while one was open for 8% of the time, Pallas kernels for 22%

profile of v4, /device:TPU:0, one launch (start us, length us, event | category | flops | bytes accessed | tf_op | source)
XLA Modules:
  0.0 123.2 jit_solution(16373769129006006551)
XLA Ops:
  0.6 0.7 convert_element_type.190
  1.3 0.7 convert_convert_fusion
  2.0 0.8 multiply_convert_fusion
  2.8 0.1 pad_convert_fusion
  2.8 0.1 select_maximum_fusion.base_ref
  2.9 1.1 prepare.1
  4.0 1.6 %weigh.5.weight_ref = bf16[1,256,1024]{2,1,0:T(8,128)(2,1)S(1)} custom-call(s32[8,4,8]{2,1,0:T(4,128)} %sky_ref.21, s32[2,35]{1,0:T(2,128)} %bitcast.42, bf16[1024,1024]{1,0:T(8,128)(2,1)} %bitcast.38), custom_call_target="tpu_custom_call" | custom-call | flops 2097152 | bytes 1048576 | tf_op jit(solution)/shard_map/weigh/pallas_call | solution.py:128
  5.6 5.3 %match.7 = (bf16[256,1024]{1,0:T(8,128)(2,1)}, bf16[256,1024]{1,0:T(8,128)(2,1)}) custom-call(s32[8,4,8]{2,1,0:T(4,128)} %sky_ref.21, bf16[1024,1024]{1,0:T(8,128)(2,1)} %bitcast.26, bf16[1024,1024]{1,0:T(8,128)(2,1)} %bitcast.27, bf16[1024,1024]{1,0:T(8,128)(2,1)} %bitcast.28, bf16[256,1152]{1,0:T(8,128)(2,1)S(1)} %get-tuple-element.19.column_ref, ...), custom_call_target="tpu_custom_call" | custom-call | flops 1962934272 | bytes 2097152 | tf_op jit(solution)/shard_map/match/pallas_call | solution.py:218
  11.0 3.0 %collective-permute-start.3 = (bf16[256,1024]{1,0:T(8,128)(2,1)}, bf16[256,1024]{1,0:T(8,128)(2,1)}, u32[]{:S(2)}, u32[]{:S(2)}) collective-permute-start(bf16[256,1024]{1,0:T(8,128)(2,1)} %get-tuple-element.26), channel_id=1, source_target_pairs={{0,4},{4,0},{8,12},{12,8},{16,20},{20,16},{24,28},{28,24},{1,5},{5... | collective-permute-start | bytes 1572872 | tf_op jit(solution)/shard_map/ppermute | solution.py:424
  14.0 2.8 %weigh.3.weight_ref = bf16[2,256,1024]{2,1,0:T(8,128)(2,1)S(1)} custom-call(s32[8,4,8]{2,1,0:T(4,128)} %sky_ref.21, s32[2,35]{1,0:T(2,128)} %bitcast.43, bf16[1024,1024]{1,0:T(8,128)(2,1)} %bitcast.39), custom_call_target="tpu_custom_call" | custom-call | flops 4194304 | bytes 2097152 | tf_op jit(solution)/shard_map/weigh/pallas_call | solution.py:128
  16.8 5.3 %match.5 = (bf16[256,1024]{1,0:T(8,128)(2,1)}, bf16[256,1024]{1,0:T(8,128)(2,1)}) custom-call(s32[8,4,8]{2,1,0:T(4,128)} %sky_ref.21, bf16[1024,1024]{1,0:T(8,128)(2,1)} %bitcast.29, bf16[1024,1024]{1,0:T(8,128)(2,1)} %bitcast.30, bf16[1024,1024]{1,0:T(8,128)(2,1)} %bitcast.31, bf16[256,1152]{1,0:T(8,128)(2,1)S(1)} %get-tuple-element.19.column_ref, ...), custom_call_target="tpu_custom_call" | custom-call | flops 1962934272 | bytes 2097152 | tf_op jit(solution)/shard_map/match/pallas_call | solution.py:218
  22.1 2.0 %collective-permute-start = (bf16[256,1024]{1,0:T(8,128)(2,1)}, bf16[256,1024]{1,0:T(8,128)(2,1)}, u32[]{:S(2)}, u32[]{:S(2)}) collective-permute-start(bf16[256,1024]{1,0:T(8,128)(2,1)} %get-tuple-element.24), channel_id=1, source_target_pairs={{0,4},{4,0},{8,12},{12,8},{16,20},{20,16},{24,28},{28,24},{1,5},{5... | collective-permute-start | bytes 1572872 | tf_op jit(solution)/shard_map/ppermute | solution.py:424
  24.1 0.9 constant_dynamic-slice_fusion
  25.0 1.6 %collective-permute-start.9 = (bf16[2,128,1024]{2,1,0:T(8,128)(2,1)}, bf16[2,128,1024]{2,1,0:T(8,128)(2,1)S(1)}, u32[]{:S(2)}, u32[]{:S(2)}) collective-permute-start(bf16[2,128,1024]{2,1,0:T(8,128)(2,1)} %constant_dynamic-slice_fusion), channel_id=1, source_target_pairs={{0,8},{4,12},{8,0},{12,4},{16,24},{20,28},{24,16},{28,20},{1,9},{5... | collective-permute-start | bytes 1572872 | tf_op jit(solution)/shard_map/ppermute | solution.py:424
  26.6 1.6 %weigh.4.weight_ref = bf16[1,256,1024]{2,1,0:T(8,128)(2,1)S(1)} custom-call(s32[8,4,8]{2,1,0:T(4,128)} %sky_ref.21, s32[2,35]{1,0:T(2,128)} %bitcast.44, bf16[1024,1024]{1,0:T(8,128)(2,1)} %bitcast.40), custom_call_target="tpu_custom_call" | custom-call | flops 2097152 | bytes 1048576 | tf_op jit(solution)/shard_map/weigh/pallas_call | solution.py:128
  28.1 5.2 %match.4 = (bf16[256,1024]{1,0:T(8,128)(2,1)}, bf16[256,1024]{1,0:T(8,128)(2,1)S(1)}) custom-call(s32[8,4,8]{2,1,0:T(4,128)} %sky_ref.21, bf16[1024,1024]{1,0:T(8,128)(2,1)} %bitcast.32, bf16[1024,1024]{1,0:T(8,128)(2,1)} %bitcast.33, bf16[1024,1024]{1,0:T(8,128)(2,1)} %bitcast.34, bf16[256,1152]{1,0:T(8,128)(2,1)S(1)} %get-tuple-element.19.column_ref, ...), custom_call_target="tpu_custom_call" | custom-call | flops 1962934272 | bytes 2097152 | tf_op jit(solution)/shard_map/match/pallas_call | solution.py:218
  33.4 5.2 %match.6 = (bf16[256,1024]{1,0:T(8,128)(2,1)}, bf16[256,1024]{1,0:T(8,128)(2,1)S(1)}) custom-call(s32[8,4,8]{2,1,0:T(4,128)} %sky_ref.21, bf16[1024,1024]{1,0:T(8,128)(2,1)} %bitcast.35, bf16[1024,1024]{1,0:T(8,128)(2,1)} %bitcast.36, bf16[1024,1024]{1,0:T(8,128)(2,1)} %bitcast.37, bf16[256,1152]{1,0:T(8,128)(2,1)S(1)} %get-tuple-element.19.column_ref, ...), custom_call_target="tpu_custom_call" | custom-call | flops 1962934272 | bytes 2097152 | tf_op jit(solution)/shard_map/match/pallas_call | solution.py:218
  38.5 1.0 add_convert_fusion.1
  39.6 0.5 collective-permute-start.4
  40.1 1.0 fusion
  41.1 1.7 %collective-permute-start.7 = (bf16[128,1024]{1,0:T(8,128)(2,1)S(1)}, bf16[128,1024]{1,0:T(8,128)(2,1)S(1)}, u32[]{:S(2)}, u32[]{:S(2)}) collective-permute-start(bf16[128,1024]{1,0:T(8,128)(2,1)S(1)} %fusion), channel_id=1, source_target_pairs={{0,8},{4,12},{8,0},{12,4},{16,24},{20,28},{24,16},{28,20},{1,9},{5... | collective-permute-start | bytes 786440 | tf_op jit(solution)/shard_map/ppermute | solution.py:424
  42.8 5.9 %collective-permute-done = bf16[256,1024]{1,0:T(8,128)(2,1)} collective-permute-done((bf16[256,1024]{1,0:T(8,128)(2,1)}, bf16[256,1024]{1,0:T(8,128)(2,1)}, u32[]{:S(2)}, u32[]{:S(2)}) %collective-permute-start) | collective-permute-done | bytes 524320 | tf_op jit(solution)/shard_map/ppermute | solution.py:424
  48.7 1.0 add_convert_fusion.2
  49.7 1.9 %collective-permute-start.1 = (bf16[128,1024]{1,0:T(8,128)(2,1)S(1)}, bf16[128,1024]{1,0:T(8,128)(2,1)S(1)}, u32[]{:S(2)}, u32[]{:S(2)}) collective-permute-start(bf16[128,1024]{1,0:T(8,128)(2,1)S(1)} %add_convert_fusion.2), channel_id=1, source_target_pairs={{0,8},{4,12},{8,0},{12,4},{16,24},{20,28},{24,16},{28,20},{1,9},{5... | collective-permute-start | bytes 786440 | tf_op jit(solution)/shard_map/ppermute | solution.py:424
  51.6 0.1 add_convert_fusion
  51.7 2.7 %collective-permute-start.10 = (bf16[2,64,1024]{2,1,0:T(8,128)(2,1)S(1)}, bf16[2,64,1024]{2,1,0:T(8,128)(2,1)S(1)}, u32[]{:S(2)}, u32[]{:S(2)}) collective-permute-start(bf16[2,64,1024]{2,1,0:T(8,128)(2,1)S(1)} %add_convert_fusion), channel_id=1, source_target_pairs={{0,16},{4,20},{8,24},{12,28},{16,0},{20,4},{24,8},{28,12},{1,17},{... | collective-permute-start | bytes 786440 | tf_op jit(solution)/shard_map/ppermute | solution.py:424
  54.3 1.0 add_convert_fusion.4
  55.3 0.4 collective-permute-start.5
  55.7 1.0 fusion.2
  56.7 2.7 %collective-permute-start.8 = (bf16[64,1024]{1,0:T(8,128)(2,1)S(1)}, bf16[64,1024]{1,0:T(8,128)(2,1)S(1)}, u32[]{:S(2)}, u32[]{:S(2)}) collective-permute-start(bf16[64,1024]{1,0:T(8,128)(2,1)S(1)} %fusion.2), channel_id=1, source_target_pairs={{0,16},{4,20},{8,24},{12,28},{16,0},{20,4},{24,8},{28,12},{1,17},{... | collective-permute-start | bytes 393224 | tf_op jit(solution)/shard_map/ppermute | solution.py:424
  59.4 4.4 %collective-permute-done.1 = bf16[128,1024]{1,0:T(8,128)(2,1)S(1)} collective-permute-done((bf16[128,1024]{1,0:T(8,128)(2,1)S(1)}, bf16[128,1024]{1,0:T(8,128)(2,1)S(1)}, u32[]{:S(2)}, u32[]{:S(2)}) %collective-permute-start.1) | collective-permute-done | bytes 262176 | tf_op jit(solution)/shard_map/ppermute | solution.py:424
  63.8 1.0 add_convert_fusion.5
  64.9 11.0 %collective-permute-done.10 = bf16[2,64,1024]{2,1,0:T(8,128)(2,1)S(1)} collective-permute-done((bf16[2,64,1024]{2,1,0:T(8,128)(2,1)S(1)}, bf16[2,64,1024]{2,1,0:T(8,128)(2,1)S(1)}, u32[]{:S(2)}, u32[]{:S(2)}) %collective-permute-start.10) | collective-permute-done | bytes 262176 | tf_op jit(solution)/shard_map/ppermute | solution.py:424
  75.9 1.6 %collective-permute-start.11 = (bf16[64,1024]{1,0:T(8,128)(2,1)S(1)}, bf16[64,1024]{1,0:T(8,128)(2,1)S(1)}, u32[]{:S(2)}, u32[]{:S(2)}) collective-permute-start(bf16[64,1024]{1,0:T(8,128)(2,1)S(1)} %fusion.11), channel_id=1, source_target_pairs={{0,4},{4,0},{8,12},{12,8},{16,20},{20,16},{24,28},{28,24},{1,5},{5... | collective-permute-start | bytes 393224 | tf_op jit(solution)/shard_map/ppermute | solution.py:424
  77.5 1.1 collective-permute-done.5
  78.7 2.0 %collective-permute-done.8 = bf16[64,1024]{1,0:T(8,128)(2,1)S(1)} collective-permute-done((bf16[64,1024]{1,0:T(8,128)(2,1)S(1)}, bf16[64,1024]{1,0:T(8,128)(2,1)S(1)}, u32[]{:S(2)}, u32[]{:S(2)}) %collective-permute-start.8) | collective-permute-done | bytes 131104 | tf_op jit(solution)/shard_map/ppermute | solution.py:424
  80.6 1.2 fusion.10.refs_2_.refs_0_
  81.9 3.1 %collective-permute-start.19 = (bf16[64,1024]{1,0:T(8,128)(2,1)S(1)}, bf16[64,1024]{1,0:T(8,128)(2,1)S(1)}, u32[]{:S(2)}, u32[]{:S(2)}) collective-permute-start(bf16[64,1024]{1,0:T(8,128)(2,1)S(1)} %fusion.10.refs_2_.refs_0_), channel_id=1, source_target_pairs={{0,8},{4,12},{8,0},{12,4},{16,24},{20,28},{24,16},{28,20},{1,9},{5... | collective-permute-start | bytes 393224 | tf_op jit(solution)/shard_map/ppermute | solution.py:424
  85.0 1.5 %collective-permute-start.22 = (bf16[64,1024]{1,0:T(8,128)(2,1)S(1)}, bf16[64,1024]{1,0:T(8,128)(2,1)S(1)}, u32[]{:S(2)}, u32[]{:S(2)}) collective-permute-start(bf16[64,1024]{1,0:T(8,128)(2,1)S(1)} %fusion.10.refs_2_.refs_0_), channel_id=1, source_target_pairs={{0,4},{4,0},{8,12},{12,8},{16,20},{20,16},{24,28},{28,24},{1,5},{5... | collective-permute-start | bytes 393224 | tf_op jit(solution)/shard_map/ppermute | solution.py:424
  86.5 1.0 convert_add_fusion.3
  87.5 0.1 fusion.9.refs_2_.refs_1_
  87.7 0.1 collective-permute-start.13
  87.8 3.8 %collective-permute-done.20.refs_4_.refs_2_ = bf16[64,1024]{1,0:T(8,128)(2,1)S(1)} collective-permute-done((bf16[64,1024]{1,0:T(8,128)(2,1)S(1)}, bf16[64,1024]{1,0:T(8,128)(2,1)S(1)}, u32[]{:S(2)}, u32[]{:S(2)}) %collective-permute-start.20) | collective-permute-done | bytes 131104 | tf_op jit(solution)/shard_map/ppermute | solution.py:424
  91.6 2.0 %collective-permute-start.12 = (bf16[64,1024]{1,0:T(8,128)(2,1)S(1)}, bf16[64,1024]{1,0:T(8,128)(2,1)S(1)}, u32[]{:S(2)}, u32[]{:S(2)}) collective-permute-start(bf16[64,1024]{1,0:T(8,128)(2,1)S(1)} %fusion.9.refs_2_.refs_1_), channel_id=1, source_target_pairs={{0,8},{4,12},{8,0},{12,4},{16,24},{20,28},{24,16},{28,20},{1,9},{5... | collective-permute-start | bytes 393224 | tf_op jit(solution)/shard_map/ppermute | solution.py:424
  93.7 1.3 %collective-permute-start.23 = (bf16[64,1024]{1,0:T(8,128)(2,1)S(1)}, bf16[64,1024]{1,0:T(8,128)(2,1)S(1)}, u32[]{:S(2)}, u32[]{:S(2)}) collective-permute-start(bf16[64,1024]{1,0:T(8,128)(2,1)S(1)} %collective-permute-done.19.refs_3_.refs_1_), channel_id=1, source_target_pairs={{0,4},{4,0},{8,12},{12,8},{16,20},{20,16},{24,28},{28,24},{1,5},{5... | collective-permute-start | bytes 393224 | tf_op jit(solution)/shard_map/ppermute | solution.py:424
  94.9 0.8 collective-permute-start.24
  95.7 2.0 %collective-permute-done.21.refs_5_.refs_3_ = bf16[64,1024]{1,0:T(8,128)(2,1)S(1)} collective-permute-done((bf16[64,1024]{1,0:T(8,128)(2,1)S(1)}, bf16[64,1024]{1,0:T(8,128)(2,1)S(1)}, u32[]{:S(2)}, u32[]{:S(2)}) %collective-permute-start.21) | collective-permute-done | bytes 131104 | tf_op jit(solution)/shard_map/ppermute | solution.py:424
  97.8 1.4 %collective-permute-start.25 = (bf16[64,1024]{1,0:T(8,128)(2,1)S(1)}, bf16[64,1024]{1,0:T(8,128)(2,1)S(1)}, u32[]{:S(2)}, u32[]{:S(2)}) collective-permute-start(bf16[64,1024]{1,0:T(8,128)(2,1)S(1)} %collective-permute-done.21.refs_5_.refs_3_), channel_id=1, source_target_pairs={{0,4},{4,0},{8,12},{12,8},{16,20},{20,16},{24,28},{28,24},{1,5},{5... | collective-permute-start | bytes 393224 | tf_op jit(solution)/shard_map/ppermute | solution.py:424
  99.2 1.4 %collective-permute-start.15 = (bf16[64,1024]{1,0:T(8,128)(2,1)S(1)}, bf16[64,1024]{1,0:T(8,128)(2,1)S(1)}, u32[]{:S(2)}, u32[]{:S(2)}) collective-permute-start(bf16[64,1024]{1,0:T(8,128)(2,1)S(1)} %fusion.9.refs_2_.refs_1_), channel_id=1, source_target_pairs={{0,4},{4,0},{8,12},{12,8},{16,20},{20,16},{24,28},{28,24},{1,5},{5... | collective-permute-start | bytes 393224 | tf_op jit(solution)/shard_map/ppermute | solution.py:424
  100.6 0.7 collective-permute-start.17
  101.3 1.3 %collective-permute-done.24.refs_8_.refs_6_ = bf16[64,1024]{1,0:T(8,128)(2,1)S(1)} collective-permute-done((bf16[64,1024]{1,0:T(8,128)(2,1)S(1)}, bf16[64,1024]{1,0:T(8,128)(2,1)S(1)}, u32[]{:S(2)}, u32[]{:S(2)}) %collective-permute-start.24) | collective-permute-done | bytes 131104 | tf_op jit(solution)/shard_map/ppermute | solution.py:424
  102.7 1.5 %collective-permute-start.16 = (bf16[64,1024]{1,0:T(8,128)(2,1)S(1)}, bf16[64,1024]{1,0:T(8,128)(2,1)S(1)}, u32[]{:S(2)}, u32[]{:S(2)}) collective-permute-start(bf16[64,1024]{1,0:T(8,128)(2,1)S(1)} %collective-permute-done.12.refs_3_.refs_2_), channel_id=1, source_target_pairs={{0,4},{4,0},{8,12},{12,8},{16,20},{20,16},{24,28},{28,24},{1,5},{5... | collective-permute-start | bytes 393224 | tf_op jit(solution)/shard_map/ppermute | solution.py:424
  104.1 0.6 collective-permute-start.18
  104.7 0.8 collective-permute-done.25.refs_9_.refs_7_
  105.5 1.2 %smooth.1.refs_0_ = bf16[2,256,128]{2,1,0:T(8,128)(2,1)S(1)} custom-call(s32[8,4,8]{2,1,0:T(4,128)} %sky_ref.21, bf16[256,128]{1,0:T(8,128)(2,1)S(1)} %get-tuple-element.30.across_ref, bf16[64,1024]{1,0:T(8,128)(2,1)S(1)} %fusion.10.refs_2_.refs_0_, bf16[64,1024]{1,0:T(8,128)(2,1)S(1)} %collective-permute-done.19.refs_3_.refs_1_, ...), custom_call_target="tpu_custom_call" | custom-call | flops 33554432 | bytes 1048576 | tf_op jit(solution)/shard_map/smooth/pallas_call | solution.py:343
  106.7 1.6 %collective-permute-done.15.refs_6_.refs_5_ = bf16[64,1024]{1,0:T(8,128)(2,1)S(1)} collective-permute-done((bf16[64,1024]{1,0:T(8,128)(2,1)S(1)}, bf16[64,1024]{1,0:T(8,128)(2,1)S(1)}, u32[]{:S(2)}, u32[]{:S(2)}) %collective-permute-start.15) | collective-permute-done | bytes 131104 | tf_op jit(solution)/shard_map/ppermute | solution.py:424
  108.3 3.0 %collective-permute-done.16.refs_7_.refs_6_ = bf16[64,1024]{1,0:T(8,128)(2,1)S(1)} collective-permute-done((bf16[64,1024]{1,0:T(8,128)(2,1)S(1)}, bf16[64,1024]{1,0:T(8,128)(2,1)S(1)}, u32[]{:S(2)}, u32[]{:S(2)}) %collective-permute-start.16) | collective-permute-done | bytes 131104 | tf_op jit(solution)/shard_map/ppermute | solution.py:424
  111.3 1.4 %collective-permute-done.18.refs_9_.refs_8_ = bf16[64,1024]{1,0:T(8,128)(2,1)S(1)} collective-permute-done((bf16[64,1024]{1,0:T(8,128)(2,1)S(1)}, bf16[64,1024]{1,0:T(8,128)(2,1)S(1)}, u32[]{:S(2)}, u32[]{:S(2)}) %collective-permute-start.18) | collective-permute-done | bytes 131104 | tf_op jit(solution)/shard_map/ppermute | solution.py:424
  112.7 1.5 %power.1 = (f32[256,128]{1,0:T(8,128)S(1)}, bf16[256,128]{1,0:T(8,128)(2,1)S(1)}, bf16[256,128]{1,0:T(8,128)(2,1)S(1)}, bf16[256,128]{1,0:T(8,128)(2,1)S(1)}) custom-call(s32[8,4,8]{2,1,0:T(4,128)} %sky_ref.21, bf16[256,128]{1,0:T(8,128)(2,1)S(1)} %get-tuple-element.30.across_ref, bf16[128,160]{1,0:T(8,128)(2,1)S(1)} %get-tuple-element.31.down_ref, ...), custom_call_target="tpu_custom_call" | custom-call | flops 78643200 | bytes 1572864 | tf_op jit(solution)/shard_map/power/pallas_call | solution.py:393
  114.3 1.5 %collective-permute-start.27 = (bf16[256,128]{1,0:T(8,128)(2,1)S(1)}, bf16[256,128]{1,0:T(8,128)(2,1)S(1)}, u32[]{:S(2)}, u32[]{:S(2)}) collective-permute-start(bf16[256,128]{1,0:T(8,128)(2,1)S(1)} %get-tuple-element.34), channel_id=1, source_target_pairs={{0,2},{1,3},{2,0},{3,1},{4,6},{5,7},{6,4},{7,5},{8,10},{9,11},{10,... | collective-permute-start | bytes 196616 | tf_op jit(solution)/shard_map/ppermute | solution.py:500
  115.8 1.4 %collective-permute-start.28 = (bf16[256,128]{1,0:T(8,128)(2,1)S(1)}, bf16[256,128]{1,0:T(8,128)(2,1)S(1)}, u32[]{:S(2)}, u32[]{:S(2)}) collective-permute-start(bf16[256,128]{1,0:T(8,128)(2,1)S(1)} %get-tuple-element.35), channel_id=1, source_target_pairs={{0,3},{1,0},{2,1},{3,2},{4,7},{5,4},{6,5},{7,6},{8,11},{9,8},{10,9... | collective-permute-start | bytes 196616 | tf_op jit(solution)/shard_map/ppermute | solution.py:500
  117.2 2.6 %subtract.2.refs_10_ = bf16[2,2,256,1024]{3,2,1,0:T(8,128)(2,1)} custom-call(s32[8,4,8]{2,1,0:T(4,128)} %sky_ref.21, bf16[256,1024]{1,0:T(8,128)(2,1)} %get-tuple-element.28.refs_0_, bf16[256,1024]{1,0:T(8,128)(2,1)} %get-tuple-element.29.refs_1_, bf16[64,1024]{1,0:T(8,128)(2,1)S(1)} %fusion.10.refs_2_.refs_0_, ...), custom_call_target="tpu_custom_call" | custom-call | flops 524288 | bytes 3145728 | tf_op jit(solution)/shard_map/subtract/pallas_call | solution.py:297
  119.9 2.6 %subtract.3 = bf16[2,2,256,1024]{3,2,1,0:T(8,128)(2,1)} custom-call(s32[8,4,8]{2,1,0:T(4,128)} %sky_ref.21, bf16[256,1024]{1,0:T(8,128)(2,1)} %get-tuple-element.21.refs_0_, bf16[256,1024]{1,0:T(8,128)(2,1)} %get-tuple-element.22.refs_1_, bf16[64,1024]{1,0:T(8,128)(2,1)S(1)} %fusion.9.refs_2_.refs_1_, ...), custom_call_target="tpu_custom_call", output_to_operand_aliasing={{}: (11, {})} | custom-call | flops 524288 | bytes 3145728 | tf_op jit(solution)/shard_map/subtract/pallas_call | solution.py:297
  122.5 0.7 convert_add_fusion.4
  (24 shorter events, 0.4 us)
Async XLA Ops:
  11.0 27.6 %collective-permute-start.3 = (bf16[256,1024]{1,0:T(8,128)(2,1)}, bf16[256,1024]{1,0:T(8,128)(2,1)}, u32[]{:S(2)}, u32[]{:S(2)}) collective-permute-start(bf16[256,1024]{1,0:T(8,128)(2,1)} %get-tuple-element.26), channel_id=1, source_target_pairs={{0,4},{4,0},{8,12},{12,8},{16,20},{20,16},{24,28},{28,24},{1,5},{5... | collective-permute-start | bytes 1572872 | tf_op jit(solution)/shard_map/ppermute | solution.py:424
  14.0 26.1 %collective-permute-start.6 = (bf16[256,1024]{1,0:T(8,128)(2,1)S(1)}, bf16[256,1024]{1,0:T(8,128)(2,1)}, u32[]{:S(2)}, u32[]{:S(2)}) collective-permute-start(bf16[256,1024]{1,0:T(8,128)(2,1)S(1)} %bitcast.25), channel_id=1, source_target_pairs={{0,4},{4,0},{8,12},{12,8},{16,20},{20,16},{24,28},{28,24},{1,5},{5... | collective-permute-start | bytes 1572872 | tf_op jit(solution)/shard_map/ppermute | solution.py:424
  22.1 26.6 %collective-permute-start = (bf16[256,1024]{1,0:T(8,128)(2,1)}, bf16[256,1024]{1,0:T(8,128)(2,1)}, u32[]{:S(2)}, u32[]{:S(2)}) collective-permute-start(bf16[256,1024]{1,0:T(8,128)(2,1)} %get-tuple-element.24), channel_id=1, source_target_pairs={{0,4},{4,0},{8,12},{12,8},{16,20},{20,16},{24,28},{28,24},{1,5},{5... | collective-permute-start | bytes 1572872 | tf_op jit(solution)/shard_map/ppermute | solution.py:424
  25.0 26.6 %collective-permute-start.9 = (bf16[2,128,1024]{2,1,0:T(8,128)(2,1)}, bf16[2,128,1024]{2,1,0:T(8,128)(2,1)S(1)}, u32[]{:S(2)}, u32[]{:S(2)}) collective-permute-start(bf16[2,128,1024]{2,1,0:T(8,128)(2,1)} %constant_dynamic-slice_fusion), channel_id=1, source_target_pairs={{0,8},{4,12},{8,0},{12,4},{16,24},{20,28},{24,16},{28,20},{1,9},{5... | collective-permute-start | bytes 1572872 | tf_op jit(solution)/shard_map/ppermute | solution.py:424
  39.6 14.7 %collective-permute-start.4 = (bf16[128,1024]{1,0:T(8,128)(2,1)S(1)}, bf16[128,1024]{1,0:T(8,128)(2,1)S(1)}, u32[]{:S(2)}, u32[]{:S(2)}) collective-permute-start(bf16[128,1024]{1,0:T(8,128)(2,1)S(1)} %add_convert_fusion.1), channel_id=1, source_target_pairs={{0,8},{4,12},{8,0},{12,4},{16,24},{20,28},{24,16},{28,20},{1,9},{5... | collective-permute-start | bytes 786440 | tf_op jit(solution)/shard_map/ppermute | solution.py:424
  41.1 14.6 %collective-permute-start.7 = (bf16[128,1024]{1,0:T(8,128)(2,1)S(1)}, bf16[128,1024]{1,0:T(8,128)(2,1)S(1)}, u32[]{:S(2)}, u32[]{:S(2)}) collective-permute-start(bf16[128,1024]{1,0:T(8,128)(2,1)S(1)} %fusion), channel_id=1, source_target_pairs={{0,8},{4,12},{8,0},{12,4},{16,24},{20,28},{24,16},{28,20},{1,9},{5... | collective-permute-start | bytes 786440 | tf_op jit(solution)/shard_map/ppermute | solution.py:424
  49.7 14.1 %collective-permute-start.1 = (bf16[128,1024]{1,0:T(8,128)(2,1)S(1)}, bf16[128,1024]{1,0:T(8,128)(2,1)S(1)}, u32[]{:S(2)}, u32[]{:S(2)}) collective-permute-start(bf16[128,1024]{1,0:T(8,128)(2,1)S(1)} %add_convert_fusion.2), channel_id=1, source_target_pairs={{0,8},{4,12},{8,0},{12,4},{16,24},{20,28},{24,16},{28,20},{1,9},{5... | collective-permute-start | bytes 786440 | tf_op jit(solution)/shard_map/ppermute | solution.py:424
  51.7 24.2 %collective-permute-start.10 = (bf16[2,64,1024]{2,1,0:T(8,128)(2,1)S(1)}, bf16[2,64,1024]{2,1,0:T(8,128)(2,1)S(1)}, u32[]{:S(2)}, u32[]{:S(2)}) collective-permute-start(bf16[2,64,1024]{2,1,0:T(8,128)(2,1)S(1)} %add_convert_fusion), channel_id=1, source_target_pairs={{0,16},{4,20},{8,24},{12,28},{16,0},{20,4},{24,8},{28,12},{1,17},{... | collective-permute-start | bytes 786440 | tf_op jit(solution)/shard_map/ppermute | solution.py:424
  55.3 23.3 %collective-permute-start.5 = (bf16[64,1024]{1,0:T(8,128)(2,1)S(1)}, bf16[64,1024]{1,0:T(8,128)(2,1)S(1)}, u32[]{:S(2)}, u32[]{:S(2)}) collective-permute-start(bf16[64,1024]{1,0:T(8,128)(2,1)S(1)} %add_convert_fusion.4), channel_id=1, source_target_pairs={{0,16},{4,20},{8,24},{12,28},{16,0},{20,4},{24,8},{28,12},{1,17},{... | collective-permute-start | bytes 393224 | tf_op jit(solution)/shard_map/ppermute | solution.py:424
  56.7 23.9 %collective-permute-start.8 = (bf16[64,1024]{1,0:T(8,128)(2,1)S(1)}, bf16[64,1024]{1,0:T(8,128)(2,1)S(1)}, u32[]{:S(2)}, u32[]{:S(2)}) collective-permute-start(bf16[64,1024]{1,0:T(8,128)(2,1)S(1)} %fusion.2), channel_id=1, source_target_pairs={{0,16},{4,20},{8,24},{12,28},{16,0},{20,4},{24,8},{28,12},{1,17},{... | collective-permute-start | bytes 393224 | tf_op jit(solution)/shard_map/ppermute | solution.py:424
  64.8 21.7 %collective-permute-start.2 = (bf16[64,1024]{1,0:T(8,128)(2,1)S(1)}, bf16[64,1024]{1,0:T(8,128)(2,1)S(1)}, u32[]{:S(2)}, u32[]{:S(2)}) collective-permute-start(bf16[64,1024]{1,0:T(8,128)(2,1)S(1)} %add_convert_fusion.5), channel_id=1, source_target_pairs={{0,16},{4,20},{8,24},{12,28},{16,0},{20,4},{24,8},{28,12},{1,17},{... | collective-permute-start | bytes 393224 | tf_op jit(solution)/shard_map/ppermute | solution.py:424
  75.9 11.6 %collective-permute-start.11 = (bf16[64,1024]{1,0:T(8,128)(2,1)S(1)}, bf16[64,1024]{1,0:T(8,128)(2,1)S(1)}, u32[]{:S(2)}, u32[]{:S(2)}) collective-permute-start(bf16[64,1024]{1,0:T(8,128)(2,1)S(1)} %fusion.11), channel_id=1, source_target_pairs={{0,4},{4,0},{8,12},{12,8},{16,20},{20,16},{24,28},{28,24},{1,5},{5... | collective-permute-start | bytes 393224 | tf_op jit(solution)/shard_map/ppermute | solution.py:424
  81.9 9.8 %collective-permute-start.20 = (bf16[64,1024]{1,0:T(8,128)(2,1)S(1)}, bf16[64,1024]{1,0:T(8,128)(2,1)S(1)}, u32[]{:S(2)}, u32[]{:S(2)}) collective-permute-start(bf16[64,1024]{1,0:T(8,128)(2,1)S(1)} %fusion.10.refs_2_.refs_0_), channel_id=1, source_target_pairs={{0,16},{4,20},{8,24},{12,28},{16,0},{20,4},{24,8},{28,12},{1,17},{... | collective-permute-start | bytes 393224 | tf_op jit(solution)/shard_map/ppermute | solution.py:424
  81.9 11.7 %collective-permute-start.19 = (bf16[64,1024]{1,0:T(8,128)(2,1)S(1)}, bf16[64,1024]{1,0:T(8,128)(2,1)S(1)}, u32[]{:S(2)}, u32[]{:S(2)}) collective-permute-start(bf16[64,1024]{1,0:T(8,128)(2,1)S(1)} %fusion.10.refs_2_.refs_0_), channel_id=1, source_target_pairs={{0,8},{4,12},{8,0},{12,4},{16,24},{20,28},{24,16},{28,20},{1,9},{5... | collective-permute-start | bytes 393224 | tf_op jit(solution)/shard_map/ppermute | solution.py:424
  85.0 9.9 %collective-permute-start.22 = (bf16[64,1024]{1,0:T(8,128)(2,1)S(1)}, bf16[64,1024]{1,0:T(8,128)(2,1)S(1)}, u32[]{:S(2)}, u32[]{:S(2)}) collective-permute-start(bf16[64,1024]{1,0:T(8,128)(2,1)S(1)} %fusion.10.refs_2_.refs_0_), channel_id=1, source_target_pairs={{0,4},{4,0},{8,12},{12,8},{16,20},{20,16},{24,28},{28,24},{1,5},{5... | collective-permute-start | bytes 393224 | tf_op jit(solution)/shard_map/ppermute | solution.py:424
  87.7 8.0 %collective-permute-start.13 = (bf16[64,1024]{1,0:T(8,128)(2,1)S(1)}, bf16[64,1024]{1,0:T(8,128)(2,1)S(1)}, u32[]{:S(2)}, u32[]{:S(2)}) collective-permute-start(bf16[64,1024]{1,0:T(8,128)(2,1)S(1)} %fusion.9.refs_2_.refs_1_), channel_id=1, source_target_pairs={{0,16},{4,20},{8,24},{12,28},{16,0},{20,4},{24,8},{28,12},{1,17},{... | collective-permute-start | bytes 393224 | tf_op jit(solution)/shard_map/ppermute | solution.py:424
  91.6 6.1 %collective-permute-start.21 = (bf16[64,1024]{1,0:T(8,128)(2,1)S(1)}, bf16[64,1024]{1,0:T(8,128)(2,1)S(1)}, u32[]{:S(2)}, u32[]{:S(2)}) collective-permute-start(bf16[64,1024]{1,0:T(8,128)(2,1)S(1)} %collective-permute-done.20.refs_4_.refs_2_), channel_id=1, source_target_pairs={{0,8},{4,12},{8,0},{12,4},{16,24},{20,28},{24,16},{28,20},{1,9},{5... | collective-permute-start | bytes 393224 | tf_op jit(solution)/shard_map/ppermute | solution.py:424
  91.6 7.6 %collective-permute-start.12 = (bf16[64,1024]{1,0:T(8,128)(2,1)S(1)}, bf16[64,1024]{1,0:T(8,128)(2,1)S(1)}, u32[]{:S(2)}, u32[]{:S(2)}) collective-permute-start(bf16[64,1024]{1,0:T(8,128)(2,1)S(1)} %fusion.9.refs_2_.refs_1_), channel_id=1, source_target_pairs={{0,8},{4,12},{8,0},{12,4},{16,24},{20,28},{24,16},{28,20},{1,9},{5... | collective-permute-start | bytes 393224 | tf_op jit(solution)/shard_map/ppermute | solution.py:424
  93.7 7.0 %collective-permute-start.23 = (bf16[64,1024]{1,0:T(8,128)(2,1)S(1)}, bf16[64,1024]{1,0:T(8,128)(2,1)S(1)}, u32[]{:S(2)}, u32[]{:S(2)}) collective-permute-start(bf16[64,1024]{1,0:T(8,128)(2,1)S(1)} %collective-permute-done.19.refs_3_.refs_1_), channel_id=1, source_target_pairs={{0,4},{4,0},{8,12},{12,8},{16,20},{20,16},{24,28},{28,24},{1,5},{5... | collective-permute-start | bytes 393224 | tf_op jit(solution)/shard_map/ppermute | solution.py:424
  94.9 7.7 %collective-permute-start.24 = (bf16[64,1024]{1,0:T(8,128)(2,1)S(1)}, bf16[64,1024]{1,0:T(8,128)(2,1)S(1)}, u32[]{:S(2)}, u32[]{:S(2)}) collective-permute-start(bf16[64,1024]{1,0:T(8,128)(2,1)S(1)} %collective-permute-done.20.refs_4_.refs_2_), channel_id=1, source_target_pairs={{0,4},{4,0},{8,12},{12,8},{16,20},{20,16},{24,28},{28,24},{1,5},{5... | collective-permute-start | bytes 393224 | tf_op jit(solution)/shard_map/ppermute | solution.py:424
  95.7 8.4 %collective-permute-start.14 = (bf16[64,1024]{1,0:T(8,128)(2,1)S(1)}, bf16[64,1024]{1,0:T(8,128)(2,1)S(1)}, u32[]{:S(2)}, u32[]{:S(2)}) collective-permute-start(bf16[64,1024]{1,0:T(8,128)(2,1)S(1)} %collective-permute-done.13.refs_4_.refs_3_), channel_id=1, source_target_pairs={{0,8},{4,12},{8,0},{12,4},{16,24},{20,28},{24,16},{28,20},{1,9},{5... | collective-permute-start | bytes 393224 | tf_op jit(solution)/shard_map/ppermute | solution.py:424
  97.8 7.7 %collective-permute-start.25 = (bf16[64,1024]{1,0:T(8,128)(2,1)S(1)}, bf16[64,1024]{1,0:T(8,128)(2,1)S(1)}, u32[]{:S(2)}, u32[]{:S(2)}) collective-permute-start(bf16[64,1024]{1,0:T(8,128)(2,1)S(1)} %collective-permute-done.21.refs_5_.refs_3_), channel_id=1, source_target_pairs={{0,4},{4,0},{8,12},{12,8},{16,20},{20,16},{24,28},{28,24},{1,5},{5... | collective-permute-start | bytes 393224 | tf_op jit(solution)/shard_map/ppermute | solution.py:424
  99.2 9.1 %collective-permute-start.15 = (bf16[64,1024]{1,0:T(8,128)(2,1)S(1)}, bf16[64,1024]{1,0:T(8,128)(2,1)S(1)}, u32[]{:S(2)}, u32[]{:S(2)}) collective-permute-start(bf16[64,1024]{1,0:T(8,128)(2,1)S(1)} %fusion.9.refs_2_.refs_1_), channel_id=1, source_target_pairs={{0,4},{4,0},{8,12},{12,8},{16,20},{20,16},{24,28},{28,24},{1,5},{5... | collective-permute-start | bytes 393224 | tf_op jit(solution)/shard_map/ppermute | solution.py:424
  100.6 10.7 %collective-permute-start.17 = (bf16[64,1024]{1,0:T(8,128)(2,1)S(1)}, bf16[64,1024]{1,0:T(8,128)(2,1)S(1)}, u32[]{:S(2)}, u32[]{:S(2)}) collective-permute-start(bf16[64,1024]{1,0:T(8,128)(2,1)S(1)} %collective-permute-done.13.refs_4_.refs_3_), channel_id=1, source_target_pairs={{0,4},{4,0},{8,12},{12,8},{16,20},{20,16},{24,28},{28,24},{1,5},{5... | collective-permute-start | bytes 393224 | tf_op jit(solution)/shard_map/ppermute | solution.py:424
  102.7 8.6 %collective-permute-start.16 = (bf16[64,1024]{1,0:T(8,128)(2,1)S(1)}, bf16[64,1024]{1,0:T(8,128)(2,1)S(1)}, u32[]{:S(2)}, u32[]{:S(2)}) collective-permute-start(bf16[64,1024]{1,0:T(8,128)(2,1)S(1)} %collective-permute-done.12.refs_3_.refs_2_), channel_id=1, source_target_pairs={{0,4},{4,0},{8,12},{12,8},{16,20},{20,16},{24,28},{28,24},{1,5},{5... | collective-permute-start | bytes 393224 | tf_op jit(solution)/shard_map/ppermute | solution.py:424
  104.1 8.6 %collective-permute-start.18 = (bf16[64,1024]{1,0:T(8,128)(2,1)S(1)}, bf16[64,1024]{1,0:T(8,128)(2,1)S(1)}, u32[]{:S(2)}, u32[]{:S(2)}) collective-permute-start(bf16[64,1024]{1,0:T(8,128)(2,1)S(1)} %collective-permute-done.14.refs_5_.refs_4_), channel_id=1, source_target_pairs={{0,4},{4,0},{8,12},{12,8},{16,20},{20,16},{24,28},{28,24},{1,5},{5... | collective-permute-start | bytes 393224 | tf_op jit(solution)/shard_map/ppermute | solution.py:424
  114.2 8.3 %collective-permute-start.26 = (bf16[256,128]{1,0:T(8,128)(2,1)S(1)}, bf16[256,128]{1,0:T(8,128)(2,1)S(1)}, u32[]{:S(2)}, u32[]{:S(2)}) collective-permute-start(bf16[256,128]{1,0:T(8,128)(2,1)S(1)} %get-tuple-element.33), channel_id=1, source_target_pairs={{0,1},{1,2},{2,3},{3,0},{4,5},{5,6},{6,7},{7,4},{8,9},{9,10},{10,1... | collective-permute-start | bytes 196616 | tf_op jit(solution)/shard_map/ppermute | solution.py:500
  114.3 8.2 %collective-permute-start.27 = (bf16[256,128]{1,0:T(8,128)(2,1)S(1)}, bf16[256,128]{1,0:T(8,128)(2,1)S(1)}, u32[]{:S(2)}, u32[]{:S(2)}) collective-permute-start(bf16[256,128]{1,0:T(8,128)(2,1)S(1)} %get-tuple-element.34), channel_id=1, source_target_pairs={{0,2},{1,3},{2,0},{3,1},{4,6},{5,7},{6,4},{7,5},{8,10},{9,11},{10,... | collective-permute-start | bytes 196616 | tf_op jit(solution)/shard_map/ppermute | solution.py:500
  115.8 6.7 %collective-permute-start.28 = (bf16[256,128]{1,0:T(8,128)(2,1)S(1)}, bf16[256,128]{1,0:T(8,128)(2,1)S(1)}, u32[]{:S(2)}, u32[]{:S(2)}) collective-permute-start(bf16[256,128]{1,0:T(8,128)(2,1)S(1)} %get-tuple-element.35), channel_id=1, source_target_pairs={{0,3},{1,0},{2,1},{3,2},{4,7},{5,4},{6,5},{7,6},{8,11},{9,8},{10,9... | collective-permute-start | bytes 196616 | tf_op jit(solution)/shard_map/ppermute | solution.py:500

commit v5 on v4

--- a/solution.py
+++ b/solution.py
@@ -473,9 +473,10 @@
     smoothed = [None] * CHUNKS
     difference = None
     for c in range(CHUNKS):
-        numer = total(reduce_line([product_own[c], product_in[c]]))
+        terms = reduce_line([product_own[c], product_in[c]])
         if c:
-            numer, _ = lax.optimization_barrier((numer, block))
+            terms[-1], _ = lax.optimization_barrier((terms[-1], block))
+        numer = total(terms)
         block = (numer / jnp.maximum(denoms[c], 1.0)).astype(BF16)
         near, far = {0: block}, {}
         far[0] = exchange(block, 0)

time: 124 us -> 124 us (level)
  no operation moved by 1% of the time
where the time goes in v5:
time: 124 us; the launch traced here: 123 us
  waiting for transfers between devices  38.5 us (31%)
  Pallas kernels  36.2 us (29%)
  starting transfers between devices  35.3 us (28%)
  other arithmetic  11.5 us (9%)
    ppermute x26, waiting for transfers between devices, exchange(): lax.ppermute(block, 'sky', [(i, i ^ 1 << bit) for i in range(sky_count)])  38.5 us
    ppermute x26, starting transfers between devices, exchange(): lax.ppermute(block, 'sky', [(i, i ^ 1 << bit) for i in range(sky_count)])  32.4 us
    pallas_call x4, Pallas kernels, match(): pl.pallas_call(functools.partial(match_kernel, sky_count, which, chunk *...  21.1 us
    convert_element_type x7, other arithmetic, reduce_line(): arrived = exchange(leaving.astype(BF16), bit)  6.15 us
    pallas_call x3, Pallas kernels, weigh(): pl.pallas_call(functools.partial(weight_kernel, sky_count, halves, chunk,...  5.97 us
    pallas_call x2, Pallas kernels, subtract(): pl.pallas_call(functools.partial(difference_kernel, sky_count, pair, line...  5.27 us
    ppermute x3, starting transfers between devices, body(): detection = detection + lax.ppermute(powers[step], 'band', ring).astype(F32)  2.97 us
  transfers between devices with their start and end apart: 29, of which 12 were waited for; matrix products, arithmetic and copies ran while one was open for 8% of the time, Pallas kernels for 22%

profile of v5, /device:TPU:0, one launch (start us, length us, event | category | flops | bytes accessed | tf_op | source)
XLA Modules:
  0.0 123.2 jit_solution(1129594302041313458)
XLA Ops:
  0.6 0.7 convert_element_type.190
  1.3 0.7 convert_convert_fusion
  2.0 0.8 multiply_convert_fusion
  2.8 0.1 pad_convert_fusion
  2.8 0.1 select_maximum_fusion.base_ref
  2.9 1.1 prepare.1
  4.0 1.6 %weigh.5.weight_ref = bf16[1,256,1024]{2,1,0:T(8,128)(2,1)S(1)} custom-call(s32[8,4,8]{2,1,0:T(4,128)} %sky_ref.21, s32[2,35]{1,0:T(2,128)} %bitcast.42, bf16[1024,1024]{1,0:T(8,128)(2,1)} %bitcast.38), custom_call_target="tpu_custom_call" | custom-call | flops 2097152 | bytes 1048576 | tf_op jit(solution)/shard_map/weigh/pallas_call | solution.py:128
  5.6 5.3 %match.7 = (bf16[256,1024]{1,0:T(8,128)(2,1)}, bf16[256,1024]{1,0:T(8,128)(2,1)}) custom-call(s32[8,4,8]{2,1,0:T(4,128)} %sky_ref.21, bf16[1024,1024]{1,0:T(8,128)(2,1)} %bitcast.26, bf16[1024,1024]{1,0:T(8,128)(2,1)} %bitcast.27, bf16[1024,1024]{1,0:T(8,128)(2,1)} %bitcast.28, bf16[256,1152]{1,0:T(8,128)(2,1)S(1)} %get-tuple-element.19.column_ref, ...), custom_call_target="tpu_custom_call" | custom-call | flops 1962934272 | bytes 2097152 | tf_op jit(solution)/shard_map/match/pallas_call | solution.py:218
  11.0 3.0 %collective-permute-start.3 = (bf16[256,1024]{1,0:T(8,128)(2,1)}, bf16[256,1024]{1,0:T(8,128)(2,1)}, u32[]{:S(2)}, u32[]{:S(2)}) collective-permute-start(bf16[256,1024]{1,0:T(8,128)(2,1)} %get-tuple-element.26), channel_id=1, source_target_pairs={{0,4},{4,0},{8,12},{12,8},{16,20},{20,16},{24,28},{28,24},{1,5},{5... | collective-permute-start | bytes 1572872 | tf_op jit(solution)/shard_map/ppermute | solution.py:424
  14.0 2.8 %weigh.3.weight_ref = bf16[2,256,1024]{2,1,0:T(8,128)(2,1)S(1)} custom-call(s32[8,4,8]{2,1,0:T(4,128)} %sky_ref.21, s32[2,35]{1,0:T(2,128)} %bitcast.43, bf16[1024,1024]{1,0:T(8,128)(2,1)} %bitcast.39), custom_call_target="tpu_custom_call" | custom-call | flops 4194304 | bytes 2097152 | tf_op jit(solution)/shard_map/weigh/pallas_call | solution.py:128
  16.8 5.3 %match.5 = (bf16[256,1024]{1,0:T(8,128)(2,1)}, bf16[256,1024]{1,0:T(8,128)(2,1)}) custom-call(s32[8,4,8]{2,1,0:T(4,128)} %sky_ref.21, bf16[1024,1024]{1,0:T(8,128)(2,1)} %bitcast.29, bf16[1024,1024]{1,0:T(8,128)(2,1)} %bitcast.30, bf16[1024,1024]{1,0:T(8,128)(2,1)} %bitcast.31, bf16[256,1152]{1,0:T(8,128)(2,1)S(1)} %get-tuple-element.19.column_ref, ...), custom_call_target="tpu_custom_call" | custom-call | flops 1962934272 | bytes 2097152 | tf_op jit(solution)/shard_map/match/pallas_call | solution.py:218
  22.1 2.0 %collective-permute-start = (bf16[256,1024]{1,0:T(8,128)(2,1)}, bf16[256,1024]{1,0:T(8,128)(2,1)}, u32[]{:S(2)}, u32[]{:S(2)}) collective-permute-start(bf16[256,1024]{1,0:T(8,128)(2,1)} %get-tuple-element.24), channel_id=1, source_target_pairs={{0,4},{4,0},{8,12},{12,8},{16,20},{20,16},{24,28},{28,24},{1,5},{5... | collective-permute-start | bytes 1572872 | tf_op jit(solution)/shard_map/ppermute | solution.py:424
  24.1 0.9 constant_dynamic-slice_fusion
  25.0 1.6 %collective-permute-start.9 = (bf16[2,128,1024]{2,1,0:T(8,128)(2,1)}, bf16[2,128,1024]{2,1,0:T(8,128)(2,1)S(1)}, u32[]{:S(2)}, u32[]{:S(2)}) collective-permute-start(bf16[2,128,1024]{2,1,0:T(8,128)(2,1)} %constant_dynamic-slice_fusion), channel_id=1, source_target_pairs={{0,8},{4,12},{8,0},{12,4},{16,24},{20,28},{24,16},{28,20},{1,9},{5... | collective-permute-start | bytes 1572872 | tf_op jit(solution)/shard_map/ppermute | solution.py:424
  26.6 1.6 %weigh.4.weight_ref = bf16[1,256,1024]{2,1,0:T(8,128)(2,1)S(1)} custom-call(s32[8,4,8]{2,1,0:T(4,128)} %sky_ref.21, s32[2,35]{1,0:T(2,128)} %bitcast.44, bf16[1024,1024]{1,0:T(8,128)(2,1)} %bitcast.40), custom_call_target="tpu_custom_call" | custom-call | flops 2097152 | bytes 1048576 | tf_op jit(solution)/shard_map/weigh/pallas_call | solution.py:128
  28.1 5.2 %match.4 = (bf16[256,1024]{1,0:T(8,128)(2,1)}, bf16[256,1024]{1,0:T(8,128)(2,1)S(1)}) custom-call(s32[8,4,8]{2,1,0:T(4,128)} %sky_ref.21, bf16[1024,1024]{1,0:T(8,128)(2,1)} %bitcast.32, bf16[1024,1024]{1,0:T(8,128)(2,1)} %bitcast.33, bf16[1024,1024]{1,0:T(8,128)(2,1)} %bitcast.34, bf16[256,1152]{1,0:T(8,128)(2,1)S(1)} %get-tuple-element.19.column_ref, ...), custom_call_target="tpu_custom_call" | custom-call | flops 1962934272 | bytes 2097152 | tf_op jit(solution)/shard_map/match/pallas_call | solution.py:218
  33.4 5.2 %match.6 = (bf16[256,1024]{1,0:T(8,128)(2,1)}, bf16[256,1024]{1,0:T(8,128)(2,1)S(1)}) custom-call(s32[8,4,8]{2,1,0:T(4,128)} %sky_ref.21, bf16[1024,1024]{1,0:T(8,128)(2,1)} %bitcast.35, bf16[1024,1024]{1,0:T(8,128)(2,1)} %bitcast.36, bf16[1024,1024]{1,0:T(8,128)(2,1)} %bitcast.37, bf16[256,1152]{1,0:T(8,128)(2,1)S(1)} %get-tuple-element.19.column_ref, ...), custom_call_target="tpu_custom_call" | custom-call | flops 1962934272 | bytes 2097152 | tf_op jit(solution)/shard_map/match/pallas_call | solution.py:218
  38.5 1.0 add_convert_fusion.1
  39.6 0.5 collective-permute-start.4
  40.1 1.0 fusion
  41.1 1.7 %collective-permute-start.7 = (bf16[128,1024]{1,0:T(8,128)(2,1)S(1)}, bf16[128,1024]{1,0:T(8,128)(2,1)S(1)}, u32[]{:S(2)}, u32[]{:S(2)}) collective-permute-start(bf16[128,1024]{1,0:T(8,128)(2,1)S(1)} %fusion), channel_id=1, source_target_pairs={{0,8},{4,12},{8,0},{12,4},{16,24},{20,28},{24,16},{28,20},{1,9},{5... | collective-permute-start | bytes 786440 | tf_op jit(solution)/shard_map/ppermute | solution.py:424
  42.8 5.9 %collective-permute-done = bf16[256,1024]{1,0:T(8,128)(2,1)} collective-permute-done((bf16[256,1024]{1,0:T(8,128)(2,1)}, bf16[256,1024]{1,0:T(8,128)(2,1)}, u32[]{:S(2)}, u32[]{:S(2)}) %collective-permute-start) | collective-permute-done | bytes 524320 | tf_op jit(solution)/shard_map/ppermute | solution.py:424
  48.7 1.0 add_convert_fusion.2
  49.7 1.9 %collective-permute-start.1 = (bf16[128,1024]{1,0:T(8,128)(2,1)S(1)}, bf16[128,1024]{1,0:T(8,128)(2,1)S(1)}, u32[]{:S(2)}, u32[]{:S(2)}) collective-permute-start(bf16[128,1024]{1,0:T(8,128)(2,1)S(1)} %add_convert_fusion.2), channel_id=1, source_target_pairs={{0,8},{4,12},{8,0},{12,4},{16,24},{20,28},{24,16},{28,20},{1,9},{5... | collective-permute-start | bytes 786440 | tf_op jit(solution)/shard_map/ppermute | solution.py:424
  51.6 0.1 add_convert_fusion
  51.7 2.7 %collective-permute-start.10 = (bf16[2,64,1024]{2,1,0:T(8,128)(2,1)S(1)}, bf16[2,64,1024]{2,1,0:T(8,128)(2,1)S(1)}, u32[]{:S(2)}, u32[]{:S(2)}) collective-permute-start(bf16[2,64,1024]{2,1,0:T(8,128)(2,1)S(1)} %add_convert_fusion), channel_id=1, source_target_pairs={{0,16},{4,20},{8,24},{12,28},{16,0},{20,4},{24,8},{28,12},{1,17},{... | collective-permute-start | bytes 786440 | tf_op jit(solution)/shard_map/ppermute | solution.py:424
  54.3 1.0 add_convert_fusion.4
  55.3 0.4 collective-permute-start.5
  55.7 1.0 fusion.2
  56.7 2.7 %collective-permute-start.8 = (bf16[64,1024]{1,0:T(8,128)(2,1)S(1)}, bf16[64,1024]{1,0:T(8,128)(2,1)S(1)}, u32[]{:S(2)}, u32[]{:S(2)}) collective-permute-start(bf16[64,1024]{1,0:T(8,128)(2,1)S(1)} %fusion.2), channel_id=1, source_target_pairs={{0,16},{4,20},{8,24},{12,28},{16,0},{20,4},{24,8},{28,12},{1,17},{... | collective-permute-start | bytes 393224 | tf_op jit(solution)/shard_map/ppermute | solution.py:424
  59.4 4.4 %collective-permute-done.1 = bf16[128,1024]{1,0:T(8,128)(2,1)S(1)} collective-permute-done((bf16[128,1024]{1,0:T(8,128)(2,1)S(1)}, bf16[128,1024]{1,0:T(8,128)(2,1)S(1)}, u32[]{:S(2)}, u32[]{:S(2)}) %collective-permute-start.1) | collective-permute-done | bytes 262176 | tf_op jit(solution)/shard_map/ppermute | solution.py:424
  63.8 1.0 add_convert_fusion.5
  64.9 11.0 %collective-permute-done.10 = bf16[2,64,1024]{2,1,0:T(8,128)(2,1)S(1)} collective-permute-done((bf16[2,64,1024]{2,1,0:T(8,128)(2,1)S(1)}, bf16[2,64,1024]{2,1,0:T(8,128)(2,1)S(1)}, u32[]{:S(2)}, u32[]{:S(2)}) %collective-permute-start.10) | collective-permute-done | bytes 262176 | tf_op jit(solution)/shard_map/ppermute | solution.py:424
  75.8 0.1 fusion.11
  75.9 1.6 %collective-permute-start.11 = (bf16[64,1024]{1,0:T(8,128)(2,1)S(1)}, bf16[64,1024]{1,0:T(8,128)(2,1)S(1)}, u32[]{:S(2)}, u32[]{:S(2)}) collective-permute-start(bf16[64,1024]{1,0:T(8,128)(2,1)S(1)} %fusion.11), channel_id=1, source_target_pairs={{0,4},{4,0},{8,12},{12,8},{16,20},{20,16},{24,28},{28,24},{1,5},{5... | collective-permute-start | bytes 393224 | tf_op jit(solution)/shard_map/ppermute | solution.py:424
  77.5 1.1 collective-permute-done.5
  78.7 2.0 %collective-permute-done.8 = bf16[64,1024]{1,0:T(8,128)(2,1)S(1)} collective-permute-done((bf16[64,1024]{1,0:T(8,128)(2,1)S(1)}, bf16[64,1024]{1,0:T(8,128)(2,1)S(1)}, u32[]{:S(2)}, u32[]{:S(2)}) %collective-permute-start.8) | collective-permute-done | bytes 131104 | tf_op jit(solution)/shard_map/ppermute | solution.py:424
  80.6 1.2 fusion.10.refs_2_.refs_0_
  81.9 3.1 %collective-permute-start.19 = (bf16[64,1024]{1,0:T(8,128)(2,1)S(1)}, bf16[64,1024]{1,0:T(8,128)(2,1)S(1)}, u32[]{:S(2)}, u32[]{:S(2)}) collective-permute-start(bf16[64,1024]{1,0:T(8,128)(2,1)S(1)} %fusion.10.refs_2_.refs_0_), channel_id=1, source_target_pairs={{0,8},{4,12},{8,0},{12,4},{16,24},{20,28},{24,16},{28,20},{1,9},{5... | collective-permute-start | bytes 393224 | tf_op jit(solution)/shard_map/ppermute | solution.py:424
  85.0 1.5 %collective-permute-start.22 = (bf16[64,1024]{1,0:T(8,128)(2,1)S(1)}, bf16[64,1024]{1,0:T(8,128)(2,1)S(1)}, u32[]{:S(2)}, u32[]{:S(2)}) collective-permute-start(bf16[64,1024]{1,0:T(8,128)(2,1)S(1)} %fusion.10.refs_2_.refs_0_), channel_id=1, source_target_pairs={{0,4},{4,0},{8,12},{12,8},{16,20},{20,16},{24,28},{28,24},{1,5},{5... | collective-permute-start | bytes 393224 | tf_op jit(solution)/shard_map/ppermute | solution.py:424
  86.5 1.1 fusion.9.refs_2_.refs_1_
  87.6 0.1 collective-permute-start.13
  87.8 3.9 %collective-permute-done.20.refs_4_.refs_2_ = bf16[64,1024]{1,0:T(8,128)(2,1)S(1)} collective-permute-done((bf16[64,1024]{1,0:T(8,128)(2,1)S(1)}, bf16[64,1024]{1,0:T(8,128)(2,1)S(1)}, u32[]{:S(2)}, u32[]{:S(2)}) %collective-permute-start.20) | collective-permute-done | bytes 131104 | tf_op jit(solution)/shard_map/ppermute | solution.py:424
  91.6 2.0 %collective-permute-start.12 = (bf16[64,1024]{1,0:T(8,128)(2,1)S(1)}, bf16[64,1024]{1,0:T(8,128)(2,1)S(1)}, u32[]{:S(2)}, u32[]{:S(2)}) collective-permute-start(bf16[64,1024]{1,0:T(8,128)(2,1)S(1)} %fusion.9.refs_2_.refs_1_), channel_id=1, source_target_pairs={{0,8},{4,12},{8,0},{12,4},{16,24},{20,28},{24,16},{28,20},{1,9},{5... | collective-permute-start | bytes 393224 | tf_op jit(solution)/shard_map/ppermute | solution.py:424
  93.7 1.2 collective-permute-start.23
  94.9 0.8 collective-permute-start.24
  95.7 2.0 %collective-permute-done.21.refs_5_.refs_3_ = bf16[64,1024]{1,0:T(8,128)(2,1)S(1)} collective-permute-done((bf16[64,1024]{1,0:T(8,128)(2,1)S(1)}, bf16[64,1024]{1,0:T(8,128)(2,1)S(1)}, u32[]{:S(2)}, u32[]{:S(2)}) %collective-permute-start.21) | collective-permute-done | bytes 131104 | tf_op jit(solution)/shard_map/ppermute | solution.py:424
  97.8 1.4 %collective-permute-start.25 = (bf16[64,1024]{1,0:T(8,128)(2,1)S(1)}, bf16[64,1024]{1,0:T(8,128)(2,1)S(1)}, u32[]{:S(2)}, u32[]{:S(2)}) collective-permute-start(bf16[64,1024]{1,0:T(8,128)(2,1)S(1)} %collective-permute-done.21.refs_5_.refs_3_), channel_id=1, source_target_pairs={{0,4},{4,0},{8,12},{12,8},{16,20},{20,16},{24,28},{28,24},{1,5},{5... | collective-permute-start | bytes 393224 | tf_op jit(solution)/shard_map/ppermute | solution.py:424
  99.2 1.4 %collective-permute-start.15 = (bf16[64,1024]{1,0:T(8,128)(2,1)S(1)}, bf16[64,1024]{1,0:T(8,128)(2,1)S(1)}, u32[]{:S(2)}, u32[]{:S(2)}) collective-permute-start(bf16[64,1024]{1,0:T(8,128)(2,1)S(1)} %fusion.9.refs_2_.refs_1_), channel_id=1, source_target_pairs={{0,4},{4,0},{8,12},{12,8},{16,20},{20,16},{24,28},{28,24},{1,5},{5... | collective-permute-start | bytes 393224 | tf_op jit(solution)/shard_map/ppermute | solution.py:424
  100.6 0.7 collective-permute-start.17
  101.3 1.4 %collective-permute-done.24.refs_8_.refs_6_ = bf16[64,1024]{1,0:T(8,128)(2,1)S(1)} collective-permute-done((bf16[64,1024]{1,0:T(8,128)(2,1)S(1)}, bf16[64,1024]{1,0:T(8,128)(2,1)S(1)}, u32[]{:S(2)}, u32[]{:S(2)}) %collective-permute-start.24) | collective-permute-done | bytes 131104 | tf_op jit(solution)/shard_map/ppermute | solution.py:424
  102.7 1.4 %collective-permute-start.16 = (bf16[64,1024]{1,0:T(8,128)(2,1)S(1)}, bf16[64,1024]{1,0:T(8,128)(2,1)S(1)}, u32[]{:S(2)}, u32[]{:S(2)}) collective-permute-start(bf16[64,1024]{1,0:T(8,128)(2,1)S(1)} %collective-permute-done.12.refs_3_.refs_2_), channel_id=1, source_target_pairs={{0,4},{4,0},{8,12},{12,8},{16,20},{20,16},{24,28},{28,24},{1,5},{5... | collective-permute-start | bytes 393224 | tf_op jit(solution)/shard_map/ppermute | solution.py:424
  104.1 0.6 collective-permute-start.18
  104.7 0.8 collective-permute-done.25.refs_9_.refs_7_
  105.5 1.2 %smooth.1.refs_0_ = bf16[2,256,128]{2,1,0:T(8,128)(2,1)S(1)} custom-call(s32[8,4,8]{2,1,0:T(4,128)} %sky_ref.21, bf16[256,128]{1,0:T(8,128)(2,1)S(1)} %get-tuple-element.30.across_ref, bf16[64,1024]{1,0:T(8,128)(2,1)S(1)} %fusion.10.refs_2_.refs_0_, bf16[64,1024]{1,0:T(8,128)(2,1)S(1)} %collective-permute-done.19.refs_3_.refs_1_, ...), custom_call_target="tpu_custom_call" | custom-call | flops 33554432 | bytes 1048576 | tf_op jit(solution)/shard_map/smooth/pallas_call | solution.py:343
  106.8 1.6 %collective-permute-done.15.refs_6_.refs_5_ = bf16[64,1024]{1,0:T(8,128)(2,1)S(1)} collective-permute-done((bf16[64,1024]{1,0:T(8,128)(2,1)S(1)}, bf16[64,1024]{1,0:T(8,128)(2,1)S(1)}, u32[]{:S(2)}, u32[]{:S(2)}) %collective-permute-start.15) | collective-permute-done | bytes 131104 | tf_op jit(solution)/shard_map/ppermute | solution.py:424
  108.3 3.0 %collective-permute-done.16.refs_7_.refs_6_ = bf16[64,1024]{1,0:T(8,128)(2,1)S(1)} collective-permute-done((bf16[64,1024]{1,0:T(8,128)(2,1)S(1)}, bf16[64,1024]{1,0:T(8,128)(2,1)S(1)}, u32[]{:S(2)}, u32[]{:S(2)}) %collective-permute-start.16) | collective-permute-done | bytes 131104 | tf_op jit(solution)/shard_map/ppermute | solution.py:424
  111.3 1.4 %collective-permute-done.18.refs_9_.refs_8_ = bf16[64,1024]{1,0:T(8,128)(2,1)S(1)} collective-permute-done((bf16[64,1024]{1,0:T(8,128)(2,1)S(1)}, bf16[64,1024]{1,0:T(8,128)(2,1)S(1)}, u32[]{:S(2)}, u32[]{:S(2)}) %collective-permute-start.18) | collective-permute-done | bytes 131104 | tf_op jit(solution)/shard_map/ppermute | solution.py:424
  112.7 1.5 %power.1 = (f32[256,128]{1,0:T(8,128)S(1)}, bf16[256,128]{1,0:T(8,128)(2,1)S(1)}, bf16[256,128]{1,0:T(8,128)(2,1)S(1)}, bf16[256,128]{1,0:T(8,128)(2,1)S(1)}) custom-call(s32[8,4,8]{2,1,0:T(4,128)} %sky_ref.21, bf16[256,128]{1,0:T(8,128)(2,1)S(1)} %get-tuple-element.30.across_ref, bf16[128,160]{1,0:T(8,128)(2,1)S(1)} %get-tuple-element.31.down_ref, ...), custom_call_target="tpu_custom_call" | custom-call | flops 78643200 | bytes 1572864 | tf_op jit(solution)/shard_map/power/pallas_call | solution.py:393
  114.3 1.5 %collective-permute-start.27 = (bf16[256,128]{1,0:T(8,128)(2,1)S(1)}, bf16[256,128]{1,0:T(8,128)(2,1)S(1)}, u32[]{:S(2)}, u32[]{:S(2)}) collective-permute-start(bf16[256,128]{1,0:T(8,128)(2,1)S(1)} %get-tuple-element.34), channel_id=1, source_target_pairs={{0,2},{1,3},{2,0},{3,1},{4,6},{5,7},{6,4},{7,5},{8,10},{9,11},{10,... | collective-permute-start | bytes 196616 | tf_op jit(solution)/shard_map/ppermute | solution.py:501
  115.8 1.4 %collective-permute-start.28 = (bf16[256,128]{1,0:T(8,128)(2,1)S(1)}, bf16[256,128]{1,0:T(8,128)(2,1)S(1)}, u32[]{:S(2)}, u32[]{:S(2)}) collective-permute-start(bf16[256,128]{1,0:T(8,128)(2,1)S(1)} %get-tuple-element.35), channel_id=1, source_target_pairs={{0,3},{1,0},{2,1},{3,2},{4,7},{5,4},{6,5},{7,6},{8,11},{9,8},{10,9... | collective-permute-start | bytes 196616 | tf_op jit(solution)/shard_map/ppermute | solution.py:501
  117.2 2.6 %subtract.2.refs_10_ = bf16[2,2,256,1024]{3,2,1,0:T(8,128)(2,1)} custom-call(s32[8,4,8]{2,1,0:T(4,128)} %sky_ref.21, bf16[256,1024]{1,0:T(8,128)(2,1)} %get-tuple-element.28.refs_0_, bf16[256,1024]{1,0:T(8,128)(2,1)} %get-tuple-element.29.refs_1_, bf16[64,1024]{1,0:T(8,128)(2,1)S(1)} %fusion.10.refs_2_.refs_0_, ...), custom_call_target="tpu_custom_call" | custom-call | flops 524288 | bytes 3145728 | tf_op jit(solution)/shard_map/subtract/pallas_call | solution.py:297
  119.9 2.6 %subtract.3 = bf16[2,2,256,1024]{3,2,1,0:T(8,128)(2,1)} custom-call(s32[8,4,8]{2,1,0:T(4,128)} %sky_ref.21, bf16[256,1024]{1,0:T(8,128)(2,1)} %get-tuple-element.21.refs_0_, bf16[256,1024]{1,0:T(8,128)(2,1)} %get-tuple-element.22.refs_1_, bf16[64,1024]{1,0:T(8,128)(2,1)S(1)} %fusion.9.refs_2_.refs_1_, ...), custom_call_target="tpu_custom_call", output_to_operand_aliasing={{}: (11, {})} | custom-call | flops 524288 | bytes 3145728 | tf_op jit(solution)/shard_map/subtract/pallas_call | solution.py:297
  122.5 0.7 convert_add_fusion.3
  (23 shorter events, 0.3 us)
Async XLA Ops:
  11.0 27.6 %collective-permute-start.3 = (bf16[256,1024]{1,0:T(8,128)(2,1)}, bf16[256,1024]{1,0:T(8,128)(2,1)}, u32[]{:S(2)}, u32[]{:S(2)}) collective-permute-start(bf16[256,1024]{1,0:T(8,128)(2,1)} %get-tuple-element.26), channel_id=1, source_target_pairs={{0,4},{4,0},{8,12},{12,8},{16,20},{20,16},{24,28},{28,24},{1,5},{5... | collective-permute-start | bytes 1572872 | tf_op jit(solution)/shard_map/ppermute | solution.py:424
  14.0 26.1 %collective-permute-start.6 = (bf16[256,1024]{1,0:T(8,128)(2,1)S(1)}, bf16[256,1024]{1,0:T(8,128)(2,1)}, u32[]{:S(2)}, u32[]{:S(2)}) collective-permute-start(bf16[256,1024]{1,0:T(8,128)(2,1)S(1)} %bitcast.25), channel_id=1, source_target_pairs={{0,4},{4,0},{8,12},{12,8},{16,20},{20,16},{24,28},{28,24},{1,5},{5... | collective-permute-start | bytes 1572872 | tf_op jit(solution)/shard_map/ppermute | solution.py:424
  22.1 26.6 %collective-permute-start = (bf16[256,1024]{1,0:T(8,128)(2,1)}, bf16[256,1024]{1,0:T(8,128)(2,1)}, u32[]{:S(2)}, u32[]{:S(2)}) collective-permute-start(bf16[256,1024]{1,0:T(8,128)(2,1)} %get-tuple-element.24), channel_id=1, source_target_pairs={{0,4},{4,0},{8,12},{12,8},{16,20},{20,16},{24,28},{28,24},{1,5},{5... | collective-permute-start | bytes 1572872 | tf_op jit(solution)/shard_map/ppermute | solution.py:424
  25.0 26.6 %collective-permute-start.9 = (bf16[2,128,1024]{2,1,0:T(8,128)(2,1)}, bf16[2,128,1024]{2,1,0:T(8,128)(2,1)S(1)}, u32[]{:S(2)}, u32[]{:S(2)}) collective-permute-start(bf16[2,128,1024]{2,1,0:T(8,128)(2,1)} %constant_dynamic-slice_fusion), channel_id=1, source_target_pairs={{0,8},{4,12},{8,0},{12,4},{16,24},{20,28},{24,16},{28,20},{1,9},{5... | collective-permute-start | bytes 1572872 | tf_op jit(solution)/shard_map/ppermute | solution.py:424
  39.6 14.7 %collective-permute-start.4 = (bf16[128,1024]{1,0:T(8,128)(2,1)S(1)}, bf16[128,1024]{1,0:T(8,128)(2,1)S(1)}, u32[]{:S(2)}, u32[]{:S(2)}) collective-permute-start(bf16[128,1024]{1,0:T(8,128)(2,1)S(1)} %add_convert_fusion.1), channel_id=1, source_target_pairs={{0,8},{4,12},{8,0},{12,4},{16,24},{20,28},{24,16},{28,20},{1,9},{5... | collective-permute-start | bytes 786440 | tf_op jit(solution)/shard_map/ppermute | solution.py:424
  41.1 14.6 %collective-permute-start.7 = (bf16[128,1024]{1,0:T(8,128)(2,1)S(1)}, bf16[128,1024]{1,0:T(8,128)(2,1)S(1)}, u32[]{:S(2)}, u32[]{:S(2)}) collective-permute-start(bf16[128,1024]{1,0:T(8,128)(2,1)S(1)} %fusion), channel_id=1, source_target_pairs={{0,8},{4,12},{8,0},{12,4},{16,24},{20,28},{24,16},{28,20},{1,9},{5... | collective-permute-start | bytes 786440 | tf_op jit(solution)/shard_map/ppermute | solution.py:424
  49.7 14.1 %collective-permute-start.1 = (bf16[128,1024]{1,0:T(8,128)(2,1)S(1)}, bf16[128,1024]{1,0:T(8,128)(2,1)S(1)}, u32[]{:S(2)}, u32[]{:S(2)}) collective-permute-start(bf16[128,1024]{1,0:T(8,128)(2,1)S(1)} %add_convert_fusion.2), channel_id=1, source_target_pairs={{0,8},{4,12},{8,0},{12,4},{16,24},{20,28},{24,16},{28,20},{1,9},{5... | collective-permute-start | bytes 786440 | tf_op jit(solution)/shard_map/ppermute | solution.py:424
  51.7 24.2 %collective-permute-start.10 = (bf16[2,64,1024]{2,1,0:T(8,128)(2,1)S(1)}, bf16[2,64,1024]{2,1,0:T(8,128)(2,1)S(1)}, u32[]{:S(2)}, u32[]{:S(2)}) collective-permute-start(bf16[2,64,1024]{2,1,0:T(8,128)(2,1)S(1)} %add_convert_fusion), channel_id=1, source_target_pairs={{0,16},{4,20},{8,24},{12,28},{16,0},{20,4},{24,8},{28,12},{1,17},{... | collective-permute-start | bytes 786440 | tf_op jit(solution)/shard_map/ppermute | solution.py:424
  55.3 23.3 %collective-permute-start.5 = (bf16[64,1024]{1,0:T(8,128)(2,1)S(1)}, bf16[64,1024]{1,0:T(8,128)(2,1)S(1)}, u32[]{:S(2)}, u32[]{:S(2)}) collective-permute-start(bf16[64,1024]{1,0:T(8,128)(2,1)S(1)} %add_convert_fusion.4), channel_id=1, source_target_pairs={{0,16},{4,20},{8,24},{12,28},{16,0},{20,4},{24,8},{28,12},{1,17},{... | collective-permute-start | bytes 393224 | tf_op jit(solution)/shard_map/ppermute | solution.py:424
  56.7 23.9 %collective-permute-start.8 = (bf16[64,1024]{1,0:T(8,128)(2,1)S(1)}, bf16[64,1024]{1,0:T(8,128)(2,1)S(1)}, u32[]{:S(2)}, u32[]{:S(2)}) collective-permute-start(bf16[64,1024]{1,0:T(8,128)(2,1)S(1)} %fusion.2), channel_id=1, source_target_pairs={{0,16},{4,20},{8,24},{12,28},{16,0},{20,4},{24,8},{28,12},{1,17},{... | collective-permute-start | bytes 393224 | tf_op jit(solution)/shard_map/ppermute | solution.py:424
  64.8 21.7 %collective-permute-start.2 = (bf16[64,1024]{1,0:T(8,128)(2,1)S(1)}, bf16[64,1024]{1,0:T(8,128)(2,1)S(1)}, u32[]{:S(2)}, u32[]{:S(2)}) collective-permute-start(bf16[64,1024]{1,0:T(8,128)(2,1)S(1)} %add_convert_fusion.5), channel_id=1, source_target_pairs={{0,16},{4,20},{8,24},{12,28},{16,0},{20,4},{24,8},{28,12},{1,17},{... | collective-permute-start | bytes 393224 | tf_op jit(solution)/shard_map/ppermute | solution.py:424
  75.9 10.6 %collective-permute-start.11 = (bf16[64,1024]{1,0:T(8,128)(2,1)S(1)}, bf16[64,1024]{1,0:T(8,128)(2,1)S(1)}, u32[]{:S(2)}, u32[]{:S(2)}) collective-permute-start(bf16[64,1024]{1,0:T(8,128)(2,1)S(1)} %fusion.11), channel_id=1, source_target_pairs={{0,4},{4,0},{8,12},{12,8},{16,20},{20,16},{24,28},{28,24},{1,5},{5... | collective-permute-start | bytes 393224 | tf_op jit(solution)/shard_map/ppermute | solution.py:424
  81.9 9.8 %collective-permute-start.20 = (bf16[64,1024]{1,0:T(8,128)(2,1)S(1)}, bf16[64,1024]{1,0:T(8,128)(2,1)S(1)}, u32[]{:S(2)}, u32[]{:S(2)}) collective-permute-start(bf16[64,1024]{1,0:T(8,128)(2,1)S(1)} %fusion.10.refs_2_.refs_0_), channel_id=1, source_target_pairs={{0,16},{4,20},{8,24},{12,28},{16,0},{20,4},{24,8},{28,12},{1,17},{... | collective-permute-start | bytes 393224 | tf_op jit(solution)/shard_map/ppermute | solution.py:424
  81.9 11.7 %collective-permute-start.19 = (bf16[64,1024]{1,0:T(8,128)(2,1)S(1)}, bf16[64,1024]{1,0:T(8,128)(2,1)S(1)}, u32[]{:S(2)}, u32[]{:S(2)}) collective-permute-start(bf16[64,1024]{1,0:T(8,128)(2,1)S(1)} %fusion.10.refs_2_.refs_0_), channel_id=1, source_target_pairs={{0,8},{4,12},{8,0},{12,4},{16,24},{20,28},{24,16},{28,20},{1,9},{5... | collective-permute-start | bytes 393224 | tf_op jit(solution)/shard_map/ppermute | solution.py:424
  85.0 9.9 %collective-permute-start.22 = (bf16[64,1024]{1,0:T(8,128)(2,1)S(1)}, bf16[64,1024]{1,0:T(8,128)(2,1)S(1)}, u32[]{:S(2)}, u32[]{:S(2)}) collective-permute-start(bf16[64,1024]{1,0:T(8,128)(2,1)S(1)} %fusion.10.refs_2_.refs_0_), channel_id=1, source_target_pairs={{0,4},{4,0},{8,12},{12,8},{16,20},{20,16},{24,28},{28,24},{1,5},{5... | collective-permute-start | bytes 393224 | tf_op jit(solution)/shard_map/ppermute | solution.py:424
  87.6 8.1 %collective-permute-start.13 = (bf16[64,1024]{1,0:T(8,128)(2,1)S(1)}, bf16[64,1024]{1,0:T(8,128)(2,1)S(1)}, u32[]{:S(2)}, u32[]{:S(2)}) collective-permute-start(bf16[64,1024]{1,0:T(8,128)(2,1)S(1)} %fusion.9.refs_2_.refs_1_), channel_id=1, source_target_pairs={{0,16},{4,20},{8,24},{12,28},{16,0},{20,4},{24,8},{28,12},{1,17},{... | collective-permute-start | bytes 393224 | tf_op jit(solution)/shard_map/ppermute | solution.py:424
  91.6 6.1 %collective-permute-start.21 = (bf16[64,1024]{1,0:T(8,128)(2,1)S(1)}, bf16[64,1024]{1,0:T(8,128)(2,1)S(1)}, u32[]{:S(2)}, u32[]{:S(2)}) collective-permute-start(bf16[64,1024]{1,0:T(8,128)(2,1)S(1)} %collective-permute-done.20.refs_4_.refs_2_), channel_id=1, source_target_pairs={{0,8},{4,12},{8,0},{12,4},{16,24},{20,28},{24,16},{28,20},{1,9},{5... | collective-permute-start | bytes 393224 | tf_op jit(solution)/shard_map/ppermute | solution.py:424
  91.6 7.6 %collective-permute-start.12 = (bf16[64,1024]{1,0:T(8,128)(2,1)S(1)}, bf16[64,1024]{1,0:T(8,128)(2,1)S(1)}, u32[]{:S(2)}, u32[]{:S(2)}) collective-permute-start(bf16[64,1024]{1,0:T(8,128)(2,1)S(1)} %fusion.9.refs_2_.refs_1_), channel_id=1, source_target_pairs={{0,8},{4,12},{8,0},{12,4},{16,24},{20,28},{24,16},{28,20},{1,9},{5... | collective-permute-start | bytes 393224 | tf_op jit(solution)/shard_map/ppermute | solution.py:424
  93.7 6.9 %collective-permute-start.23 = (bf16[64,1024]{1,0:T(8,128)(2,1)S(1)}, bf16[64,1024]{1,0:T(8,128)(2,1)S(1)}, u32[]{:S(2)}, u32[]{:S(2)}) collective-permute-start(bf16[64,1024]{1,0:T(8,128)(2,1)S(1)} %collective-permute-done.19.refs_3_.refs_1_), channel_id=1, source_target_pairs={{0,4},{4,0},{8,12},{12,8},{16,20},{20,16},{24,28},{28,24},{1,5},{5... | collective-permute-start | bytes 393224 | tf_op jit(solution)/shard_map/ppermute | solution.py:424
  94.9 7.8 %collective-permute-start.24 = (bf16[64,1024]{1,0:T(8,128)(2,1)S(1)}, bf16[64,1024]{1,0:T(8,128)(2,1)S(1)}, u32[]{:S(2)}, u32[]{:S(2)}) collective-permute-start(bf16[64,1024]{1,0:T(8,128)(2,1)S(1)} %collective-permute-done.20.refs_4_.refs_2_), channel_id=1, source_target_pairs={{0,4},{4,0},{8,12},{12,8},{16,20},{20,16},{24,28},{28,24},{1,5},{5... | collective-permute-start | bytes 393224 | tf_op jit(solution)/shard_map/ppermute | solution.py:424
  95.7 8.4 %collective-permute-start.14 = (bf16[64,1024]{1,0:T(8,128)(2,1)S(1)}, bf16[64,1024]{1,0:T(8,128)(2,1)S(1)}, u32[]{:S(2)}, u32[]{:S(2)}) collective-permute-start(bf16[64,1024]{1,0:T(8,128)(2,1)S(1)} %collective-permute-done.13.refs_4_.refs_3_), channel_id=1, source_target_pairs={{0,8},{4,12},{8,0},{12,4},{16,24},{20,28},{24,16},{28,20},{1,9},{5... | collective-permute-start | bytes 393224 | tf_op jit(solution)/shard_map/ppermute | solution.py:424
  97.8 7.8 %collective-permute-start.25 = (bf16[64,1024]{1,0:T(8,128)(2,1)S(1)}, bf16[64,1024]{1,0:T(8,128)(2,1)S(1)}, u32[]{:S(2)}, u32[]{:S(2)}) collective-permute-start(bf16[64,1024]{1,0:T(8,128)(2,1)S(1)} %collective-permute-done.21.refs_5_.refs_3_), channel_id=1, source_target_pairs={{0,4},{4,0},{8,12},{12,8},{16,20},{20,16},{24,28},{28,24},{1,5},{5... | collective-permute-start | bytes 393224 | tf_op jit(solution)/shard_map/ppermute | solution.py:424
  99.2 9.1 %collective-permute-start.15 = (bf16[64,1024]{1,0:T(8,128)(2,1)S(1)}, bf16[64,1024]{1,0:T(8,128)(2,1)S(1)}, u32[]{:S(2)}, u32[]{:S(2)}) collective-permute-start(bf16[64,1024]{1,0:T(8,128)(2,1)S(1)} %fusion.9.refs_2_.refs_1_), channel_id=1, source_target_pairs={{0,4},{4,0},{8,12},{12,8},{16,20},{20,16},{24,28},{28,24},{1,5},{5... | collective-permute-start | bytes 393224 | tf_op jit(solution)/shard_map/ppermute | solution.py:424
  100.6 10.7 %collective-permute-start.17 = (bf16[64,1024]{1,0:T(8,128)(2,1)S(1)}, bf16[64,1024]{1,0:T(8,128)(2,1)S(1)}, u32[]{:S(2)}, u32[]{:S(2)}) collective-permute-start(bf16[64,1024]{1,0:T(8,128)(2,1)S(1)} %collective-permute-done.13.refs_4_.refs_3_), channel_id=1, source_target_pairs={{0,4},{4,0},{8,12},{12,8},{16,20},{20,16},{24,28},{28,24},{1,5},{5... | collective-permute-start | bytes 393224 | tf_op jit(solution)/shard_map/ppermute | solution.py:424
  102.7 8.6 %collective-permute-start.16 = (bf16[64,1024]{1,0:T(8,128)(2,1)S(1)}, bf16[64,1024]{1,0:T(8,128)(2,1)S(1)}, u32[]{:S(2)}, u32[]{:S(2)}) collective-permute-start(bf16[64,1024]{1,0:T(8,128)(2,1)S(1)} %collective-permute-done.12.refs_3_.refs_2_), channel_id=1, source_target_pairs={{0,4},{4,0},{8,12},{12,8},{16,20},{20,16},{24,28},{28,24},{1,5},{5... | collective-permute-start | bytes 393224 | tf_op jit(solution)/shard_map/ppermute | solution.py:424
  104.1 8.6 %collective-permute-start.18 = (bf16[64,1024]{1,0:T(8,128)(2,1)S(1)}, bf16[64,1024]{1,0:T(8,128)(2,1)S(1)}, u32[]{:S(2)}, u32[]{:S(2)}) collective-permute-start(bf16[64,1024]{1,0:T(8,128)(2,1)S(1)} %collective-permute-done.14.refs_5_.refs_4_), channel_id=1, source_target_pairs={{0,4},{4,0},{8,12},{12,8},{16,20},{20,16},{24,28},{28,24},{1,5},{5... | collective-permute-start | bytes 393224 | tf_op jit(solution)/shard_map/ppermute | solution.py:424
  114.2 8.3 %collective-permute-start.26 = (bf16[256,128]{1,0:T(8,128)(2,1)S(1)}, bf16[256,128]{1,0:T(8,128)(2,1)S(1)}, u32[]{:S(2)}, u32[]{:S(2)}) collective-permute-start(bf16[256,128]{1,0:T(8,128)(2,1)S(1)} %get-tuple-element.33), channel_id=1, source_target_pairs={{0,1},{1,2},{2,3},{3,0},{4,5},{5,6},{6,7},{7,4},{8,9},{9,10},{10,1... | collective-permute-start | bytes 196616 | tf_op jit(solution)/shard_map/ppermute | solution.py:501
  114.3 8.2 %collective-permute-start.27 = (bf16[256,128]{1,0:T(8,128)(2,1)S(1)}, bf16[256,128]{1,0:T(8,128)(2,1)S(1)}, u32[]{:S(2)}, u32[]{:S(2)}) collective-permute-start(bf16[256,128]{1,0:T(8,128)(2,1)S(1)} %get-tuple-element.34), channel_id=1, source_target_pairs={{0,2},{1,3},{2,0},{3,1},{4,6},{5,7},{6,4},{7,5},{8,10},{9,11},{10,... | collective-permute-start | bytes 196616 | tf_op jit(solution)/shard_map/ppermute | solution.py:501
  115.8 6.7 %collective-permute-start.28 = (bf16[256,128]{1,0:T(8,128)(2,1)S(1)}, bf16[256,128]{1,0:T(8,128)(2,1)S(1)}, u32[]{:S(2)}, u32[]{:S(2)}) collective-permute-start(bf16[256,128]{1,0:T(8,128)(2,1)S(1)} %get-tuple-element.35), channel_id=1, source_target_pairs={{0,3},{1,0},{2,1},{3,2},{4,7},{5,4},{6,5},{7,6},{8,11},{9,8},{10,9... | collective-permute-start | bytes 196616 | tf_op jit(solution)/shard_map/ppermute | solution.py:501

commit v6 on v5

--- a/solution.py
+++ b/solution.py
@@ -259,59 +259,6 @@
     return row
 
 
-def piece_rows(step, line, chunk_rows, part_rows):
-    row = row_of(lax.axis_index("sky") // 2 ^ step, line, chunk_rows)
-    return pl.ds(pl.multiple_of(row, part_rows), part_rows)
-
-
-def difference_kernel(sky_count, pair, line, sky_ref, *refs):
-    matched = refs[:pair]
-    pieces = refs[pair : pair + pair * line]
-    out_ref = refs[-1]
-    start = start_column(sky_ref)
-    part_rows = pieces[0].shape[0]
-    chunk_rows, side = matched[0].shape
-    for group in range(pair):
-        half = half_of((OWN, OTHER)[group])
-        for step in range(line):
-            rows = piece_rows(step, line, chunk_rows, part_rows)
-            piece = pieces[group * line + step]
-            for tile in range(side // TILE):
-                window = slice(tile * TILE, (tile + 1) * TILE)
-                source = pl.multiple_of(lax.rem(start + tile, sky_count) * TILE, TILE)
-                picked = piece[:, pl.ds(source, TILE)].astype(F32)
-                out_ref[half, 0, rows, window] = (matched[group][rows, window].astype(F32) - picked).astype(BF16)
-
-
-def subtract(matched, pieces, sky_columns, chunk, before, sky_count):
-    chunk_rows, side = matched[0].shape
-    pair = len(matched)
-    line = len(pieces) // pair
-    operands = [*map(in_hbm, matched), *pieces]
-    specs = [SCALARS] + [pl.BlockSpec(array.shape, lambda i: (0, 0)) for array in operands]
-    aliases = {}
-    if before is not None:
-        operands.append(before)
-        specs.append(pl.BlockSpec(memory_space=pl.ANY))
-        aliases = {len(operands): 0}
-    return pl.pallas_call(
-        functools.partial(difference_kernel, sky_count, pair, line),
-        out_shape=jax.ShapeDtypeStruct((pair, CHUNKS, chunk_rows, side), BF16),
-        grid_spec=pltpu.PrefetchScalarGridSpec(
-            num_scalar_prefetch=0,
-            grid=(1,),
-            in_specs=specs,
-            out_specs=pl.BlockSpec((pair, 1, chunk_rows, side), lambda i: (0, chunk, 0, 0)),
-        ),
-        input_output_aliases=aliases,
-        cost_estimate=pl.CostEstimate(
-            flops=pair * chunk_rows * side, bytes_accessed=pair * chunk_rows * side * 6, transcendentals=0
-        ),
-        compiler_params=pltpu.CompilerParams(vmem_limit_bytes=24 << 20),
-        name="subtract",
-    )(in_hbm(sky_columns), *operands)
-
-
 def smooth_pieces(sky_count, line, across, pieces, chunk_rows, store):
     def column(piece, away):
         source = lax.rem(lax.axis_index("sky") + away, sky_count) * TILE
@@ -327,33 +274,96 @@
             store(half_of((OWN, OTHER)[group]), row, jnp.dot(window, across, preferred_element_type=F32).astype(BF16))
 
 
-def smooth_kernel(sky_count, line, sky_ref, across_ref, *refs):
-    pieces, out_ref = refs[:-1], refs[-1]
-    part_rows, chunk_rows = pieces[0].shape[0], out_ref.shape[1]
-
-    def store(half, row, values):
-        out_ref[half, pl.ds(pl.multiple_of(row, part_rows), part_rows), :] = values
-
-    smooth_pieces(sky_count, line, across_ref[...], pieces, chunk_rows, store)
-
-
-def smooth(pieces, across_band, sky_columns, pair, chunk_rows, sky_count):
-    line = len(pieces) // pair
-    operands = [across_band, *pieces]
+def finish_kernel(sky_count, line, jobs, with_smooth, sky_ref, *refs):
+    count = len(jobs)
+    if with_smooth:
+        across_ref, refs = refs[0], refs[1:]
+    matched, refs = refs[:count], refs[count:]
+    pieces, refs = refs[: count * line], refs[count * line :]
+    if not with_smooth:
+        refs = refs[1:]
+    out_ref, refs = refs[0], refs[1:]
+    if with_smooth:
+        smooth_ref, refs = refs[0], refs[1:]
+    taken, ready, taken_sem, ready_sem = refs if with_smooth else (None, *refs[:1], None, *refs[1:])
+    chunk_rows, side = matched[0].shape
+    part_rows = pieces[0].shape[0]
+    start = start_column(sky_ref)
+    arriving = []
+    if with_smooth:
+        arriving = [
+            pltpu.make_async_copy(matched[index], taken.at[index], taken_sem.at[index]) for index in range(count)
+        ]
+    for copy in arriving:
+        copy.start()
+    if with_smooth:
+
+        def store(half, row, values):
+            smooth_ref[half, pl.ds(pl.multiple_of(row, part_rows), part_rows), :] = values
+
+        smooth_pieces(sky_count, line, across_ref[...], pieces[: 2 * line], chunk_rows, store)
+    leaving = []
+    for index, (which, chunk) in enumerate(jobs):
+        source_ref = matched[index]
+        if with_smooth:
+            arriving[index].wait()
+            source_ref = taken.at[index]
+        for step in range(line):
+            row = row_of(lax.axis_index("sky") // 2 ^ step, line, chunk_rows)
+            rows = pl.ds(pl.multiple_of(row, part_rows), part_rows)
+            piece = pieces[index * line + step]
+            for tile in range(side // TILE):
+                window = slice(tile * TILE, (tile + 1) * TILE)
+                source = pl.multiple_of(lax.rem(start + tile, sky_count) * TILE, TILE)
+                picked = piece[:, pl.ds(source, TILE)].astype(F32)
+                ready[index, rows, window] = (source_ref[rows, window].astype(F32) - picked).astype(BF16)
+        copy = pltpu.make_async_copy(ready.at[index], out_ref.at[half_of(which), chunk], ready_sem.at[index])
+        copy.start()
+        leaving.append(copy)
+    for copy in leaving:
+        copy.wait()
+
+
+def finish(jobs, matched, pieces, across_band, sky_columns, before, sky_count):
+    chunk_rows, side = matched[0].shape
+    count = len(jobs)
+    line = len(pieces) // count
+    with_smooth = before is None
+    place = pl.BlockSpec(memory_space=pl.ANY)
+    operands = [*map(in_hbm, matched), *pieces]
+    specs = [pl.BlockSpec(array.shape, lambda i: (0, 0)) for array in operands]
+    scratch = [pltpu.VMEM((count, chunk_rows, side), BF16), pltpu.SemaphoreType.DMA((count,))]
+    if with_smooth:
+        operands = [across_band, *operands]
+        specs = [pl.BlockSpec(across_band.shape, lambda i: (0, 0))] + [place] * count + specs[count:]
+        scratch = [scratch[0], scratch[0], scratch[1], scratch[1]]
+    specs = [SCALARS] + specs
+    shapes = [pltpu.HBM((2, CHUNKS, chunk_rows, side), BF16)]
+    outs = [place]
+    aliases = {}
+    if with_smooth:
+        shapes.append(jax.ShapeDtypeStruct((2, chunk_rows, TILE), BF16))
+        outs.append(pl.BlockSpec((2, chunk_rows, TILE), lambda i: (0, 0, 0)))
+    else:
+        operands.append(before)
+        specs.append(place)
+        aliases = {len(operands): 0}
     return pl.pallas_call(
-        functools.partial(smooth_kernel, sky_count, line),
-        out_shape=jax.ShapeDtypeStruct((pair, chunk_rows, TILE), BF16),
+        functools.partial(finish_kernel, sky_count, line, jobs, with_smooth),
+        out_shape=shapes,
         grid_spec=pltpu.PrefetchScalarGridSpec(
             num_scalar_prefetch=0,
             grid=(1,),
-            in_specs=[SCALARS] + [pl.BlockSpec(array.shape, lambda i: (0, 0)) for array in operands],
-            out_specs=pl.BlockSpec((pair, chunk_rows, TILE), lambda i: (0, 0, 0)),
-        ),
+            in_specs=specs,
+            out_specs=outs,
+            scratch_shapes=scratch,
+        ),
+        input_output_aliases=aliases,
         cost_estimate=pl.CostEstimate(
-            flops=pair * chunk_rows * TILE * 512, bytes_accessed=pair * chunk_rows * sky_count * TILE * 2, transcendentals=0
+            flops=count * chunk_rows * side, bytes_accessed=count * chunk_rows * side * 6, transcendentals=0
         ),
         compiler_params=pltpu.CompilerParams(vmem_limit_bytes=LATE_GRANT),
-        name="smooth",
+        name="finish",
     )(in_hbm(sky_columns), *operands)
 
 
@@ -470,8 +480,7 @@
         total([t[1] for t in both_terms] + [both_in]),
     ]
 
-    smoothed = [None] * CHUNKS
-    difference = None
+    gathered = []
     for c in range(CHUNKS):
         terms = reduce_line([product_own[c], product_in[c]])
         if c:
@@ -486,15 +495,17 @@
                 near[step] = exchange(near[held], bit + 1)
         for step in range(1, line):
             far[step] = exchange(near[step], 0)
-        pieces = [near[step] for step in range(line)] + [far[step] for step in range(line)]
-        if c < CHUNKS - 1:
-            smoothed[c] = smooth(pieces, across_band, sky_columns, pair, chunk_rows, sky_count)
-        else:
-            powers = power(
-                smoothed[:-1], pieces, across_band, down_band, sky_columns, pair, sky_count, band_count
-            )
-        difference = subtract([home[c], away[c]], pieces, sky_columns, c, difference, sky_count)
-
+        gathered.append([[group[step] for step in range(line)] for group in (near, far)])
+
+    (near_first, far_first), (near_last, far_last) = gathered
+    early = ((OWN, 0), (OTHER, 0), (OWN, 1))
+    difference, smoothed = finish(
+        early, [home[0], away[0], home[1]], near_first + far_first + near_last, across_band, sky_columns, None, sky_count
+    )
+    powers = power(
+        [smoothed], near_last + far_last, across_band, down_band, sky_columns, pair, sky_count, band_count
+    )
+    (difference,) = finish(((OTHER, 1),), [away[1]], far_last, across_band, sky_columns, difference, sky_count)
     detection = powers[0]
     for step in range(1, band_count):
         ring = [(i, (i + step) % band_count) for i in range(band_count)]

time: 124 us -> 123 us (level)
  starting transfers between devices: 35.3 us -> 41.1 us
  waiting for transfers between devices: 38.5 us -> 32.7 us
    ppermute x26, waiting for transfers between devices: 38.5 us -> 32.7 us  [exchange(): lax.ppermute(block, 'sky', [(i, i ^ 1 << bit) for i in range(sky_count)])]
    ppermute x26, starting transfers between devices: 32.4 us -> 38.1 us  [exchange(): lax.ppermute(block, 'sky', [(i, i ^ 1 << bit) for i in range(sky_count)])]
    pallas_call x3 -> x2, Pallas kernels: 6.51 us -> 5.52 us  [finish(): pl.pallas_call(functools.partial(finish_kernel, sky_count, line, jobs, wi...]
  transfers between devices with their start and end apart: 29 -> 29, of which waited for: 12 -> 12; matrix products, arithmetic and copies ran while one was open for 8% -> 8% of each run, Pallas kernels for 22% -> 21%
where the time goes in v6:
time: 123 us; the launch traced here: 122 us
  starting transfers between devices  41.1 us (33%)
  Pallas kernels  35.2 us (29%)
  waiting for transfers between devices  32.7 us (27%)
  other arithmetic  11.5 us (9%)
    ppermute x26, starting transfers between devices, exchange(): lax.ppermute(block, 'sky', [(i, i ^ 1 << bit) for i in range(sky_count)])  38.1 us
    ppermute x26, waiting for transfers between devices, exchange(): lax.ppermute(block, 'sky', [(i, i ^ 1 << bit) for i in range(sky_count)])  32.7 us
    pallas_call x4, Pallas kernels, match(): pl.pallas_call(functools.partial(match_kernel, sky_count, which, chunk *...  21.1 us
    convert_element_type x7, other arithmetic, reduce_line(): arrived = exchange(leaving.astype(BF16), bit)  6.15 us
    pallas_call x3, Pallas kernels, weigh(): pl.pallas_call(functools.partial(weight_kernel, sky_count, halves, chunk,...  5.97 us
    pallas_call x2, Pallas kernels, finish(): pl.pallas_call(functools.partial(finish_kernel, sky_count, line, jobs, wi...  5.52 us
    ppermute x3, starting transfers between devices, body(): detection = detection + lax.ppermute(powers[step], 'band', ring).astype(F32)  3.02 us
  transfers between devices with their start and end apart: 29, of which 12 were waited for; matrix products, arithmetic and copies ran while one was open for 8% of the time, Pallas kernels for 21%

profile of v6, /device:TPU:0, one launch (start us, length us, event | category | flops | bytes accessed | tf_op | source)
XLA Modules:
  0.0 122.2 jit_solution(12317146603343108158)
XLA Ops:
  0.6 0.7 convert_element_type.190
  1.3 0.7 convert_convert_fusion
  2.0 0.8 multiply_convert_fusion
  2.8 0.1 pad_convert_fusion
  2.8 0.1 select_maximum_fusion.base_ref
  2.9 1.1 prepare.1
  4.0 1.6 %weigh.5.weight_ref = bf16[1,256,1024]{2,1,0:T(8,128)(2,1)S(1)} custom-call(s32[8,4,8]{2,1,0:T(4,128)} %sky_ref.19, s32[2,35]{1,0:T(2,128)} %bitcast.42, bf16[1024,1024]{1,0:T(8,128)(2,1)} %bitcast.38), custom_call_target="tpu_custom_call" | custom-call | flops 2097152 | bytes 1048576 | tf_op jit(solution)/shard_map/weigh/pallas_call | solution.py:128
  5.6 5.3 %match.7 = (bf16[256,1024]{1,0:T(8,128)(2,1)}, bf16[256,1024]{1,0:T(8,128)(2,1)}) custom-call(s32[8,4,8]{2,1,0:T(4,128)} %sky_ref.19, bf16[1024,1024]{1,0:T(8,128)(2,1)} %bitcast.26, bf16[1024,1024]{1,0:T(8,128)(2,1)} %bitcast.27, bf16[1024,1024]{1,0:T(8,128)(2,1)} %bitcast.28, bf16[256,1152]{1,0:T(8,128)(2,1)S(1)} %get-tuple-element.21.column_ref, ...), custom_call_target="tpu_custom_call" | custom-call | flops 1962934272 | bytes 2097152 | tf_op jit(solution)/shard_map/match/pallas_call | solution.py:218
  10.9 3.0 %collective-permute-start.3 = (bf16[256,1024]{1,0:T(8,128)(2,1)}, bf16[256,1024]{1,0:T(8,128)(2,1)}, u32[]{:S(2)}, u32[]{:S(2)}) collective-permute-start(bf16[256,1024]{1,0:T(8,128)(2,1)} %get-tuple-element.27), channel_id=1, source_target_pairs={{0,4},{4,0},{8,12},{12,8},{16,20},{20,16},{24,28},{28,24},{1,5},{5... | collective-permute-start | bytes 1572872 | tf_op jit(solution)/shard_map/ppermute | solution.py:434
  14.0 2.8 %weigh.3.weight_ref = bf16[2,256,1024]{2,1,0:T(8,128)(2,1)S(1)} custom-call(s32[8,4,8]{2,1,0:T(4,128)} %sky_ref.19, s32[2,35]{1,0:T(2,128)} %bitcast.43, bf16[1024,1024]{1,0:T(8,128)(2,1)} %bitcast.39), custom_call_target="tpu_custom_call" | custom-call | flops 4194304 | bytes 2097152 | tf_op jit(solution)/shard_map/weigh/pallas_call | solution.py:128
  16.8 5.3 %match.4 = (bf16[256,1024]{1,0:T(8,128)(2,1)}, bf16[256,1024]{1,0:T(8,128)(2,1)}) custom-call(s32[8,4,8]{2,1,0:T(4,128)} %sky_ref.19, bf16[1024,1024]{1,0:T(8,128)(2,1)} %bitcast.29, bf16[1024,1024]{1,0:T(8,128)(2,1)} %bitcast.30, bf16[1024,1024]{1,0:T(8,128)(2,1)} %bitcast.31, bf16[256,1152]{1,0:T(8,128)(2,1)S(1)} %get-tuple-element.21.column_ref, ...), custom_call_target="tpu_custom_call" | custom-call | flops 1962934272 | bytes 2097152 | tf_op jit(solution)/shard_map/match/pallas_call | solution.py:218
  22.1 2.0 %collective-permute-start = (bf16[256,1024]{1,0:T(8,128)(2,1)}, bf16[256,1024]{1,0:T(8,128)(2,1)}, u32[]{:S(2)}, u32[]{:S(2)}) collective-permute-start(bf16[256,1024]{1,0:T(8,128)(2,1)} %get-tuple-element.25), channel_id=1, source_target_pairs={{0,4},{4,0},{8,12},{12,8},{16,20},{20,16},{24,28},{28,24},{1,5},{5... | collective-permute-start | bytes 1572872 | tf_op jit(solution)/shard_map/ppermute | solution.py:434
  24.1 0.8 constant_dynamic-slice_fusion
  24.9 1.6 %collective-permute-start.9 = (bf16[2,128,1024]{2,1,0:T(8,128)(2,1)}, bf16[2,128,1024]{2,1,0:T(8,128)(2,1)S(1)}, u32[]{:S(2)}, u32[]{:S(2)}) collective-permute-start(bf16[2,128,1024]{2,1,0:T(8,128)(2,1)} %constant_dynamic-slice_fusion), channel_id=1, source_target_pairs={{0,8},{4,12},{8,0},{12,4},{16,24},{20,28},{24,16},{28,20},{1,9},{5... | collective-permute-start | bytes 1572872 | tf_op jit(solution)/shard_map/ppermute | solution.py:434
  26.5 1.6 %weigh.4.weight_ref = bf16[1,256,1024]{2,1,0:T(8,128)(2,1)S(1)} custom-call(s32[8,4,8]{2,1,0:T(4,128)} %sky_ref.19, s32[2,35]{1,0:T(2,128)} %bitcast.44, bf16[1024,1024]{1,0:T(8,128)(2,1)} %bitcast.40), custom_call_target="tpu_custom_call" | custom-call | flops 2097152 | bytes 1048576 | tf_op jit(solution)/shard_map/weigh/pallas_call | solution.py:128
  28.1 5.2 %match.5 = (bf16[256,1024]{1,0:T(8,128)(2,1)}, bf16[256,1024]{1,0:T(8,128)(2,1)S(1)}) custom-call(s32[8,4,8]{2,1,0:T(4,128)} %sky_ref.19, bf16[1024,1024]{1,0:T(8,128)(2,1)} %bitcast.32, bf16[1024,1024]{1,0:T(8,128)(2,1)} %bitcast.33, bf16[1024,1024]{1,0:T(8,128)(2,1)} %bitcast.34, bf16[256,1152]{1,0:T(8,128)(2,1)S(1)} %get-tuple-element.21.column_ref, ...), custom_call_target="tpu_custom_call" | custom-call | flops 1962934272 | bytes 2097152 | tf_op jit(solution)/shard_map/match/pallas_call | solution.py:218
  33.3 5.2 %match.6 = (bf16[256,1024]{1,0:T(8,128)(2,1)}, bf16[256,1024]{1,0:T(8,128)(2,1)S(1)}) custom-call(s32[8,4,8]{2,1,0:T(4,128)} %sky_ref.19, bf16[1024,1024]{1,0:T(8,128)(2,1)} %bitcast.35, bf16[1024,1024]{1,0:T(8,128)(2,1)} %bitcast.36, bf16[1024,1024]{1,0:T(8,128)(2,1)} %bitcast.37, bf16[256,1152]{1,0:T(8,128)(2,1)S(1)} %get-tuple-element.21.column_ref, ...), custom_call_target="tpu_custom_call" | custom-call | flops 1962934272 | bytes 2097152 | tf_op jit(solution)/shard_map/match/pallas_call | solution.py:218
  38.5 1.0 add_convert_fusion.1
  39.6 0.5 collective-permute-start.4
  40.1 1.0 fusion
  41.1 1.7 %collective-permute-start.7 = (bf16[128,1024]{1,0:T(8,128)(2,1)S(1)}, bf16[128,1024]{1,0:T(8,128)(2,1)S(1)}, u32[]{:S(2)}, u32[]{:S(2)}) collective-permute-start(bf16[128,1024]{1,0:T(8,128)(2,1)S(1)} %fusion), channel_id=1, source_target_pairs={{0,8},{4,12},{8,0},{12,4},{16,24},{20,28},{24,16},{28,20},{1,9},{5... | collective-permute-start | bytes 786440 | tf_op jit(solution)/shard_map/ppermute | solution.py:434
  42.7 5.9 %collective-permute-done = bf16[256,1024]{1,0:T(8,128)(2,1)} collective-permute-done((bf16[256,1024]{1,0:T(8,128)(2,1)}, bf16[256,1024]{1,0:T(8,128)(2,1)}, u32[]{:S(2)}, u32[]{:S(2)}) %collective-permute-start) | collective-permute-done | bytes 524320 | tf_op jit(solution)/shard_map/ppermute | solution.py:434
  48.7 1.0 add_convert_fusion.2
  49.7 1.9 %collective-permute-start.1 = (bf16[128,1024]{1,0:T(8,128)(2,1)S(1)}, bf16[128,1024]{1,0:T(8,128)(2,1)S(1)}, u32[]{:S(2)}, u32[]{:S(2)}) collective-permute-start(bf16[128,1024]{1,0:T(8,128)(2,1)S(1)} %add_convert_fusion.2), channel_id=1, source_target_pairs={{0,8},{4,12},{8,0},{12,4},{16,24},{20,28},{24,16},{28,20},{1,9},{5... | collective-permute-start | bytes 786440 | tf_op jit(solution)/shard_map/ppermute | solution.py:434
  51.5 0.1 add_convert_fusion
  51.6 2.7 %collective-permute-start.10 = (bf16[2,64,1024]{2,1,0:T(8,128)(2,1)S(1)}, bf16[2,64,1024]{2,1,0:T(8,128)(2,1)S(1)}, u32[]{:S(2)}, u32[]{:S(2)}) collective-permute-start(bf16[2,64,1024]{2,1,0:T(8,128)(2,1)S(1)} %add_convert_fusion), channel_id=1, source_target_pairs={{0,16},{4,20},{8,24},{12,28},{16,0},{20,4},{24,8},{28,12},{1,17},{... | collective-permute-start | bytes 786440 | tf_op jit(solution)/shard_map/ppermute | solution.py:434
  54.3 1.0 add_convert_fusion.4
  55.3 0.4 collective-permute-start.5
  55.7 1.0 fusion.2
  56.7 2.7 %collective-permute-start.8 = (bf16[64,1024]{1,0:T(8,128)(2,1)S(1)}, bf16[64,1024]{1,0:T(8,128)(2,1)S(1)}, u32[]{:S(2)}, u32[]{:S(2)}) collective-permute-start(bf16[64,1024]{1,0:T(8,128)(2,1)S(1)} %fusion.2), channel_id=1, source_target_pairs={{0,16},{4,20},{8,24},{12,28},{16,0},{20,4},{24,8},{28,12},{1,17},{... | collective-permute-start | bytes 393224 | tf_op jit(solution)/shard_map/ppermute | solution.py:434
  59.4 4.4 %collective-permute-done.1 = bf16[128,1024]{1,0:T(8,128)(2,1)S(1)} collective-permute-done((bf16[128,1024]{1,0:T(8,128)(2,1)S(1)}, bf16[128,1024]{1,0:T(8,128)(2,1)S(1)}, u32[]{:S(2)}, u32[]{:S(2)}) %collective-permute-start.1) | collective-permute-done | bytes 262176 | tf_op jit(solution)/shard_map/ppermute | solution.py:434
  63.8 1.0 add_convert_fusion.5
  64.8 0.1 collective-permute-start.2
  64.8 11.0 %collective-permute-done.10 = bf16[2,64,1024]{2,1,0:T(8,128)(2,1)S(1)} collective-permute-done((bf16[2,64,1024]{2,1,0:T(8,128)(2,1)S(1)}, bf16[2,64,1024]{2,1,0:T(8,128)(2,1)S(1)}, u32[]{:S(2)}, u32[]{:S(2)}) %collective-permute-start.10) | collective-permute-done | bytes 262176 | tf_op jit(solution)/shard_map/ppermute | solution.py:434
  75.8 0.1 fusion.11
  75.9 1.6 %collective-permute-start.11 = (bf16[64,1024]{1,0:T(8,128)(2,1)S(1)}, bf16[64,1024]{1,0:T(8,128)(2,1)S(1)}, u32[]{:S(2)}, u32[]{:S(2)}) collective-permute-start(bf16[64,1024]{1,0:T(8,128)(2,1)S(1)} %fusion.11), channel_id=1, source_target_pairs={{0,4},{4,0},{8,12},{12,8},{16,20},{20,16},{24,28},{28,24},{1,5},{5... | collective-permute-start | bytes 393224 | tf_op jit(solution)/shard_map/ppermute | solution.py:434
  77.5 1.1 collective-permute-done.5
  78.6 2.0 %collective-permute-done.8 = bf16[64,1024]{1,0:T(8,128)(2,1)S(1)} collective-permute-done((bf16[64,1024]{1,0:T(8,128)(2,1)S(1)}, bf16[64,1024]{1,0:T(8,128)(2,1)S(1)}, u32[]{:S(2)}, u32[]{:S(2)}) %collective-permute-start.8) | collective-permute-done | bytes 131104 | tf_op jit(solution)/shard_map/ppermute | solution.py:434
  80.6 1.2 fusion.10.refs_4_
  81.9 1.7 %collective-permute-done.2 = bf16[64,1024]{1,0:T(8,128)(2,1)S(1)} collective-permute-done((bf16[64,1024]{1,0:T(8,128)(2,1)S(1)}, bf16[64,1024]{1,0:T(8,128)(2,1)S(1)}, u32[]{:S(2)}, u32[]{:S(2)}) %collective-permute-start.2) | collective-permute-done | bytes 131104 | tf_op jit(solution)/shard_map/ppermute | solution.py:434
  83.6 1.1 fusion.9.refs_12_.refs_1_
  84.7 1.3 %collective-permute-start.15 = (bf16[64,1024]{1,0:T(8,128)(2,1)S(1)}, bf16[64,1024]{1,0:T(8,128)(2,1)S(1)}, u32[]{:S(2)}, u32[]{:S(2)}) collective-permute-start(bf16[64,1024]{1,0:T(8,128)(2,1)S(1)} %fusion.9.refs_12_.refs_1_), channel_id=1, source_target_pairs={{0,16},{4,20},{8,24},{12,28},{16,0},{20,4},{24,8},{28,12},{1,17},{... | collective-permute-start | bytes 393224 | tf_op jit(solution)/shard_map/ppermute | solution.py:434
  86.0 5.9 %collective-permute-start.19 = (bf16[64,1024]{1,0:T(8,128)(2,1)S(1)}, bf16[64,1024]{1,0:T(8,128)(2,1)S(1)}, u32[]{:S(2)}, u32[]{:S(2)}) collective-permute-start(bf16[64,1024]{1,0:T(8,128)(2,1)S(1)} %fusion.10.refs_4_), channel_id=1, source_target_pairs={{0,8},{4,12},{8,0},{12,4},{16,24},{20,28},{24,16},{28,20},{1,9},{5... | collective-permute-start | bytes 393224 | tf_op jit(solution)/shard_map/ppermute | solution.py:434
  91.9 2.0 %collective-permute-start.21 = (bf16[64,1024]{1,0:T(8,128)(2,1)S(1)}, bf16[64,1024]{1,0:T(8,128)(2,1)S(1)}, u32[]{:S(2)}, u32[]{:S(2)}) collective-permute-start(bf16[64,1024]{1,0:T(8,128)(2,1)S(1)} %collective-permute-done.20.refs_6_), channel_id=1, source_target_pairs={{0,8},{4,12},{8,0},{12,4},{16,24},{20,28},{24,16},{28,20},{1,9},{5... | collective-permute-start | bytes 393224 | tf_op jit(solution)/shard_map/ppermute | solution.py:434
  93.9 1.5 %collective-permute-start.22 = (bf16[64,1024]{1,0:T(8,128)(2,1)S(1)}, bf16[64,1024]{1,0:T(8,128)(2,1)S(1)}, u32[]{:S(2)}, u32[]{:S(2)}) collective-permute-start(bf16[64,1024]{1,0:T(8,128)(2,1)S(1)} %fusion.10.refs_4_), channel_id=1, source_target_pairs={{0,4},{4,0},{8,12},{12,8},{16,20},{20,16},{24,28},{28,24},{1,5},{5... | collective-permute-start | bytes 393224 | tf_op jit(solution)/shard_map/ppermute | solution.py:434
  95.5 0.6 collective-permute-done.19.refs_5_
  96.1 1.5 %collective-permute-start.23 = (bf16[64,1024]{1,0:T(8,128)(2,1)S(1)}, bf16[64,1024]{1,0:T(8,128)(2,1)S(1)}, u32[]{:S(2)}, u32[]{:S(2)}) collective-permute-start(bf16[64,1024]{1,0:T(8,128)(2,1)S(1)} %collective-permute-done.19.refs_5_), channel_id=1, source_target_pairs={{0,4},{4,0},{8,12},{12,8},{16,20},{20,16},{24,28},{28,24},{1,5},{5... | collective-permute-start | bytes 393224 | tf_op jit(solution)/shard_map/ppermute | solution.py:434
  97.6 1.4 %collective-permute-start.24 = (bf16[64,1024]{1,0:T(8,128)(2,1)S(1)}, bf16[64,1024]{1,0:T(8,128)(2,1)S(1)}, u32[]{:S(2)}, u32[]{:S(2)}) collective-permute-start(bf16[64,1024]{1,0:T(8,128)(2,1)S(1)} %collective-permute-done.20.refs_6_), channel_id=1, source_target_pairs={{0,4},{4,0},{8,12},{12,8},{16,20},{20,16},{24,28},{28,24},{1,5},{5... | collective-permute-start | bytes 393224 | tf_op jit(solution)/shard_map/ppermute | solution.py:434
  99.0 1.4 %collective-permute-start.25 = (bf16[64,1024]{1,0:T(8,128)(2,1)S(1)}, bf16[64,1024]{1,0:T(8,128)(2,1)S(1)}, u32[]{:S(2)}, u32[]{:S(2)}) collective-permute-start(bf16[64,1024]{1,0:T(8,128)(2,1)S(1)} %collective-permute-done.21.refs_7_), channel_id=1, source_target_pairs={{0,4},{4,0},{8,12},{12,8},{16,20},{20,16},{24,28},{28,24},{1,5},{5... | collective-permute-start | bytes 393224 | tf_op jit(solution)/shard_map/ppermute | solution.py:434
  100.4 1.4 %collective-permute-start.12 = (bf16[64,1024]{1,0:T(8,128)(2,1)S(1)}, bf16[64,1024]{1,0:T(8,128)(2,1)S(1)}, u32[]{:S(2)}, u32[]{:S(2)}) collective-permute-start(bf16[64,1024]{1,0:T(8,128)(2,1)S(1)} %fusion.9.refs_12_.refs_1_), channel_id=1, source_target_pairs={{0,4},{4,0},{8,12},{12,8},{16,20},{20,16},{24,28},{28,24},{1,5},{5... | collective-permute-start | bytes 393224 | tf_op jit(solution)/shard_map/ppermute | solution.py:434
  101.8 0.6 collective-permute-start.16
  102.4 0.7 collective-permute-done.23.refs_9_
  103.1 1.5 %collective-permute-start.14 = (bf16[64,1024]{1,0:T(8,128)(2,1)S(1)}, bf16[64,1024]{1,0:T(8,128)(2,1)S(1)}, u32[]{:S(2)}, u32[]{:S(2)}) collective-permute-start(bf16[64,1024]{1,0:T(8,128)(2,1)S(1)} %collective-permute-done.13.refs_13_.refs_2_), channel_id=1, source_target_pairs={{0,4},{4,0},{8,12},{12,8},{16,20},{20,16},{24,28},{28,24},{1,5},{5... | collective-permute-start | bytes 393224 | tf_op jit(solution)/shard_map/ppermute | solution.py:434
  104.6 1.3 %collective-permute-done.24.refs_10_ = bf16[64,1024]{1,0:T(8,128)(2,1)S(1)} collective-permute-done((bf16[64,1024]{1,0:T(8,128)(2,1)S(1)}, bf16[64,1024]{1,0:T(8,128)(2,1)S(1)}, u32[]{:S(2)}, u32[]{:S(2)}) %collective-permute-start.24) | collective-permute-done | bytes 131104 | tf_op jit(solution)/shard_map/ppermute | solution.py:434
  105.9 1.5 %collective-permute-start.18 = (bf16[64,1024]{1,0:T(8,128)(2,1)S(1)}, bf16[64,1024]{1,0:T(8,128)(2,1)S(1)}, u32[]{:S(2)}, u32[]{:S(2)}) collective-permute-start(bf16[64,1024]{1,0:T(8,128)(2,1)S(1)} %collective-permute-done.17.refs_15_.refs_4_), channel_id=1, source_target_pairs={{0,4},{4,0},{8,12},{12,8},{16,20},{20,16},{24,28},{28,24},{1,5},{5... | collective-permute-start | bytes 393224 | tf_op jit(solution)/shard_map/ppermute | solution.py:434
  107.4 1.3 %collective-permute-done.25.refs_11_ = bf16[64,1024]{1,0:T(8,128)(2,1)S(1)} collective-permute-done((bf16[64,1024]{1,0:T(8,128)(2,1)S(1)}, bf16[64,1024]{1,0:T(8,128)(2,1)S(1)}, u32[]{:S(2)}, u32[]{:S(2)}) %collective-permute-start.25) | collective-permute-done | bytes 131104 | tf_op jit(solution)/shard_map/ppermute | solution.py:434
  108.7 3.5 %finish.2 = (bf16[2,2,256,1024]{3,2,1,0:T(8,128)(2,1)}, bf16[2,256,128]{2,1,0:T(8,128)(2,1)S(1)}) custom-call(s32[8,4,8]{2,1,0:T(4,128)} %sky_ref.19, bf16[256,128]{1,0:T(8,128)(2,1)S(1)} %get-tuple-element.29.refs_0_.across_ref, bf16[256,1024]{1,0:T(8,128)(2,1)} %get-tuple-element.30.refs_1_, bf16[256,1024]{1,0:T(8,128)(2,1)} %get-tuple-element.31.refs_2_, ...), custom_call_target="tpu_custom_call" | custom-call | flops 786432 | bytes 4718592 | tf_op jit(solution)/shard_map/finish/pallas_call | solution.py:351
  112.2 1.2 %collective-permute-done.14.refs_2_.refs_6_ = bf16[64,1024]{1,0:T(8,128)(2,1)S(1)} collective-permute-done((bf16[64,1024]{1,0:T(8,128)(2,1)S(1)}, bf16[64,1024]{1,0:T(8,128)(2,1)S(1)}, u32[]{:S(2)}, u32[]{:S(2)}) %collective-permute-start.14) | collective-permute-done | bytes 131104 | tf_op jit(solution)/shard_map/ppermute | solution.py:434
  113.5 1.4 %collective-permute-done.18.refs_4_.refs_8_ = bf16[64,1024]{1,0:T(8,128)(2,1)S(1)} collective-permute-done((bf16[64,1024]{1,0:T(8,128)(2,1)S(1)}, bf16[64,1024]{1,0:T(8,128)(2,1)S(1)}, u32[]{:S(2)}, u32[]{:S(2)}) %collective-permute-start.18) | collective-permute-done | bytes 131104 | tf_op jit(solution)/shard_map/ppermute | solution.py:434
  114.9 1.5 %power.1 = (f32[256,128]{1,0:T(8,128)S(1)}, bf16[256,128]{1,0:T(8,128)(2,1)S(1)}, bf16[256,128]{1,0:T(8,128)(2,1)S(1)}, bf16[256,128]{1,0:T(8,128)(2,1)S(1)}) custom-call(s32[8,4,8]{2,1,0:T(4,128)} %sky_ref.19, bf16[256,128]{1,0:T(8,128)(2,1)S(1)} %get-tuple-element.29.refs_0_.across_ref, bf16[128,160]{1,0:T(8,128)(2,1)S(1)} %get-tuple-element.34.down_ref, ...), custom_call_target="tpu_custom_call" | custom-call | flops 78643200 | bytes 1572864 | tf_op jit(solution)/shard_map/power/pallas_call | solution.py:403
  116.5 1.6 %collective-permute-start.27 = (bf16[256,128]{1,0:T(8,128)(2,1)S(1)}, bf16[256,128]{1,0:T(8,128)(2,1)S(1)}, u32[]{:S(2)}, u32[]{:S(2)}) collective-permute-start(bf16[256,128]{1,0:T(8,128)(2,1)S(1)} %get-tuple-element.38), channel_id=1, source_target_pairs={{0,2},{1,3},{2,0},{3,1},{4,6},{5,7},{6,4},{7,5},{8,10},{9,11},{10,... | collective-permute-start | bytes 196616 | tf_op jit(solution)/shard_map/ppermute | solution.py:512
  118.1 1.4 %collective-permute-start.28 = (bf16[256,128]{1,0:T(8,128)(2,1)S(1)}, bf16[256,128]{1,0:T(8,128)(2,1)S(1)}, u32[]{:S(2)}, u32[]{:S(2)}) collective-permute-start(bf16[256,128]{1,0:T(8,128)(2,1)S(1)} %get-tuple-element.39), channel_id=1, source_target_pairs={{0,3},{1,0},{2,1},{3,2},{4,7},{5,4},{6,5},{7,6},{8,11},{9,8},{10,9... | collective-permute-start | bytes 196616 | tf_op jit(solution)/shard_map/ppermute | solution.py:512
  119.4 2.0 %finish.3 = bf16[2,2,256,1024]{3,2,1,0:T(8,128)(2,1)} custom-call(s32[8,4,8]{2,1,0:T(4,128)} %sky_ref.19, bf16[256,1024]{1,0:T(8,128)(2,1)} %get-tuple-element.23.refs_0_, bf16[64,1024]{1,0:T(8,128)(2,1)S(1)} %collective-permute-done.12.refs_1_.refs_5_, bf16[64,1024]{1,0:T(8,128)(2,1)S(1)} %collective-permute-done.14.refs_2_.refs_6_, ...), custom_call_target="tpu_custom_call", output_to_operand_aliasing={{}: (6, {})} | custom-call | flops 262144 | bytes 1572864 | tf_op jit(solution)/shard_map/finish/pallas_call | solution.py:351
  121.5 0.7 convert_add_fusion.3
  (22 shorter events, 0.3 us)
Async XLA Ops:
  10.9 27.6 %collective-permute-start.3 = (bf16[256,1024]{1,0:T(8,128)(2,1)}, bf16[256,1024]{1,0:T(8,128)(2,1)}, u32[]{:S(2)}, u32[]{:S(2)}) collective-permute-start(bf16[256,1024]{1,0:T(8,128)(2,1)} %get-tuple-element.27), channel_id=1, source_target_pairs={{0,4},{4,0},{8,12},{12,8},{16,20},{20,16},{24,28},{28,24},{1,5},{5... | collective-permute-start | bytes 1572872 | tf_op jit(solution)/shard_map/ppermute | solution.py:434
  13.9 26.1 %collective-permute-start.6 = (bf16[256,1024]{1,0:T(8,128)(2,1)S(1)}, bf16[256,1024]{1,0:T(8,128)(2,1)}, u32[]{:S(2)}, u32[]{:S(2)}) collective-permute-start(bf16[256,1024]{1,0:T(8,128)(2,1)S(1)} %bitcast.25), channel_id=1, source_target_pairs={{0,4},{4,0},{8,12},{12,8},{16,20},{20,16},{24,28},{28,24},{1,5},{5... | collective-permute-start | bytes 1572872 | tf_op jit(solution)/shard_map/ppermute | solution.py:434
  22.1 26.5 %collective-permute-start = (bf16[256,1024]{1,0:T(8,128)(2,1)}, bf16[256,1024]{1,0:T(8,128)(2,1)}, u32[]{:S(2)}, u32[]{:S(2)}) collective-permute-start(bf16[256,1024]{1,0:T(8,128)(2,1)} %get-tuple-element.25), channel_id=1, source_target_pairs={{0,4},{4,0},{8,12},{12,8},{16,20},{20,16},{24,28},{28,24},{1,5},{5... | collective-permute-start | bytes 1572872 | tf_op jit(solution)/shard_map/ppermute | solution.py:434
  24.9 26.6 %collective-permute-start.9 = (bf16[2,128,1024]{2,1,0:T(8,128)(2,1)}, bf16[2,128,1024]{2,1,0:T(8,128)(2,1)S(1)}, u32[]{:S(2)}, u32[]{:S(2)}) collective-permute-start(bf16[2,128,1024]{2,1,0:T(8,128)(2,1)} %constant_dynamic-slice_fusion), channel_id=1, source_target_pairs={{0,8},{4,12},{8,0},{12,4},{16,24},{20,28},{24,16},{28,20},{1,9},{5... | collective-permute-start | bytes 1572872 | tf_op jit(solution)/shard_map/ppermute | solution.py:434
  39.6 14.7 %collective-permute-start.4 = (bf16[128,1024]{1,0:T(8,128)(2,1)S(1)}, bf16[128,1024]{1,0:T(8,128)(2,1)S(1)}, u32[]{:S(2)}, u32[]{:S(2)}) collective-permute-start(bf16[128,1024]{1,0:T(8,128)(2,1)S(1)} %add_convert_fusion.1), channel_id=1, source_target_pairs={{0,8},{4,12},{8,0},{12,4},{16,24},{20,28},{24,16},{28,20},{1,9},{5... | collective-permute-start | bytes 786440 | tf_op jit(solution)/shard_map/ppermute | solution.py:434
  41.1 14.6 %collective-permute-start.7 = (bf16[128,1024]{1,0:T(8,128)(2,1)S(1)}, bf16[128,1024]{1,0:T(8,128)(2,1)S(1)}, u32[]{:S(2)}, u32[]{:S(2)}) collective-permute-start(bf16[128,1024]{1,0:T(8,128)(2,1)S(1)} %fusion), channel_id=1, source_target_pairs={{0,8},{4,12},{8,0},{12,4},{16,24},{20,28},{24,16},{28,20},{1,9},{5... | collective-permute-start | bytes 786440 | tf_op jit(solution)/shard_map/ppermute | solution.py:434
  49.7 14.1 %collective-permute-start.1 = (bf16[128,1024]{1,0:T(8,128)(2,1)S(1)}, bf16[128,1024]{1,0:T(8,128)(2,1)S(1)}, u32[]{:S(2)}, u32[]{:S(2)}) collective-permute-start(bf16[128,1024]{1,0:T(8,128)(2,1)S(1)} %add_convert_fusion.2), channel_id=1, source_target_pairs={{0,8},{4,12},{8,0},{12,4},{16,24},{20,28},{24,16},{28,20},{1,9},{5... | collective-permute-start | bytes 786440 | tf_op jit(solution)/shard_map/ppermute | solution.py:434
  51.6 24.2 %collective-permute-start.10 = (bf16[2,64,1024]{2,1,0:T(8,128)(2,1)S(1)}, bf16[2,64,1024]{2,1,0:T(8,128)(2,1)S(1)}, u32[]{:S(2)}, u32[]{:S(2)}) collective-permute-start(bf16[2,64,1024]{2,1,0:T(8,128)(2,1)S(1)} %add_convert_fusion), channel_id=1, source_target_pairs={{0,16},{4,20},{8,24},{12,28},{16,0},{20,4},{24,8},{28,12},{1,17},{... | collective-permute-start | bytes 786440 | tf_op jit(solution)/shard_map/ppermute | solution.py:434
  55.3 23.3 %collective-permute-start.5 = (bf16[64,1024]{1,0:T(8,128)(2,1)S(1)}, bf16[64,1024]{1,0:T(8,128)(2,1)S(1)}, u32[]{:S(2)}, u32[]{:S(2)}) collective-permute-start(bf16[64,1024]{1,0:T(8,128)(2,1)S(1)} %add_convert_fusion.4), channel_id=1, source_target_pairs={{0,16},{4,20},{8,24},{12,28},{16,0},{20,4},{24,8},{28,12},{1,17},{... | collective-permute-start | bytes 393224 | tf_op jit(solution)/shard_map/ppermute | solution.py:434
  56.7 23.9 %collective-permute-start.8 = (bf16[64,1024]{1,0:T(8,128)(2,1)S(1)}, bf16[64,1024]{1,0:T(8,128)(2,1)S(1)}, u32[]{:S(2)}, u32[]{:S(2)}) collective-permute-start(bf16[64,1024]{1,0:T(8,128)(2,1)S(1)} %fusion.2), channel_id=1, source_target_pairs={{0,16},{4,20},{8,24},{12,28},{16,0},{20,4},{24,8},{28,12},{1,17},{... | collective-permute-start | bytes 393224 | tf_op jit(solution)/shard_map/ppermute | solution.py:434
  64.8 18.8 %collective-permute-start.2 = (bf16[64,1024]{1,0:T(8,128)(2,1)S(1)}, bf16[64,1024]{1,0:T(8,128)(2,1)S(1)}, u32[]{:S(2)}, u32[]{:S(2)}) collective-permute-start(bf16[64,1024]{1,0:T(8,128)(2,1)S(1)} %add_convert_fusion.5), channel_id=1, source_target_pairs={{0,16},{4,20},{8,24},{12,28},{16,0},{20,4},{24,8},{28,12},{1,17},{... | collective-permute-start | bytes 393224 | tf_op jit(solution)/shard_map/ppermute | solution.py:434
  75.9 7.7 %collective-permute-start.11 = (bf16[64,1024]{1,0:T(8,128)(2,1)S(1)}, bf16[64,1024]{1,0:T(8,128)(2,1)S(1)}, u32[]{:S(2)}, u32[]{:S(2)}) collective-permute-start(bf16[64,1024]{1,0:T(8,128)(2,1)S(1)} %fusion.11), channel_id=1, source_target_pairs={{0,4},{4,0},{8,12},{12,8},{16,20},{20,16},{24,28},{28,24},{1,5},{5... | collective-permute-start | bytes 393224 | tf_op jit(solution)/shard_map/ppermute | solution.py:434
  81.8 10.1 %collective-permute-start.20 = (bf16[64,1024]{1,0:T(8,128)(2,1)S(1)}, bf16[64,1024]{1,0:T(8,128)(2,1)S(1)}, u32[]{:S(2)}, u32[]{:S(2)}) collective-permute-start(bf16[64,1024]{1,0:T(8,128)(2,1)S(1)} %fusion.10.refs_4_), channel_id=1, source_target_pairs={{0,16},{4,20},{8,24},{12,28},{16,0},{20,4},{24,8},{28,12},{1,17},{... | collective-permute-start | bytes 393224 | tf_op jit(solution)/shard_map/ppermute | solution.py:434
  84.7 10.7 %collective-permute-start.15 = (bf16[64,1024]{1,0:T(8,128)(2,1)S(1)}, bf16[64,1024]{1,0:T(8,128)(2,1)S(1)}, u32[]{:S(2)}, u32[]{:S(2)}) collective-permute-start(bf16[64,1024]{1,0:T(8,128)(2,1)S(1)} %fusion.9.refs_12_.refs_1_), channel_id=1, source_target_pairs={{0,16},{4,20},{8,24},{12,28},{16,0},{20,4},{24,8},{28,12},{1,17},{... | collective-permute-start | bytes 393224 | tf_op jit(solution)/shard_map/ppermute | solution.py:434
  86.0 10.0 %collective-permute-start.19 = (bf16[64,1024]{1,0:T(8,128)(2,1)S(1)}, bf16[64,1024]{1,0:T(8,128)(2,1)S(1)}, u32[]{:S(2)}, u32[]{:S(2)}) collective-permute-start(bf16[64,1024]{1,0:T(8,128)(2,1)S(1)} %fusion.10.refs_4_), channel_id=1, source_target_pairs={{0,8},{4,12},{8,0},{12,4},{16,24},{20,28},{24,16},{28,20},{1,9},{5... | collective-permute-start | bytes 393224 | tf_op jit(solution)/shard_map/ppermute | solution.py:434
  91.9 5.7 %collective-permute-start.13 = (bf16[64,1024]{1,0:T(8,128)(2,1)S(1)}, bf16[64,1024]{1,0:T(8,128)(2,1)S(1)}, u32[]{:S(2)}, u32[]{:S(2)}) collective-permute-start(bf16[64,1024]{1,0:T(8,128)(2,1)S(1)} %fusion.9.refs_12_.refs_1_), channel_id=1, source_target_pairs={{0,8},{4,12},{8,0},{12,4},{16,24},{20,28},{24,16},{28,20},{1,9},{5... | collective-permute-start | bytes 393224 | tf_op jit(solution)/shard_map/ppermute | solution.py:434
  91.9 7.1 %collective-permute-start.21 = (bf16[64,1024]{1,0:T(8,128)(2,1)S(1)}, bf16[64,1024]{1,0:T(8,128)(2,1)S(1)}, u32[]{:S(2)}, u32[]{:S(2)}) collective-permute-start(bf16[64,1024]{1,0:T(8,128)(2,1)S(1)} %collective-permute-done.20.refs_6_), channel_id=1, source_target_pairs={{0,8},{4,12},{8,0},{12,4},{16,24},{20,28},{24,16},{28,20},{1,9},{5... | collective-permute-start | bytes 393224 | tf_op jit(solution)/shard_map/ppermute | solution.py:434
  93.9 6.5 %collective-permute-start.22 = (bf16[64,1024]{1,0:T(8,128)(2,1)S(1)}, bf16[64,1024]{1,0:T(8,128)(2,1)S(1)}, u32[]{:S(2)}, u32[]{:S(2)}) collective-permute-start(bf16[64,1024]{1,0:T(8,128)(2,1)S(1)} %fusion.10.refs_4_), channel_id=1, source_target_pairs={{0,4},{4,0},{8,12},{12,8},{16,20},{20,16},{24,28},{28,24},{1,5},{5... | collective-permute-start | bytes 393224 | tf_op jit(solution)/shard_map/ppermute | solution.py:434
  95.4 6.4 %collective-permute-start.17 = (bf16[64,1024]{1,0:T(8,128)(2,1)S(1)}, bf16[64,1024]{1,0:T(8,128)(2,1)S(1)}, u32[]{:S(2)}, u32[]{:S(2)}) collective-permute-start(bf16[64,1024]{1,0:T(8,128)(2,1)S(1)} %collective-permute-done.15.refs_14_.refs_3_), channel_id=1, source_target_pairs={{0,8},{4,12},{8,0},{12,4},{16,24},{20,28},{24,16},{28,20},{1,9},{5... | collective-permute-start | bytes 393224 | tf_op jit(solution)/shard_map/ppermute | solution.py:434
  96.1 7.0 %collective-permute-start.23 = (bf16[64,1024]{1,0:T(8,128)(2,1)S(1)}, bf16[64,1024]{1,0:T(8,128)(2,1)S(1)}, u32[]{:S(2)}, u32[]{:S(2)}) collective-permute-start(bf16[64,1024]{1,0:T(8,128)(2,1)S(1)} %collective-permute-done.19.refs_5_), channel_id=1, source_target_pairs={{0,4},{4,0},{8,12},{12,8},{16,20},{20,16},{24,28},{28,24},{1,5},{5... | collective-permute-start | bytes 393224 | tf_op jit(solution)/shard_map/ppermute | solution.py:434
  97.6 8.3 %collective-permute-start.24 = (bf16[64,1024]{1,0:T(8,128)(2,1)S(1)}, bf16[64,1024]{1,0:T(8,128)(2,1)S(1)}, u32[]{:S(2)}, u32[]{:S(2)}) collective-permute-start(bf16[64,1024]{1,0:T(8,128)(2,1)S(1)} %collective-permute-done.20.refs_6_), channel_id=1, source_target_pairs={{0,4},{4,0},{8,12},{12,8},{16,20},{20,16},{24,28},{28,24},{1,5},{5... | collective-permute-start | bytes 393224 | tf_op jit(solution)/shard_map/ppermute | solution.py:434
  99.0 9.7 %collective-permute-start.25 = (bf16[64,1024]{1,0:T(8,128)(2,1)S(1)}, bf16[64,1024]{1,0:T(8,128)(2,1)S(1)}, u32[]{:S(2)}, u32[]{:S(2)}) collective-permute-start(bf16[64,1024]{1,0:T(8,128)(2,1)S(1)} %collective-permute-done.21.refs_7_), channel_id=1, source_target_pairs={{0,4},{4,0},{8,12},{12,8},{16,20},{20,16},{24,28},{28,24},{1,5},{5... | collective-permute-start | bytes 393224 | tf_op jit(solution)/shard_map/ppermute | solution.py:434
  100.4 11.8 %collective-permute-start.12 = (bf16[64,1024]{1,0:T(8,128)(2,1)S(1)}, bf16[64,1024]{1,0:T(8,128)(2,1)S(1)}, u32[]{:S(2)}, u32[]{:S(2)}) collective-permute-start(bf16[64,1024]{1,0:T(8,128)(2,1)S(1)} %fusion.9.refs_12_.refs_1_), channel_id=1, source_target_pairs={{0,4},{4,0},{8,12},{12,8},{16,20},{20,16},{24,28},{28,24},{1,5},{5... | collective-permute-start | bytes 393224 | tf_op jit(solution)/shard_map/ppermute | solution.py:434
  101.8 11.7 %collective-permute-start.16 = (bf16[64,1024]{1,0:T(8,128)(2,1)S(1)}, bf16[64,1024]{1,0:T(8,128)(2,1)S(1)}, u32[]{:S(2)}, u32[]{:S(2)}) collective-permute-start(bf16[64,1024]{1,0:T(8,128)(2,1)S(1)} %collective-permute-done.15.refs_14_.refs_3_), channel_id=1, source_target_pairs={{0,4},{4,0},{8,12},{12,8},{16,20},{20,16},{24,28},{28,24},{1,5},{5... | collective-permute-start | bytes 393224 | tf_op jit(solution)/shard_map/ppermute | solution.py:434
  103.1 10.3 %collective-permute-start.14 = (bf16[64,1024]{1,0:T(8,128)(2,1)S(1)}, bf16[64,1024]{1,0:T(8,128)(2,1)S(1)}, u32[]{:S(2)}, u32[]{:S(2)}) collective-permute-start(bf16[64,1024]{1,0:T(8,128)(2,1)S(1)} %collective-permute-done.13.refs_13_.refs_2_), channel_id=1, source_target_pairs={{0,4},{4,0},{8,12},{12,8},{16,20},{20,16},{24,28},{28,24},{1,5},{5... | collective-permute-start | bytes 393224 | tf_op jit(solution)/shard_map/ppermute | solution.py:434
  105.9 8.9 %collective-permute-start.18 = (bf16[64,1024]{1,0:T(8,128)(2,1)S(1)}, bf16[64,1024]{1,0:T(8,128)(2,1)S(1)}, u32[]{:S(2)}, u32[]{:S(2)}) collective-permute-start(bf16[64,1024]{1,0:T(8,128)(2,1)S(1)} %collective-permute-done.17.refs_15_.refs_4_), channel_id=1, source_target_pairs={{0,4},{4,0},{8,12},{12,8},{16,20},{20,16},{24,28},{28,24},{1,5},{5... | collective-permute-start | bytes 393224 | tf_op jit(solution)/shard_map/ppermute | solution.py:434
  116.4 5.1 %collective-permute-start.26 = (bf16[256,128]{1,0:T(8,128)(2,1)S(1)}, bf16[256,128]{1,0:T(8,128)(2,1)S(1)}, u32[]{:S(2)}, u32[]{:S(2)}) collective-permute-start(bf16[256,128]{1,0:T(8,128)(2,1)S(1)} %get-tuple-element.37), channel_id=1, source_target_pairs={{0,1},{1,2},{2,3},{3,0},{4,5},{5,6},{6,7},{7,4},{8,9},{9,10},{10,1... | collective-permute-start | bytes 196616 | tf_op jit(solution)/shard_map/ppermute | solution.py:512
  116.5 5.0 %collective-permute-start.27 = (bf16[256,128]{1,0:T(8,128)(2,1)S(1)}, bf16[256,128]{1,0:T(8,128)(2,1)S(1)}, u32[]{:S(2)}, u32[]{:S(2)}) collective-permute-start(bf16[256,128]{1,0:T(8,128)(2,1)S(1)} %get-tuple-element.38), channel_id=1, source_target_pairs={{0,2},{1,3},{2,0},{3,1},{4,6},{5,7},{6,4},{7,5},{8,10},{9,11},{10,... | collective-permute-start | bytes 196616 | tf_op jit(solution)/shard_map/ppermute | solution.py:512
  118.1 3.5 %collective-permute-start.28 = (bf16[256,128]{1,0:T(8,128)(2,1)S(1)}, bf16[256,128]{1,0:T(8,128)(2,1)S(1)}, u32[]{:S(2)}, u32[]{:S(2)}) collective-permute-start(bf16[256,128]{1,0:T(8,128)(2,1)S(1)} %get-tuple-element.39), channel_id=1, source_target_pairs={{0,3},{1,0},{2,1},{3,2},{4,7},{5,4},{6,5},{7,6},{8,11},{9,8},{10,9... | collective-permute-start | bytes 196616 | tf_op jit(solution)/shard_map/ppermute | solution.py:512

commit v7 on v6

--- a/solution.py
+++ b/solution.py
@@ -367,7 +367,7 @@
     )(in_hbm(sky_columns), *operands)
 
 
-def power_kernel(sky_count, line, band_count, sky_ref, across_ref, down_ref, *refs):
+def power_kernel(sky_count, line, band_count, across_ref, down_ref, *refs):
     sources = refs[: CHUNKS - 1]
     pieces = refs[CHUNKS - 1 : -band_count - 1]
     powers, smoothed = refs[-band_count - 1 : -1], refs[-1]
@@ -396,7 +396,7 @@
             powers[step][inner * TILE : (inner + 1) * TILE, :] = (filtered * filtered).astype(powers[step].dtype)
 
 
-def power(sources, pieces, across_band, down_band, sky_columns, pair, sky_count, band_count):
+def power(sources, pieces, across_band, down_band, pair, sky_count, band_count):
     line = len(pieces) // pair
     side = CHUNKS * pair * line * pieces[0].shape[0]
     operands = [across_band, down_band, *sources, *pieces]
@@ -408,15 +408,14 @@
         grid_spec=pltpu.PrefetchScalarGridSpec(
             num_scalar_prefetch=0,
             grid=(1,),
-            in_specs=[SCALARS]
-            + [pl.BlockSpec(array.shape, lambda i, n=array.ndim: (0,) * n) for array in operands],
+            in_specs=[pl.BlockSpec(array.shape, lambda i, n=array.ndim: (0,) * n) for array in operands],
             out_specs=[pl.BlockSpec((side // band_count, TILE), lambda i: (0, 0))] * band_count,
             scratch_shapes=[pltpu.VMEM((side + 2 * EDGE, TILE), BF16)],
         ),
         cost_estimate=pl.CostEstimate(flops=side * TILE * 600, bytes_accessed=side * TILE * 12, transcendentals=0),
         compiler_params=pltpu.CompilerParams(vmem_limit_bytes=LATE_GRANT),
         name="power",
-    )(in_hbm(sky_columns), *operands)
+    )(*operands)
 
 
 def body(exposures, inv_variance, mask_planes, sky_columns, basis_rows, basis_cols, match_coeffs, detect_taps):
@@ -503,7 +502,7 @@
         early, [home[0], away[0], home[1]], near_first + far_first + near_last, across_band, sky_columns, None, sky_count
     )
     powers = power(
-        [smoothed], near_last + far_last, across_band, down_band, sky_columns, pair, sky_count, band_count
+        [smoothed], near_last + far_last, across_band, down_band, pair, sky_count, band_count
     )
     (difference,) = finish(((OTHER, 1),), [away[1]], far_last, across_band, sky_columns, difference, sky_count)
     detection = powers[0]

time: 123 us -> 122 us (level)
  no operation moved by 1% of the time
where the time goes in v7:
time: 122 us; the launch traced here: 121 us
  starting transfers between devices  41.1 us (34%)
  Pallas kernels  34.2 us (28%)
  waiting for transfers between devices  32.7 us (27%)
  other arithmetic  11.5 us (9%)
    ppermute x26, starting transfers between devices, exchange(): lax.ppermute(block, 'sky', [(i, i ^ 1 << bit) for i in range(sky_count)])  38.1 us
    ppermute x26, waiting for transfers between devices, exchange(): lax.ppermute(block, 'sky', [(i, i ^ 1 << bit) for i in range(sky_count)])  32.7 us
    pallas_call x4, Pallas kernels, match(): pl.pallas_call(functools.partial(match_kernel, sky_count, which, chunk *...  21.1 us
    convert_element_type x7, other arithmetic, reduce_line(): arrived = exchange(leaving.astype(BF16), bit)  6.15 us
    pallas_call x3, Pallas kernels, weigh(): pl.pallas_call(functools.partial(weight_kernel, sky_count, halves, chunk,...  5.97 us
    pallas_call x2, Pallas kernels, finish(): pl.pallas_call(functools.partial(finish_kernel, sky_count, line, jobs, wi...  5.52 us
    ppermute x3, starting transfers between devices, body(): detection = detection + lax.ppermute(powers[step], 'band', ring).astype(F32)  3.02 us
  transfers between devices with their start and end apart: 29, of which 12 were waited for; matrix products, arithmetic and copies ran while one was open for 8% of the time, Pallas kernels for 21%

profile of v7, /device:TPU:0, one launch (start us, length us, event | category | flops | bytes accessed | tf_op | source)
XLA Modules:
  0.0 121.3 jit_solution(7026170391881965929)
XLA Ops:
  0.6 0.7 convert_element_type.190
  1.3 0.7 convert_convert_fusion
  2.0 0.8 multiply_convert_fusion
  2.8 0.1 pad_convert_fusion
  2.8 0.1 select_maximum_fusion.base_ref
  2.9 1.1 prepare.1
  4.0 1.6 %weigh.5.weight_ref = bf16[1,256,1024]{2,1,0:T(8,128)(2,1)S(1)} custom-call(s32[8,4,8]{2,1,0:T(4,128)} %sky_ref.17, s32[2,35]{1,0:T(2,128)} %bitcast.42, bf16[1024,1024]{1,0:T(8,128)(2,1)} %bitcast.38), custom_call_target="tpu_custom_call" | custom-call | flops 2097152 | bytes 1048576 | tf_op jit(solution)/shard_map/weigh/pallas_call | solution.py:128
  5.6 5.3 %match.7 = (bf16[256,1024]{1,0:T(8,128)(2,1)}, bf16[256,1024]{1,0:T(8,128)(2,1)}) custom-call(s32[8,4,8]{2,1,0:T(4,128)} %sky_ref.17, bf16[1024,1024]{1,0:T(8,128)(2,1)} %bitcast.26, bf16[1024,1024]{1,0:T(8,128)(2,1)} %bitcast.27, bf16[1024,1024]{1,0:T(8,128)(2,1)} %bitcast.28, bf16[256,1152]{1,0:T(8,128)(2,1)S(1)} %get-tuple-element.21.column_ref, ...), custom_call_target="tpu_custom_call" | custom-call | flops 1962934272 | bytes 2097152 | tf_op jit(solution)/shard_map/match/pallas_call | solution.py:218
  10.9 3.0 %collective-permute-start.3 = (bf16[256,1024]{1,0:T(8,128)(2,1)}, bf16[256,1024]{1,0:T(8,128)(2,1)}, u32[]{:S(2)}, u32[]{:S(2)}) collective-permute-start(bf16[256,1024]{1,0:T(8,128)(2,1)} %get-tuple-element.27), channel_id=1, source_target_pairs={{0,4},{4,0},{8,12},{12,8},{16,20},{20,16},{24,28},{28,24},{1,5},{5... | collective-permute-start | bytes 1572872 | tf_op jit(solution)/shard_map/ppermute | solution.py:433
  14.0 2.8 %weigh.3.weight_ref = bf16[2,256,1024]{2,1,0:T(8,128)(2,1)S(1)} custom-call(s32[8,4,8]{2,1,0:T(4,128)} %sky_ref.17, s32[2,35]{1,0:T(2,128)} %bitcast.43, bf16[1024,1024]{1,0:T(8,128)(2,1)} %bitcast.39), custom_call_target="tpu_custom_call" | custom-call | flops 4194304 | bytes 2097152 | tf_op jit(solution)/shard_map/weigh/pallas_call | solution.py:128
  16.8 5.3 %match.4 = (bf16[256,1024]{1,0:T(8,128)(2,1)}, bf16[256,1024]{1,0:T(8,128)(2,1)}) custom-call(s32[8,4,8]{2,1,0:T(4,128)} %sky_ref.17, bf16[1024,1024]{1,0:T(8,128)(2,1)} %bitcast.29, bf16[1024,1024]{1,0:T(8,128)(2,1)} %bitcast.30, bf16[1024,1024]{1,0:T(8,128)(2,1)} %bitcast.31, bf16[256,1152]{1,0:T(8,128)(2,1)S(1)} %get-tuple-element.21.column_ref, ...), custom_call_target="tpu_custom_call" | custom-call | flops 1962934272 | bytes 2097152 | tf_op jit(solution)/shard_map/match/pallas_call | solution.py:218
  22.1 2.0 %collective-permute-start = (bf16[256,1024]{1,0:T(8,128)(2,1)}, bf16[256,1024]{1,0:T(8,128)(2,1)}, u32[]{:S(2)}, u32[]{:S(2)}) collective-permute-start(bf16[256,1024]{1,0:T(8,128)(2,1)} %get-tuple-element.25), channel_id=1, source_target_pairs={{0,4},{4,0},{8,12},{12,8},{16,20},{20,16},{24,28},{28,24},{1,5},{5... | collective-permute-start | bytes 1572872 | tf_op jit(solution)/shard_map/ppermute | solution.py:433
  24.1 0.8 constant_dynamic-slice_fusion
  24.9 1.6 %collective-permute-start.9 = (bf16[2,128,1024]{2,1,0:T(8,128)(2,1)}, bf16[2,128,1024]{2,1,0:T(8,128)(2,1)S(1)}, u32[]{:S(2)}, u32[]{:S(2)}) collective-permute-start(bf16[2,128,1024]{2,1,0:T(8,128)(2,1)} %constant_dynamic-slice_fusion), channel_id=1, source_target_pairs={{0,8},{4,12},{8,0},{12,4},{16,24},{20,28},{24,16},{28,20},{1,9},{5... | collective-permute-start | bytes 1572872 | tf_op jit(solution)/shard_map/ppermute | solution.py:433
  26.5 1.6 %weigh.4.weight_ref = bf16[1,256,1024]{2,1,0:T(8,128)(2,1)S(1)} custom-call(s32[8,4,8]{2,1,0:T(4,128)} %sky_ref.17, s32[2,35]{1,0:T(2,128)} %bitcast.44, bf16[1024,1024]{1,0:T(8,128)(2,1)} %bitcast.40), custom_call_target="tpu_custom_call" | custom-call | flops 2097152 | bytes 1048576 | tf_op jit(solution)/shard_map/weigh/pallas_call | solution.py:128
  28.1 5.2 %match.5 = (bf16[256,1024]{1,0:T(8,128)(2,1)}, bf16[256,1024]{1,0:T(8,128)(2,1)S(1)}) custom-call(s32[8,4,8]{2,1,0:T(4,128)} %sky_ref.17, bf16[1024,1024]{1,0:T(8,128)(2,1)} %bitcast.32, bf16[1024,1024]{1,0:T(8,128)(2,1)} %bitcast.33, bf16[1024,1024]{1,0:T(8,128)(2,1)} %bitcast.34, bf16[256,1152]{1,0:T(8,128)(2,1)S(1)} %get-tuple-element.21.column_ref, ...), custom_call_target="tpu_custom_call" | custom-call | flops 1962934272 | bytes 2097152 | tf_op jit(solution)/shard_map/match/pallas_call | solution.py:218
  33.3 5.2 %match.6 = (bf16[256,1024]{1,0:T(8,128)(2,1)}, bf16[256,1024]{1,0:T(8,128)(2,1)S(1)}) custom-call(s32[8,4,8]{2,1,0:T(4,128)} %sky_ref.17, bf16[1024,1024]{1,0:T(8,128)(2,1)} %bitcast.35, bf16[1024,1024]{1,0:T(8,128)(2,1)} %bitcast.36, bf16[1024,1024]{1,0:T(8,128)(2,1)} %bitcast.37, bf16[256,1152]{1,0:T(8,128)(2,1)S(1)} %get-tuple-element.21.column_ref, ...), custom_call_target="tpu_custom_call" | custom-call | flops 1962934272 | bytes 2097152 | tf_op jit(solution)/shard_map/match/pallas_call | solution.py:218
  38.5 1.0 add_convert_fusion.1
  39.6 0.5 collective-permute-start.4
  40.1 1.0 fusion
  41.1 1.7 %collective-permute-start.7 = (bf16[128,1024]{1,0:T(8,128)(2,1)S(1)}, bf16[128,1024]{1,0:T(8,128)(2,1)S(1)}, u32[]{:S(2)}, u32[]{:S(2)}) collective-permute-start(bf16[128,1024]{1,0:T(8,128)(2,1)S(1)} %fusion), channel_id=1, source_target_pairs={{0,8},{4,12},{8,0},{12,4},{16,24},{20,28},{24,16},{28,20},{1,9},{5... | collective-permute-start | bytes 786440 | tf_op jit(solution)/shard_map/ppermute | solution.py:433
  42.7 5.9 %collective-permute-done = bf16[256,1024]{1,0:T(8,128)(2,1)} collective-permute-done((bf16[256,1024]{1,0:T(8,128)(2,1)}, bf16[256,1024]{1,0:T(8,128)(2,1)}, u32[]{:S(2)}, u32[]{:S(2)}) %collective-permute-start) | collective-permute-done | bytes 524320 | tf_op jit(solution)/shard_map/ppermute | solution.py:433
  48.7 1.0 add_convert_fusion.2
  49.7 1.9 %collective-permute-start.1 = (bf16[128,1024]{1,0:T(8,128)(2,1)S(1)}, bf16[128,1024]{1,0:T(8,128)(2,1)S(1)}, u32[]{:S(2)}, u32[]{:S(2)}) collective-permute-start(bf16[128,1024]{1,0:T(8,128)(2,1)S(1)} %add_convert_fusion.2), channel_id=1, source_target_pairs={{0,8},{4,12},{8,0},{12,4},{16,24},{20,28},{24,16},{28,20},{1,9},{5... | collective-permute-start | bytes 786440 | tf_op jit(solution)/shard_map/ppermute | solution.py:433
  51.5 0.1 add_convert_fusion
  51.6 2.7 %collective-permute-start.10 = (bf16[2,64,1024]{2,1,0:T(8,128)(2,1)S(1)}, bf16[2,64,1024]{2,1,0:T(8,128)(2,1)S(1)}, u32[]{:S(2)}, u32[]{:S(2)}) collective-permute-start(bf16[2,64,1024]{2,1,0:T(8,128)(2,1)S(1)} %add_convert_fusion), channel_id=1, source_target_pairs={{0,16},{4,20},{8,24},{12,28},{16,0},{20,4},{24,8},{28,12},{1,17},{... | collective-permute-start | bytes 786440 | tf_op jit(solution)/shard_map/ppermute | solution.py:433
  54.3 1.0 add_convert_fusion.4
  55.3 0.4 collective-permute-start.5
  55.7 1.0 fusion.2
  56.7 2.7 %collective-permute-start.8 = (bf16[64,1024]{1,0:T(8,128)(2,1)S(1)}, bf16[64,1024]{1,0:T(8,128)(2,1)S(1)}, u32[]{:S(2)}, u32[]{:S(2)}) collective-permute-start(bf16[64,1024]{1,0:T(8,128)(2,1)S(1)} %fusion.2), channel_id=1, source_target_pairs={{0,16},{4,20},{8,24},{12,28},{16,0},{20,4},{24,8},{28,12},{1,17},{... | collective-permute-start | bytes 393224 | tf_op jit(solution)/shard_map/ppermute | solution.py:433
  59.4 4.4 %collective-permute-done.1 = bf16[128,1024]{1,0:T(8,128)(2,1)S(1)} collective-permute-done((bf16[128,1024]{1,0:T(8,128)(2,1)S(1)}, bf16[128,1024]{1,0:T(8,128)(2,1)S(1)}, u32[]{:S(2)}, u32[]{:S(2)}) %collective-permute-start.1) | collective-permute-done | bytes 262176 | tf_op jit(solution)/shard_map/ppermute | solution.py:433
  63.8 1.0 add_convert_fusion.5
  64.8 0.1 collective-permute-start.2
  64.8 11.0 %collective-permute-done.10 = bf16[2,64,1024]{2,1,0:T(8,128)(2,1)S(1)} collective-permute-done((bf16[2,64,1024]{2,1,0:T(8,128)(2,1)S(1)}, bf16[2,64,1024]{2,1,0:T(8,128)(2,1)S(1)}, u32[]{:S(2)}, u32[]{:S(2)}) %collective-permute-start.10) | collective-permute-done | bytes 262176 | tf_op jit(solution)/shard_map/ppermute | solution.py:433
  75.8 0.1 fusion.11
  75.9 1.6 %collective-permute-start.11 = (bf16[64,1024]{1,0:T(8,128)(2,1)S(1)}, bf16[64,1024]{1,0:T(8,128)(2,1)S(1)}, u32[]{:S(2)}, u32[]{:S(2)}) collective-permute-start(bf16[64,1024]{1,0:T(8,128)(2,1)S(1)} %fusion.11), channel_id=1, source_target_pairs={{0,4},{4,0},{8,12},{12,8},{16,20},{20,16},{24,28},{28,24},{1,5},{5... | collective-permute-start | bytes 393224 | tf_op jit(solution)/shard_map/ppermute | solution.py:433
  77.5 1.1 collective-permute-done.5
  78.6 2.0 %collective-permute-done.8 = bf16[64,1024]{1,0:T(8,128)(2,1)S(1)} collective-permute-done((bf16[64,1024]{1,0:T(8,128)(2,1)S(1)}, bf16[64,1024]{1,0:T(8,128)(2,1)S(1)}, u32[]{:S(2)}, u32[]{:S(2)}) %collective-permute-start.8) | collective-permute-done | bytes 131104 | tf_op jit(solution)/shard_map/ppermute | solution.py:433
  80.6 1.2 %fusion.10.refs_4_ = bf16[64,1024]{1,0:T(8,128)(2,1)S(1)} fusion(bf16[64,1024]{1,0:T(8,128)(2,1)S(1)} %collective-permute-done.8, bf16[64,1024]{1,0:T(8,128)(2,1)S(1)} %collective-permute-done.5, bf16[128,1024]{1,0:T(8,128)(2,1)S(1)} %collective-permute-done.7, s32[]{:T(128)S(6)} %select_n.14, bf16[256,1024]{1,0:T(8,128)(2,1)} %collective-permute-done.6, ...), kind=kLoop, calls=%fused_computation.20 | loop fusion | flops 1114112 | bytes 1179656 | tf_op jit(solution)/shard_map/convert_element_type | solution.py:488
  81.9 1.7 %collective-permute-done.2 = bf16[64,1024]{1,0:T(8,128)(2,1)S(1)} collective-permute-done((bf16[64,1024]{1,0:T(8,128)(2,1)S(1)}, bf16[64,1024]{1,0:T(8,128)(2,1)S(1)}, u32[]{:S(2)}, u32[]{:S(2)}) %collective-permute-start.2) | collective-permute-done | bytes 131104 | tf_op jit(solution)/shard_map/ppermute | solution.py:433
  83.6 1.1 fusion.9.refs_12_.refs_1_
  84.7 1.3 %collective-permute-start.15 = (bf16[64,1024]{1,0:T(8,128)(2,1)S(1)}, bf16[64,1024]{1,0:T(8,128)(2,1)S(1)}, u32[]{:S(2)}, u32[]{:S(2)}) collective-permute-start(bf16[64,1024]{1,0:T(8,128)(2,1)S(1)} %fusion.9.refs_12_.refs_1_), channel_id=1, source_target_pairs={{0,16},{4,20},{8,24},{12,28},{16,0},{20,4},{24,8},{28,12},{1,17},{... | collective-permute-start | bytes 393224 | tf_op jit(solution)/shard_map/ppermute | solution.py:433
  86.0 5.9 %collective-permute-start.19 = (bf16[64,1024]{1,0:T(8,128)(2,1)S(1)}, bf16[64,1024]{1,0:T(8,128)(2,1)S(1)}, u32[]{:S(2)}, u32[]{:S(2)}) collective-permute-start(bf16[64,1024]{1,0:T(8,128)(2,1)S(1)} %fusion.10.refs_4_), channel_id=1, source_target_pairs={{0,8},{4,12},{8,0},{12,4},{16,24},{20,28},{24,16},{28,20},{1,9},{5... | collective-permute-start | bytes 393224 | tf_op jit(solution)/shard_map/ppermute | solution.py:433
  91.9 2.0 %collective-permute-start.21 = (bf16[64,1024]{1,0:T(8,128)(2,1)S(1)}, bf16[64,1024]{1,0:T(8,128)(2,1)S(1)}, u32[]{:S(2)}, u32[]{:S(2)}) collective-permute-start(bf16[64,1024]{1,0:T(8,128)(2,1)S(1)} %collective-permute-done.20.refs_6_), channel_id=1, source_target_pairs={{0,8},{4,12},{8,0},{12,4},{16,24},{20,28},{24,16},{28,20},{1,9},{5... | collective-permute-start | bytes 393224 | tf_op jit(solution)/shard_map/ppermute | solution.py:433
  93.9 1.5 %collective-permute-start.22 = (bf16[64,1024]{1,0:T(8,128)(2,1)S(1)}, bf16[64,1024]{1,0:T(8,128)(2,1)S(1)}, u32[]{:S(2)}, u32[]{:S(2)}) collective-permute-start(bf16[64,1024]{1,0:T(8,128)(2,1)S(1)} %fusion.10.refs_4_), channel_id=1, source_target_pairs={{0,4},{4,0},{8,12},{12,8},{16,20},{20,16},{24,28},{28,24},{1,5},{5... | collective-permute-start | bytes 393224 | tf_op jit(solution)/shard_map/ppermute | solution.py:433
  95.5 0.6 collective-permute-done.19.refs_5_
  96.1 1.5 %collective-permute-start.23 = (bf16[64,1024]{1,0:T(8,128)(2,1)S(1)}, bf16[64,1024]{1,0:T(8,128)(2,1)S(1)}, u32[]{:S(2)}, u32[]{:S(2)}) collective-permute-start(bf16[64,1024]{1,0:T(8,128)(2,1)S(1)} %collective-permute-done.19.refs_5_), channel_id=1, source_target_pairs={{0,4},{4,0},{8,12},{12,8},{16,20},{20,16},{24,28},{28,24},{1,5},{5... | collective-permute-start | bytes 393224 | tf_op jit(solution)/shard_map/ppermute | solution.py:433
  97.6 1.4 %collective-permute-start.24 = (bf16[64,1024]{1,0:T(8,128)(2,1)S(1)}, bf16[64,1024]{1,0:T(8,128)(2,1)S(1)}, u32[]{:S(2)}, u32[]{:S(2)}) collective-permute-start(bf16[64,1024]{1,0:T(8,128)(2,1)S(1)} %collective-permute-done.20.refs_6_), channel_id=1, source_target_pairs={{0,4},{4,0},{8,12},{12,8},{16,20},{20,16},{24,28},{28,24},{1,5},{5... | collective-permute-start | bytes 393224 | tf_op jit(solution)/shard_map/ppermute | solution.py:433
  99.0 1.4 %collective-permute-start.25 = (bf16[64,1024]{1,0:T(8,128)(2,1)S(1)}, bf16[64,1024]{1,0:T(8,128)(2,1)S(1)}, u32[]{:S(2)}, u32[]{:S(2)}) collective-permute-start(bf16[64,1024]{1,0:T(8,128)(2,1)S(1)} %collective-permute-done.21.refs_7_), channel_id=1, source_target_pairs={{0,4},{4,0},{8,12},{12,8},{16,20},{20,16},{24,28},{28,24},{1,5},{5... | collective-permute-start | bytes 393224 | tf_op jit(solution)/shard_map/ppermute | solution.py:433
  100.4 1.4 %collective-permute-start.12 = (bf16[64,1024]{1,0:T(8,128)(2,1)S(1)}, bf16[64,1024]{1,0:T(8,128)(2,1)S(1)}, u32[]{:S(2)}, u32[]{:S(2)}) collective-permute-start(bf16[64,1024]{1,0:T(8,128)(2,1)S(1)} %fusion.9.refs_12_.refs_1_), channel_id=1, source_target_pairs={{0,4},{4,0},{8,12},{12,8},{16,20},{20,16},{24,28},{28,24},{1,5},{5... | collective-permute-start | bytes 393224 | tf_op jit(solution)/shard_map/ppermute | solution.py:433
  101.8 0.6 collective-permute-start.16
  102.4 0.7 collective-permute-done.23.refs_9_
  103.1 1.5 %collective-permute-start.14 = (bf16[64,1024]{1,0:T(8,128)(2,1)S(1)}, bf16[64,1024]{1,0:T(8,128)(2,1)S(1)}, u32[]{:S(2)}, u32[]{:S(2)}) collective-permute-start(bf16[64,1024]{1,0:T(8,128)(2,1)S(1)} %collective-permute-done.13.refs_13_.refs_2_), channel_id=1, source_target_pairs={{0,4},{4,0},{8,12},{12,8},{16,20},{20,16},{24,28},{28,24},{1,5},{5... | collective-permute-start | bytes 393224 | tf_op jit(solution)/shard_map/ppermute | solution.py:433
  104.6 1.3 %collective-permute-done.24.refs_10_ = bf16[64,1024]{1,0:T(8,128)(2,1)S(1)} collective-permute-done((bf16[64,1024]{1,0:T(8,128)(2,1)S(1)}, bf16[64,1024]{1,0:T(8,128)(2,1)S(1)}, u32[]{:S(2)}, u32[]{:S(2)}) %collective-permute-start.24) | collective-permute-done | bytes 131104 | tf_op jit(solution)/shard_map/ppermute | solution.py:433
  105.9 1.5 %collective-permute-start.18 = (bf16[64,1024]{1,0:T(8,128)(2,1)S(1)}, bf16[64,1024]{1,0:T(8,128)(2,1)S(1)}, u32[]{:S(2)}, u32[]{:S(2)}) collective-permute-start(bf16[64,1024]{1,0:T(8,128)(2,1)S(1)} %collective-permute-done.17.refs_15_.refs_4_), channel_id=1, source_target_pairs={{0,4},{4,0},{8,12},{12,8},{16,20},{20,16},{24,28},{28,24},{1,5},{5... | collective-permute-start | bytes 393224 | tf_op jit(solution)/shard_map/ppermute | solution.py:433
  107.4 1.3 %collective-permute-done.25.refs_11_ = bf16[64,1024]{1,0:T(8,128)(2,1)S(1)} collective-permute-done((bf16[64,1024]{1,0:T(8,128)(2,1)S(1)}, bf16[64,1024]{1,0:T(8,128)(2,1)S(1)}, u32[]{:S(2)}, u32[]{:S(2)}) %collective-permute-start.25) | collective-permute-done | bytes 131104 | tf_op jit(solution)/shard_map/ppermute | solution.py:433
  108.7 3.5 %finish.2 = (bf16[2,2,256,1024]{3,2,1,0:T(8,128)(2,1)}, bf16[2,256,128]{2,1,0:T(8,128)(2,1)S(1)}) custom-call(s32[8,4,8]{2,1,0:T(4,128)} %sky_ref.17, bf16[256,128]{1,0:T(8,128)(2,1)S(1)} %get-tuple-element.29.refs_0_.across_ref, bf16[256,1024]{1,0:T(8,128)(2,1)} %get-tuple-element.30.refs_1_, bf16[256,1024]{1,0:T(8,128)(2,1)} %get-tuple-element.31.refs_2_, ...), custom_call_target="tpu_custom_call" | custom-call | flops 786432 | bytes 4718592 | tf_op jit(solution)/shard_map/finish/pallas_call | solution.py:351
  112.2 1.2 %collective-permute-done.14.refs_2_.refs_6_ = bf16[64,1024]{1,0:T(8,128)(2,1)S(1)} collective-permute-done((bf16[64,1024]{1,0:T(8,128)(2,1)S(1)}, bf16[64,1024]{1,0:T(8,128)(2,1)S(1)}, u32[]{:S(2)}, u32[]{:S(2)}) %collective-permute-start.14) | collective-permute-done | bytes 131104 | tf_op jit(solution)/shard_map/ppermute | solution.py:433
  113.5 1.4 %collective-permute-done.18.refs_4_.refs_8_ = bf16[64,1024]{1,0:T(8,128)(2,1)S(1)} collective-permute-done((bf16[64,1024]{1,0:T(8,128)(2,1)S(1)}, bf16[64,1024]{1,0:T(8,128)(2,1)S(1)}, u32[]{:S(2)}, u32[]{:S(2)}) %collective-permute-start.18) | collective-permute-done | bytes 131104 | tf_op jit(solution)/shard_map/ppermute | solution.py:433
  114.9 0.6 power.1
  115.6 1.6 %collective-permute-start.27 = (bf16[256,128]{1,0:T(8,128)(2,1)S(1)}, bf16[256,128]{1,0:T(8,128)(2,1)S(1)}, u32[]{:S(2)}, u32[]{:S(2)}) collective-permute-start(bf16[256,128]{1,0:T(8,128)(2,1)S(1)} %get-tuple-element.38), channel_id=1, source_target_pairs={{0,2},{1,3},{2,0},{3,1},{4,6},{5,7},{6,4},{7,5},{8,10},{9,11},{10,... | collective-permute-start | bytes 196616 | tf_op jit(solution)/shard_map/ppermute | solution.py:511
  117.1 1.4 %collective-permute-start.28 = (bf16[256,128]{1,0:T(8,128)(2,1)S(1)}, bf16[256,128]{1,0:T(8,128)(2,1)S(1)}, u32[]{:S(2)}, u32[]{:S(2)}) collective-permute-start(bf16[256,128]{1,0:T(8,128)(2,1)S(1)} %get-tuple-element.39), channel_id=1, source_target_pairs={{0,3},{1,0},{2,1},{3,2},{4,7},{5,4},{6,5},{7,6},{8,11},{9,8},{10,9... | collective-permute-start | bytes 196616 | tf_op jit(solution)/shard_map/ppermute | solution.py:511
  118.5 2.0 %finish.3 = bf16[2,2,256,1024]{3,2,1,0:T(8,128)(2,1)} custom-call(s32[8,4,8]{2,1,0:T(4,128)} %sky_ref.17, bf16[256,1024]{1,0:T(8,128)(2,1)} %get-tuple-element.23.refs_0_, bf16[64,1024]{1,0:T(8,128)(2,1)S(1)} %collective-permute-done.12.refs_1_.refs_5_, bf16[64,1024]{1,0:T(8,128)(2,1)S(1)} %collective-permute-done.14.refs_2_.refs_6_, ...), custom_call_target="tpu_custom_call", output_to_operand_aliasing={{}: (6, {})} | custom-call | flops 262144 | bytes 1572864 | tf_op jit(solution)/shard_map/finish/pallas_call | solution.py:351
  120.6 0.7 convert_add_fusion.3
  (22 shorter events, 0.3 us)
Async XLA Ops:
  10.9 27.6 %collective-permute-start.3 = (bf16[256,1024]{1,0:T(8,128)(2,1)}, bf16[256,1024]{1,0:T(8,128)(2,1)}, u32[]{:S(2)}, u32[]{:S(2)}) collective-permute-start(bf16[256,1024]{1,0:T(8,128)(2,1)} %get-tuple-element.27), channel_id=1, source_target_pairs={{0,4},{4,0},{8,12},{12,8},{16,20},{20,16},{24,28},{28,24},{1,5},{5... | collective-permute-start | bytes 1572872 | tf_op jit(solution)/shard_map/ppermute | solution.py:433
  13.9 26.1 %collective-permute-start.6 = (bf16[256,1024]{1,0:T(8,128)(2,1)S(1)}, bf16[256,1024]{1,0:T(8,128)(2,1)}, u32[]{:S(2)}, u32[]{:S(2)}) collective-permute-start(bf16[256,1024]{1,0:T(8,128)(2,1)S(1)} %bitcast.25), channel_id=1, source_target_pairs={{0,4},{4,0},{8,12},{12,8},{16,20},{20,16},{24,28},{28,24},{1,5},{5... | collective-permute-start | bytes 1572872 | tf_op jit(solution)/shard_map/ppermute | solution.py:433
  22.1 26.5 %collective-permute-start = (bf16[256,1024]{1,0:T(8,128)(2,1)}, bf16[256,1024]{1,0:T(8,128)(2,1)}, u32[]{:S(2)}, u32[]{:S(2)}) collective-permute-start(bf16[256,1024]{1,0:T(8,128)(2,1)} %get-tuple-element.25), channel_id=1, source_target_pairs={{0,4},{4,0},{8,12},{12,8},{16,20},{20,16},{24,28},{28,24},{1,5},{5... | collective-permute-start | bytes 1572872 | tf_op jit(solution)/shard_map/ppermute | solution.py:433
  24.9 26.6 %collective-permute-start.9 = (bf16[2,128,1024]{2,1,0:T(8,128)(2,1)}, bf16[2,128,1024]{2,1,0:T(8,128)(2,1)S(1)}, u32[]{:S(2)}, u32[]{:S(2)}) collective-permute-start(bf16[2,128,1024]{2,1,0:T(8,128)(2,1)} %constant_dynamic-slice_fusion), channel_id=1, source_target_pairs={{0,8},{4,12},{8,0},{12,4},{16,24},{20,28},{24,16},{28,20},{1,9},{5... | collective-permute-start | bytes 1572872 | tf_op jit(solution)/shard_map/ppermute | solution.py:433
  39.6 14.7 %collective-permute-start.4 = (bf16[128,1024]{1,0:T(8,128)(2,1)S(1)}, bf16[128,1024]{1,0:T(8,128)(2,1)S(1)}, u32[]{:S(2)}, u32[]{:S(2)}) collective-permute-start(bf16[128,1024]{1,0:T(8,128)(2,1)S(1)} %add_convert_fusion.1), channel_id=1, source_target_pairs={{0,8},{4,12},{8,0},{12,4},{16,24},{20,28},{24,16},{28,20},{1,9},{5... | collective-permute-start | bytes 786440 | tf_op jit(solution)/shard_map/ppermute | solution.py:433
  41.1 14.6 %collective-permute-start.7 = (bf16[128,1024]{1,0:T(8,128)(2,1)S(1)}, bf16[128,1024]{1,0:T(8,128)(2,1)S(1)}, u32[]{:S(2)}, u32[]{:S(2)}) collective-permute-start(bf16[128,1024]{1,0:T(8,128)(2,1)S(1)} %fusion), channel_id=1, source_target_pairs={{0,8},{4,12},{8,0},{12,4},{16,24},{20,28},{24,16},{28,20},{1,9},{5... | collective-permute-start | bytes 786440 | tf_op jit(solution)/shard_map/ppermute | solution.py:433
  49.7 14.1 %collective-permute-start.1 = (bf16[128,1024]{1,0:T(8,128)(2,1)S(1)}, bf16[128,1024]{1,0:T(8,128)(2,1)S(1)}, u32[]{:S(2)}, u32[]{:S(2)}) collective-permute-start(bf16[128,1024]{1,0:T(8,128)(2,1)S(1)} %add_convert_fusion.2), channel_id=1, source_target_pairs={{0,8},{4,12},{8,0},{12,4},{16,24},{20,28},{24,16},{28,20},{1,9},{5... | collective-permute-start | bytes 786440 | tf_op jit(solution)/shard_map/ppermute | solution.py:433
  51.6 24.2 %collective-permute-start.10 = (bf16[2,64,1024]{2,1,0:T(8,128)(2,1)S(1)}, bf16[2,64,1024]{2,1,0:T(8,128)(2,1)S(1)}, u32[]{:S(2)}, u32[]{:S(2)}) collective-permute-start(bf16[2,64,1024]{2,1,0:T(8,128)(2,1)S(1)} %add_convert_fusion), channel_id=1, source_target_pairs={{0,16},{4,20},{8,24},{12,28},{16,0},{20,4},{24,8},{28,12},{1,17},{... | collective-permute-start | bytes 786440 | tf_op jit(solution)/shard_map/ppermute | solution.py:433
  55.3 23.3 %collective-permute-start.5 = (bf16[64,1024]{1,0:T(8,128)(2,1)S(1)}, bf16[64,1024]{1,0:T(8,128)(2,1)S(1)}, u32[]{:S(2)}, u32[]{:S(2)}) collective-permute-start(bf16[64,1024]{1,0:T(8,128)(2,1)S(1)} %add_convert_fusion.4), channel_id=1, source_target_pairs={{0,16},{4,20},{8,24},{12,28},{16,0},{20,4},{24,8},{28,12},{1,17},{... | collective-permute-start | bytes 393224 | tf_op jit(solution)/shard_map/ppermute | solution.py:433
  56.7 23.9 %collective-permute-start.8 = (bf16[64,1024]{1,0:T(8,128)(2,1)S(1)}, bf16[64,1024]{1,0:T(8,128)(2,1)S(1)}, u32[]{:S(2)}, u32[]{:S(2)}) collective-permute-start(bf16[64,1024]{1,0:T(8,128)(2,1)S(1)} %fusion.2), channel_id=1, source_target_pairs={{0,16},{4,20},{8,24},{12,28},{16,0},{20,4},{24,8},{28,12},{1,17},{... | collective-permute-start | bytes 393224 | tf_op jit(solution)/shard_map/ppermute | solution.py:433
  64.8 18.8 %collective-permute-start.2 = (bf16[64,1024]{1,0:T(8,128)(2,1)S(1)}, bf16[64,1024]{1,0:T(8,128)(2,1)S(1)}, u32[]{:S(2)}, u32[]{:S(2)}) collective-permute-start(bf16[64,1024]{1,0:T(8,128)(2,1)S(1)} %add_convert_fusion.5), channel_id=1, source_target_pairs={{0,16},{4,20},{8,24},{12,28},{16,0},{20,4},{24,8},{28,12},{1,17},{... | collective-permute-start | bytes 393224 | tf_op jit(solution)/shard_map/ppermute | solution.py:433
  75.9 7.7 %collective-permute-start.11 = (bf16[64,1024]{1,0:T(8,128)(2,1)S(1)}, bf16[64,1024]{1,0:T(8,128)(2,1)S(1)}, u32[]{:S(2)}, u32[]{:S(2)}) collective-permute-start(bf16[64,1024]{1,0:T(8,128)(2,1)S(1)} %fusion.11), channel_id=1, source_target_pairs={{0,4},{4,0},{8,12},{12,8},{16,20},{20,16},{24,28},{28,24},{1,5},{5... | collective-permute-start | bytes 393224 | tf_op jit(solution)/shard_map/ppermute | solution.py:433
  81.8 10.1 %collective-permute-start.20 = (bf16[64,1024]{1,0:T(8,128)(2,1)S(1)}, bf16[64,1024]{1,0:T(8,128)(2,1)S(1)}, u32[]{:S(2)}, u32[]{:S(2)}) collective-permute-start(bf16[64,1024]{1,0:T(8,128)(2,1)S(1)} %fusion.10.refs_4_), channel_id=1, source_target_pairs={{0,16},{4,20},{8,24},{12,28},{16,0},{20,4},{24,8},{28,12},{1,17},{... | collective-permute-start | bytes 393224 | tf_op jit(solution)/shard_map/ppermute | solution.py:433
  84.7 10.7 %collective-permute-start.15 = (bf16[64,1024]{1,0:T(8,128)(2,1)S(1)}, bf16[64,1024]{1,0:T(8,128)(2,1)S(1)}, u32[]{:S(2)}, u32[]{:S(2)}) collective-permute-start(bf16[64,1024]{1,0:T(8,128)(2,1)S(1)} %fusion.9.refs_12_.refs_1_), channel_id=1, source_target_pairs={{0,16},{4,20},{8,24},{12,28},{16,0},{20,4},{24,8},{28,12},{1,17},{... | collective-permute-start | bytes 393224 | tf_op jit(solution)/shard_map/ppermute | solution.py:433
  86.0 10.0 %collective-permute-start.19 = (bf16[64,1024]{1,0:T(8,128)(2,1)S(1)}, bf16[64,1024]{1,0:T(8,128)(2,1)S(1)}, u32[]{:S(2)}, u32[]{:S(2)}) collective-permute-start(bf16[64,1024]{1,0:T(8,128)(2,1)S(1)} %fusion.10.refs_4_), channel_id=1, source_target_pairs={{0,8},{4,12},{8,0},{12,4},{16,24},{20,28},{24,16},{28,20},{1,9},{5... | collective-permute-start | bytes 393224 | tf_op jit(solution)/shard_map/ppermute | solution.py:433
  91.9 5.7 %collective-permute-start.13 = (bf16[64,1024]{1,0:T(8,128)(2,1)S(1)}, bf16[64,1024]{1,0:T(8,128)(2,1)S(1)}, u32[]{:S(2)}, u32[]{:S(2)}) collective-permute-start(bf16[64,1024]{1,0:T(8,128)(2,1)S(1)} %fusion.9.refs_12_.refs_1_), channel_id=1, source_target_pairs={{0,8},{4,12},{8,0},{12,4},{16,24},{20,28},{24,16},{28,20},{1,9},{5... | collective-permute-start | bytes 393224 | tf_op jit(solution)/shard_map/ppermute | solution.py:433
  91.9 7.1 %collective-permute-start.21 = (bf16[64,1024]{1,0:T(8,128)(2,1)S(1)}, bf16[64,1024]{1,0:T(8,128)(2,1)S(1)}, u32[]{:S(2)}, u32[]{:S(2)}) collective-permute-start(bf16[64,1024]{1,0:T(8,128)(2,1)S(1)} %collective-permute-done.20.refs_6_), channel_id=1, source_target_pairs={{0,8},{4,12},{8,0},{12,4},{16,24},{20,28},{24,16},{28,20},{1,9},{5... | collective-permute-start | bytes 393224 | tf_op jit(solution)/shard_map/ppermute | solution.py:433
  93.9 6.5 %collective-permute-start.22 = (bf16[64,1024]{1,0:T(8,128)(2,1)S(1)}, bf16[64,1024]{1,0:T(8,128)(2,1)S(1)}, u32[]{:S(2)}, u32[]{:S(2)}) collective-permute-start(bf16[64,1024]{1,0:T(8,128)(2,1)S(1)} %fusion.10.refs_4_), channel_id=1, source_target_pairs={{0,4},{4,0},{8,12},{12,8},{16,20},{20,16},{24,28},{28,24},{1,5},{5... | collective-permute-start | bytes 393224 | tf_op jit(solution)/shard_map/ppermute | solution.py:433
  95.4 6.4 %collective-permute-start.17 = (bf16[64,1024]{1,0:T(8,128)(2,1)S(1)}, bf16[64,1024]{1,0:T(8,128)(2,1)S(1)}, u32[]{:S(2)}, u32[]{:S(2)}) collective-permute-start(bf16[64,1024]{1,0:T(8,128)(2,1)S(1)} %collective-permute-done.15.refs_14_.refs_3_), channel_id=1, source_target_pairs={{0,8},{4,12},{8,0},{12,4},{16,24},{20,28},{24,16},{28,20},{1,9},{5... | collective-permute-start | bytes 393224 | tf_op jit(solution)/shard_map/ppermute | solution.py:433
  96.1 7.0 %collective-permute-start.23 = (bf16[64,1024]{1,0:T(8,128)(2,1)S(1)}, bf16[64,1024]{1,0:T(8,128)(2,1)S(1)}, u32[]{:S(2)}, u32[]{:S(2)}) collective-permute-start(bf16[64,1024]{1,0:T(8,128)(2,1)S(1)} %collective-permute-done.19.refs_5_), channel_id=1, source_target_pairs={{0,4},{4,0},{8,12},{12,8},{16,20},{20,16},{24,28},{28,24},{1,5},{5... | collective-permute-start | bytes 393224 | tf_op jit(solution)/shard_map/ppermute | solution.py:433
  97.6 8.3 %collective-permute-start.24 = (bf16[64,1024]{1,0:T(8,128)(2,1)S(1)}, bf16[64,1024]{1,0:T(8,128)(2,1)S(1)}, u32[]{:S(2)}, u32[]{:S(2)}) collective-permute-start(bf16[64,1024]{1,0:T(8,128)(2,1)S(1)} %collective-permute-done.20.refs_6_), channel_id=1, source_target_pairs={{0,4},{4,0},{8,12},{12,8},{16,20},{20,16},{24,28},{28,24},{1,5},{5... | collective-permute-start | bytes 393224 | tf_op jit(solution)/shard_map/ppermute | solution.py:433
  99.0 9.7 %collective-permute-start.25 = (bf16[64,1024]{1,0:T(8,128)(2,1)S(1)}, bf16[64,1024]{1,0:T(8,128)(2,1)S(1)}, u32[]{:S(2)}, u32[]{:S(2)}) collective-permute-start(bf16[64,1024]{1,0:T(8,128)(2,1)S(1)} %collective-permute-done.21.refs_7_), channel_id=1, source_target_pairs={{0,4},{4,0},{8,12},{12,8},{16,20},{20,16},{24,28},{28,24},{1,5},{5... | collective-permute-start | bytes 393224 | tf_op jit(solution)/shard_map/ppermute | solution.py:433
  100.4 11.8 %collective-permute-start.12 = (bf16[64,1024]{1,0:T(8,128)(2,1)S(1)}, bf16[64,1024]{1,0:T(8,128)(2,1)S(1)}, u32[]{:S(2)}, u32[]{:S(2)}) collective-permute-start(bf16[64,1024]{1,0:T(8,128)(2,1)S(1)} %fusion.9.refs_12_.refs_1_), channel_id=1, source_target_pairs={{0,4},{4,0},{8,12},{12,8},{16,20},{20,16},{24,28},{28,24},{1,5},{5... | collective-permute-start | bytes 393224 | tf_op jit(solution)/shard_map/ppermute | solution.py:433
  101.8 11.7 %collective-permute-start.16 = (bf16[64,1024]{1,0:T(8,128)(2,1)S(1)}, bf16[64,1024]{1,0:T(8,128)(2,1)S(1)}, u32[]{:S(2)}, u32[]{:S(2)}) collective-permute-start(bf16[64,1024]{1,0:T(8,128)(2,1)S(1)} %collective-permute-done.15.refs_14_.refs_3_), channel_id=1, source_target_pairs={{0,4},{4,0},{8,12},{12,8},{16,20},{20,16},{24,28},{28,24},{1,5},{5... | collective-permute-start | bytes 393224 | tf_op jit(solution)/shard_map/ppermute | solution.py:433
  103.1 10.3 %collective-permute-start.14 = (bf16[64,1024]{1,0:T(8,128)(2,1)S(1)}, bf16[64,1024]{1,0:T(8,128)(2,1)S(1)}, u32[]{:S(2)}, u32[]{:S(2)}) collective-permute-start(bf16[64,1024]{1,0:T(8,128)(2,1)S(1)} %collective-permute-done.13.refs_13_.refs_2_), channel_id=1, source_target_pairs={{0,4},{4,0},{8,12},{12,8},{16,20},{20,16},{24,28},{28,24},{1,5},{5... | collective-permute-start | bytes 393224 | tf_op jit(solution)/shard_map/ppermute | solution.py:433
  105.9 8.9 %collective-permute-start.18 = (bf16[64,1024]{1,0:T(8,128)(2,1)S(1)}, bf16[64,1024]{1,0:T(8,128)(2,1)S(1)}, u32[]{:S(2)}, u32[]{:S(2)}) collective-permute-start(bf16[64,1024]{1,0:T(8,128)(2,1)S(1)} %collective-permute-done.17.refs_15_.refs_4_), channel_id=1, source_target_pairs={{0,4},{4,0},{8,12},{12,8},{16,20},{20,16},{24,28},{28,24},{1,5},{5... | collective-permute-start | bytes 393224 | tf_op jit(solution)/shard_map/ppermute | solution.py:433
  115.5 5.1 %collective-permute-start.26 = (bf16[256,128]{1,0:T(8,128)(2,1)S(1)}, bf16[256,128]{1,0:T(8,128)(2,1)S(1)}, u32[]{:S(2)}, u32[]{:S(2)}) collective-permute-start(bf16[256,128]{1,0:T(8,128)(2,1)S(1)} %get-tuple-element.37), channel_id=1, source_target_pairs={{0,1},{1,2},{2,3},{3,0},{4,5},{5,6},{6,7},{7,4},{8,9},{9,10},{10,1... | collective-permute-start | bytes 196616 | tf_op jit(solution)/shard_map/ppermute | solution.py:511
  115.6 5.0 %collective-permute-start.27 = (bf16[256,128]{1,0:T(8,128)(2,1)S(1)}, bf16[256,128]{1,0:T(8,128)(2,1)S(1)}, u32[]{:S(2)}, u32[]{:S(2)}) collective-permute-start(bf16[256,128]{1,0:T(8,128)(2,1)S(1)} %get-tuple-element.38), channel_id=1, source_target_pairs={{0,2},{1,3},{2,0},{3,1},{4,6},{5,7},{6,4},{7,5},{8,10},{9,11},{10,... | collective-permute-start | bytes 196616 | tf_op jit(solution)/shard_map/ppermute | solution.py:511
  117.1 3.5 %collective-permute-start.28 = (bf16[256,128]{1,0:T(8,128)(2,1)S(1)}, bf16[256,128]{1,0:T(8,128)(2,1)S(1)}, u32[]{:S(2)}, u32[]{:S(2)}) collective-permute-start(bf16[256,128]{1,0:T(8,128)(2,1)S(1)} %get-tuple-element.39), channel_id=1, source_target_pairs={{0,3},{1,0},{2,1},{3,2},{4,7},{5,4},{6,5},{7,6},{8,11},{9,8},{10,9... | collective-permute-start | bytes 196616 | tf_op jit(solution)/shard_map/ppermute | solution.py:511

commit v8 on v7

--- a/solution.py
+++ b/solution.py
@@ -26,10 +26,14 @@
 
 
 def in_hbm(array):
+    if array.ndim == 1:
+        return array
     return pltpu.with_memory_space_constraint(array, pltpu.HBM)
 
 
 def start_column(sky_ref):
+    if len(sky_ref.shape) == 1:
+        return sky_ref[0]
     return sky_ref[lax.axis_index("sky"), lax.axis_index("band"), 0]
 
 
@@ -450,15 +454,17 @@
     words = mask_planes[0, 0]
     variance = inv_variance[0, 0]
 
-    def weighing(halves, chunk):
-        return weigh(variance, words, sky_columns, halves, chunk, chunk_rows, sky_count)
+    own_row = sky_columns[own_sky, lax.axis_index("band")]
+
+    def weighing(halves, chunk, places=own_row):
+        return weigh(variance, words, places, halves, chunk, chunk_rows, sky_count)
 
     def matching(weight, which, half_slot, chunk):
         return match(
-            picture, column_band, row_band, weight, which, sky_columns, half_slot, chunk, half_rows, sky_count
+            picture, column_band, row_band, weight, which, own_row, half_slot, chunk, half_rows, sky_count
         )
 
-    weight_other = weighing((OTHER,), 0)
+    weight_other = weighing((OTHER,), 0, sky_columns)
     weight_in = exchange(weight_other[0], 0)
     weight_both = weighing((OTHER, OWN), 1)
     both_terms = reduce_line([weight_both])
@@ -499,12 +505,12 @@
     (near_first, far_first), (near_last, far_last) = gathered
     early = ((OWN, 0), (OTHER, 0), (OWN, 1))
     difference, smoothed = finish(
-        early, [home[0], away[0], home[1]], near_first + far_first + near_last, across_band, sky_columns, None, sky_count
+        early, [home[0], away[0], home[1]], near_first + far_first + near_last, across_band, own_row, None, sky_count
     )
     powers = power(
         [smoothed], near_last + far_last, across_band, down_band, pair, sky_count, band_count
     )
-    (difference,) = finish(((OTHER, 1),), [away[1]], far_last, across_band, sky_columns, difference, sky_count)
+    (difference,) = finish(((OTHER, 1),), [away[1]], far_last, across_band, own_row, difference, sky_count)
     detection = powers[0]
     for step in range(1, band_count):
         ring = [(i, (i + step) % band_count) for i in range(band_count)]

time: 122 us -> 123 us (level)
  Pallas kernels: 34.2 us -> 32.9 us
  transfers between devices with their start and end apart: 29 -> 29, of which waited for: 12 -> 12; matrix products, arithmetic and copies ran while one was open for 8% -> 8% of each run, Pallas kernels for 21% -> 20%
where the time goes in v8:
time: 123 us; the launch traced here: 122 us
  starting transfers between devices  41.3 us (34%)
  waiting for transfers between devices  33.7 us (27%)
  Pallas kernels  32.9 us (27%)
  other arithmetic  11.5 us (9%)
  local copies, waits for them, and re-layouts  1.54 us (1%)
    ppermute x26, starting transfers between devices, exchange(): lax.ppermute(block, 'sky', [(i, i ^ 1 << bit) for i in range(sky_count)])  38.2 us
    ppermute x26, waiting for transfers between devices, exchange(): lax.ppermute(block, 'sky', [(i, i ^ 1 << bit) for i in range(sky_count)])  33.7 us
    pallas_call x4, Pallas kernels, match(): pl.pallas_call(functools.partial(match_kernel, sky_count, which, chunk *...  20.3 us
    convert_element_type x7, other arithmetic, reduce_line(): arrived = exchange(leaving.astype(BF16), bit)  6.15 us
    pallas_call x3, Pallas kernels, weigh(): pl.pallas_call(functools.partial(weight_kernel, sky_count, halves, chunk,...  5.6 us
    pallas_call x2, Pallas kernels, finish(): pl.pallas_call(functools.partial(finish_kernel, sky_count, line, jobs, wi...  5.28 us
    ppermute x3, starting transfers between devices, body(): detection = detection + lax.ppermute(powers[step], 'band', ring).astype(F32)  3.05 us
  transfers between devices with their start and end apart: 29, of which 12 were waited for; matrix products, arithmetic and copies ran while one was open for 8% of the time, Pallas kernels for 20%

profile of v8, /device:TPU:0, one launch (start us, length us, event | category | flops | bytes accessed | tf_op | source)
XLA Modules:
  0.0 121.8 jit_solution(17061074976701829493)
XLA Ops:
  0.6 0.7 convert_element_type.190
  1.3 0.7 convert_convert_fusion
  2.0 0.8 multiply_convert_fusion
  2.8 0.1 pad_convert_fusion
  2.8 0.1 select_maximum_fusion.base_ref
  2.9 1.1 prepare.1
  4.0 0.7 fusion.13.sky_ref
  4.7 1.6 %weigh.5.weight_ref = bf16[1,256,1024]{2,1,0:T(8,128)(2,1)S(1)} custom-call(s32[8,4,8]{2,1,0:T(4,128)} %sky_ref.1, s32[2,35]{1,0:T(2,128)} %bitcast.44, bf16[1024,1024]{1,0:T(8,128)(2,1)} %bitcast.40), custom_call_target="tpu_custom_call" | custom-call | flops 2097152 | bytes 1048576 | tf_op jit(solution)/shard_map/weigh/pallas_call | solution.py:132
  6.3 5.1 %match.7 = (bf16[256,1024]{1,0:T(8,128)(2,1)}, bf16[256,1024]{1,0:T(8,128)(2,1)}) custom-call(s32[8]{0:T(128)S(1)} %fusion.13.sky_ref, bf16[1024,1024]{1,0:T(8,128)(2,1)} %bitcast.28, bf16[1024,1024]{1,0:T(8,128)(2,1)} %bitcast.29, bf16[1024,1024]{1,0:T(8,128)(2,1)} %bitcast.30, bf16[256,1152]{1,0:T(8,128)(2,1)S(1)} %get-tuple-element.21.column_ref, ...), custom_call_target="tpu_custom_call" | custom-call | flops 1962934272 | bytes 2097152 | tf_op jit(solution)/shard_map/match/pallas_call | solution.py:222
  11.4 3.0 %collective-permute-start.3 = (bf16[256,1024]{1,0:T(8,128)(2,1)}, bf16[256,1024]{1,0:T(8,128)(2,1)}, u32[]{:S(2)}, u32[]{:S(2)}) collective-permute-start(bf16[256,1024]{1,0:T(8,128)(2,1)} %get-tuple-element.27), channel_id=1, source_target_pairs={{0,4},{4,0},{8,12},{12,8},{16,20},{20,16},{24,28},{28,24},{1,5},{5... | collective-permute-start | bytes 1572872 | tf_op jit(solution)/shard_map/ppermute | solution.py:437
  14.4 2.6 %weigh.3.weight_ref = bf16[2,256,1024]{2,1,0:T(8,128)(2,1)S(1)} custom-call(s32[8]{0:T(128)S(1)} %fusion.13.sky_ref, s32[2,35]{1,0:T(2,128)} %bitcast.45, bf16[1024,1024]{1,0:T(8,128)(2,1)} %bitcast.41), custom_call_target="tpu_custom_call" | custom-call | flops 4194304 | bytes 2097152 | tf_op jit(solution)/shard_map/weigh/pallas_call | solution.py:132
  17.1 5.1 %match.4 = (bf16[256,1024]{1,0:T(8,128)(2,1)}, bf16[256,1024]{1,0:T(8,128)(2,1)}) custom-call(s32[8]{0:T(128)S(1)} %fusion.13.sky_ref, bf16[1024,1024]{1,0:T(8,128)(2,1)} %bitcast.31, bf16[1024,1024]{1,0:T(8,128)(2,1)} %bitcast.32, bf16[1024,1024]{1,0:T(8,128)(2,1)} %bitcast.33, bf16[256,1152]{1,0:T(8,128)(2,1)S(1)} %get-tuple-element.21.column_ref, ...), custom_call_target="tpu_custom_call" | custom-call | flops 1962934272 | bytes 2097152 | tf_op jit(solution)/shard_map/match/pallas_call | solution.py:222
  22.2 2.0 %collective-permute-start = (bf16[256,1024]{1,0:T(8,128)(2,1)}, bf16[256,1024]{1,0:T(8,128)(2,1)}, u32[]{:S(2)}, u32[]{:S(2)}) collective-permute-start(bf16[256,1024]{1,0:T(8,128)(2,1)} %get-tuple-element.25), channel_id=1, source_target_pairs={{0,4},{4,0},{8,12},{12,8},{16,20},{20,16},{24,28},{28,24},{1,5},{5... | collective-permute-start | bytes 1572872 | tf_op jit(solution)/shard_map/ppermute | solution.py:437
  24.2 0.8 constant_dynamic-slice_fusion
  25.0 1.6 %collective-permute-start.9 = (bf16[2,128,1024]{2,1,0:T(8,128)(2,1)}, bf16[2,128,1024]{2,1,0:T(8,128)(2,1)S(1)}, u32[]{:S(2)}, u32[]{:S(2)}) collective-permute-start(bf16[2,128,1024]{2,1,0:T(8,128)(2,1)} %constant_dynamic-slice_fusion), channel_id=1, source_target_pairs={{0,8},{4,12},{8,0},{12,4},{16,24},{20,28},{24,16},{28,20},{1,9},{5... | collective-permute-start | bytes 1572872 | tf_op jit(solution)/shard_map/ppermute | solution.py:437
  26.6 1.4 %weigh.4.weight_ref = bf16[1,256,1024]{2,1,0:T(8,128)(2,1)S(1)} custom-call(s32[8]{0:T(128)S(1)} %fusion.13.sky_ref, s32[2,35]{1,0:T(2,128)} %bitcast.46, bf16[1024,1024]{1,0:T(8,128)(2,1)} %bitcast.42), custom_call_target="tpu_custom_call" | custom-call | flops 2097152 | bytes 1048576 | tf_op jit(solution)/shard_map/weigh/pallas_call | solution.py:132
  28.1 5.0 %match.5 = (bf16[256,1024]{1,0:T(8,128)(2,1)}, bf16[256,1024]{1,0:T(8,128)(2,1)S(1)}) custom-call(s32[8]{0:T(128)S(1)} %fusion.13.sky_ref, bf16[1024,1024]{1,0:T(8,128)(2,1)} %bitcast.34, bf16[1024,1024]{1,0:T(8,128)(2,1)} %bitcast.35, bf16[1024,1024]{1,0:T(8,128)(2,1)} %bitcast.36, bf16[256,1152]{1,0:T(8,128)(2,1)S(1)} %get-tuple-element.21.column_ref, ...), custom_call_target="tpu_custom_call" | custom-call | flops 1962934272 | bytes 2097152 | tf_op jit(solution)/shard_map/match/pallas_call | solution.py:222
  33.1 5.0 %match.6 = (bf16[256,1024]{1,0:T(8,128)(2,1)}, bf16[256,1024]{1,0:T(8,128)(2,1)S(1)}) custom-call(s32[8]{0:T(128)S(1)} %fusion.13.sky_ref, bf16[1024,1024]{1,0:T(8,128)(2,1)} %bitcast.37, bf16[1024,1024]{1,0:T(8,128)(2,1)} %bitcast.38, bf16[1024,1024]{1,0:T(8,128)(2,1)} %bitcast.39, bf16[256,1152]{1,0:T(8,128)(2,1)S(1)} %get-tuple-element.21.column_ref, ...), custom_call_target="tpu_custom_call" | custom-call | flops 1962934272 | bytes 2097152 | tf_op jit(solution)/shard_map/match/pallas_call | solution.py:222
  38.2 1.0 add_convert_fusion.1
  39.2 0.5 collective-permute-start.4
  39.7 1.0 fusion
  40.7 1.7 %collective-permute-start.7 = (bf16[128,1024]{1,0:T(8,128)(2,1)S(1)}, bf16[128,1024]{1,0:T(8,128)(2,1)S(1)}, u32[]{:S(2)}, u32[]{:S(2)}) collective-permute-start(bf16[128,1024]{1,0:T(8,128)(2,1)S(1)} %fusion), channel_id=1, source_target_pairs={{0,8},{4,12},{8,0},{12,4},{16,24},{20,28},{24,16},{28,20},{1,9},{5... | collective-permute-start | bytes 786440 | tf_op jit(solution)/shard_map/ppermute | solution.py:437
  42.4 6.8 %collective-permute-done = bf16[256,1024]{1,0:T(8,128)(2,1)} collective-permute-done((bf16[256,1024]{1,0:T(8,128)(2,1)}, bf16[256,1024]{1,0:T(8,128)(2,1)}, u32[]{:S(2)}, u32[]{:S(2)}) %collective-permute-start) | collective-permute-done | bytes 524320 | tf_op jit(solution)/shard_map/ppermute | solution.py:437
  49.1 1.0 add_convert_fusion.2
  50.1 1.8 %collective-permute-start.1 = (bf16[128,1024]{1,0:T(8,128)(2,1)S(1)}, bf16[128,1024]{1,0:T(8,128)(2,1)S(1)}, u32[]{:S(2)}, u32[]{:S(2)}) collective-permute-start(bf16[128,1024]{1,0:T(8,128)(2,1)S(1)} %add_convert_fusion.2), channel_id=1, source_target_pairs={{0,8},{4,12},{8,0},{12,4},{16,24},{20,28},{24,16},{28,20},{1,9},{5... | collective-permute-start | bytes 786440 | tf_op jit(solution)/shard_map/ppermute | solution.py:437
  52.0 0.1 add_convert_fusion
  52.1 2.7 %collective-permute-start.10 = (bf16[2,64,1024]{2,1,0:T(8,128)(2,1)S(1)}, bf16[2,64,1024]{2,1,0:T(8,128)(2,1)S(1)}, u32[]{:S(2)}, u32[]{:S(2)}) collective-permute-start(bf16[2,64,1024]{2,1,0:T(8,128)(2,1)S(1)} %add_convert_fusion), channel_id=1, source_target_pairs={{0,16},{4,20},{8,24},{12,28},{16,0},{20,4},{24,8},{28,12},{1,17},{... | collective-permute-start | bytes 786440 | tf_op jit(solution)/shard_map/ppermute | solution.py:437
  54.8 1.0 add_convert_fusion.4
  55.8 0.4 collective-permute-start.5
  56.2 1.0 fusion.2
  57.2 2.7 %collective-permute-start.8 = (bf16[64,1024]{1,0:T(8,128)(2,1)S(1)}, bf16[64,1024]{1,0:T(8,128)(2,1)S(1)}, u32[]{:S(2)}, u32[]{:S(2)}) collective-permute-start(bf16[64,1024]{1,0:T(8,128)(2,1)S(1)} %fusion.2), channel_id=1, source_target_pairs={{0,16},{4,20},{8,24},{12,28},{16,0},{20,4},{24,8},{28,12},{1,17},{... | collective-permute-start | bytes 393224 | tf_op jit(solution)/shard_map/ppermute | solution.py:437
  59.8 3.2 %collective-permute-done.1 = bf16[128,1024]{1,0:T(8,128)(2,1)S(1)} collective-permute-done((bf16[128,1024]{1,0:T(8,128)(2,1)S(1)}, bf16[128,1024]{1,0:T(8,128)(2,1)S(1)}, u32[]{:S(2)}, u32[]{:S(2)}) %collective-permute-start.1) | collective-permute-done | bytes 262176 | tf_op jit(solution)/shard_map/ppermute | solution.py:437
  63.1 1.0 add_convert_fusion.5
  64.1 0.4 collective-permute-start.2
  64.5 11.8 %collective-permute-done.10 = bf16[2,64,1024]{2,1,0:T(8,128)(2,1)S(1)} collective-permute-done((bf16[2,64,1024]{2,1,0:T(8,128)(2,1)S(1)}, bf16[2,64,1024]{2,1,0:T(8,128)(2,1)S(1)}, u32[]{:S(2)}, u32[]{:S(2)}) %collective-permute-start.10) | collective-permute-done | bytes 262176 | tf_op jit(solution)/shard_map/ppermute | solution.py:437
  76.4 1.6 %collective-permute-start.11 = (bf16[64,1024]{1,0:T(8,128)(2,1)S(1)}, bf16[64,1024]{1,0:T(8,128)(2,1)S(1)}, u32[]{:S(2)}, u32[]{:S(2)}) collective-permute-start(bf16[64,1024]{1,0:T(8,128)(2,1)S(1)} %fusion.11), channel_id=1, source_target_pairs={{0,4},{4,0},{8,12},{12,8},{16,20},{20,16},{24,28},{28,24},{1,5},{5... | collective-permute-start | bytes 393224 | tf_op jit(solution)/shard_map/ppermute | solution.py:437
  77.9 1.1 collective-permute-done.5
  79.1 2.0 %collective-permute-done.8 = bf16[64,1024]{1,0:T(8,128)(2,1)S(1)} collective-permute-done((bf16[64,1024]{1,0:T(8,128)(2,1)S(1)}, bf16[64,1024]{1,0:T(8,128)(2,1)S(1)}, u32[]{:S(2)}, u32[]{:S(2)}) %collective-permute-start.8) | collective-permute-done | bytes 131104 | tf_op jit(solution)/shard_map/ppermute | solution.py:437
  81.1 1.2 fusion.10.refs_4_
  82.4 1.7 %collective-permute-done.2 = bf16[64,1024]{1,0:T(8,128)(2,1)S(1)} collective-permute-done((bf16[64,1024]{1,0:T(8,128)(2,1)S(1)}, bf16[64,1024]{1,0:T(8,128)(2,1)S(1)}, u32[]{:S(2)}, u32[]{:S(2)}) %collective-permute-start.2) | collective-permute-done | bytes 131104 | tf_op jit(solution)/shard_map/ppermute | solution.py:437
  84.1 1.1 fusion.9.refs_12_.refs_1_
  85.2 1.3 %collective-permute-start.15 = (bf16[64,1024]{1,0:T(8,128)(2,1)S(1)}, bf16[64,1024]{1,0:T(8,128)(2,1)S(1)}, u32[]{:S(2)}, u32[]{:S(2)}) collective-permute-start(bf16[64,1024]{1,0:T(8,128)(2,1)S(1)} %fusion.9.refs_12_.refs_1_), channel_id=1, source_target_pairs={{0,16},{4,20},{8,24},{12,28},{16,0},{20,4},{24,8},{28,12},{1,17},{... | collective-permute-start | bytes 393224 | tf_op jit(solution)/shard_map/ppermute | solution.py:437
  86.5 6.0 %collective-permute-start.19 = (bf16[64,1024]{1,0:T(8,128)(2,1)S(1)}, bf16[64,1024]{1,0:T(8,128)(2,1)S(1)}, u32[]{:S(2)}, u32[]{:S(2)}) collective-permute-start(bf16[64,1024]{1,0:T(8,128)(2,1)S(1)} %fusion.10.refs_4_), channel_id=1, source_target_pairs={{0,8},{4,12},{8,0},{12,4},{16,24},{20,28},{24,16},{28,20},{1,9},{5... | collective-permute-start | bytes 393224 | tf_op jit(solution)/shard_map/ppermute | solution.py:437
  92.5 2.0 %collective-permute-start.21 = (bf16[64,1024]{1,0:T(8,128)(2,1)S(1)}, bf16[64,1024]{1,0:T(8,128)(2,1)S(1)}, u32[]{:S(2)}, u32[]{:S(2)}) collective-permute-start(bf16[64,1024]{1,0:T(8,128)(2,1)S(1)} %collective-permute-done.20.refs_6_), channel_id=1, source_target_pairs={{0,8},{4,12},{8,0},{12,4},{16,24},{20,28},{24,16},{28,20},{1,9},{5... | collective-permute-start | bytes 393224 | tf_op jit(solution)/shard_map/ppermute | solution.py:437
  94.5 1.4 %collective-permute-start.22 = (bf16[64,1024]{1,0:T(8,128)(2,1)S(1)}, bf16[64,1024]{1,0:T(8,128)(2,1)S(1)}, u32[]{:S(2)}, u32[]{:S(2)}) collective-permute-start(bf16[64,1024]{1,0:T(8,128)(2,1)S(1)} %fusion.10.refs_4_), channel_id=1, source_target_pairs={{0,4},{4,0},{8,12},{12,8},{16,20},{20,16},{24,28},{28,24},{1,5},{5... | collective-permute-start | bytes 393224 | tf_op jit(solution)/shard_map/ppermute | solution.py:437
  95.9 0.6 collective-permute-done.19.refs_5_
  96.5 1.5 %collective-permute-start.23 = (bf16[64,1024]{1,0:T(8,128)(2,1)S(1)}, bf16[64,1024]{1,0:T(8,128)(2,1)S(1)}, u32[]{:S(2)}, u32[]{:S(2)}) collective-permute-start(bf16[64,1024]{1,0:T(8,128)(2,1)S(1)} %collective-permute-done.19.refs_5_), channel_id=1, source_target_pairs={{0,4},{4,0},{8,12},{12,8},{16,20},{20,16},{24,28},{28,24},{1,5},{5... | collective-permute-start | bytes 393224 | tf_op jit(solution)/shard_map/ppermute | solution.py:437
  98.0 1.4 %collective-permute-start.24 = (bf16[64,1024]{1,0:T(8,128)(2,1)S(1)}, bf16[64,1024]{1,0:T(8,128)(2,1)S(1)}, u32[]{:S(2)}, u32[]{:S(2)}) collective-permute-start(bf16[64,1024]{1,0:T(8,128)(2,1)S(1)} %collective-permute-done.20.refs_6_), channel_id=1, source_target_pairs={{0,4},{4,0},{8,12},{12,8},{16,20},{20,16},{24,28},{28,24},{1,5},{5... | collective-permute-start | bytes 393224 | tf_op jit(solution)/shard_map/ppermute | solution.py:437
  99.4 1.4 %collective-permute-start.25 = (bf16[64,1024]{1,0:T(8,128)(2,1)S(1)}, bf16[64,1024]{1,0:T(8,128)(2,1)S(1)}, u32[]{:S(2)}, u32[]{:S(2)}) collective-permute-start(bf16[64,1024]{1,0:T(8,128)(2,1)S(1)} %collective-permute-done.21.refs_7_), channel_id=1, source_target_pairs={{0,4},{4,0},{8,12},{12,8},{16,20},{20,16},{24,28},{28,24},{1,5},{5... | collective-permute-start | bytes 393224 | tf_op jit(solution)/shard_map/ppermute | solution.py:437
  100.9 1.4 %collective-permute-start.12 = (bf16[64,1024]{1,0:T(8,128)(2,1)S(1)}, bf16[64,1024]{1,0:T(8,128)(2,1)S(1)}, u32[]{:S(2)}, u32[]{:S(2)}) collective-permute-start(bf16[64,1024]{1,0:T(8,128)(2,1)S(1)} %fusion.9.refs_12_.refs_1_), channel_id=1, source_target_pairs={{0,4},{4,0},{8,12},{12,8},{16,20},{20,16},{24,28},{28,24},{1,5},{5... | collective-permute-start | bytes 393224 | tf_op jit(solution)/shard_map/ppermute | solution.py:437
  102.2 0.7 collective-permute-start.16
  102.9 0.8 collective-permute-done.23.refs_9_
  103.7 1.4 %collective-permute-start.14 = (bf16[64,1024]{1,0:T(8,128)(2,1)S(1)}, bf16[64,1024]{1,0:T(8,128)(2,1)S(1)}, u32[]{:S(2)}, u32[]{:S(2)}) collective-permute-start(bf16[64,1024]{1,0:T(8,128)(2,1)S(1)} %collective-permute-done.13.refs_13_.refs_2_), channel_id=1, source_target_pairs={{0,4},{4,0},{8,12},{12,8},{16,20},{20,16},{24,28},{28,24},{1,5},{5... | collective-permute-start | bytes 393224 | tf_op jit(solution)/shard_map/ppermute | solution.py:437
  105.0 1.4 %collective-permute-done.24.refs_10_ = bf16[64,1024]{1,0:T(8,128)(2,1)S(1)} collective-permute-done((bf16[64,1024]{1,0:T(8,128)(2,1)S(1)}, bf16[64,1024]{1,0:T(8,128)(2,1)S(1)}, u32[]{:S(2)}, u32[]{:S(2)}) %collective-permute-start.24) | collective-permute-done | bytes 131104 | tf_op jit(solution)/shard_map/ppermute | solution.py:437
  106.5 1.4 %collective-permute-start.18 = (bf16[64,1024]{1,0:T(8,128)(2,1)S(1)}, bf16[64,1024]{1,0:T(8,128)(2,1)S(1)}, u32[]{:S(2)}, u32[]{:S(2)}) collective-permute-start(bf16[64,1024]{1,0:T(8,128)(2,1)S(1)} %collective-permute-done.17.refs_15_.refs_4_), channel_id=1, source_target_pairs={{0,4},{4,0},{8,12},{12,8},{16,20},{20,16},{24,28},{28,24},{1,5},{5... | collective-permute-start | bytes 393224 | tf_op jit(solution)/shard_map/ppermute | solution.py:437
  107.8 1.4 %collective-permute-done.25.refs_11_ = bf16[64,1024]{1,0:T(8,128)(2,1)S(1)} collective-permute-done((bf16[64,1024]{1,0:T(8,128)(2,1)S(1)}, bf16[64,1024]{1,0:T(8,128)(2,1)S(1)}, u32[]{:S(2)}, u32[]{:S(2)}) %collective-permute-start.25) | collective-permute-done | bytes 131104 | tf_op jit(solution)/shard_map/ppermute | solution.py:437
  109.3 3.2 %finish.2 = (bf16[2,2,256,1024]{3,2,1,0:T(8,128)(2,1)}, bf16[2,256,128]{2,1,0:T(8,128)(2,1)S(1)}) custom-call(s32[8]{0:T(128)S(1)} %fusion.13.sky_ref, bf16[256,128]{1,0:T(8,128)(2,1)S(1)} %get-tuple-element.29.refs_0_.across_ref, bf16[256,1024]{1,0:T(8,128)(2,1)} %get-tuple-element.30.refs_1_, bf16[256,1024]{1,0:T(8,128)(2,1)} %get-tuple-element.31.refs_2_, ...), custom_call_target="tpu_custom_call" | custom-call | flops 786432 | bytes 4718592 | tf_op jit(solution)/shard_map/finish/pallas_call | solution.py:355
  112.5 1.4 %collective-permute-done.14.refs_2_.refs_6_ = bf16[64,1024]{1,0:T(8,128)(2,1)S(1)} collective-permute-done((bf16[64,1024]{1,0:T(8,128)(2,1)S(1)}, bf16[64,1024]{1,0:T(8,128)(2,1)S(1)}, u32[]{:S(2)}, u32[]{:S(2)}) %collective-permute-start.14) | collective-permute-done | bytes 131104 | tf_op jit(solution)/shard_map/ppermute | solution.py:437
  113.9 1.4 %collective-permute-done.18.refs_4_.refs_8_ = bf16[64,1024]{1,0:T(8,128)(2,1)S(1)} collective-permute-done((bf16[64,1024]{1,0:T(8,128)(2,1)S(1)}, bf16[64,1024]{1,0:T(8,128)(2,1)S(1)}, u32[]{:S(2)}, u32[]{:S(2)}) %collective-permute-start.18) | collective-permute-done | bytes 131104 | tf_op jit(solution)/shard_map/ppermute | solution.py:437
  115.3 0.6 power.1
  116.0 1.6 %collective-permute-start.27 = (bf16[256,128]{1,0:T(8,128)(2,1)S(1)}, bf16[256,128]{1,0:T(8,128)(2,1)S(1)}, u32[]{:S(2)}, u32[]{:S(2)}) collective-permute-start(bf16[256,128]{1,0:T(8,128)(2,1)S(1)} %get-tuple-element.38), channel_id=1, source_target_pairs={{0,2},{1,3},{2,0},{3,1},{4,6},{5,7},{6,4},{7,5},{8,10},{9,11},{10,... | collective-permute-start | bytes 196616 | tf_op jit(solution)/shard_map/ppermute | solution.py:517
  117.6 1.4 %collective-permute-start.28 = (bf16[256,128]{1,0:T(8,128)(2,1)S(1)}, bf16[256,128]{1,0:T(8,128)(2,1)S(1)}, u32[]{:S(2)}, u32[]{:S(2)}) collective-permute-start(bf16[256,128]{1,0:T(8,128)(2,1)S(1)} %get-tuple-element.39), channel_id=1, source_target_pairs={{0,3},{1,0},{2,1},{3,2},{4,7},{5,4},{6,5},{7,6},{8,11},{9,8},{10,9... | collective-permute-start | bytes 196616 | tf_op jit(solution)/shard_map/ppermute | solution.py:517
  119.0 2.1 %finish.3 = bf16[2,2,256,1024]{3,2,1,0:T(8,128)(2,1)} custom-call(s32[8]{0:T(128)S(1)} %fusion.13.sky_ref, bf16[256,1024]{1,0:T(8,128)(2,1)} %get-tuple-element.23.refs_0_, bf16[64,1024]{1,0:T(8,128)(2,1)S(1)} %collective-permute-done.12.refs_1_.refs_5_, ...), custom_call_target="tpu_custom_call", output_to_operand_aliasing={{}: (6, {})} | custom-call | flops 262144 | bytes 1572864 | tf_op jit(solution)/shard_map/finish/pallas_call | solution.py:355
  121.1 0.7 convert_add_fusion.3
  (23 shorter events, 0.4 us)
Async XLA Ops:
  11.4 26.8 %collective-permute-start.3 = (bf16[256,1024]{1,0:T(8,128)(2,1)}, bf16[256,1024]{1,0:T(8,128)(2,1)}, u32[]{:S(2)}, u32[]{:S(2)}) collective-permute-start(bf16[256,1024]{1,0:T(8,128)(2,1)} %get-tuple-element.27), channel_id=1, source_target_pairs={{0,4},{4,0},{8,12},{12,8},{16,20},{20,16},{24,28},{28,24},{1,5},{5... | collective-permute-start | bytes 1572872 | tf_op jit(solution)/shard_map/ppermute | solution.py:437
  14.4 25.3 %collective-permute-start.6 = (bf16[256,1024]{1,0:T(8,128)(2,1)S(1)}, bf16[256,1024]{1,0:T(8,128)(2,1)}, u32[]{:S(2)}, u32[]{:S(2)}) collective-permute-start(bf16[256,1024]{1,0:T(8,128)(2,1)S(1)} %bitcast.27), channel_id=1, source_target_pairs={{0,4},{4,0},{8,12},{12,8},{16,20},{20,16},{24,28},{28,24},{1,5},{5... | collective-permute-start | bytes 1572872 | tf_op jit(solution)/shard_map/ppermute | solution.py:437
  22.2 26.9 %collective-permute-start = (bf16[256,1024]{1,0:T(8,128)(2,1)}, bf16[256,1024]{1,0:T(8,128)(2,1)}, u32[]{:S(2)}, u32[]{:S(2)}) collective-permute-start(bf16[256,1024]{1,0:T(8,128)(2,1)} %get-tuple-element.25), channel_id=1, source_target_pairs={{0,4},{4,0},{8,12},{12,8},{16,20},{20,16},{24,28},{28,24},{1,5},{5... | collective-permute-start | bytes 1572872 | tf_op jit(solution)/shard_map/ppermute | solution.py:437
  25.0 26.9 %collective-permute-start.9 = (bf16[2,128,1024]{2,1,0:T(8,128)(2,1)}, bf16[2,128,1024]{2,1,0:T(8,128)(2,1)S(1)}, u32[]{:S(2)}, u32[]{:S(2)}) collective-permute-start(bf16[2,128,1024]{2,1,0:T(8,128)(2,1)} %constant_dynamic-slice_fusion), channel_id=1, source_target_pairs={{0,8},{4,12},{8,0},{12,4},{16,24},{20,28},{24,16},{28,20},{1,9},{5... | collective-permute-start | bytes 1572872 | tf_op jit(solution)/shard_map/ppermute | solution.py:437
  39.2 15.6 %collective-permute-start.4 = (bf16[128,1024]{1,0:T(8,128)(2,1)S(1)}, bf16[128,1024]{1,0:T(8,128)(2,1)S(1)}, u32[]{:S(2)}, u32[]{:S(2)}) collective-permute-start(bf16[128,1024]{1,0:T(8,128)(2,1)S(1)} %add_convert_fusion.1), channel_id=1, source_target_pairs={{0,8},{4,12},{8,0},{12,4},{16,24},{20,28},{24,16},{28,20},{1,9},{5... | collective-permute-start | bytes 786440 | tf_op jit(solution)/shard_map/ppermute | solution.py:437
  40.7 15.5 %collective-permute-start.7 = (bf16[128,1024]{1,0:T(8,128)(2,1)S(1)}, bf16[128,1024]{1,0:T(8,128)(2,1)S(1)}, u32[]{:S(2)}, u32[]{:S(2)}) collective-permute-start(bf16[128,1024]{1,0:T(8,128)(2,1)S(1)} %fusion), channel_id=1, source_target_pairs={{0,8},{4,12},{8,0},{12,4},{16,24},{20,28},{24,16},{28,20},{1,9},{5... | collective-permute-start | bytes 786440 | tf_op jit(solution)/shard_map/ppermute | solution.py:437
  50.1 12.9 %collective-permute-start.1 = (bf16[128,1024]{1,0:T(8,128)(2,1)S(1)}, bf16[128,1024]{1,0:T(8,128)(2,1)S(1)}, u32[]{:S(2)}, u32[]{:S(2)}) collective-permute-start(bf16[128,1024]{1,0:T(8,128)(2,1)S(1)} %add_convert_fusion.2), channel_id=1, source_target_pairs={{0,8},{4,12},{8,0},{12,4},{16,24},{20,28},{24,16},{28,20},{1,9},{5... | collective-permute-start | bytes 786440 | tf_op jit(solution)/shard_map/ppermute | solution.py:437
  52.1 24.2 %collective-permute-start.10 = (bf16[2,64,1024]{2,1,0:T(8,128)(2,1)S(1)}, bf16[2,64,1024]{2,1,0:T(8,128)(2,1)S(1)}, u32[]{:S(2)}, u32[]{:S(2)}) collective-permute-start(bf16[2,64,1024]{2,1,0:T(8,128)(2,1)S(1)} %add_convert_fusion), channel_id=1, source_target_pairs={{0,16},{4,20},{8,24},{12,28},{16,0},{20,4},{24,8},{28,12},{1,17},{... | collective-permute-start | bytes 786440 | tf_op jit(solution)/shard_map/ppermute | solution.py:437
  55.8 23.3 %collective-permute-start.5 = (bf16[64,1024]{1,0:T(8,128)(2,1)S(1)}, bf16[64,1024]{1,0:T(8,128)(2,1)S(1)}, u32[]{:S(2)}, u32[]{:S(2)}) collective-permute-start(bf16[64,1024]{1,0:T(8,128)(2,1)S(1)} %add_convert_fusion.4), channel_id=1, source_target_pairs={{0,16},{4,20},{8,24},{12,28},{16,0},{20,4},{24,8},{28,12},{1,17},{... | collective-permute-start | bytes 393224 | tf_op jit(solution)/shard_map/ppermute | solution.py:437
  57.2 23.9 %collective-permute-start.8 = (bf16[64,1024]{1,0:T(8,128)(2,1)S(1)}, bf16[64,1024]{1,0:T(8,128)(2,1)S(1)}, u32[]{:S(2)}, u32[]{:S(2)}) collective-permute-start(bf16[64,1024]{1,0:T(8,128)(2,1)S(1)} %fusion.2), channel_id=1, source_target_pairs={{0,16},{4,20},{8,24},{12,28},{16,0},{20,4},{24,8},{28,12},{1,17},{... | collective-permute-start | bytes 393224 | tf_op jit(solution)/shard_map/ppermute | solution.py:437
  64.1 20.0 %collective-permute-start.2 = (bf16[64,1024]{1,0:T(8,128)(2,1)S(1)}, bf16[64,1024]{1,0:T(8,128)(2,1)S(1)}, u32[]{:S(2)}, u32[]{:S(2)}) collective-permute-start(bf16[64,1024]{1,0:T(8,128)(2,1)S(1)} %add_convert_fusion.5), channel_id=1, source_target_pairs={{0,16},{4,20},{8,24},{12,28},{16,0},{20,4},{24,8},{28,12},{1,17},{... | collective-permute-start | bytes 393224 | tf_op jit(solution)/shard_map/ppermute | solution.py:437
  76.4 7.7 %collective-permute-start.11 = (bf16[64,1024]{1,0:T(8,128)(2,1)S(1)}, bf16[64,1024]{1,0:T(8,128)(2,1)S(1)}, u32[]{:S(2)}, u32[]{:S(2)}) collective-permute-start(bf16[64,1024]{1,0:T(8,128)(2,1)S(1)} %fusion.11), channel_id=1, source_target_pairs={{0,4},{4,0},{8,12},{12,8},{16,20},{20,16},{24,28},{28,24},{1,5},{5... | collective-permute-start | bytes 393224 | tf_op jit(solution)/shard_map/ppermute | solution.py:437
  82.3 10.2 %collective-permute-start.20 = (bf16[64,1024]{1,0:T(8,128)(2,1)S(1)}, bf16[64,1024]{1,0:T(8,128)(2,1)S(1)}, u32[]{:S(2)}, u32[]{:S(2)}) collective-permute-start(bf16[64,1024]{1,0:T(8,128)(2,1)S(1)} %fusion.10.refs_4_), channel_id=1, source_target_pairs={{0,16},{4,20},{8,24},{12,28},{16,0},{20,4},{24,8},{28,12},{1,17},{... | collective-permute-start | bytes 393224 | tf_op jit(solution)/shard_map/ppermute | solution.py:437
  85.2 10.7 %collective-permute-start.15 = (bf16[64,1024]{1,0:T(8,128)(2,1)S(1)}, bf16[64,1024]{1,0:T(8,128)(2,1)S(1)}, u32[]{:S(2)}, u32[]{:S(2)}) collective-permute-start(bf16[64,1024]{1,0:T(8,128)(2,1)S(1)} %fusion.9.refs_12_.refs_1_), channel_id=1, source_target_pairs={{0,16},{4,20},{8,24},{12,28},{16,0},{20,4},{24,8},{28,12},{1,17},{... | collective-permute-start | bytes 393224 | tf_op jit(solution)/shard_map/ppermute | solution.py:437
  86.5 10.0 %collective-permute-start.19 = (bf16[64,1024]{1,0:T(8,128)(2,1)S(1)}, bf16[64,1024]{1,0:T(8,128)(2,1)S(1)}, u32[]{:S(2)}, u32[]{:S(2)}) collective-permute-start(bf16[64,1024]{1,0:T(8,128)(2,1)S(1)} %fusion.10.refs_4_), channel_id=1, source_target_pairs={{0,8},{4,12},{8,0},{12,4},{16,24},{20,28},{24,16},{28,20},{1,9},{5... | collective-permute-start | bytes 393224 | tf_op jit(solution)/shard_map/ppermute | solution.py:437
  92.5 5.6 %collective-permute-start.13 = (bf16[64,1024]{1,0:T(8,128)(2,1)S(1)}, bf16[64,1024]{1,0:T(8,128)(2,1)S(1)}, u32[]{:S(2)}, u32[]{:S(2)}) collective-permute-start(bf16[64,1024]{1,0:T(8,128)(2,1)S(1)} %fusion.9.refs_12_.refs_1_), channel_id=1, source_target_pairs={{0,8},{4,12},{8,0},{12,4},{16,24},{20,28},{24,16},{28,20},{1,9},{5... | collective-permute-start | bytes 393224 | tf_op jit(solution)/shard_map/ppermute | solution.py:437
  92.5 7.0 %collective-permute-start.21 = (bf16[64,1024]{1,0:T(8,128)(2,1)S(1)}, bf16[64,1024]{1,0:T(8,128)(2,1)S(1)}, u32[]{:S(2)}, u32[]{:S(2)}) collective-permute-start(bf16[64,1024]{1,0:T(8,128)(2,1)S(1)} %collective-permute-done.20.refs_6_), channel_id=1, source_target_pairs={{0,8},{4,12},{8,0},{12,4},{16,24},{20,28},{24,16},{28,20},{1,9},{5... | collective-permute-start | bytes 393224 | tf_op jit(solution)/shard_map/ppermute | solution.py:437
  94.5 6.4 %collective-permute-start.22 = (bf16[64,1024]{1,0:T(8,128)(2,1)S(1)}, bf16[64,1024]{1,0:T(8,128)(2,1)S(1)}, u32[]{:S(2)}, u32[]{:S(2)}) collective-permute-start(bf16[64,1024]{1,0:T(8,128)(2,1)S(1)} %fusion.10.refs_4_), channel_id=1, source_target_pairs={{0,4},{4,0},{8,12},{12,8},{16,20},{20,16},{24,28},{28,24},{1,5},{5... | collective-permute-start | bytes 393224 | tf_op jit(solution)/shard_map/ppermute | solution.py:437
  95.9 6.4 %collective-permute-start.17 = (bf16[64,1024]{1,0:T(8,128)(2,1)S(1)}, bf16[64,1024]{1,0:T(8,128)(2,1)S(1)}, u32[]{:S(2)}, u32[]{:S(2)}) collective-permute-start(bf16[64,1024]{1,0:T(8,128)(2,1)S(1)} %collective-permute-done.15.refs_14_.refs_3_), channel_id=1, source_target_pairs={{0,8},{4,12},{8,0},{12,4},{16,24},{20,28},{24,16},{28,20},{1,9},{5... | collective-permute-start | bytes 393224 | tf_op jit(solution)/shard_map/ppermute | solution.py:437
  96.5 7.1 %collective-permute-start.23 = (bf16[64,1024]{1,0:T(8,128)(2,1)S(1)}, bf16[64,1024]{1,0:T(8,128)(2,1)S(1)}, u32[]{:S(2)}, u32[]{:S(2)}) collective-permute-start(bf16[64,1024]{1,0:T(8,128)(2,1)S(1)} %collective-permute-done.19.refs_5_), channel_id=1, source_target_pairs={{0,4},{4,0},{8,12},{12,8},{16,20},{20,16},{24,28},{28,24},{1,5},{5... | collective-permute-start | bytes 393224 | tf_op jit(solution)/shard_map/ppermute | solution.py:437
  98.0 8.4 %collective-permute-start.24 = (bf16[64,1024]{1,0:T(8,128)(2,1)S(1)}, bf16[64,1024]{1,0:T(8,128)(2,1)S(1)}, u32[]{:S(2)}, u32[]{:S(2)}) collective-permute-start(bf16[64,1024]{1,0:T(8,128)(2,1)S(1)} %collective-permute-done.20.refs_6_), channel_id=1, source_target_pairs={{0,4},{4,0},{8,12},{12,8},{16,20},{20,16},{24,28},{28,24},{1,5},{5... | collective-permute-start | bytes 393224 | tf_op jit(solution)/shard_map/ppermute | solution.py:437
  99.4 9.8 %collective-permute-start.25 = (bf16[64,1024]{1,0:T(8,128)(2,1)S(1)}, bf16[64,1024]{1,0:T(8,128)(2,1)S(1)}, u32[]{:S(2)}, u32[]{:S(2)}) collective-permute-start(bf16[64,1024]{1,0:T(8,128)(2,1)S(1)} %collective-permute-done.21.refs_7_), channel_id=1, source_target_pairs={{0,4},{4,0},{8,12},{12,8},{16,20},{20,16},{24,28},{28,24},{1,5},{5... | collective-permute-start | bytes 393224 | tf_op jit(solution)/shard_map/ppermute | solution.py:437
  100.9 11.7 %collective-permute-start.12 = (bf16[64,1024]{1,0:T(8,128)(2,1)S(1)}, bf16[64,1024]{1,0:T(8,128)(2,1)S(1)}, u32[]{:S(2)}, u32[]{:S(2)}) collective-permute-start(bf16[64,1024]{1,0:T(8,128)(2,1)S(1)} %fusion.9.refs_12_.refs_1_), channel_id=1, source_target_pairs={{0,4},{4,0},{8,12},{12,8},{16,20},{20,16},{24,28},{28,24},{1,5},{5... | collective-permute-start | bytes 393224 | tf_op jit(solution)/shard_map/ppermute | solution.py:437
  102.2 11.7 %collective-permute-start.16 = (bf16[64,1024]{1,0:T(8,128)(2,1)S(1)}, bf16[64,1024]{1,0:T(8,128)(2,1)S(1)}, u32[]{:S(2)}, u32[]{:S(2)}) collective-permute-start(bf16[64,1024]{1,0:T(8,128)(2,1)S(1)} %collective-permute-done.15.refs_14_.refs_3_), channel_id=1, source_target_pairs={{0,4},{4,0},{8,12},{12,8},{16,20},{20,16},{24,28},{28,24},{1,5},{5... | collective-permute-start | bytes 393224 | tf_op jit(solution)/shard_map/ppermute | solution.py:437
  103.7 10.2 %collective-permute-start.14 = (bf16[64,1024]{1,0:T(8,128)(2,1)S(1)}, bf16[64,1024]{1,0:T(8,128)(2,1)S(1)}, u32[]{:S(2)}, u32[]{:S(2)}) collective-permute-start(bf16[64,1024]{1,0:T(8,128)(2,1)S(1)} %collective-permute-done.13.refs_13_.refs_2_), channel_id=1, source_target_pairs={{0,4},{4,0},{8,12},{12,8},{16,20},{20,16},{24,28},{28,24},{1,5},{5... | collective-permute-start | bytes 393224 | tf_op jit(solution)/shard_map/ppermute | solution.py:437
  106.5 8.8 %collective-permute-start.18 = (bf16[64,1024]{1,0:T(8,128)(2,1)S(1)}, bf16[64,1024]{1,0:T(8,128)(2,1)S(1)}, u32[]{:S(2)}, u32[]{:S(2)}) collective-permute-start(bf16[64,1024]{1,0:T(8,128)(2,1)S(1)} %collective-permute-done.17.refs_15_.refs_4_), channel_id=1, source_target_pairs={{0,4},{4,0},{8,12},{12,8},{16,20},{20,16},{24,28},{28,24},{1,5},{5... | collective-permute-start | bytes 393224 | tf_op jit(solution)/shard_map/ppermute | solution.py:437
  115.9 5.1 %collective-permute-start.26 = (bf16[256,128]{1,0:T(8,128)(2,1)S(1)}, bf16[256,128]{1,0:T(8,128)(2,1)S(1)}, u32[]{:S(2)}, u32[]{:S(2)}) collective-permute-start(bf16[256,128]{1,0:T(8,128)(2,1)S(1)} %get-tuple-element.37), channel_id=1, source_target_pairs={{0,1},{1,2},{2,3},{3,0},{4,5},{5,6},{6,7},{7,4},{8,9},{9,10},{10,1... | collective-permute-start | bytes 196616 | tf_op jit(solution)/shard_map/ppermute | solution.py:517
  116.0 5.1 %collective-permute-start.27 = (bf16[256,128]{1,0:T(8,128)(2,1)S(1)}, bf16[256,128]{1,0:T(8,128)(2,1)S(1)}, u32[]{:S(2)}, u32[]{:S(2)}) collective-permute-start(bf16[256,128]{1,0:T(8,128)(2,1)S(1)} %get-tuple-element.38), channel_id=1, source_target_pairs={{0,2},{1,3},{2,0},{3,1},{4,6},{5,7},{6,4},{7,5},{8,10},{9,11},{10,... | collective-permute-start | bytes 196616 | tf_op jit(solution)/shard_map/ppermute | solution.py:517
  117.6 3.5 %collective-permute-start.28 = (bf16[256,128]{1,0:T(8,128)(2,1)S(1)}, bf16[256,128]{1,0:T(8,128)(2,1)S(1)}, u32[]{:S(2)}, u32[]{:S(2)}) collective-permute-start(bf16[256,128]{1,0:T(8,128)(2,1)S(1)} %get-tuple-element.39), channel_id=1, source_target_pairs={{0,3},{1,0},{2,1},{3,2},{4,7},{5,4},{6,5},{7,6},{8,11},{9,8},{10,9... | collective-permute-start | bytes 196616 | tf_op jit(solution)/shard_map/ppermute | solution.py:517
